TPU v7x, 32 devices: a whole 2x2x4 slice. The times are simulated.
32 devices in a mesh: ctx: 4 (over y, x), exp: 8 (over z, core).
Axes of the slice: x: 2, y: 2, z: 4, core: 2. Of those that a mesh axis runs over, the one named last changes fastest.
Arguments:
- inputs: bfloat16 [4, 6144, 768], P('ctx', 'exp'), may hold values from -6 to 6
- prev_logits: float32 [4, 6144, 12], P('ctx', 'exp'), may hold values from -4 to 4
- routes: int32 [4, 6144, 2], P('ctx', 'exp'), may hold values from 0 to 11, all different within a row; in each aligned block of 768 rows (0 to 767, 768 to 1535, ..., all dimensions but the last counted through in order) at most 144 rows name the same one
- attn_gain: float32 [768], replicated, may hold values from 0.25 to 1.75
- w_qkv: bfloat16 [768, 2304], replicated, may hold values from -0.21875 to 0.21875
- w_out: bfloat16 [768, 768], replicated, may hold values from -0.875 to 0.875
- moe_gain: float32 [768], replicated, may hold values from 0.25 to 1.75
- router: bfloat16 [768, 12], replicated, may hold values from -0.109375 to 0.109375
- const_gate: bfloat16 [2, 768, 2], replicated, may hold values from -0.21875 to 0.21875
- const_vec: float32 [2, 768], replicated, may hold values from -12 to 12
- w_gate: bfloat16 [8, 768, 2048], P('exp'), may hold values from -0.21875 to 0.21875
- w_up: bfloat16 [8, 768, 2048], P('exp'), may hold values from -0.21875 to 0.21875
- w_down: bfloat16 [8, 2048, 768], P('exp'), may hold values from -1.5 to 1.5
- out_grad: bfloat16 [4, 6144, 768], P('ctx', 'exp'), may hold values from -6 to 6
Outputs:
- mixed_out: bfloat16 [4, 6144, 768], P('ctx', 'exp')
- d_inputs: float32 [4, 6144, 768], P('ctx', 'exp')
- d_prev: float32 [4, 6144, 12], P('ctx', 'exp')
- d_attn_gain: float32 [768], replicated
- d_w_qkv: float32 [768, 2304], replicated
- d_w_out: float32 [768, 768], replicated
- d_moe_gain: float32 [768], replicated
- d_router: float32 [768, 12], replicated
- d_const_gate: float32 [2, 768, 2], replicated
- d_const_vec: float32 [2, 768], replicated
- d_w_gate: float32 [8, 768, 2048], P('exp', 'ctx')
- d_w_up: float32 [8, 768, 2048], P('exp', 'ctx')
- d_w_down: float32 [8, 2048, 768], P('exp', 'ctx')
Inputs may be any that keep to these rules, and one draw needn't show every extreme that they name: `routes`: each row names two different experts. Among the 768 rows of one device no expert is named by more than 144 rows, and on some devices one is named by exactly 144.
All inputs are finite; a program needn't handle non-finite values.
Results may differ from a plain program's by a relative error of at most 0.015.
Values may be sent and summed in bfloat16 or wider, within the bound.
No kernel may reach another device: no remote copies, remote signals or barrier semaphores. Data moves between devices by JAX's collectives and lax.ppermute only.
A program may use at most 256 MiB of HBM per device.

v0:
```python
from functools import partial

import jax
import jax.numpy as jnp
from jax import lax
from jax.sharding import PartitionSpec as P

HEADS = 12
HEAD_DIM = 64
FFN_EXPERTS = 8
ALL_EXPERTS = 12
CONT_LEN = 512


masked_value = -1e30
epsilon = 1e-06
highest = lax.Precision.HIGHEST


def rms_forward(tensor, gain_vec):
    inverse = lax.rsqrt(jnp.mean(tensor * tensor, axis=-1, keepdims=True) + epsilon)
    return (tensor * inverse * gain_vec, inverse)


def rms_backward(tensor, inverse, gain_vec, upstream):
    scaled = upstream * gain_vec
    d_gain = jnp.sum(upstream * tensor * inverse, axis=0)
    d_tensor = inverse * scaled - tensor * inverse**3 * jnp.mean(
        scaled * tensor, axis=-1, keepdims=True
    )
    return (d_tensor, d_gain)


def route_slots(route_rows):
    flat_ids = route_rows.reshape(-1)
    onehot = (flat_ids[:, None] == jnp.arange(ALL_EXPERTS, dtype=jnp.int32)[None, :]).astype(
        jnp.int32
    )
    before = jnp.cumsum(onehot, axis=0) - onehot
    return jnp.sum(before * onehot, axis=1).reshape(route_rows.shape)


def split_heads(tensor):
    reshaped = tensor.reshape(tensor.shape[:-1] + (HEADS, HEAD_DIM))
    return jnp.moveaxis(reshaped, -2, 0)


def join_heads(tensor):
    moved_axes = jnp.moveaxis(tensor, 0, -2)
    return moved_axes.reshape(moved_axes.shape[:-2] + (HEADS * HEAD_DIM,))


def head_forward(allowed, operands):
    queries, key_rows, value_rows = operands
    raw_scores = jnp.einsum(
        "qd,kd->qk", queries, key_rows, preferred_element_type=jnp.float32
    ) * HEAD_DIM ** (-0.5)
    masked = jnp.where(allowed, raw_scores, masked_value)
    row_peak = jnp.max(masked, axis=-1, keepdims=True)
    unnormed = jnp.exp(masked - row_peak)
    row_total = jnp.sum(unnormed, axis=-1, keepdims=True)
    weights_soft = (unnormed / row_total).astype(jnp.bfloat16)
    result = jnp.einsum("qk,kd->qd", weights_soft, value_rows, preferred_element_type=jnp.float32)
    return (result, row_peak[..., 0] + jnp.log(row_total[..., 0]))


def head_backward(allowed, operands):
    queries, key_rows, value_rows, upstream, log_total = operands
    raw_scores = jnp.einsum(
        "qd,kd->qk", queries, key_rows, preferred_element_type=jnp.float32
    ) * HEAD_DIM ** (-0.5)
    masked = jnp.where(allowed, raw_scores, masked_value)
    probs_full = jnp.where(allowed, jnp.exp(masked - log_total[..., None]), 0.0)
    d_values = jnp.einsum(
        "qk,qd->kd", probs_full.astype(jnp.bfloat16), upstream, preferred_element_type=jnp.float32
    )
    d_probs = jnp.einsum("qd,kd->qk", upstream, value_rows, preferred_element_type=jnp.float32)
    d_scores = probs_full * (d_probs - jnp.sum(probs_full * d_probs, axis=-1, keepdims=True))
    d_scores = d_scores.astype(jnp.bfloat16)
    d_queries = jnp.einsum(
        "qk,kd->qd", d_scores, key_rows, preferred_element_type=jnp.float32
    ) * HEAD_DIM ** (-0.5)
    d_keys = jnp.einsum(
        "qk,qd->kd", d_scores, queries, preferred_element_type=jnp.float32
    ) * HEAD_DIM ** (-0.5)
    return (d_queries, d_keys, d_values)


def body(
    inputs,
    prev_logits,
    routes,
    attn_gain,
    w_qkv,
    w_out,
    moe_gain,
    router,
    const_gate,
    const_vec,
    w_gate,
    w_up,
    w_down,
    out_grad,
):
    model_width = inputs.shape[2]
    tok_rows = inputs.shape[1]
    prompt_local = tok_rows - CONT_LEN
    prompt_len = prompt_local * lax.axis_size("ctx")
    split_parts = lax.axis_size("exp") // FFN_EXPERTS
    capacity = max(4, tok_rows // 64 * 12)
    tokens_in = inputs[0].astype(jnp.float32)
    normed_attn, inverse_attn = rms_forward(tokens_in, attn_gain)
    act_low = normed_attn.astype(jnp.bfloat16)
    projected = jnp.dot(act_low, w_qkv, preferred_element_type=jnp.float32).astype(jnp.bfloat16)
    queries = projected[:, :model_width]
    kv_local = projected[:prompt_local, model_width:]
    own_kv = projected[prompt_local:, model_width:]
    gathered = lax.all_gather(kv_local, "ctx", axis=0, tiled=True)
    row_index = jnp.arange(tok_rows, dtype=jnp.int32)
    query_pos = lax.axis_index("ctx") * prompt_local + row_index
    cont_pos = row_index - prompt_local
    key_index = jnp.arange(prompt_len + CONT_LEN, dtype=jnp.int32)
    in_prompt = key_index[None, :] < prompt_len
    prompt_mask = in_prompt & (key_index[None, :] <= query_pos[:, None])
    cont_mask = in_prompt | (key_index[None, :] - prompt_len <= cont_pos[:, None])
    allowed = jnp.where((row_index < prompt_local)[:, None], prompt_mask, cont_mask)
    all_kv = jnp.concatenate([gathered, own_kv], axis=0)
    heads_out, row_lse = lax.map(
        partial(head_forward, allowed),
        (
            split_heads(queries),
            split_heads(all_kv[:, :model_width]),
            split_heads(all_kv[:, model_width:]),
        ),
    )
    mixed_low = join_heads(heads_out).astype(jnp.bfloat16)
    hidden = tokens_in + jnp.dot(mixed_low, w_out, preferred_element_type=jnp.float32)
    normed_moe, inverse_moe = rms_forward(hidden, moe_gain)
    moe_low = normed_moe.astype(jnp.bfloat16)
    logits = jnp.dot(moe_low, router, preferred_element_type=jnp.float32) + prev_logits[0]
    route_ids = routes[0]
    probs_all = jax.nn.softmax(logits, axis=-1)
    gate_values = jnp.take_along_axis(probs_all, route_ids, axis=-1)
    const_logits = jnp.einsum(
        "td,cda->tca", moe_low, const_gate, preferred_element_type=jnp.float32
    )
    alphas = jax.nn.softmax(const_logits, axis=-1)
    const_out = alphas[..., 0:1] * normed_moe[:, None, :] + alphas[..., 1:2] * const_vec[None]
    slot_index = route_slots(route_ids)
    is_ffn = route_ids < FFN_EXPERTS
    expert_ids = jnp.where(is_ffn, route_ids, FFN_EXPERTS)
    token_ids = jnp.broadcast_to(jnp.arange(tok_rows, dtype=jnp.int32)[:, None], route_ids.shape)
    dispatch = (
        jnp.full((FFN_EXPERTS, capacity), tok_rows, jnp.int32)
        .at[expert_ids, slot_index]
        .set(token_ids, mode="drop")
    )
    padded = jnp.concatenate([moe_low, jnp.zeros((1, model_width), jnp.bfloat16)], axis=0)
    dealt = padded[dispatch]
    received = lax.all_to_all(
        jnp.repeat(dealt, split_parts, axis=0), "exp", split_axis=0, concat_axis=0, tiled=True
    )
    leading = received.shape[:2]
    flat_rows = received.reshape(-1, model_width)
    gate_pre = jnp.dot(flat_rows, w_gate[0], preferred_element_type=jnp.float32)
    up_pre = jnp.dot(flat_rows, w_up[0], preferred_element_type=jnp.float32)
    inner_act = (jax.nn.silu(gate_pre) * up_pre).astype(jnp.bfloat16)
    partial_out = jnp.dot(inner_act, w_down[0], preferred_element_type=jnp.float32).astype(
        jnp.bfloat16
    )
    partial_out, kept_rows, gate_kept, up_kept = (
        partial_out.reshape(leading + (model_width,)),
        received,
        gate_pre.reshape(leading + (-1,)),
        up_pre.reshape(leading + (-1,)),
    )
    returned = lax.all_to_all(partial_out, "exp", split_axis=0, concat_axis=0, tiled=True)
    expert_out = jnp.sum(
        returned.reshape(FFN_EXPERTS, split_parts, capacity, model_width).astype(jnp.float32),
        axis=1,
    )
    position = expert_ids * capacity + slot_index
    picked = jnp.where(
        is_ffn[..., None], expert_out.reshape(-1, model_width)[jnp.where(is_ffn, position, 0)], 0.0
    )
    selected = picked + jnp.where(
        (route_ids == FFN_EXPERTS + 1)[..., None], normed_moe[:, None, :], 0.0
    )
    selected = selected + jnp.where(
        (route_ids == FFN_EXPERTS + 2)[..., None], const_out[:, 0:1], 0.0
    )
    selected = selected + jnp.where(
        (route_ids == FFN_EXPERTS + 3)[..., None], const_out[:, 1:2], 0.0
    )
    mixed_out = (hidden + jnp.sum(gate_values[..., None] * selected, axis=1)).astype(jnp.bfloat16)[
        None
    ]
    upstream = out_grad[0].astype(jnp.float32)
    d_gate_values = jnp.sum(upstream[:, None, :] * selected, axis=-1)
    weighted = gate_values[..., None] * upstream[:, None, :]
    flat_position = jnp.where(is_ffn, position, FFN_EXPERTS * capacity)
    d_expert = (
        jnp.zeros((FFN_EXPERTS * capacity, model_width), jnp.float32)
        .at[flat_position]
        .set(weighted, mode="drop")
    )
    d_expert_low = d_expert.astype(jnp.bfloat16).reshape(FFN_EXPERTS, capacity, model_width)
    incoming_grad = lax.all_to_all(
        jnp.repeat(d_expert_low, split_parts, axis=0),
        "exp",
        split_axis=0,
        concat_axis=0,
        tiled=True,
    )
    flat_rows = kept_rows.reshape(-1, model_width)
    flat_grad = incoming_grad.reshape(-1, model_width)
    gate_flat = gate_kept.reshape(flat_rows.shape[0], -1)
    up_flat = up_kept.reshape(flat_rows.shape[0], -1)
    sigmoid_gate = jax.nn.sigmoid(gate_flat)
    silu_gate = gate_flat * sigmoid_gate
    inner_act = (silu_gate * up_flat).astype(jnp.bfloat16)
    d_inner = jnp.dot(flat_grad, w_down[0].T, preferred_element_type=jnp.float32)
    d_w_down_local = jnp.dot(inner_act.T, flat_grad, preferred_element_type=jnp.float32)
    d_gate_pre = (
        d_inner * up_flat * sigmoid_gate * (1.0 + gate_flat * (1.0 - sigmoid_gate))
    ).astype(jnp.bfloat16)
    d_up_pre = (d_inner * silu_gate).astype(jnp.bfloat16)
    d_w_gate_local = jnp.dot(flat_rows.T, d_gate_pre, preferred_element_type=jnp.float32)
    d_w_up_local = jnp.dot(flat_rows.T, d_up_pre, preferred_element_type=jnp.float32)
    gate_up_local = jnp.stack([d_w_gate_local, d_w_up_local])[None]
    down_local = d_w_down_local[None]
    d_rows = jnp.dot(d_gate_pre, w_gate[0].T, preferred_element_type=jnp.float32) + jnp.dot(
        d_up_pre, w_up[0].T, preferred_element_type=jnp.float32
    )
    row_grads = lax.all_to_all(
        d_rows.reshape(kept_rows.shape).astype(jnp.bfloat16),
        "exp",
        split_axis=0,
        concat_axis=0,
        tiled=True,
    ).astype(jnp.float32)
    d_dispatch = jnp.sum(row_grads.reshape(FFN_EXPERTS, split_parts, capacity, model_width), axis=1)
    expert_sums = (
        lax.psum_scatter(
            gate_up_local.astype(jnp.bfloat16), "ctx", scatter_dimension=2, tiled=True
        ).astype(jnp.float32),
        lax.psum_scatter(
            down_local.astype(jnp.bfloat16), "ctx", scatter_dimension=1, tiled=True
        ).astype(jnp.float32),
    )
    total_gate_up = expert_sums[0][0]
    total_down = expert_sums[1][0]
    d_moe_low = (
        jnp.zeros((tok_rows + 1, model_width), jnp.float32).at[dispatch].add(d_dispatch)[:tok_rows]
    )
    onehot_routes = (route_ids[..., None] == jnp.arange(ALL_EXPERTS, dtype=jnp.int32)).astype(
        jnp.float32
    )
    d_probs = jnp.sum(onehot_routes * d_gate_values[..., None], axis=1)
    d_logits = probs_all * (d_probs - jnp.sum(probs_all * d_probs, axis=-1, keepdims=True))
    moe_wide = moe_low.astype(jnp.float32)
    d_router = jnp.dot(moe_wide.T, d_logits, precision=highest)
    d_moe_low = d_moe_low + jnp.dot(d_logits, router.astype(jnp.float32).T, precision=highest)
    const_weight = jnp.stack(
        [
            jnp.sum(jnp.where(route_ids == FFN_EXPERTS + 2 + offset, gate_values, 0.0), axis=1)
            for offset in range(2)
        ],
        axis=1,
    )
    d_const_out = const_weight[..., None] * upstream[:, None, :]
    d_alpha = jnp.stack(
        [
            jnp.sum(d_const_out * normed_moe[:, None, :], axis=-1),
            jnp.sum(d_const_out * const_vec[None], axis=-1),
        ],
        axis=-1,
    )
    d_const_logits = alphas * (d_alpha - jnp.sum(alphas * d_alpha, axis=-1, keepdims=True))
    d_const_gate = jnp.einsum("td,tca->cda", moe_wide, d_const_logits, precision=highest)
    d_moe_low = d_moe_low + jnp.einsum(
        "tca,cda->td", d_const_logits, const_gate.astype(jnp.float32), precision=highest
    )
    d_const_vec = jnp.sum(d_const_out * alphas[..., 1:2], axis=0)
    copy_weight = jnp.sum(jnp.where(route_ids == FFN_EXPERTS + 1, gate_values, 0.0), axis=1)
    d_normed = (
        d_moe_low
        + copy_weight[:, None] * upstream
        + jnp.sum(d_const_out * alphas[..., 0:1], axis=1)
    )
    d_hidden_norm, d_moe_gain = rms_backward(hidden, inverse_moe, moe_gain, d_normed)
    d_hidden = upstream + d_hidden_norm
    d_attn_low = d_hidden.astype(jnp.bfloat16)
    d_w_out = jnp.dot(mixed_low.T, d_attn_low, preferred_element_type=jnp.float32)
    d_mixed = jnp.dot(d_attn_low, w_out.T, preferred_element_type=jnp.float32).astype(jnp.bfloat16)
    kv_back = lax.all_gather(kv_local, "ctx", axis=0, tiled=True)
    all_back = jnp.concatenate([kv_back, own_kv], axis=0)
    d_heads = lax.map(
        partial(head_backward, allowed),
        (
            split_heads(queries),
            split_heads(all_back[:, :model_width]),
            split_heads(all_back[:, model_width:]),
            split_heads(d_mixed),
            row_lse,
        ),
    )
    d_queries = join_heads(d_heads[0])
    kv_grad = jnp.concatenate([join_heads(d_heads[1]), join_heads(d_heads[2])], axis=-1)
    own_prompt_grad = lax.psum_scatter(
        kv_grad[:prompt_len].astype(jnp.bfloat16), "ctx", scatter_dimension=0, tiled=True
    ).astype(jnp.float32)
    kv_rows = jnp.concatenate([own_prompt_grad, kv_grad[prompt_len:]], axis=0)
    d_projected = jnp.concatenate([d_queries, kv_rows], axis=-1).astype(jnp.bfloat16)
    d_w_qkv = jnp.dot(act_low.T, d_projected, preferred_element_type=jnp.float32)
    d_act = jnp.dot(d_projected, w_qkv.T, preferred_element_type=jnp.float32)
    d_tokens_norm, d_attn_gain = rms_backward(tokens_in, inverse_attn, attn_gain, d_act)
    d_inputs = (d_hidden + d_tokens_norm)[None]
    dense_sums = lax.psum(
        (d_attn_gain, d_w_qkv, d_w_out, d_moe_gain, d_router, d_const_gate, d_const_vec),
        ("ctx", "exp"),
    )
    return (
        mixed_out,
        d_inputs,
        d_logits[None],
        dense_sums[0],
        dense_sums[1],
        dense_sums[2],
        dense_sums[3],
        dense_sums[4],
        dense_sums[5],
        dense_sums[6],
        total_gate_up[0][None],
        total_gate_up[1][None],
        total_down[None],
    )


def solution(mesh):
    return jax.shard_map(
        body,
        mesh=mesh,
        in_specs=(
            P("ctx", "exp", None),
            P("ctx", "exp", None),
            P("ctx", "exp", None),
            P(),
            P(),
            P(),
            P(),
            P(),
            P(),
            P(),
            P("exp", None, None),
            P("exp", None, None),
            P("exp", None, None),
            P("ctx", "exp", None),
        ),
        out_specs=(
            P("ctx", "exp", None),
            P("ctx", "exp", None),
            P("ctx", "exp", None),
            P(),
            P(),
            P(),
            P(),
            P(),
            P(),
            P(),
            P("exp", "ctx", None),
            P("exp", "ctx", None),
            P("exp", "ctx", None),
        ),
        check_vma=False,
    )
```

profile of v0, /device:TPU:0, one launch (start us, length us, event | category | flops | bytes accessed | tf_op | source)
XLA Modules:
  0.0 1069.2 jit_solution(18259728918760266135)
XLA Ops:
  26.2 7.3 reduce-window.6
  91.6 130.8 %while.28 = (s32[]{:T(128)}, bf16[12,768,64]{1,2,0:T(8,128)(2,1)}, f32[12,768]{1,0:T(8,128)}, bf16[12,768,64]{2,1,0:T(8,128)(2,1)}, bf16[12,1536,64]{2,1,0:T(8,1...) while((s32[]{:T(128)}, bf16[12,768,64]{1,2,0:T(8,128)(2,1)}, ...), condition=%wide.region_4.5_spmd.clone, body=%wide.region_1.4_spmd.clone.sunk | while | flops 317324544 | bytes 34315476 | solution.py:128
  230.3 7.2 gather_fusion
  237.4 6.6 all-to-all-start
  252.5 11.5 %gather_fusion.2 = f32[1536]{0:T(1024)S(1)} fusion(f32[768,12]{0,1:T(8,128)} %fusion.115, s32[1536]{0:T(1024)S(1)} %reshape.454), kind=kCustom, calls=%fused_computation.2 | custom fusion | bytes 24576 | tf_op jit(solution)/shard_map/jit(take_along_axis)/gather | solution.py:143
  268.5 7.0 broadcast_multiply_fusion
  275.5 6.9 reshape.464
  282.4 9.7 scatter_custom_fusion
  313.2 10.1 fusion.65
  323.3 7.7 fusion.69
  331.0 12.1 %all-to-all-done.2 = bf16[8,144,768]{2,1,0:T(8,128)(2,1)} async-done(((bf16[8,144,768]{2,1,0:T(8,128)(2,1)}), bf16[8,144,768]{2,1,0:T(8,128)(2,1)}, u32[]{:S(2)}, u32[]{:S(2)}) %all-to-all-start.2) | async-done | bytes 1769504 | tf_op jit(solution)/shard_map/all_to_all | solution.py:208
  343.1 16.6 %multiply_convert_fusion.1 = (bf16[1152,2048]{1,0:T(8,128)(2,1)}, bf16[1152,2048]{1,0:T(8,128)(2,1)}, bf16[1152,2048]{1,0:T(8,128)(2,1)}) fusion(f32[1152,2048]{1,0:T(8,128)} %fusion.69, f32[1152,2048]{1,0:T(8,128)} %fusion.65, bf16[1152,768]{1,0:T(8,128)(2,1)} %bitcast.27, bf16[1,2048,768]{2,1,0:T(8,128)(2,1)} %param.30), kind=kOutput, calls=%fused_computation.66 | convolution fusion | flops 3659268096 | bytes 37945344 | tf_op jit(solution)/shard_map/dot_general | solution.py:222
  359.7 7.4 convolution_convert_fusion.4
  388.9 6.8 fusion.67
  395.8 7.5 fusion.60
  403.3 10.5 all-to-all-done.1
  421.9 8.9 gather_fusion.1
  430.7 6.7 reshape.447
  437.4 38.7 %fusion.57 = (f32[2,768]{1,0:T(2,128)}, f32[768,768]{1,0:T(8,128)}, f32[768,2]{1,0:T(8,128)}, f32[768,2]{1,0:T(8,128)}, f32[768,768]{1,0:T(8,128)}, /*index=5*/f32[768,2]{1,0:T(8,128)}) fusion(f32[768,2]{1,0:T(8,128)} %copy.148, f32[768,768]{1,0:T(8,128)} %bitcast_convert_fusion.1, f32[768,2]{1,0:T(8,128)} %bitcast.275, f32[768,2]{1,0:T(8,128)} %bitcast.273, ...), kind=kLoop, calls=%fused_computation.86 | loop fusion | flops 22407168 | bytes 18935808 | tf_op jit(solution)/shard_map/reduce_sum | solution.py:284
  488.5 13.2 %scatter_custom_fusion.1 = f32[769,768]{1,0:T(8,128)} fusion(s32[1152]{0:T(1024)} %copy-done.33, bf16[1152,768]{1,0:T(8,128)(2,1)} %bitcast.65, f32[]{:T(128)} %constant.56.clone.1), kind=kCustom, calls=%fused_computation.95 | custom fusion | flops 1769472 | bytes 4132352 | tf_op jit(solution)/shard_map/scatter-add | solution.py:254
  501.8 7.0 multiply_reduce_fusion.3
  517.6 168.1 %while.29 = (s32[]{:T(128)}, bf16[12,768,64]{1,2,0:T(8,128)(2,1)}, bf16[12,1536,64]{1,2,0:T(8,128)(2,1)}, bf16[12,1536,64]{1,2,0:T(8,128)(2,1)}, bf16[12,768,64]...) while((s32[]{:T(128)}, bf16[12,768,64]{1,2,0:T(8,128)(2,1)}, ...), condition=%wide.region_30.31_spmd.clone, body=%wide.region_28.30_spmd.clone.sunk | while | flops 772816128 | bytes 38401196 | solution.py:298
  690.7 8.9 fusion.73
  699.6 7.2 fusion.71
  706.8 7.4 fusion.72
  723.0 12.9 %reduce-scatter.4.cloned.1.call-done = bf16[256,1536]{0,1:T(8,128)(2,1)} async-done(((bf16[1024,1536]{0,1:T(8,128)(2,1)}), bf16[256,1536]{0,1:T(8,128)(2,1)}) %reduce-scatter.4.cloned.1.call-update) | async-done | bytes 786448 | tf_op jit(solution)/shard_map/reduce_scatter | solution.py:310
  735.9 8.5 fusion.90
  750.9 31.9 %reduce-scatter.8.cloned.1.call-done = bf16[1,512,768]{2,1,0:T(8,128)(2,1)} async-done(((bf16[1,2048,768]{2,1,0:T(8,128)(2,1)}), bf16[1,512,768]{2,1,0:T(8,128)(2,1)}) %reduce-scatter.8.cloned.1.call-update) | async-done | bytes 786448 | tf_op jit(solution)/shard_map/reduce_scatter | solution.py:247
  785.4 6.9 fusion.84
  792.3 41.7 %all-reduce.1 = (f32[768]{0:T(1024)}, f32[768]{0:T(1024)}, f32[768,12]{0,1:T(8,128)}, f32[2,768,2]{1,2,0:T(2,128)}, f32[2,768]{1,0:T(2,128)}) all-reduce(f32[768]{0:T(1024)} %get-tuple-element.381, f32[768]{0:T(1024)} %get-tuple-element.377, f32[768,12]{0,1:T(8,128)} %fusion.130, ...), channel_id=1, replica_groups=mesh['ctx'=4,'exp'=8] {'ctx','exp'}, use_global_device_ids=true, to_apply=%region_34.35 | all-reduce | flops 15360 | bytes 122880 | tf_op jit(solution)/shard_map/psum | solution.py:319
  840.5 16.3 %reduce-scatter.6.cloned.1.call-done = bf16[1,2,192,2048]{3,2,1,0:T(8,128)(2,1)} async-done(((bf16[1,2,768,2048]{3,2,1,0:T(8,128)(2,1)}), bf16[1,2,192,2048]{3,2,1,0:T(8,128)(2,1)}) %reduce-scatter.6.cloned.1.call-update) | async-done | bytes 1572880 | tf_op jit(solution)/shard_map/reduce_scatter | solution.py:244
  860.4 194.1 %all-reduce.5.cloned.1.call-done = (f32[768,2304]{1,0:T(8,128)}, f32[768,768]{1,0:T(8,128)}) async-done(((f32[768,2304]{1,0:T(8,128)}, f32[768,768]{1,0:T(8,128)}), (f32[768,2304]{1,0:T(8,128)}, f32[768,768]{1,0:T(8,128)})) %all-reduce.5.cloned.1.call-update) | async-done | bytes 9437200 | tf_op jit(solution)/shard_map/psum | solution.py:319
  (466 shorter events, 509.1 us)
Async XLA Ops:
  7.2 58.8 %all-gather.2.cloned.1.call-start = ((), (), s32[]{:S(2)}) async-start(), calls=%async_computation.7 | async-start | bytes 3932160 | tf_op jit(solution)/shard_map/all_gather | solution.py:118
  9.6 4.9 copy-start.36
  57.5 7.3 copy-start.33
  131.0 4.2 copy-start.42
  152.8 4.2 copy-start.42
  196.4 4.2 copy-start.42
  218.2 4.2 copy-start.42
  237.4 58.0 %all-to-all-start = ((bf16[8,144,768]{2,1,0:T(8,128)(2,1)}), bf16[8,144,768]{2,1,0:T(8,128)(2,1)}, u32[]{:S(2)}, u32[]{:S(2)}) async-start(bf16[8,144,768]{2,1,0:T(8,128)(2,1)} %bitcast.269), calls=%async_computation | async-start | bytes 3538944 | tf_op jit(solution)/shard_map/all_to_all | solution.py:160
  295.4 47.7 %all-to-all-start.2 = ((bf16[8,144,768]{2,1,0:T(8,128)(2,1)}), bf16[8,144,768]{2,1,0:T(8,128)(2,1)}, u32[]{:S(2)}, u32[]{:S(2)}) async-start(bf16[8,144,768]{2,1,0:T(8,128)(2,1)} %bitcast.270), calls=%async_computation.2 | async-start | bytes 3538944 | tf_op jit(solution)/shard_map/all_to_all | solution.py:208
  308.0 15.3 %copy-start.28 = (f32[768,2]{0,1:T(2,128)}, f32[768,2]{0,1:T(2,128)S(1)}, u32[]{:S(2)}) copy-start(f32[768,2]{0,1:T(2,128)S(1)} %get-tuple-element.485) | copy-start | bytes 18436
  313.2 10.1 copy-start.47
  343.1 16.6 %copy-start.46 = (bf16[1,2048,768]{2,1,0:T(8,128)(2,1)S(1)}, bf16[1,2048,768]{2,1,0:T(8,128)(2,1)}, u32[]{:S(2)}) copy-start(bf16[1,2048,768]{2,1,0:T(8,128)(2,1)} %param.30) | copy-start | bytes 9437188
  367.1 4.6 copy-start.34
  367.1 46.7 %all-to-all-start.1 = ((bf16[8,144,768]{2,1,0:T(8,128)(2,1)}), bf16[8,144,768]{2,1,0:T(8,128)(2,1)}, u32[]{:S(2)}, u32[]{:S(2)}) async-start(bf16[8,144,768]{2,1,0:T(8,128)(2,1)} %bitcast.277), calls=%async_computation.1 | async-start | bytes 3538944 | tf_op jit(solution)/shard_map/all_to_all | solution.py:177
  388.9 6.9 copy-start.48
  413.8 74.7 %all-to-all-start.3 = ((bf16[8,144,768]{2,1,0:T(8,128)(2,1)}), bf16[8,144,768]{2,1,0:T(8,128)(2,1)}, u32[]{:S(2)}, u32[]{:S(2)}) async-start(bf16[8,144,768]{2,1,0:T(8,128)(2,1)} %bitcast.276), calls=%async_computation.3 | async-start | bytes 3538944 | tf_op jit(solution)/shard_map/all_to_all | solution.py:235
  418.1 317.8 %reduce-scatter.4.cloned.1.call-start = ((), (), s32[]{:S(2)}) async-start(), calls=%async_computation.8 | async-start | bytes 3932160 | tf_op jit(solution)/shard_map/reduce_scatter | solution.py:310
  437.4 45.5 %copy-start.21 = (f32[768]{0:T(1024)S(1)}, f32[768]{0:T(1024)}, u32[]{:S(2)}) copy-start(f32[768]{0:T(1024)} %copy-done.20) | copy-start | bytes 9220
  437.4 47.8 %copy-start.19 = (f32[768,2,2]{0,2,1:T(2,128)S(1)}, f32[768,2,2]{0,2,1:T(2,128)}, u32[]{:S(2)}) copy-start(f32[768,2,2]{0,2,1:T(2,128)} %copy-done.18) | copy-start | bytes 36868
  488.5 13.2 %copy-start.26 = (f32[768]{0:T(1024)S(1)}, f32[768]{0:T(1024)}, u32[]{:S(2)}) copy-start(f32[768]{0:T(1024)} %copy-done.25) | copy-start | bytes 9220
  501.7 7.1 copy-start.5
  501.7 7.1 copy-start.6
  501.8 7.1 copy-start.10
  501.8 7.1 copy-start.31
  501.8 7.0 copy-start.38
  690.4 92.4 %reduce-scatter.8.cloned.1.call-start = ((), (), s32[]{:S(2)}) async-start(), calls=%async_computation.10 | async-start | bytes 3932160 | tf_op jit(solution)/shard_map/reduce_scatter | solution.py:247
  699.6 157.2 %reduce-scatter.6.cloned.1.call-start = ((), (), s32[]{:S(2)}) async-start(), calls=%async_computation.9 | async-start | bytes 7864320 | tf_op jit(solution)/shard_map/reduce_scatter | solution.py:244
  717.4 337.1 %all-reduce.5.cloned.1.call-start = ((), (), s32[]{:S(2)}) async-start(), calls=%async_computation.11 | async-start | bytes 18874368 | tf_op jit(solution)/shard_map/psum | solution.py:319
  720.5 15.4 %copy-start.37 = (f32[768]{0:T(1024)S(1)}, f32[768]{0:T(1024)}, u32[]{:S(2)}) copy-start(f32[768]{0:T(1024)} %copy-done.36) | copy-start | bytes 9220
  785.4 6.9 copy-start.29
  785.4 49.4 %copy-start.35 = (f32[768]{0:T(1024)S(1)}, f32[768]{0:T(1024)}, u32[]{:S(2)}) copy-start(f32[768]{0:T(1024)} %get-tuple-element.477) | copy-start | bytes 9220
  1054.5 6.6 copy-start.14
  (71 other events, 185.8 us)
Sparse Core Ops, SparseCore 0:
  17.3 46.6 all-gather.1
  690.6 45.2 reduce-scatter.3
  738.9 43.9 reduce-scatter.7
  785.7 71.0 reduce-scatter.5
  863.1 191.2 all-reduce.4
where the time goes:
time: 1080 us; the launch traced here: 1070 us
  matrix products  367 us (34%)
  waiting for transfers between devices  278 us (26%)
  local copies, waits for them, and re-layouts  200 us (19%)
  other arithmetic  146 us (14%)
  blocking collectives  41.7 us (4%)
  starting transfers between devices  21.9 us (2%)
  between operations  14.5 us (1%)
    psum x1, waiting for transfers between devices, body(): lax.psum((d_attn_gain, d_w_qkv, d_w_out, d_moe_gain, d_router, d_const_ga...  194 us
    dot_general x12, matrix products, head_forward(): jnp.einsum('qk,kd->qd', weights_soft, value_rows, preferred_element_type=...  50.2 us
    dot_general x12, matrix products, head_backward(): jnp.einsum('qd,kd->qk', queries, key_rows, preferred_element_type=jnp.flo...  48.2 us
    unnamed x106, local copies, waits for them, and re-layouts  45.2 us
    psum x1, blocking collectives, body(): lax.psum((d_attn_gain, d_w_qkv, d_w_out, d_moe_gain, d_router, d_const_ga...  41.7 us
    reduce_sum x1, other arithmetic, body(): d_const_vec = jnp.sum(d_const_out * alphas[..., 1:2], axis=0)  38.7 us
    dot_general x12, matrix products, head_forward(): jnp.einsum('qd,kd->qk', queries, key_rows, preferred_element_type=jnp.flo...  38.3 us
    reduce_scatter x1, waiting for transfers between devices, body(): lax.psum_scatter(down_local.astype(jnp.bfloat16), 'ctx', scatter_dimensio...  31.9 us
  transfers between devices with their start and end apart: 9, of which 6 were waited for; matrix products, arithmetic and copies ran while one was open for 28% of the time, Pallas kernels for 0%

commit v1 on v0

v1 whole, which is shorter than its diff:
```python
import functools, math
import jax, jax.numpy as jnp
from jax import lax
from jax.experimental import pallas as pl
from jax.experimental.pallas import tpu as pltpu

HEADS = 12
HEAD_DIM = 64
CONT_LEN = 512
LOG2E = 1.4426950408889634
SCALE = HEAD_DIM ** -0.5
bf16 = jnp.bfloat16
f32 = jnp.float32
NEG = -1e30


def dot_nt(a, b):
    return lax.dot_general(a, b, (((1,), (1,)), ((), ())), preferred_element_type=f32)


def dot_nn(a, b):
    return jnp.dot(a, b, preferred_element_type=f32)


def query_tiles(tok, plen):
    tiles = [(0, plen, True)]
    step = 256
    for start in range(plen, tok, step):
        tiles.append((start, step, False))
    return tiles


def attention_forward_kernel(plen, flags_ref, q_ref, k_ref, v_ref, kr_ref, vr_ref, o_ref, lse_ref):
    tok = q_ref.shape[0]
    remote = kr_ref.shape[0]
    lane = lax.broadcasted_iota(jnp.int32, (1, 128), 1)
    low_half = lane < HEAD_DIM
    c = SCALE * LOG2E
    one = jnp.ones((), bf16)
    zero = jnp.zeros((), bf16)
    for start, size, is_prompt in query_tiles(tok, plen):
        accs, peaks = [], []
        for head in range(2):
            mine = low_half if head == 0 else ~low_half
            qh = jnp.where(mine, q_ref[start : start + size, :], zero)
            pieces = []
            row = lax.broadcasted_iota(jnp.int32, (size, size), 0)
            col = lax.broadcasted_iota(jnp.int32, (size, size), 1)
            diag = dot_nt(qh, k_ref[start : start + size, :])
            pieces.append((jnp.where(col <= row, diag, NEG), v_ref, start, size))
            if is_prompt:
                for j in range(remote // plen):
                    s = dot_nt(qh, kr_ref[j * plen : (j + 1) * plen, :])
                    pieces.append((s + flags_ref[j], vr_ref, j * plen, plen))
            else:
                s = dot_nt(qh, k_ref[0:start, :])
                pieces.append((s, v_ref, 0, start))
                s = dot_nt(qh, kr_ref[...])
                pieces.append((s, vr_ref, 0, remote))
            peak = None
            for s, _, _, _ in pieces:
                m = jnp.max(s, axis=1, keepdims=True)
                peak = m if peak is None else jnp.maximum(peak, m)
            shift = peak * c
            acc = None
            for s, ref, at, n in pieces:
                p = jnp.exp2(s * c - shift).astype(bf16)
                vh = jnp.where(mine, ref[at : at + n, :], one)
                part = dot_nn(p, vh)
                acc = part if acc is None else acc + part
            accs.append(acc)
            peaks.append(shift)
        num = jnp.where(low_half, accs[0], accs[1])
        den = pltpu.roll(jnp.where(low_half, accs[1], accs[0]), HEAD_DIM, 1)
        o_ref[start : start + size, :] = (num / den).astype(bf16)
        logs = jnp.where(low_half, peaks[0], peaks[1]) + jnp.log2(den)
        turned = logs.T
        lse_ref[0, 0:8, start : start + size] = turned[0:8, :]
        lse_ref[0, 8:16, start : start + size] = turned[HEAD_DIM : HEAD_DIM + 8, :]


def attention_forward(flags, proj, kv_rem, plen):
    tok, width = proj.shape[0], proj.shape[1] // 3
    remote = kv_rem.shape[0]
    pairs = width // 128
    return pl.pallas_call(
        functools.partial(attention_forward_kernel, plen),
        grid=(pairs,),
        in_specs=[
            pl.BlockSpec(memory_space=pltpu.SMEM),
            pl.BlockSpec((tok, 128), lambda i: (0, i)),
            pl.BlockSpec((tok, 128), lambda i: (0, pairs + i)),
            pl.BlockSpec((tok, 128), lambda i: (0, 2 * pairs + i)),
            pl.BlockSpec((remote, 128), lambda i: (0, i)),
            pl.BlockSpec((remote, 128), lambda i: (0, pairs + i)),
        ],
        out_specs=[
            pl.BlockSpec((tok, 128), lambda i: (0, i)),
            pl.BlockSpec((1, 16, tok), lambda i: (i, 0, 0)),
        ],
        out_shape=[
            jax.ShapeDtypeStruct((tok, width), bf16),
            jax.ShapeDtypeStruct((pairs, 16, tok), f32),
        ],
        compiler_params=pltpu.CompilerParams(vmem_limit_bytes=48 * 2**20),
        cost_estimate=pl.CostEstimate(flops=4 * tok * (tok + remote) * width, bytes_accessed=2 * (tok * 4 + remote * 2) * width, transcendentals=tok * (tok + remote) * HEADS),
        name="attention_forward",
    )(flags, proj, proj, proj, kv_rem, kv_rem)


def attention_backward_kernel(plen, flags_ref, q_ref, k_ref, v_ref, kr_ref, vr_ref, o_ref, do_ref, lse_ref,
                              dq_ref, dk_ref, dv_ref, dkr_ref, dvr_ref, kt, krt, dka, dva, dkra, dvra):
    tok = q_ref.shape[0]
    remote = kr_ref.shape[0]
    lane = lax.broadcasted_iota(jnp.int32, (1, 128), 1)
    low_half = lane < HEAD_DIM
    c = SCALE * LOG2E
    zero = jnp.zeros((), bf16)
    kt[...] = k_ref[...].T
    krt[...] = kr_ref[...].T
    dka[...] = jnp.zeros_like(dka)
    dva[...] = jnp.zeros_like(dva)
    dkra[...] = jnp.zeros_like(dkra)
    dvra[...] = jnp.zeros_like(dvra)
    pick = lax.broadcasted_iota(jnp.int32, (16, 128), 0) // 8 == lax.broadcasted_iota(jnp.int32, (16, 128), 1) // HEAD_DIM
    pick = jnp.where(pick, 1.0, 0.0).astype(bf16)
    for start, size, is_prompt in query_tiles(tok, plen):
        rows = slice(start, start + size)
        product = do_ref[rows, :].astype(f32) * o_ref[rows, :].astype(f32)
        high = product.astype(bf16)
        rest = (product - high.astype(f32)).astype(bf16)
        delta = dot_nt(pick, high) + dot_nt(pick, rest)
        dqt = []
        for head in range(2):
            mine = low_half if head == 0 else ~low_half
            qh = jnp.where(mine, q_ref[rows, :], zero)
            doh = jnp.where(mine, do_ref[rows, :], zero)
            lse_row = lse_ref[0, 8 * head : 8 * head + 1, rows]
            delta_row = delta[8 * head : 8 * head + 1, :]
            segments = [(k_ref, v_ref, kt, dka, dva, start, size, "diag")]
            if is_prompt:
                for j in range(remote // plen):
                    segments.append((kr_ref, vr_ref, krt, dkra, dvra, j * plen, plen, j))
            else:
                segments.append((k_ref, v_ref, kt, dka, dva, 0, start, None))
                segments.append((kr_ref, vr_ref, krt, dkra, dvra, 0, remote, None))
            total = None
            for kk, vv, tt, dk_acc, dv_acc, at, n, mode in segments:
                keys = slice(at, at + n)
                st = dot_nt(kk[keys, :], qh) * c - lse_row
                if mode == "diag":
                    key = lax.broadcasted_iota(jnp.int32, (n, size), 0)
                    query = lax.broadcasted_iota(jnp.int32, (n, size), 1)
                    st = jnp.where(key <= query, st, NEG)
                elif mode is not None:
                    st = st + flags_ref[mode]
                pt = jnp.exp2(st)
                dpt = dot_nt(vv[keys, :], doh)
                dst = (pt * (dpt - delta_row)).astype(bf16)
                dv_acc[keys, :] += dot_nn(pt.astype(bf16), doh)
                dk_acc[keys, :] += dot_nn(dst, qh)
                part = dot_nn(tt[head * HEAD_DIM : (head + 1) * HEAD_DIM, keys], dst)
                total = part if total is None else total + part
            dqt.append(total)
        dq_ref[rows, :] = (jnp.concatenate(dqt, axis=0).T * SCALE).astype(bf16)
    dk_ref[...] = (dka[...] * SCALE).astype(bf16)
    dv_ref[...] = dva[...].astype(bf16)
    dkr_ref[...] = (dkra[...] * SCALE).astype(bf16)
    dvr_ref[...] = dvra[...].astype(bf16)


def attention_backward(flags, proj, kv_rem, mixed, d_mixed, lse, plen):
    tok, width = mixed.shape
    remote = kv_rem.shape[0]
    pairs = width // 128
    own = pl.BlockSpec((tok, 128), lambda i: (0, i))
    far = pl.BlockSpec((remote, 128), lambda i: (0, i))
    return pl.pallas_call(
        functools.partial(attention_backward_kernel, plen),
        grid=(pairs,),
        in_specs=[
            pl.BlockSpec(memory_space=pltpu.SMEM),
            own,
            pl.BlockSpec((tok, 128), lambda i: (0, pairs + i)),
            pl.BlockSpec((tok, 128), lambda i: (0, 2 * pairs + i)),
            far,
            pl.BlockSpec((remote, 128), lambda i: (0, pairs + i)),
            own,
            own,
            pl.BlockSpec((1, 16, tok), lambda i: (i, 0, 0)),
        ],
        out_specs=[own, own, own, far, far],
        out_shape=[jax.ShapeDtypeStruct((tok, width), bf16)] * 3 + [jax.ShapeDtypeStruct((remote, width), bf16)] * 2,
        scratch_shapes=[
            pltpu.VMEM((128, tok), bf16),
            pltpu.VMEM((128, remote), bf16),
            pltpu.VMEM((tok, 128), f32),
            pltpu.VMEM((tok, 128), f32),
            pltpu.VMEM((remote, 128), f32),
            pltpu.VMEM((remote, 128), f32),
        ],
        compiler_params=pltpu.CompilerParams(vmem_limit_bytes=48 * 2**20),
        cost_estimate=pl.CostEstimate(flops=10 * tok * (tok + remote) * width, bytes_accessed=2 * (tok * 8 + remote * 4) * width, transcendentals=tok * (tok + remote) * HEADS),
        name="attention_backward",
    )(flags, proj, proj, proj, kv_rem, kv_rem, mixed, d_mixed, lse)


FFN_EXPERTS = 8
ALL_EXPERTS = 12
EXTRA = 128
SMALL = 8
epsilon = 1e-06


def dot_tn(a, b):
    return lax.dot_general(a, b, (((0,), (0,)), ((), ())), preferred_element_type=f32)


def split_low(value, parts):
    pieces = []
    for _ in range(parts):
        piece = value.astype(bf16)
        pieces.append(piece)
        value = value - piece.astype(f32)
    return pieces


def route_kernel(groups, home_ref, ids_ref, grad_ref, prev_ref, *out_refs):
    tok, width = grad_ref.shape
    count = len(groups)
    turned_refs, chosen_refs, early_ref = out_refs[:count], out_refs[count : 2 * count], out_refs[2 * count]
    expert = lax.broadcasted_iota(jnp.int32, (16, tok), 0)
    names = [ids_ref[k : k + 1, :] == expert for k in range(2)]
    both = jnp.where(names[0] | names[1], 1.0, 0.0).astype(bf16)
    earlier = lax.broadcasted_iota(jnp.int32, (tok, tok), 0) < lax.broadcasted_iota(jnp.int32, (tok, tok), 1)
    before = dot_nn(both, jnp.where(earlier, 1.0, 0.0).astype(bf16))
    pieces = [piece.astype(f32) for piece in split_low(prev_ref[...], 3)]
    extra = (pieces[0] + pltpu.roll(pieces[1], 16, 1) + pltpu.roll(pieces[2], 32, 1)).astype(bf16)
    slot = [jnp.sum(jnp.where(n, before, 0.0), axis=0, keepdims=True).astype(jnp.int32) for n in names]
    for (first, size), turned_ref, chosen_ref in zip(groups, turned_refs, chosen_refs):
        spots = lax.broadcasted_iota(jnp.int32, (FFN_EXPERTS * size, tok), 0)
        hit = None
        for k in range(2):
            ids = ids_ref[k : k + 1, :]
            inside = (ids < FFN_EXPERTS) & (slot[k] >= first) & (slot[k] < first + size)
            place = jnp.where(inside, ids * size + slot[k] - first, -1)
            hit = spots == place if hit is None else hit | (spots == place)
        turned = jnp.where(hit, 1.0, 0.0).astype(bf16)
        turned_ref[...] = turned
        chosen_ref[...] = turned.T
        grads = dot_nn(turned, grad_ref[...]).astype(bf16)
        extras = dot_nn(turned, extra).astype(bf16)
        for e in range(FFN_EXPERTS):
            early_ref[e, first : first + size, 0:width] = grads[e * size : (e + 1) * size]
            early_ref[e, first : first + size, width : width + EXTRA] = extras[e * size : (e + 1) * size]


def route_plan(home, ids, grad, prev, groups):
    tok, width = grad.shape
    counts = [FFN_EXPERTS * size for _, size in groups]
    whole = pl.BlockSpec(memory_space=pltpu.VMEM)
    out = pl.pallas_call(
        functools.partial(route_kernel, groups),
        in_specs=[pl.BlockSpec(memory_space=pltpu.SMEM), whole, whole, whole],
        out_specs=[whole] * (2 * len(groups) + 1),
        out_shape=[jax.ShapeDtypeStruct((n, tok), bf16) for n in counts]
        + [jax.ShapeDtypeStruct((tok, n), bf16) for n in counts]
        + [jax.ShapeDtypeStruct((FFN_EXPERTS, sum(counts) // FFN_EXPERTS, width + EXTRA), bf16)],
        compiler_params=pltpu.CompilerParams(vmem_limit_bytes=48 * 2**20),
        cost_estimate=pl.CostEstimate(flops=2 * sum(counts) * tok * (width + EXTRA), bytes_accessed=4 * sum(counts) * width, transcendentals=0),
        name="route_plan",
    )(home, ids, grad, prev)
    return out[: len(groups)], out[len(groups) : -1], out[-1]


def expert_kernel(group, home_ref, rows_ref, early_ref, router_ref, wg_ref, wu_ref, wd_ref,
                  out_ref, drow_ref, dout_ref, inner_ref, dgate_ref, dup_ref, acc_out, acc_row, probs_ref):
    width = rows_ref.shape[1]
    step, steps = pl.program_id(0), pl.num_programs(0)
    home = home_ref[0]
    lane = lax.broadcasted_iota(jnp.int32, (1, EXTRA), 1)
    slots = slice(group[0], group[0] + group[1])

    @pl.when(step == 0)
    def _():
        extra = early_ref[:, slots, width : width + EXTRA].astype(f32).reshape(-1, EXTRA)
        logits = extra + pltpu.roll(extra, EXTRA - 16, 1) + pltpu.roll(extra, EXTRA - 32, 1)
        logits = logits + dot_nn(rows_ref[...], router_ref[...])
        logits = jnp.where(lane < ALL_EXPERTS, logits, NEG)
        unnormed = jnp.exp(logits - jnp.max(logits, axis=1, keepdims=True))
        probs = unnormed / jnp.sum(unnormed, axis=1, keepdims=True)
        probs_ref[...] = probs
        gate = jnp.sum(jnp.where(lane == home, probs, 0.0), axis=1, keepdims=True)
        dout_ref[...] = (gate * early_ref[:, slots, 0:width].astype(f32).reshape(-1, width)).astype(bf16)
        acc_out[...] = jnp.zeros_like(acc_out)
        acc_row[...] = jnp.zeros_like(acc_row)

    rows = rows_ref[...]
    gate_pre = dot_nn(rows, wg_ref[0])
    up_pre = dot_nn(rows, wu_ref[0])
    d_inner = dot_nt(dout_ref[...], wd_ref[0])
    sigmoid = jax.nn.sigmoid(gate_pre)
    silu = gate_pre * sigmoid
    inner = (silu * up_pre).astype(bf16)
    d_gate = (d_inner * up_pre * (sigmoid * (1.0 + gate_pre * (1.0 - sigmoid)))).astype(bf16)
    d_up = (d_inner * silu).astype(bf16)
    inner_ref[...] = inner
    dgate_ref[...] = d_gate
    dup_ref[...] = d_up
    acc_out[...] += dot_nn(inner, wd_ref[0])
    acc_row[...] += dot_nt(d_gate, wg_ref[0]) + dot_nt(d_up, wu_ref[0])

    @pl.when(step == steps - 1)
    def _():
        probs = probs_ref[...]
        gate = jnp.sum(jnp.where(lane == home, probs, 0.0), axis=1, keepdims=True)
        out = acc_out[...].astype(bf16).astype(f32)
        d_row_gate = jnp.sum(out * early_ref[:, slots, 0:width].astype(f32).reshape(-1, width), axis=1, keepdims=True)
        out_ref[:, 0:width] = (gate * out).astype(bf16)
        extra = jnp.zeros((out.shape[0], EXTRA), f32)
        for i, piece in enumerate(split_low(d_row_gate, 3)):
            extra = jnp.where(lane == home + 16 * i, piece.astype(f32), extra)
        out_ref[:, width : width + EXTRA] = extra.astype(bf16)
        term = d_row_gate * gate * (jnp.where(lane == home, 1.0, 0.0) - probs)
        high, rest = split_low(term, 2)
        drow_ref[...] = (acc_row[...] + dot_nt(high, router_ref[...]) + dot_nt(rest, router_ref[...])).astype(bf16)


def expert_pass(group, home, rows, early, router_pad, w_gate, w_up, w_down):
    count, width = rows.shape
    ff = w_gate.shape[2]
    tile = min(512, ff)
    full = pl.BlockSpec((count, width), lambda j: (0, 0))
    wide = pl.BlockSpec((count, width + EXTRA), lambda j: (0, 0))
    tall = pl.BlockSpec((1, width, tile), lambda j: (0, 0, j))
    piece = pl.BlockSpec((count, tile), lambda j: (0, j))
    return pl.pallas_call(
        functools.partial(expert_kernel, group),
        grid=(ff // tile,),
        in_specs=[
            pl.BlockSpec(memory_space=pltpu.SMEM),
            full,
            pl.BlockSpec(early.shape, lambda j: (0, 0, 0)),
            pl.BlockSpec((width, EXTRA), lambda j: (0, 0)),
            tall,
            tall,
            pl.BlockSpec((1, tile, width), lambda j: (0, j, 0)),
        ],
        out_specs=[wide, full, full, piece, piece, piece],
        out_shape=[
            jax.ShapeDtypeStruct((count, width + EXTRA), bf16),
            jax.ShapeDtypeStruct((count, width), bf16),
            jax.ShapeDtypeStruct((count, width), bf16),
        ]
        + [jax.ShapeDtypeStruct((count, ff), bf16)] * 3,
        scratch_shapes=[pltpu.VMEM((count, width), f32), pltpu.VMEM((count, width), f32), pltpu.VMEM((count, EXTRA), f32)],
        compiler_params=pltpu.CompilerParams(vmem_limit_bytes=48 * 2**20),
        cost_estimate=pl.CostEstimate(flops=12 * count * width * ff, bytes_accessed=6 * width * ff + 2 * count * (5 * width + 3 * ff), transcendentals=count * ff),
        name="expert_pass",
    )(home, rows, early, router_pad, w_gate, w_up, w_down)


def weight_kernel(count, *refs):
    rows, douts, inners, dgates, dups = (refs[i * count : (i + 1) * count] for i in range(5))
    gate_up_ref, down_ref = refs[5 * count : 5 * count + 2]
    turned = refs[5 * count + 2 :]

    @pl.when(pl.program_id(0) == 0)
    def _():
        for ref, scratch in zip(rows, turned):
            scratch[...] = ref[...].T

    gate_up_ref[0] = sum(dot_nn(t[...], d[...]) for t, d in zip(turned, dgates)).astype(bf16)
    gate_up_ref[1] = sum(dot_nn(t[...], d[...]) for t, d in zip(turned, dups)).astype(bf16)
    down_ref[...] = sum(dot_nn(i[...].T, d[...]) for i, d in zip(inners, douts)).astype(bf16)


def weight_gradients(rows, douts, inners, dgates, dups):
    count = len(rows)
    width, ff = rows[0].shape[1], inners[0].shape[1]
    tile = min(512, ff)
    total = sum(r.shape[0] for r in rows)
    full = [pl.BlockSpec(r.shape, lambda j: (0, 0)) for r in rows]
    piece = [pl.BlockSpec((r.shape[0], tile), lambda j: (0, j)) for r in rows]
    return pl.pallas_call(
        functools.partial(weight_kernel, count),
        grid=(ff // tile,),
        in_specs=full + full + piece * 3,
        out_specs=[pl.BlockSpec((2, width, tile), lambda j: (0, 0, j)), pl.BlockSpec((tile, width), lambda j: (j, 0))],
        out_shape=[jax.ShapeDtypeStruct((2, width, ff), bf16), jax.ShapeDtypeStruct((ff, width), bf16)],
        scratch_shapes=[pltpu.VMEM((width, r.shape[0]), bf16) for r in rows],
        compiler_params=pltpu.CompilerParams(vmem_limit_bytes=48 * 2**20),
        cost_estimate=pl.CostEstimate(flops=6 * total * width * ff, bytes_accessed=6 * width * ff + 2 * total * (2 * width + 3 * ff), transcendentals=0),
        name="weight_gradients",
    )(*rows, *douts, *inners, *dgates, *dups)


ANYWHERE = pl.BlockSpec(memory_space=pltpu.VMEM)
SCALARS = pl.BlockSpec(memory_space=pltpu.SMEM)


def inverse_rms(value):
    return lax.rsqrt(jnp.mean(value * value, axis=1, keepdims=True) + epsilon)


def after_attention_kernel(count, mixed_ref, x_ref, w_ref, gain_ref, *refs):
    turned, (hidden_ref, low_ref), sent = refs[:count], refs[count : count + 2], refs[count + 2 :]
    hidden = x_ref[...].astype(f32) + dot_nn(mixed_ref[...], w_ref[...])
    low = (hidden * inverse_rms(hidden) * gain_ref[...]).astype(bf16)
    hidden_ref[...] = hidden
    low_ref[...] = low
    for t, s in zip(turned, sent):
        s[...] = dot_nn(t[...], low).astype(bf16)


def after_attention(mixed, x, w_out, gain, turned):
    tok, width = x.shape
    rows = sum(t.shape[0] for t in turned)
    out = pl.pallas_call(
        functools.partial(after_attention_kernel, len(turned)),
        in_specs=[ANYWHERE] * (4 + len(turned)),
        out_specs=[ANYWHERE] * (2 + len(turned)),
        out_shape=[jax.ShapeDtypeStruct((tok, width), f32), jax.ShapeDtypeStruct((tok, width), bf16)]
        + [jax.ShapeDtypeStruct((t.shape[0], width), bf16) for t in turned],
        compiler_params=pltpu.CompilerParams(vmem_limit_bytes=40 * 2**20),
        cost_estimate=pl.CostEstimate(flops=2 * tok * width * (width + rows), bytes_accessed=2 * width * (6 * tok + 2 * rows), transcendentals=0),
        name="after_attention",
    )(mixed, x, w_out, gain, *turned)
    return out[0], out[1], out[2:]


def place(value, lane, at):
    return jnp.where(lane == at, value, 0.0)


def local_kernel(hidden_ref, low_ref, grad_ref, prev_ref, ids_ref, mix_ref, gain_ref, vec_ref, out_ref, dnormed_ref, probs_ref, dprobs_ref, small_ref):
    lane = lax.broadcasted_iota(jnp.int32, (1, EXTRA), 1)
    hidden = hidden_ref[...]
    normed = hidden * inverse_rms(hidden) * gain_ref[...]
    low = low_ref[...]
    grad = grad_ref[...].astype(f32)
    raw = dot_nn(low, mix_ref[...])
    logits = jnp.where(lane < ALL_EXPERTS, raw + prev_ref[...], NEG)
    unnormed = jnp.exp(logits - jnp.max(logits, axis=1, keepdims=True))
    probs = unnormed / jnp.sum(unnormed, axis=1, keepdims=True)
    named = (ids_ref[:, 0:1] == lane) | (ids_ref[:, 1:2] == lane)
    gates = jnp.where(named, probs, 0.0)
    copy_gate = gates[:, FFN_EXPERTS + 1 : FFN_EXPERTS + 2]
    dots = jnp.sum(grad * normed, axis=1, keepdims=True)
    out = hidden
    weight = copy_gate
    d_probs = place(dots, lane, FFN_EXPERTS + 1)
    logit_grads = jnp.zeros_like(probs)
    mixing_terms = jnp.zeros_like(probs)
    vec_terms = jnp.zeros_like(probs)
    for c in range(2):
        vec = vec_ref[c : c + 1, :]
        gate = gates[:, FFN_EXPERTS + 2 + c : FFN_EXPERTS + 3 + c]
        at = 16 + 2 * c
        a0 = jax.nn.sigmoid(raw[:, at : at + 1] - raw[:, at + 1 : at + 2])
        a1 = jax.nn.sigmoid(raw[:, at + 1 : at + 2] - raw[:, at : at + 1])
        vec_dots = jnp.sum(grad * vec, axis=1, keepdims=True)
        weight = weight + gate * a0
        out = out + (gate * a1) * vec
        d_probs = d_probs + place(a0 * dots + a1 * vec_dots, lane, FFN_EXPERTS + 2 + c)
        d0, d1 = gate * dots, gate * vec_dots
        mean = a0 * d0 + a1 * d1
        d0, d1 = a0 * (d0 - mean), a1 * (d1 - mean)
        logit_grads = logit_grads + place(d0, lane, at) + place(d1, lane, at + 1)
        mixing_terms = mixing_terms + place(d0, lane, 2 * c) + place(d1, lane, 2 * c + 1)
        vec_terms = vec_terms + place(gate * a1, lane, 4 + c)
    d_probs = jnp.where(named, d_probs, 0.0)
    logit_grads = logit_grads + probs * (d_probs - jnp.sum(probs * d_probs, axis=1, keepdims=True))
    high, rest = split_low(logit_grads, 2)
    out_ref[...] = out + weight * normed
    dnormed_ref[...] = weight * grad + dot_nt(high, mix_ref[...]) + dot_nt(rest, mix_ref[...])
    probs_ref[...] = probs
    dprobs_ref[...] = d_probs
    sums = None
    for terms, rows in ((mixing_terms, low), (vec_terms, grad_ref[...])):
        for piece in split_low(terms.T, 2):
            part = dot_nn(piece, rows)
            sums = part if sums is None else sums + part
    small_ref[...] = sums[0:SMALL, :]


def local_part(hidden, low, grad, prev, ids, mix, gain, vec):
    tok, width = hidden.shape
    shapes = [(tok, width), (tok, width), (tok, EXTRA), (tok, EXTRA), (SMALL, width)]
    return pl.pallas_call(
        local_kernel,
        in_specs=[ANYWHERE] * 8,
        out_specs=[ANYWHERE] * 5,
        out_shape=[jax.ShapeDtypeStruct(s, f32) for s in shapes],
        compiler_params=pltpu.CompilerParams(vmem_limit_bytes=48 * 2**20),
        cost_estimate=pl.CostEstimate(flops=14 * tok * width * EXTRA, bytes_accessed=16 * tok * width, transcendentals=tok * EXTRA),
        name="local_part",
    )(hidden, low, grad, prev, ids, mix, gain, vec)


def combine_kernel(count, parts, *refs):
    chosen, got = refs[:count], refs[count : count * (1 + parts)]
    local_ref, hidden_ref, gain_ref, grad_ref, w_ref, dhidden_ref, dlow_ref, dmixed_ref, small_ref = refs[count * (1 + parts) :]
    d_normed = local_ref[...]
    for g in range(count):
        for r in range(parts):
            d_normed = d_normed + dot_nn(chosen[g][...], got[g * parts + r][...])
    hidden = hidden_ref[...]
    inverse = inverse_rms(hidden)
    scaled = d_normed * gain_ref[...]
    mean = jnp.mean(scaled * hidden, axis=1, keepdims=True)
    d_hidden = grad_ref[...].astype(f32) + inverse * scaled - hidden * (inverse * inverse * inverse * mean)
    low = d_hidden.astype(bf16)
    dhidden_ref[...] = d_hidden
    dlow_ref[...] = low
    dmixed_ref[...] = dot_nt(low, w_ref[...]).astype(bf16)
    gain = jnp.sum(d_normed * hidden * inverse, axis=0, keepdims=True)
    row = lax.broadcasted_iota(jnp.int32, (SMALL, 1), 0)
    small_ref[...] = jnp.where(row == 0, gain, 0.0)


def combine(chosen, got, local, hidden, gain, grad, w_out):
    tok, width = hidden.shape
    rows = sum(c.shape[1] for c in chosen)
    arrays = [a for group in got for a in group]
    return pl.pallas_call(
        functools.partial(combine_kernel, len(chosen), len(got[0])),
        in_specs=[ANYWHERE] * (len(chosen) + len(arrays) + 5),
        out_specs=[ANYWHERE] * 4,
        out_shape=[jax.ShapeDtypeStruct((tok, width), f32)] + [jax.ShapeDtypeStruct((tok, width), bf16)] * 2 + [jax.ShapeDtypeStruct((SMALL, width), f32)],
        compiler_params=pltpu.CompilerParams(vmem_limit_bytes=48 * 2**20),
        cost_estimate=pl.CostEstimate(flops=2 * tok * width * (rows + width), bytes_accessed=2 * width * (9 * tok + 2 * rows), transcendentals=0),
        name="combine_gradients",
    )(*chosen, *arrays, local, hidden, gain, grad, w_out)


def flat_rows(value):
    if value.shape[1] % 16:
        return value.astype(f32).reshape(-1, value.shape[2]).astype(bf16)
    return value.reshape(-1, value.shape[2])


def finish_kernel(groups, parts, *refs):
    chosen, got = refs[: len(groups)], refs[len(groups) : len(groups) + parts]
    local_ref, probs_ref, dprobs_ref, low_ref, out_ref, dlogits_ref, small_ref = refs[len(groups) + parts :]
    width = local_ref.shape[1]
    lane = lax.broadcasted_iota(jnp.int32, (1, EXTRA), 1)
    picked = None
    for c, (at, size) in zip(chosen, groups):
        for r in range(parts):
            part = dot_nn(c[...], flat_rows(got[r][:, at : at + size, :]))
            picked = part if picked is None else picked + part
    out_ref[...] = (local_ref[...] + picked[:, 0:width]).astype(bf16)
    extra = picked[:, width : width + EXTRA]
    extra = extra + pltpu.roll(extra, EXTRA - 16, 1) + pltpu.roll(extra, EXTRA - 32, 1)
    d_probs = dprobs_ref[...] + jnp.where(lane < ALL_EXPERTS, extra, 0.0)
    probs = probs_ref[...]
    d_logits = probs * (d_probs - jnp.sum(probs * d_probs, axis=1, keepdims=True))
    dlogits_ref[...] = d_logits
    high, rest = split_low(d_logits.T, 2)
    sums = dot_nn(high, low_ref[...]) + dot_nn(rest, low_ref[...])
    small_ref[...] = sums[0 : 2 * SMALL, :]


def finish(chosen, got, groups, local, probs, d_probs, low):
    tok, width = local.shape
    return pl.pallas_call(
        functools.partial(finish_kernel, groups, len(got)),
        in_specs=[ANYWHERE] * (len(chosen) + len(got) + 4),
        out_specs=[ANYWHERE] * 3,
        out_shape=[jax.ShapeDtypeStruct((tok, width), bf16), jax.ShapeDtypeStruct((tok, EXTRA), f32), jax.ShapeDtypeStruct((2 * SMALL, width), f32)],
        compiler_params=pltpu.CompilerParams(vmem_limit_bytes=48 * 2**20),
        cost_estimate=pl.CostEstimate(flops=2 * tok * 1152 * (width + EXTRA), bytes_accessed=16 * tok * width, transcendentals=0),
        name="finish_outputs",
    )(*chosen, *got, local, probs, d_probs, low)


def xor_pairs(size, mask):
    return [(i, i ^ mask) for i in range(size)]


def pack_kernel(core_ref, mixed_ref, dlow_ref, act_ref, far_ref, dq_ref, dk_ref, dv_ref, dkf_ref, dvf_ref, local_ref, gain_ref, router_ref, mine_ref, theirs_ref, mixed_t, act_t, far_t):
    core = core_ref[0]
    width = mixed_ref.shape[1]
    half, piece = width // 2, width // 8

    @pl.when(pl.program_id(0) == 0)
    def _():
        mixed_t[...] = mixed_ref[...].T
        act_t[...] = act_ref[...].T
        far_t[...] = far_ref[...].T

    for out_ref, which in ((theirs_ref, 1 - core), (mine_ref, core)):
        rows = pl.ds(pl.multiple_of(which * half, half), half)
        parts = [
            dot_nn(mixed_t[rows, :], dlow_ref[...]),
            dot_nn(act_t[rows, :], dq_ref[...]),
            dot_nn(act_t[rows, :], dk_ref[...]) + dot_nn(far_t[rows, :], dkf_ref[...]),
            dot_nn(act_t[rows, :], dv_ref[...]) + dot_nn(far_t[rows, :], dvf_ref[...]),
        ]
        for j, part in enumerate(parts):
            for k in range(4):
                out_ref[j, k, 0:piece, :] = part[k * piece : (k + 1) * piece].astype(bf16)
                small = jnp.zeros((SMALL, part.shape[1]), f32)
                if j == 0:
                    small = (local_ref[...], gain_ref[...], router_ref[0:SMALL, :], router_ref[SMALL : 2 * SMALL, :])[k]
                    small = jnp.where(which == 0, small, 0.0)
                out_ref[j, k, piece : piece + SMALL, :] = small.astype(bf16)


def pack(core, mixed, dlow, act, far, dq, dk, dv, dkf, dvf, local, gain, router):
    tok, width = mixed.shape
    remote = far.shape[0]
    tile = 256
    whole = lambda n: pl.BlockSpec((n, width), lambda i: (0, 0))
    column = lambda n: pl.BlockSpec((n, tile), lambda i: (0, i))
    out = pl.BlockSpec((4, 4, width // 8 + SMALL, tile), lambda i: (0, 0, 0, i))
    return pl.pallas_call(
        pack_kernel,
        grid=(width // tile,),
        in_specs=[
            pl.BlockSpec(memory_space=pltpu.SMEM), whole(tok), column(tok), whole(tok), whole(remote),
            column(tok), column(tok), column(tok), column(remote), column(remote),
            column(SMALL), column(SMALL), column(2 * SMALL),
        ],
        out_specs=[out, out],
        out_shape=[jax.ShapeDtypeStruct((4, 4, width // 8 + SMALL, width), bf16)] * 2,
        scratch_shapes=[pltpu.VMEM((width, tok), bf16), pltpu.VMEM((width, tok), bf16), pltpu.VMEM((width, remote), bf16)],
        compiler_params=pltpu.CompilerParams(vmem_limit_bytes=48 * 2**20),
        cost_estimate=pl.CostEstimate(flops=2 * width * width * (4 * tok + 2 * remote), bytes_accessed=2 * width * (6 * tok + 3 * remote + 4 * width), transcendentals=0),
        name="pack_gradients",
    )(core, mixed, dlow, act, far, dq, dk, dv, dkf, dvf, local, gain, router)


def sum_kernel(terms, index_ref, *refs):
    count = (len(refs)) // (terms + 1)
    for k in range(count):
        total = None
        for t in range(terms):
            value = refs[t * count + k][...].astype(f32)
            total = value if total is None else total + value
        refs[terms * count + k][...] = total.astype(bf16)


def sum_pieces(index, arrays):
    n, shape = arrays[0].shape[0], arrays[0].shape[1:]
    zeros = (0,) * len(shape)
    views = [pl.BlockSpec((1,) + shape, functools.partial(lambda k, i, s: (s[0] ^ k,) + zeros, k)) for k in range(n)]
    return pl.pallas_call(
        functools.partial(sum_kernel, len(arrays)),
        grid_spec=pltpu.PrefetchScalarGridSpec(
            num_scalar_prefetch=1,
            grid=(1,),
            in_specs=views * len(arrays),
            out_specs=[pl.BlockSpec((1,) + shape, lambda i, s: (0,) + zeros)] * n,
        ),
        out_shape=[jax.ShapeDtypeStruct((1,) + shape, bf16)] * n,
        compiler_params=pltpu.CompilerParams(vmem_limit_bytes=48 * 2**20),
        cost_estimate=pl.CostEstimate(flops=0, bytes_accessed=2 * n * math.prod(shape) * (len(arrays) + 1), transcendentals=0),
        name="sum_pieces",
    )(index, *[a for a in arrays for _ in range(n)])


def unpack_kernel(index_ref, own_ref, other_ref, out_ref):
    piece = out_ref.shape[0] // 8
    for c in range(2):
        mine = index_ref[0] == c
        for k in range(4):
            at = k ^ index_ref[2]
            value = jnp.where(mine, own_ref[0, at, 0:piece, :].astype(f32), other_ref[0, at, 0:piece, :].astype(f32))
            out_ref[(c * 4 + k) * piece : (c * 4 + k + 1) * piece, :] = value


def unpack(index, own, other, first, count):
    width = own.shape[3]
    source = pl.BlockSpec((1,) + own.shape[1:], lambda j, s: ((j + first) ^ s[1], 0, 0, 0))
    return pl.pallas_call(
        unpack_kernel,
        grid_spec=pltpu.PrefetchScalarGridSpec(
            num_scalar_prefetch=1,
            grid=(count,),
            in_specs=[source, source],
            out_specs=pl.BlockSpec((width, width), lambda j, s: (0, j)),
        ),
        out_shape=jax.ShapeDtypeStruct((width, count * width), f32),
        compiler_params=pltpu.CompilerParams(vmem_limit_bytes=32 * 2**20),
        name="unpack_sums",
    )(index, own, other)


def sum_everywhere(mine, theirs):
    me_c, me_e = lax.axis_index("ctx"), lax.axis_index("exp")
    place = lambda v: v.reshape(1)
    got = lax.ppermute(theirs, "exp", xor_pairs(8, 1))
    parts = sum_pieces(place(me_c), [mine, got])
    parts = [parts[0]] + [lax.ppermute(parts[k], "ctx", xor_pairs(4, k)) for k in range(1, 4)]
    parts = sum_pieces(place(me_e >> 1), [p[0] for p in parts])
    parts = [parts[0]] + [lax.ppermute(parts[k], "exp", xor_pairs(8, 2 * k)) for k in range(1, 4)]
    [piece] = sum_pieces(place(me_e * 0), parts)
    column = jnp.concatenate([piece] + [lax.ppermute(piece, "exp", xor_pairs(8, 2 * k)) for k in range(1, 4)], axis=0)[None]
    own = jnp.concatenate([column] + [lax.ppermute(column, "ctx", xor_pairs(4, k)) for k in range(1, 4)], axis=0)
    other = lax.ppermute(own, "exp", xor_pairs(8, 1))
    return own, other

P = jax.sharding.PartitionSpec


def rms_inverse(tensor):
    return lax.rsqrt(jnp.mean(tensor * tensor, axis=-1, keepdims=True) + epsilon)


def body(inputs, prev_logits, routes, attn_gain, w_qkv, w_out, moe_gain, router, const_gate, const_vec, w_gate, w_up, w_down, out_grad):
    n_ctx, n_exp = lax.axis_size("ctx"), lax.axis_size("exp")
    me_c, me_e = lax.axis_index("ctx"), lax.axis_index("exp")
    tok, width = inputs.shape[1], inputs.shape[2]
    plen = tok - CONT_LEN
    split = n_exp // FFN_EXPERTS
    capacity = max(4, tok // 64 * 12)
    first = -(-capacity // 32) * 16
    groups = ((0, first), (first, capacity - first))
    home = (me_e // split).reshape(1)

    def deal(value):
        value = jnp.repeat(value, split, axis=0) if split > 1 else value
        return lax.all_to_all(value, "exp", 0, 0, tiled=True)

    def give_back(value):
        value = lax.all_to_all(value, "exp", 0, 0, tiled=True)
        return [value[r::split] if split > 1 else value for r in range(split)]

    x_low = inputs[0]
    far_rows = jnp.concatenate([lax.ppermute(x_low[:plen], "ctx", xor_pairs(n_ctx, k)) for k in range(1, n_ctx)], axis=0)
    flags = jnp.where((me_c ^ jnp.arange(1, n_ctx)) < me_c, 0.0, NEG).astype(f32)

    upstream_low = out_grad[0]
    prev = jnp.pad(prev_logits[0], ((0, 0), (0, EXTRA - ALL_EXPERTS)))
    mix = jnp.concatenate([router, jnp.zeros((width, 4), bf16), const_gate[0], const_gate[1], jnp.zeros((width, EXTRA - 20), bf16)], axis=1)
    router_pad = jnp.pad(router, ((0, 0), (0, EXTRA - ALL_EXPERTS)))
    turned, chosen, early_sent = route_plan(home, routes[0].T, upstream_low, prev, groups)

    tokens_in = x_low.astype(f32)
    inverse_attn = rms_inverse(tokens_in)
    act_low = (tokens_in * inverse_attn * attn_gain).astype(bf16)
    projected = dot_nn(act_low, w_qkv).astype(bf16)
    early = deal(early_sent)
    far_in = far_rows.astype(f32)
    act_far = (far_in * rms_inverse(far_in) * attn_gain).astype(bf16)
    kv_far = dot_nn(act_far, w_qkv[:, width:]).astype(bf16)

    mixed_low, lse = attention_forward(flags, projected, kv_far, plen)
    mixed_low, early = lax.optimization_barrier((mixed_low, early))
    hidden, moe_low, sent = after_attention(mixed_low, x_low, w_out, moe_gain[None], turned)
    got = [deal(part.reshape(FFN_EXPERTS, -1, width)) for part in sent]

    local_out, d_normed_local, probs, d_probs, small_local = local_part(hidden, moe_low, upstream_low, prev, routes[0], mix, moe_gain[None], const_vec)
    got[0], local_out, d_normed_local = lax.optimization_barrier((got[0], local_out, d_normed_local))

    got = [part.reshape(-1, width) for part in got]
    passes = [expert_pass(group, home, r, early, router_pad, w_gate, w_up, w_down) for group, r in zip(groups, got)]
    d_got = [give_back(p[1].reshape(n_exp, -1, width)) for p in passes]
    gate_up_low, down_low = weight_gradients(got, [p[2] for p in passes], [p[3] for p in passes], [p[4] for p in passes], [p[5] for p in passes])
    outs = jnp.concatenate([p[0].reshape(n_exp, -1, width + EXTRA) for p in passes], axis=1)
    d_got, gate_up_low, down_low, outs = lax.optimization_barrier((d_got, gate_up_low, down_low, outs))
    out_got = give_back(outs)

    d_got = [[part.reshape(-1, width) for part in group] for group in d_got]
    d_hidden, d_attn_low, d_mixed, small_gain = combine(chosen, d_got, d_normed_local, hidden, moe_gain[None], upstream_low, w_out)

    sum_gate_up = lax.psum_scatter(gate_up_low, "ctx", scatter_dimension=1, tiled=True).astype(f32)
    sum_down = lax.psum_scatter(down_low, "ctx", scatter_dimension=0, tiled=True).astype(f32)

    dq, dk, dv, dk_far, dv_far = attention_backward(flags, projected, kv_far, mixed_low, d_mixed, lse, plen)
    dq, out_got = lax.optimization_barrier((dq, out_got))
    mixed_out, d_logits, small_router = finish(chosen, out_got, groups, local_out, probs, d_probs, moe_low)

    wq, wk, wv = (w_qkv[:, i * width : (i + 1) * width] for i in range(3))
    d_act_far = (dot_nt(dk_far, wk) + dot_nt(dv_far, wv)).astype(bf16).reshape(n_ctx - 1, plen, width)
    far_back = [lax.ppermute(d_act_far[k - 1], "ctx", xor_pairs(n_ctx, k)) for k in range(1, n_ctx)]
    d_act = dot_nt(dq, wq) + dot_nt(dk, wk) + dot_nt(dv, wv)
    d_act = jnp.concatenate([d_act[:plen] + sum(part.astype(f32) for part in far_back), d_act[plen:]], axis=0)
    scaled = d_act * attn_gain
    d_inputs = d_hidden + inverse_attn * scaled - tokens_in * inverse_attn**3 * jnp.mean(scaled * tokens_in, axis=-1, keepdims=True)

    if n_ctx == 4 and n_exp == 8:
        core, z = me_e & 1, me_e >> 1
        mine, theirs = pack(core.reshape(1), mixed_low, d_attn_low, act_low, act_far, dq, dk, dv, dk_far, dv_far, small_local, small_gain, small_router)
        own, other = sum_everywhere(mine, theirs)
        index = jnp.stack([core, me_c, z])
        out_sum = unpack(index, own, other, 0, 1)
        qkv_sum = unpack(index, own, other, 1, 3)
        small = jnp.where(core == 0, own[:, :, -SMALL:], other[:, :, -SMALL:])
        small = [lax.dynamic_slice(small, (me_c, k ^ z, 0, 0), (1, 1, SMALL, width)).reshape(SMALL, width).astype(f32) for k in range(4)]
    else:
        d_w_k = dot_tn(act_low, dk) + dot_tn(act_far, dk_far)
        d_w_v = dot_tn(act_low, dv) + dot_tn(act_far, dv_far)
        parts = [dot_tn(mixed_low, d_attn_low), dot_tn(act_low, dq), d_w_k, d_w_v, small_local, small_gain, small_router]
        out_sum, q_sum, k_sum, v_sum, *small = [p.astype(f32) for p in lax.psum([p.astype(bf16) for p in parts], ("ctx", "exp"))]
        qkv_sum = jnp.concatenate([q_sum, k_sum, v_sum], axis=1)
        small = small[:2] + [small[2][:SMALL], small[2][SMALL:]]
    d_attn_gain = jnp.sum(qkv_sum * w_qkv.astype(f32), axis=1) / attn_gain
    d_const_gate = jnp.stack([small[0][0:2].T, small[0][2:4].T])
    return (
        mixed_out[None],
        d_inputs[None],
        d_logits[None, :, :ALL_EXPERTS],
        d_attn_gain,
        qkv_sum,
        out_sum,
        small[1][0],
        jnp.concatenate([small[2], small[3][: ALL_EXPERTS - SMALL]], axis=0).T,
        d_const_gate,
        small[0][4:6],
        sum_gate_up[0][None],
        sum_gate_up[1][None],
        sum_down[None],
    )


def solution(mesh):
    rows = P("ctx", "exp", None)
    expert = P("exp", None, None)
    summed = P("exp", "ctx", None)
    return jax.shard_map(
        body,
        mesh=mesh,
        in_specs=(rows, rows, rows, P(), P(), P(), P(), P(), P(), P(), expert, expert, expert, rows),
        out_specs=(rows, rows, rows, P(), P(), P(), P(), P(), P(), P(), summed, summed, summed),
        check_vma=False,
    )
```

time: 1080 us -> 484 us (0.45)
  matrix products: 367 us -> 13.6 us
  Pallas kernels: 0 us -> 170 us
  waiting for transfers between devices: 278 us -> 129 us
  local copies, waits for them, and re-layouts: 200 us -> 55.9 us
  other arithmetic: 146 us -> 20.5 us
  starting transfers between devices: 21.9 us -> 49.9 us
  blocking collectives: 41.7 us -> 25.7 us
    dot_general x104 -> x7, matrix products: 365 us -> 13.6 us  [the longest x5 7.27 us: dot_nt(): lax.dot_general(a, b, (((1,), (1,)), ((), ())), preferred_element_type=f32)]
    psum x1 -> x0, waiting for transfers between devices: 194 us -> none  [body(): lax.psum((d_attn_gain, d_w_qkv, d_w_out, d_moe_gain, d_router, d_const_ga...]
    pallas_call x0 -> x16, Pallas kernels: none -> 170 us  [the longest x1 39.4 us: attention_backward(): pl.pallas_call(functools.partial(attention_backward_kernel, plen), grid=(...]
    ppermute x0 -> x20, waiting for transfers between devices: none -> 120 us  [the longest x3 45 us: sum_everywhere(): lax.ppermute(parts[k], 'ctx', xor_pairs(4, k))]
    reduce_scatter x3 -> x2, waiting for transfers between devices: 61 us -> 0.01 us  [the longest x1 0.01 us: body(): lax.psum_scatter(down_low, 'ctx', scatter_dimension=0, tiled=True)]
    reduce_sum x20 -> x4, other arithmetic: 54.9 us -> 4.74 us  [the longest x1 3.77 us: body(): d_attn_gain = jnp.sum(qkv_sum * w_qkv.astype(f32), axis=1) / attn_gain]
    psum x1 -> x0, blocking collectives: 41.7 us -> none  [body(): lax.psum((d_attn_gain, d_w_qkv, d_w_out, d_moe_gain, d_router, d_const_ga...]
    gather x6 -> x0, local copies, waits for them, and re-layouts: 36.5 us -> none  [the longest x2 15.6 us: body(): expert_out.reshape(-1, model_width)[jnp.where(is_ffn, position, 0)]]
  transfers between devices with their start and end apart: 9 -> 27, of which waited for: 6 -> 17; matrix products, arithmetic and copies ran while one was open for 28% -> 9% of each run, Pallas kernels for 0% -> 34%
where the time goes in v1:
time: 484 us; the launch traced here: 479 us
  Pallas kernels  170 us (35%)
  waiting for transfers between devices  129 us (27%)
  local copies, waits for them, and re-layouts  55.9 us (12%)
  starting transfers between devices  49.9 us (10%)
  blocking collectives  25.7 us (5%)
  other arithmetic  20.5 us (4%)
  between operations  14.9 us (3%)
  matrix products  13.6 us (3%)
    unnamed x172, local copies, waits for them, and re-layouts  45.7 us
    ppermute x3, waiting for transfers between devices, sum_everywhere(): lax.ppermute(parts[k], 'ctx', xor_pairs(4, k))  45 us
    pallas_call x1, Pallas kernels, attention_backward(): pl.pallas_call(functools.partial(attention_backward_kernel, plen), grid=(...  39.4 us
    pallas_call x2, Pallas kernels, expert_pass(): pl.pallas_call(functools.partial(expert_kernel, group), grid=(ff // tile,...  36.2 us
    all_to_all x1, blocking collectives, deal(): return lax.all_to_all(value, 'exp', 0, 0, tiled=True)  25.7 us
    pallas_call x1, Pallas kernels, attention_forward(): pl.pallas_call(functools.partial(attention_forward_kernel, plen), grid=(p...  23.5 us
    ppermute x3, waiting for transfers between devices, sum_everywhere(): lax.ppermute(column, 'ctx', xor_pairs(4, k))  22.9 us
    ppermute x3, waiting for transfers between devices, body(): lax.ppermute(x_low[:plen], 'ctx', xor_pairs(n_ctx, k))  16.7 us
  transfers between devices with their start and end apart: 27, of which 17 were waited for; matrix products, arithmetic and copies ran while one was open for 9% of the time, Pallas kernels for 34%

profile of v1, /device:TPU:0, one launch (start us, length us, event | category | flops | bytes accessed | tf_op | source)
XLA Modules:
  0.0 479.3 jit_solution(10288366142621523919)
XLA Ops:
  10.6 4.4 route_plan.1
  17.8 7.0 %all-to-all-start = ((bf16[8,144,896]{2,1,0:T(8,128)(2,1)}), bf16[8,144,896]{2,1,0:T(8,128)(2,1)}, u32[]{:S(2)}, u32[]{:S(2)}) async-start(bf16[8,144,896]{2,1,0:T(8,128)(2,1)} %get-tuple-element.80), calls=%async_computation | async-start | bytes 4128768 | tf_op jit(solution)/shard_map/all_to_all | solution.py:725
  30.1 8.6 %collective-permute-done.2 = bf16[256,768]{1,0:T(8,128)(2,1)S(1)} collective-permute-done((bf16[256,768]{1,0:T(8,128)(2,1)}, bf16[256,768]{1,0:T(8,128)(2,1)S(1)}, u32[]{:S(2)}, u32[]{:S(2)}) %collective-permute-start.2) | collective-permute-done | bytes 393248 | tf_op jit(solution)/shard_map/ppermute | solution.py:732
  38.7 8.0 %collective-permute-done.1 = bf16[256,768]{1,0:T(8,128)(2,1)S(1)} collective-permute-done((bf16[256,768]{1,0:T(8,128)(2,1)}, bf16[256,768]{1,0:T(8,128)(2,1)S(1)}, u32[]{:S(2)}, u32[]{:S(2)}) %collective-permute-start.1) | collective-permute-done | bytes 393248 | tf_op jit(solution)/shard_map/ppermute | solution.py:732
  52.0 4.3 convolution_convert_fusion.q_ref.k_ref.v_ref
  56.3 23.5 %attention_forward.1 = (bf16[768,768]{1,0:T(8,128)(2,1)S(1)}, f32[6,16,768]{2,1,0:T(8,128)S(1)}) custom-call(f32[3]{0:T(128)S(1)} %compare_select_fusion.flags_ref, bf16[768,2304]{1,0:T(8,128)(2,1)} %convolution_convert_fusion.q_ref.k_ref.v_ref, bf16[768,2304]{1,0:T(8,128)(2,1)} %convolution_convert_fusion.q_ref.k_ref.v_ref, ...), custom_call_target="tpu_custom_call" | custom-call | flops 3623878656 | bytes 7077888 | tf_op jit(solution)/shard_map/attention_forward/pallas_call | solution.py:86
  91.4 25.7 %all_to_all.30 = bf16[8,64,768]{2,1,0:T(8,128)(2,1)S(1)} all-to-all(bf16[8,64,768]{2,1,0:T(8,128)(2,1)S(1)} %bitcast.100), channel_id=1, replica_groups=mesh['ctx'=4,'exp'=8] {'exp'}, dimensions={0} | all-to-all | bytes 1572864 | tf_op jit(solution)/shard_map/all_to_all | solution.py:725
  117.1 4.4 all-to-all-start.1
  122.3 16.6 %expert_pass.3 = (bf16[512,896]{1,0:T(8,128)(2,1)S(1)}, bf16[512,768]{1,0:T(8,128)(2,1)S(1)}, bf16[512,768]{1,0:T(8,128)(2,1)S(1)}, bf16[512,2048]{1,0:T(8,128)(...) custom-call(s32[1]{0:T(128)} %bitcast.home_ref, bf16[512,768]{1,0:T(8,128)(2,1)S(1)} %bitcast.97, ...), custom_call_target="tpu_custom_call" | custom-call | flops 9663676416 | bytes 19660800 | tf_op jit(solution)/shard_map/expert_pass/pallas_call | solution.py:337
  142.4 4.2 all-to-all-done.1
  146.7 4.2 all-to-all-start.4
  157.6 10.5 %local_part.1 = (f32[768,768]{1,0:T(8,128)}, f32[768,768]{1,0:T(8,128)}, f32[768,128]{1,0:T(8,128)S(1)}, f32[768,128]{1,0:T(8,128)S(1)}, f32[8,768]{1,0:T(8,128)S(1)}) custom-call(f32[768,768]{1,0:T(8,128)} %copy-done.3, bf16[768,768]{1,0:T(8,128)(2,1)S(1)} %get-tuple-element.86.low_ref.refs_6_, bf16[768,768]{1,0:T(8,128)(2,1)S(1)} %bitcast.89, ...), custom_call_target="tpu_custom_call" | custom-call | flops 1056964608 | bytes 9437184 | tf_op jit(solution)/shard_map/local_part/pallas_call | solution.py:490
  170.1 19.6 %expert_pass.2 = (bf16[640,896]{1,0:T(8,128)(2,1)S(1)}, bf16[640,768]{1,0:T(8,128)(2,1)S(1)}, bf16[640,768]{1,0:T(8,128)(2,1)S(1)}, bf16[640,2048]{1,0:T(8,128)(...) custom-call(s32[1]{0:T(128)} %bitcast.home_ref, bf16[640,768]{1,0:T(8,128)(2,1)} %bitcast.10.rows_ref.refs_0_, ...), custom_call_target="tpu_custom_call" | custom-call | flops 12079595520 | bytes 22216704 | tf_op jit(solution)/shard_map/expert_pass/pallas_call | solution.py:337
  192.6 5.0 %all-to-all-start.2 = ((bf16[8,80,768]{2,1,0:T(8,128)(2,1)}), bf16[8,80,768]{2,1,0:T(8,128)(2,1)S(1)}, u32[]{:S(2)}, u32[]{:S(2)}) async-start(bf16[8,80,768]{2,1,0:T(8,128)(2,1)} %bitcast.94), calls=%async_computation.2 | async-start | bytes 1966080 | tf_op jit(solution)/shard_map/all_to_all | solution.py:728
  202.1 16.7 %weight_gradients.1 = (bf16[2,768,2048]{2,1,0:T(8,128)(2,1)}, bf16[2048,768]{1,0:T(8,128)(2,1)}) custom-call(bf16[640,768]{1,0:T(8,128)(2,1)} %bitcast.10.rows_ref.refs_0_, bf16[512,768]{1,0:T(8,128)(2,1)S(1)} %bitcast.98, bf16[640,768]{1,0:T(8,128)(2,1)S(1)} %copy-done.61, bf16[512,768]{1,0:T(8,128)(2,1)S(1)} %copy-done.63, ...), custom_call_target="tpu_custom_call" | custom-call | flops 10871635968 | bytes 27131904 | tf_op jit(solution)/shard_map/weight_gradients/pallas_call | solution.py:385
  218.7 4.1 all-to-all-done.2
  222.8 4.4 all-to-all-start.5
  229.1 7.6 %combine_gradients.1 = (f32[768,768]{1,0:T(8,128)}, bf16[768,768]{1,0:T(8,128)(2,1)S(1)}, bf16[768,768]{1,0:T(8,128)(2,1)S(1)}, f32[8,768]{1,0:T(8,128)S(1)}) custom-call(bf16[768,640]{1,0:T(8,128)(2,1)S(1)} %get-tuple-element.77.refs_0_, bf16[768,512]{1,0:T(8,128)(2,1)S(1)} %copy-done.9, bf16[640,768]{1,0:T(8,128)(2,1)S(1)} %bitcast.90, ...), custom_call_target="tpu_custom_call" | custom-call | flops 2264924160 | bytes 14155776 | tf_op jit(solution)/shard_map/combine_gradients/pallas_call | solution.py:526
  238.8 39.4 %attention_backward.1 = (bf16[768,768]{1,0:T(8,128)(2,1)S(1)}, bf16[768,768]{1,0:T(8,128)(2,1)S(1)}, bf16[768,768]{1,0:T(8,128)(2,1)S(1)}, bf16[768,768]{1,0:T(8,128)(2,1)S(1)}, bf16[768,768]{1,0:T(8,128)(2,1)S(1)}) custom-call(f32[3]{0:T(128)S(1)} %compare_select_fusion.flags_ref, bf16[768,2304]{1,0:T(8,128)(2,1)} %convolution_convert_fusion.q_ref.k_ref.v_ref, ...), custom_call_target="tpu_custom_call" | custom-call | flops 9059696640 | bytes 14155776 | tf_op jit(solution)/shard_map/attention_backward/pallas_call | solution.py:178
  284.4 6.1 %finish_outputs.1 = (bf16[768,768]{1,0:T(8,128)(2,1)}, f32[768,128]{1,0:T(8,128)S(1)}, f32[16,768]{1,0:T(8,128)S(1)}) custom-call(bf16[768,640]{1,0:T(8,128)(2,1)S(1)} %get-tuple-element.77.refs_0_, bf16[768,512]{1,0:T(8,128)(2,1)S(1)} %copy-done.10, bf16[8,144,896]{2,1,0:T(8,128)(2,1)} %all-to-all-done.5.refs_2_, f32[768,768]{1,0:T(8,128)} %get-tuple-element.114.refs_3_, ...), custom_call_target="tpu_custom_call" | custom-call | flops 1585446912 | bytes 9437184 | tf_op jit(solution)/shard_map/finish_outputs/pallas_call | solution.py:567
  291.3 9.9 %pack_gradients.1 = (bf16[4,4,104,768]{3,2,1,0:T(8,128)(2,1)}, bf16[4,4,104,768]{3,2,1,0:T(8,128)(2,1)}) custom-call(s32[1]{0:T(128)} %bitcast.22.core_ref, bf16[768,768]{1,0:T(8,128)(2,1)S(1)} %copy-done.51, bf16[768,768]{1,0:T(8,128)(2,1)S(1)} %copy-done.37, bf16[768,768]{1,0:T(8,128)(2,1)S(1)} %copy-done.19, bf16[768,768]{1,0:T(8,128)(2,1)S(1)} %copy-done.17, ...), custom_call_target="tpu_custom_call" | custom-call | flops 5435817984 | bytes 15335424 | tf_op jit(solution)/shard_map/pack_gradients/pallas_call | solution.py:618
  301.5 4.7 collective-permute-done.6.refs_4_.refs_5_.refs_6_.refs_7_
  316.0 24.5 %collective-permute-done.7 = bf16[1,4,104,768]{3,2,1,0:T(8,128)(2,1)S(1)} collective-permute-done((bf16[1,4,104,768]{3,2,1,0:T(8,128)(2,1)}, bf16[1,4,104,768]{3,2,1,0:T(8,128)(2,1)S(1)}, u32[]{:S(2)}, u32[]{:S(2)}) %collective-permute-start.7) | collective-permute-done | bytes 639008 | tf_op jit(solution)/shard_map/ppermute | solution.py:696
  340.4 5.3 %collective-permute-done.8 = bf16[1,4,104,768]{3,2,1,0:T(8,128)(2,1)S(1)} collective-permute-done((bf16[1,4,104,768]{3,2,1,0:T(8,128)(2,1)}, bf16[1,4,104,768]{3,2,1,0:T(8,128)(2,1)S(1)}, u32[]{:S(2)}, u32[]{:S(2)}) %collective-permute-start.8) | collective-permute-done | bytes 639008 | tf_op jit(solution)/shard_map/ppermute | solution.py:696
  345.7 15.2 %collective-permute-done.9 = bf16[1,4,104,768]{3,2,1,0:T(8,128)(2,1)S(1)} collective-permute-done((bf16[1,4,104,768]{3,2,1,0:T(8,128)(2,1)S(1)}, bf16[1,4,104,768]{3,2,1,0:T(8,128)(2,1)S(1)}, u32[]{:S(2)}, u32[]{:S(2)}) %collective-permute-start.9) | collective-permute-done | bytes 639008 | tf_op jit(solution)/shard_map/ppermute | solution.py:696
  369.0 8.9 %collective-permute-done.11.refs_2_ = bf16[1,104,768]{2,1,0:T(8,128)(2,1)S(1)} collective-permute-done((bf16[1,104,768]{2,1,0:T(8,128)(2,1)S(1)}, bf16[1,104,768]{2,1,0:T(8,128)(2,1)S(1)}, u32[]{:S(2)}, u32[]{:S(2)}) %collective-permute-start.11) | collective-permute-done | bytes 159776 | tf_op jit(solution)/shard_map/ppermute | solution.py:698
  386.9 6.4 %collective-permute-done.14 = bf16[1,104,768]{2,1,0:T(8,128)(2,1)S(1)} collective-permute-done((bf16[1,104,768]{2,1,0:T(8,128)(2,1)S(1)}, bf16[1,104,768]{2,1,0:T(8,128)(2,1)S(1)}, u32[]{:S(2)}, u32[]{:S(2)}) %collective-permute-start.14) | collective-permute-done | bytes 159776 | tf_op jit(solution)/shard_map/ppermute | solution.py:700
  399.3 12.4 %collective-permute-done.18 = bf16[1,4,104,768]{3,2,1,0:T(8,128)(2,1)S(1)} collective-permute-done((bf16[1,4,104,768]{3,2,1,0:T(8,128)(2,1)S(1)}, bf16[1,4,104,768]{3,2,1,0:T(8,128)(2,1)S(1)}, u32[]{:S(2)}, u32[]{:S(2)}) %collective-permute-start.18) | collective-permute-done | bytes 639008 | tf_op jit(solution)/shard_map/ppermute | solution.py:701
  411.7 10.4 %collective-permute-done.17 = bf16[1,4,104,768]{3,2,1,0:T(8,128)(2,1)S(1)} collective-permute-done((bf16[1,4,104,768]{3,2,1,0:T(8,128)(2,1)S(1)}, bf16[1,4,104,768]{3,2,1,0:T(8,128)(2,1)S(1)}, u32[]{:S(2)}, u32[]{:S(2)}) %collective-permute-start.17) | collective-permute-done | bytes 639008 | tf_op jit(solution)/shard_map/ppermute | solution.py:701
  432.8 3.9 collective-permute-done.5
  436.7 8.0 %collective-permute-done.4 = bf16[256,768]{1,0:T(8,128)(2,1)} collective-permute-done((bf16[256,768]{1,0:T(8,128)(2,1)}, bf16[256,768]{1,0:T(8,128)(2,1)}, u32[]{:S(2)}, u32[]{:S(2)}) %collective-permute-start.4) | collective-permute-done | bytes 393248 | tf_op jit(solution)/shard_map/ppermute | solution.py:778
  452.5 5.3 %unpack_sums.2 = f32[768,2304]{1,0:T(8,128)} custom-call(s32[3]{0:T(128)S(1)} %pad_add_fusion.index_ref, bf16[4,4,104,768]{3,2,1,0:T(8,128)(2,1)S(1)} %pad_maximum_fusion.own_ref, bf16[4,4,104,768]{3,2,1,0:T(8,128)(2,1)} %collective-permute-done.19.other_ref), custom_call_target="tpu_custom_call" | custom-call | tf_op jit(solution)/shard_map/unpack_sums/pallas_call | solution.py:677
  (257 shorter events, 125.0 us)
Async XLA Ops:
  17.8 63.8 %all-to-all-start = ((bf16[8,144,896]{2,1,0:T(8,128)(2,1)}), bf16[8,144,896]{2,1,0:T(8,128)(2,1)}, u32[]{:S(2)}, u32[]{:S(2)}) async-start(bf16[8,144,896]{2,1,0:T(8,128)(2,1)} %get-tuple-element.80), calls=%async_computation | async-start | bytes 4128768 | tf_op jit(solution)/shard_map/all_to_all | solution.py:725
  25.7 13.1 %collective-permute-start.2 = (bf16[256,768]{1,0:T(8,128)(2,1)}, bf16[256,768]{1,0:T(8,128)(2,1)S(1)}, u32[]{:S(2)}, u32[]{:S(2)}) collective-permute-start(bf16[256,768]{1,0:T(8,128)(2,1)} %slice_bitcast_fusion.1), channel_id=1, source_target_pairs={{0,24},{8,16},{16,8},{24,0},{1,25},{9,17},{17,9},{25,1},{2,26},{10... | collective-permute-start | bytes 1179656 | tf_op jit(solution)/shard_map/ppermute | solution.py:732
  28.1 18.6 %collective-permute-start.1 = (bf16[256,768]{1,0:T(8,128)(2,1)}, bf16[256,768]{1,0:T(8,128)(2,1)S(1)}, u32[]{:S(2)}, u32[]{:S(2)}) collective-permute-start(bf16[256,768]{1,0:T(8,128)(2,1)} %slice_bitcast_fusion.1), channel_id=1, source_target_pairs={{0,16},{8,24},{16,0},{24,8},{1,17},{9,25},{17,1},{25,9},{2,18},{10... | collective-permute-start | bytes 1179656 | tf_op jit(solution)/shard_map/ppermute | solution.py:732
  28.6 18.2 %collective-permute-start = (bf16[256,768]{1,0:T(8,128)(2,1)}, bf16[256,768]{1,0:T(8,128)(2,1)S(1)}, u32[]{:S(2)}, u32[]{:S(2)}) collective-permute-start(bf16[256,768]{1,0:T(8,128)(2,1)} %slice_bitcast_fusion.1), channel_id=1, source_target_pairs={{0,8},{8,0},{16,24},{24,16},{1,9},{9,1},{17,25},{25,17},{2,10},{10... | collective-permute-start | bytes 1179656 | tf_op jit(solution)/shard_map/ppermute | solution.py:732
  91.4 25.7 %copy-start.22 = (bf16[640,768]{1,0:T(8,128)(2,1)}, bf16[640,768]{1,0:T(8,128)(2,1)S(1)}, u32[]{:S(2)}) copy-start(bf16[640,768]{1,0:T(8,128)(2,1)S(1)} %get-tuple-element.84) | copy-start | bytes 2949124
  91.4 30.1 %copy-start.79 = (bf16[768,12]{0,1:T(8,128)(2,1)S(1)}, bf16[768,12]{0,1:T(8,128)(2,1)}, u32[]{:S(2)}) copy-start(bf16[768,12]{0,1:T(8,128)(2,1)} %param.21) | copy-start | bytes 55300
  117.1 29.6 %all-to-all-start.1 = ((bf16[8,80,768]{2,1,0:T(8,128)(2,1)}), bf16[8,80,768]{2,1,0:T(8,128)(2,1)}, u32[]{:S(2)}, u32[]{:S(2)}) async-start(bf16[8,80,768]{2,1,0:T(8,128)(2,1)} %bitcast.95), calls=%async_computation.1 | async-start | bytes 1966080 | tf_op jit(solution)/shard_map/all_to_all | solution.py:725
  122.3 28.5 %copy-start.81 = (bf16[2,768,2]{1,2,0:T(2,128)(2,1)S(1)}, bf16[2,768,2]{1,2,0:T(2,128)(2,1)}, u32[]{:S(2)}) copy-start(bf16[2,768,2]{1,2,0:T(2,128)(2,1)} %param.22) | copy-start | bytes 18436
  146.7 46.0 %all-to-all-start.4 = ((bf16[8,64,768]{2,1,0:T(8,128)(2,1)}), bf16[8,64,768]{2,1,0:T(8,128)(2,1)}, u32[]{:S(2)}, u32[]{:S(2)}) async-start(bf16[8,64,768]{2,1,0:T(8,128)(2,1)} %bitcast.99), calls=%async_computation.4 | async-start | bytes 1572864 | tf_op jit(solution)/shard_map/all_to_all | solution.py:728
  192.6 30.2 %all-to-all-start.2 = ((bf16[8,80,768]{2,1,0:T(8,128)(2,1)}), bf16[8,80,768]{2,1,0:T(8,128)(2,1)S(1)}, u32[]{:S(2)}, u32[]{:S(2)}) async-start(bf16[8,80,768]{2,1,0:T(8,128)(2,1)} %bitcast.94), calls=%async_computation.2 | async-start | bytes 1966080 | tf_op jit(solution)/shard_map/all_to_all | solution.py:728
  197.6 252.5 %reduce-scatter.5.cloned.1.call-start = ((), (), s32[]{:S(2)}) async-start(), calls=%async_computation.9 | async-start | bytes 3932160 | tf_op jit(solution)/shard_map/reduce_scatter | solution.py:770
  222.8 60.5 %all-to-all-start.5 = ((bf16[8,144,896]{2,1,0:T(8,128)(2,1)}), bf16[8,144,896]{2,1,0:T(8,128)(2,1)}, u32[]{:S(2)}, u32[]{:S(2)}) async-start(bf16[8,144,896]{2,1,0:T(8,128)(2,1)} %pad_maximum_fusion.1), calls=%async_computation.5 | async-start | bytes 4128768 | tf_op jit(solution)/shard_map/all_to_all | solution.py:728
  227.2 241.7 %reduce-scatter.3.cloned.1.call-start = ((), (), s32[]{:S(2)}) async-start(), calls=%async_computation.8 | async-start | bytes 7864320 | tf_op jit(solution)/shard_map/reduce_scatter | solution.py:769
  238.8 44.5 %copy-start.10 = (bf16[768,512]{1,0:T(8,128)(2,1)S(1)}, bf16[768,512]{1,0:T(8,128)(2,1)}, u32[]{:S(2)}) copy-start(bf16[768,512]{1,0:T(8,128)(2,1)} %copy-done.8) | copy-start | bytes 2359300
  238.8 44.5 %copy-start.28 = (f32[768,128]{1,0:T(8,128)S(1)}, f32[768,128]{1,0:T(8,128)}, u32[]{:S(2)}) copy-start(f32[768,128]{1,0:T(8,128)} %copy-done.27) | copy-start | bytes 1179652
  301.1 5.1 %collective-permute-start.6 = (bf16[4,4,104,768]{3,2,1,0:T(8,128)(2,1)}, bf16[4,4,104,768]{3,2,1,0:T(8,128)(2,1)S(1)}, u32[]{:S(2)}, u32[]{:S(2)}) collective-permute-start(bf16[4,4,104,768]{3,2,1,0:T(8,128)(2,1)} %get-tuple-element.130), channel_id=1, source_target_pairs={{0,1},{1,0},{2,3},{3,2},{4,5},{5,4},{6,7},{7,6},{8,9},{9,8},{10,11... | collective-permute-start | bytes 7667720 | tf_op jit(solution)/shard_map/ppermute | solution.py:694
  312.5 28.0 %collective-permute-start.7 = (bf16[1,4,104,768]{3,2,1,0:T(8,128)(2,1)}, bf16[1,4,104,768]{3,2,1,0:T(8,128)(2,1)S(1)}, u32[]{:S(2)}, u32[]{:S(2)}) collective-permute-start(bf16[1,4,104,768]{3,2,1,0:T(8,128)(2,1)} %get-tuple-element.132), channel_id=1, source_target_pairs={{0,8},{8,0},{16,24},{24,16},{1,9},{9,1},{17,25},{25,17},{2,10},{10... | collective-permute-start | bytes 1916936 | tf_op jit(solution)/shard_map/ppermute | solution.py:696
  314.0 31.7 %collective-permute-start.8 = (bf16[1,4,104,768]{3,2,1,0:T(8,128)(2,1)}, bf16[1,4,104,768]{3,2,1,0:T(8,128)(2,1)S(1)}, u32[]{:S(2)}, u32[]{:S(2)}) collective-permute-start(bf16[1,4,104,768]{3,2,1,0:T(8,128)(2,1)} %get-tuple-element.133), channel_id=1, source_target_pairs={{0,16},{8,24},{16,0},{24,8},{1,17},{9,25},{17,1},{25,9},{2,18},{10... | collective-permute-start | bytes 1916936 | tf_op jit(solution)/shard_map/ppermute | solution.py:696
  315.2 45.8 %collective-permute-start.9 = (bf16[1,4,104,768]{3,2,1,0:T(8,128)(2,1)S(1)}, bf16[1,4,104,768]{3,2,1,0:T(8,128)(2,1)S(1)}, u32[]{:S(2)}, u32[]{:S(2)}) collective-permute-start(bf16[1,4,104,768]{3,2,1,0:T(8,128)(2,1)S(1)} %get-tuple-element.134), channel_id=1, source_target_pairs={{0,24},{8,16},{16,8},{24,0},{1,25},{9,17},{17,9},{25,1},{2,26},{10... | collective-permute-start | bytes 1916936 | tf_op jit(solution)/shard_map/ppermute | solution.py:696
  361.3 7.8 %collective-permute-start.10 = (bf16[1,104,768]{2,1,0:T(8,128)(2,1)S(1)}, bf16[1,104,768]{2,1,0:T(8,128)(2,1)S(1)}, u32[]{:S(2)}, u32[]{:S(2)}) collective-permute-start(bf16[1,104,768]{2,1,0:T(8,128)(2,1)S(1)} %get-tuple-element.136), channel_id=1, source_target_pairs={{0,2},{1,3},{2,0},{3,1},{4,6},{5,7},{6,4},{7,5},{8,10},{9,11},{10,... | collective-permute-start | bytes 479240 | tf_op jit(solution)/shard_map/ppermute | solution.py:698
  363.1 14.8 %collective-permute-start.11 = (bf16[1,104,768]{2,1,0:T(8,128)(2,1)S(1)}, bf16[1,104,768]{2,1,0:T(8,128)(2,1)S(1)}, u32[]{:S(2)}, u32[]{:S(2)}) collective-permute-start(bf16[1,104,768]{2,1,0:T(8,128)(2,1)S(1)} %get-tuple-element.137), channel_id=1, source_target_pairs={{0,4},{1,5},{2,6},{3,7},{4,0},{5,1},{6,2},{7,3},{8,12},{9,13},{10,... | collective-permute-start | bytes 479240 | tf_op jit(solution)/shard_map/ppermute | solution.py:698
  365.5 12.4 %collective-permute-start.12 = (bf16[1,104,768]{2,1,0:T(8,128)(2,1)S(1)}, bf16[1,104,768]{2,1,0:T(8,128)(2,1)S(1)}, u32[]{:S(2)}, u32[]{:S(2)}) collective-permute-start(bf16[1,104,768]{2,1,0:T(8,128)(2,1)S(1)} %get-tuple-element.138), channel_id=1, source_target_pairs={{0,6},{1,7},{2,4},{3,5},{4,2},{5,3},{6,0},{7,1},{8,14},{9,15},{10,... | collective-permute-start | bytes 479240 | tf_op jit(solution)/shard_map/ppermute | solution.py:698
  378.0 8.9 %collective-permute-start.15 = (bf16[1,104,768]{2,1,0:T(8,128)(2,1)S(1)}, bf16[1,104,768]{2,1,0:T(8,128)(2,1)S(1)}, u32[]{:S(2)}, u32[]{:S(2)}) collective-permute-start(bf16[1,104,768]{2,1,0:T(8,128)(2,1)S(1)} %sum_pieces.5), channel_id=1, source_target_pairs={{0,6},{1,7},{2,4},{3,5},{4,2},{5,3},{6,0},{7,1},{8,14},{9,15},{10,... | collective-permute-start | bytes 479240 | tf_op jit(solution)/shard_map/ppermute | solution.py:700
  380.1 13.3 %collective-permute-start.14 = (bf16[1,104,768]{2,1,0:T(8,128)(2,1)S(1)}, bf16[1,104,768]{2,1,0:T(8,128)(2,1)S(1)}, u32[]{:S(2)}, u32[]{:S(2)}) collective-permute-start(bf16[1,104,768]{2,1,0:T(8,128)(2,1)S(1)} %sum_pieces.5), channel_id=1, source_target_pairs={{0,4},{1,5},{2,6},{3,7},{4,0},{5,1},{6,2},{7,3},{8,12},{9,13},{10,... | collective-permute-start | bytes 479240 | tf_op jit(solution)/shard_map/ppermute | solution.py:700
  383.9 9.5 %collective-permute-start.13 = (bf16[1,104,768]{2,1,0:T(8,128)(2,1)S(1)}, bf16[1,104,768]{2,1,0:T(8,128)(2,1)S(1)}, u32[]{:S(2)}, u32[]{:S(2)}) collective-permute-start(bf16[1,104,768]{2,1,0:T(8,128)(2,1)S(1)} %sum_pieces.5), channel_id=1, source_target_pairs={{0,2},{1,3},{2,0},{3,1},{4,6},{5,7},{6,4},{7,5},{8,10},{9,11},{10,... | collective-permute-start | bytes 479240 | tf_op jit(solution)/shard_map/ppermute | solution.py:700
  393.5 18.3 %collective-permute-start.18 = (bf16[1,4,104,768]{3,2,1,0:T(8,128)(2,1)S(1)}, bf16[1,4,104,768]{3,2,1,0:T(8,128)(2,1)S(1)}, u32[]{:S(2)}, u32[]{:S(2)}) collective-permute-start(bf16[1,4,104,768]{3,2,1,0:T(8,128)(2,1)S(1)} %maximum_bitcast_fusion), channel_id=1, source_target_pairs={{0,24},{8,16},{16,8},{24,0},{1,25},{9,17},{17,9},{25,1},{2,26},{10... | collective-permute-start | bytes 1916936 | tf_op jit(solution)/shard_map/ppermute | solution.py:701
  395.0 27.2 %collective-permute-start.17 = (bf16[1,4,104,768]{3,2,1,0:T(8,128)(2,1)S(1)}, bf16[1,4,104,768]{3,2,1,0:T(8,128)(2,1)S(1)}, u32[]{:S(2)}, u32[]{:S(2)}) collective-permute-start(bf16[1,4,104,768]{3,2,1,0:T(8,128)(2,1)S(1)} %maximum_bitcast_fusion), channel_id=1, source_target_pairs={{0,16},{8,24},{16,0},{24,8},{1,17},{9,25},{17,1},{25,9},{2,18},{10... | collective-permute-start | bytes 1916936 | tf_op jit(solution)/shard_map/ppermute | solution.py:701
  396.2 26.0 %collective-permute-start.16 = (bf16[1,4,104,768]{3,2,1,0:T(8,128)(2,1)S(1)}, bf16[1,4,104,768]{3,2,1,0:T(8,128)(2,1)S(1)}, u32[]{:S(2)}, u32[]{:S(2)}) collective-permute-start(bf16[1,4,104,768]{3,2,1,0:T(8,128)(2,1)S(1)} %maximum_bitcast_fusion), channel_id=1, source_target_pairs={{0,8},{8,0},{16,24},{24,16},{1,9},{9,1},{17,25},{25,17},{2,10},{10... | collective-permute-start | bytes 1916936 | tf_op jit(solution)/shard_map/ppermute | solution.py:701
  422.5 30.0 %collective-permute-start.19 = (bf16[4,4,104,768]{3,2,1,0:T(8,128)(2,1)S(1)}, bf16[4,4,104,768]{3,2,1,0:T(8,128)(2,1)}, u32[]{:S(2)}, u32[]{:S(2)}) collective-permute-start(bf16[4,4,104,768]{3,2,1,0:T(8,128)(2,1)S(1)} %pad_maximum_fusion.own_ref), channel_id=1, source_target_pairs={{0,1},{1,0},{2,3},{3,2},{4,5},{5,4},{6,7},{7,6},{8,9},{9,8},{10,11... | collective-permute-start | bytes 7667720 | tf_op jit(solution)/shard_map/ppermute | solution.py:702
  423.6 13.2 %collective-permute-start.5 = (bf16[256,768]{1,0:T(8,128)(2,1)}, bf16[256,768]{1,0:T(8,128)(2,1)}, u32[]{:S(2)}, u32[]{:S(2)}) collective-permute-start(bf16[256,768]{1,0:T(8,128)(2,1)} %get-tuple-element.157), channel_id=1, source_target_pairs={{0,24},{8,16},{16,8},{24,0},{1,25},{9,17},{17,9},{25,1},{2,26},{10... | collective-permute-start | bytes 1179656 | tf_op jit(solution)/shard_map/ppermute | solution.py:778
  425.0 19.7 %collective-permute-start.4 = (bf16[256,768]{1,0:T(8,128)(2,1)}, bf16[256,768]{1,0:T(8,128)(2,1)}, u32[]{:S(2)}, u32[]{:S(2)}) collective-permute-start(bf16[256,768]{1,0:T(8,128)(2,1)} %get-tuple-element.158), channel_id=1, source_target_pairs={{0,16},{8,24},{16,0},{24,8},{1,17},{9,25},{17,1},{25,9},{2,18},{10... | collective-permute-start | bytes 1179656 | tf_op jit(solution)/shard_map/ppermute | solution.py:778
  425.7 19.0 %collective-permute-start.3 = (bf16[256,768]{1,0:T(8,128)(2,1)S(1)}, bf16[256,768]{1,0:T(8,128)(2,1)}, u32[]{:S(2)}, u32[]{:S(2)}) collective-permute-start(bf16[256,768]{1,0:T(8,128)(2,1)S(1)} %get-tuple-element.156), channel_id=1, source_target_pairs={{0,8},{8,0},{16,24},{24,16},{1,9},{9,1},{17,25},{25,17},{2,10},{10... | collective-permute-start | bytes 1179656 | tf_op jit(solution)/shard_map/ppermute | solution.py:778
  (78 other events, 335.6 us)
Sparse Core Ops, SparseCore 0:
  222.9 42.1 reduce-scatter.4
  268.1 94.7 reduce-scatter.2

commit v2 on v1

--- a/solution.py
+++ b/solution.py
@@ -102,7 +102,7 @@
             jax.ShapeDtypeStruct((tok, width), bf16),
             jax.ShapeDtypeStruct((pairs, 16, tok), f32),
         ],
-        compiler_params=pltpu.CompilerParams(vmem_limit_bytes=48 * 2**20),
+        compiler_params=pltpu.CompilerParams(vmem_limit_bytes=60 * 2**20),
         cost_estimate=pl.CostEstimate(flops=4 * tok * (tok + remote) * width, bytes_accessed=2 * (tok * 4 + remote * 2) * width, transcendentals=tok * (tok + remote) * HEADS),
         name="attention_forward",
     )(flags, proj, proj, proj, kv_rem, kv_rem)
@@ -169,28 +169,28 @@
     dvr_ref[...] = dvra[...].astype(bf16)
 
 
-def attention_backward(flags, proj, kv_rem, mixed, d_mixed, lse, plen):
+def attention_backward(flags, proj, kv_rem, mixed, d_mixed, lse, plen, begin, count):
     tok, width = mixed.shape
     remote = kv_rem.shape[0]
     pairs = width // 128
-    own = pl.BlockSpec((tok, 128), lambda i: (0, i))
-    far = pl.BlockSpec((remote, 128), lambda i: (0, i))
+    own = lambda shift: pl.BlockSpec((tok, 128), lambda i: (0, shift + i))
+    far = lambda shift: pl.BlockSpec((remote, 128), lambda i: (0, shift + i))
     return pl.pallas_call(
         functools.partial(attention_backward_kernel, plen),
-        grid=(pairs,),
+        grid=(count,),
         in_specs=[
             pl.BlockSpec(memory_space=pltpu.SMEM),
-            own,
-            pl.BlockSpec((tok, 128), lambda i: (0, pairs + i)),
-            pl.BlockSpec((tok, 128), lambda i: (0, 2 * pairs + i)),
-            far,
-            pl.BlockSpec((remote, 128), lambda i: (0, pairs + i)),
-            own,
-            own,
-            pl.BlockSpec((1, 16, tok), lambda i: (i, 0, 0)),
+            own(begin),
+            own(pairs + begin),
+            own(2 * pairs + begin),
+            far(begin),
+            far(pairs + begin),
+            own(begin),
+            own(begin),
+            pl.BlockSpec((1, 16, tok), lambda i: (begin + i, 0, 0)),
         ],
-        out_specs=[own, own, own, far, far],
-        out_shape=[jax.ShapeDtypeStruct((tok, width), bf16)] * 3 + [jax.ShapeDtypeStruct((remote, width), bf16)] * 2,
+        out_specs=[own(0), own(0), own(0), far(0), far(0)],
+        out_shape=[jax.ShapeDtypeStruct((tok, count * 128), bf16)] * 3 + [jax.ShapeDtypeStruct((remote, count * 128), bf16)] * 2,
         scratch_shapes=[
             pltpu.VMEM((128, tok), bf16),
             pltpu.VMEM((128, remote), bf16),
@@ -199,8 +199,8 @@
             pltpu.VMEM((remote, 128), f32),
             pltpu.VMEM((remote, 128), f32),
         ],
-        compiler_params=pltpu.CompilerParams(vmem_limit_bytes=48 * 2**20),
-        cost_estimate=pl.CostEstimate(flops=10 * tok * (tok + remote) * width, bytes_accessed=2 * (tok * 8 + remote * 4) * width, transcendentals=tok * (tok + remote) * HEADS),
+        compiler_params=pltpu.CompilerParams(vmem_limit_bytes=60 * 2**20),
+        cost_estimate=pl.CostEstimate(flops=10 * tok * (tok + remote) * count * 128, bytes_accessed=2 * (tok * 8 + remote * 4) * count * 128, transcendentals=tok * (tok + remote) * 2 * count),
         name="attention_backward",
     )(flags, proj, proj, proj, kv_rem, kv_rem, mixed, d_mixed, lse)
 
@@ -266,7 +266,7 @@
         out_shape=[jax.ShapeDtypeStruct((n, tok), bf16) for n in counts]
         + [jax.ShapeDtypeStruct((tok, n), bf16) for n in counts]
         + [jax.ShapeDtypeStruct((FFN_EXPERTS, sum(counts) // FFN_EXPERTS, width + EXTRA), bf16)],
-        compiler_params=pltpu.CompilerParams(vmem_limit_bytes=48 * 2**20),
+        compiler_params=pltpu.CompilerParams(vmem_limit_bytes=60 * 2**20),
         cost_estimate=pl.CostEstimate(flops=2 * sum(counts) * tok * (width + EXTRA), bytes_accessed=4 * sum(counts) * width, transcendentals=0),
         name="route_plan",
     )(home, ids, grad, prev)
@@ -354,7 +354,7 @@
         ]
         + [jax.ShapeDtypeStruct((count, ff), bf16)] * 3,
         scratch_shapes=[pltpu.VMEM((count, width), f32), pltpu.VMEM((count, width), f32), pltpu.VMEM((count, EXTRA), f32)],
-        compiler_params=pltpu.CompilerParams(vmem_limit_bytes=48 * 2**20),
+        compiler_params=pltpu.CompilerParams(vmem_limit_bytes=60 * 2**20),
         cost_estimate=pl.CostEstimate(flops=12 * count * width * ff, bytes_accessed=6 * width * ff + 2 * count * (5 * width + 3 * ff), transcendentals=count * ff),
         name="expert_pass",
     )(home, rows, early, router_pad, w_gate, w_up, w_down)
@@ -389,7 +389,7 @@
         out_specs=[pl.BlockSpec((2, width, tile), lambda j: (0, 0, j)), pl.BlockSpec((tile, width), lambda j: (j, 0))],
         out_shape=[jax.ShapeDtypeStruct((2, width, ff), bf16), jax.ShapeDtypeStruct((ff, width), bf16)],
         scratch_shapes=[pltpu.VMEM((width, r.shape[0]), bf16) for r in rows],
-        compiler_params=pltpu.CompilerParams(vmem_limit_bytes=48 * 2**20),
+        compiler_params=pltpu.CompilerParams(vmem_limit_bytes=60 * 2**20),
         cost_estimate=pl.CostEstimate(flops=6 * total * width * ff, bytes_accessed=6 * width * ff + 2 * total * (2 * width + 3 * ff), transcendentals=0),
         name="weight_gradients",
     )(*rows, *douts, *inners, *dgates, *dups)
@@ -422,7 +422,7 @@
         out_specs=[ANYWHERE] * (2 + len(turned)),
         out_shape=[jax.ShapeDtypeStruct((tok, width), f32), jax.ShapeDtypeStruct((tok, width), bf16)]
         + [jax.ShapeDtypeStruct((t.shape[0], width), bf16) for t in turned],
-        compiler_params=pltpu.CompilerParams(vmem_limit_bytes=40 * 2**20),
+        compiler_params=pltpu.CompilerParams(vmem_limit_bytes=60 * 2**20),
         cost_estimate=pl.CostEstimate(flops=2 * tok * width * (width + rows), bytes_accessed=2 * width * (6 * tok + 2 * rows), transcendentals=0),
         name="after_attention",
     )(mixed, x, w_out, gain, *turned)
@@ -481,21 +481,40 @@
         for piece in split_low(terms.T, 2):
             part = dot_nn(piece, rows)
             sums = part if sums is None else sums + part
-    small_ref[...] = sums[0:SMALL, :]
+    sums = sums[0:SMALL, :]
+
+    @pl.when(pl.program_id(0) == 0)
+    def _():
+        small_ref[...] = sums
+
+    @pl.when(pl.program_id(0) > 0)
+    def _():
+        small_ref[...] += sums
 
 
 def local_part(hidden, low, grad, prev, ids, mix, gain, vec):
     tok, width = hidden.shape
+    block, tiles = row_tiles(tok)
     shapes = [(tok, width), (tok, width), (tok, EXTRA), (tok, EXTRA), (SMALL, width)]
     return pl.pallas_call(
         local_kernel,
-        in_specs=[ANYWHERE] * 8,
-        out_specs=[ANYWHERE] * 5,
+        grid=(tok // block,),
+        in_specs=[tiles(width), tiles(width), tiles(width), tiles(EXTRA), tiles(2), fixed(mix), fixed(gain), fixed(vec)],
+        out_specs=[tiles(width), tiles(width), tiles(EXTRA), tiles(EXTRA), pl.BlockSpec((SMALL, width), lambda i: (0, 0))],
         out_shape=[jax.ShapeDtypeStruct(s, f32) for s in shapes],
-        compiler_params=pltpu.CompilerParams(vmem_limit_bytes=48 * 2**20),
+        compiler_params=pltpu.CompilerParams(vmem_limit_bytes=60 * 2**20),
         cost_estimate=pl.CostEstimate(flops=14 * tok * width * EXTRA, bytes_accessed=16 * tok * width, transcendentals=tok * EXTRA),
         name="local_part",
     )(hidden, low, grad, prev, ids, mix, gain, vec)
+
+
+def row_tiles(tok):
+    block = 256 if tok % 256 == 0 else 128
+    return block, lambda columns: pl.BlockSpec((block, columns), lambda i: (i, 0))
+
+
+def fixed(value):
+    return pl.BlockSpec(value.shape, lambda i: (0,) * value.ndim)
 
 
 def combine_kernel(count, parts, *refs):
@@ -516,19 +535,29 @@
     dmixed_ref[...] = dot_nt(low, w_ref[...]).astype(bf16)
     gain = jnp.sum(d_normed * hidden * inverse, axis=0, keepdims=True)
     row = lax.broadcasted_iota(jnp.int32, (SMALL, 1), 0)
-    small_ref[...] = jnp.where(row == 0, gain, 0.0)
+    gain = jnp.where(row == 0, gain, 0.0)
+
+    @pl.when(pl.program_id(0) == 0)
+    def _():
+        small_ref[...] = gain
+
+    @pl.when(pl.program_id(0) > 0)
+    def _():
+        small_ref[...] += gain
 
 
 def combine(chosen, got, local, hidden, gain, grad, w_out):
     tok, width = hidden.shape
     rows = sum(c.shape[1] for c in chosen)
     arrays = [a for group in got for a in group]
+    block, tiles = row_tiles(tok)
     return pl.pallas_call(
         functools.partial(combine_kernel, len(chosen), len(got[0])),
-        in_specs=[ANYWHERE] * (len(chosen) + len(arrays) + 5),
-        out_specs=[ANYWHERE] * 4,
+        grid=(tok // block,),
+        in_specs=[tiles(c.shape[1]) for c in chosen] + [fixed(a) for a in arrays] + [tiles(width), tiles(width), fixed(gain), tiles(width), fixed(w_out)],
+        out_specs=[tiles(width)] * 3 + [pl.BlockSpec((SMALL, width), lambda i: (0, 0))],
         out_shape=[jax.ShapeDtypeStruct((tok, width), f32)] + [jax.ShapeDtypeStruct((tok, width), bf16)] * 2 + [jax.ShapeDtypeStruct((SMALL, width), f32)],
-        compiler_params=pltpu.CompilerParams(vmem_limit_bytes=48 * 2**20),
+        compiler_params=pltpu.CompilerParams(vmem_limit_bytes=60 * 2**20),
         cost_estimate=pl.CostEstimate(flops=2 * tok * width * (rows + width), bytes_accessed=2 * width * (9 * tok + 2 * rows), transcendentals=0),
         name="combine_gradients",
     )(*chosen, *arrays, local, hidden, gain, grad, w_out)
@@ -558,18 +587,27 @@
     d_logits = probs * (d_probs - jnp.sum(probs * d_probs, axis=1, keepdims=True))
     dlogits_ref[...] = d_logits
     high, rest = split_low(d_logits.T, 2)
-    sums = dot_nn(high, low_ref[...]) + dot_nn(rest, low_ref[...])
-    small_ref[...] = sums[0 : 2 * SMALL, :]
+    sums = (dot_nn(high, low_ref[...]) + dot_nn(rest, low_ref[...]))[0 : 2 * SMALL, :]
+
+    @pl.when(pl.program_id(0) == 0)
+    def _():
+        small_ref[...] = sums
+
+    @pl.when(pl.program_id(0) > 0)
+    def _():
+        small_ref[...] += sums
 
 
 def finish(chosen, got, groups, local, probs, d_probs, low):
     tok, width = local.shape
+    block, tiles = row_tiles(tok)
     return pl.pallas_call(
         functools.partial(finish_kernel, groups, len(got)),
-        in_specs=[ANYWHERE] * (len(chosen) + len(got) + 4),
-        out_specs=[ANYWHERE] * 3,
+        grid=(tok // block,),
+        in_specs=[tiles(c.shape[1]) for c in chosen] + [fixed(g) for g in got] + [tiles(width), tiles(EXTRA), tiles(EXTRA), tiles(width)],
+        out_specs=[tiles(width), tiles(EXTRA), pl.BlockSpec((2 * SMALL, width), lambda i: (0, 0))],
         out_shape=[jax.ShapeDtypeStruct((tok, width), bf16), jax.ShapeDtypeStruct((tok, EXTRA), f32), jax.ShapeDtypeStruct((2 * SMALL, width), f32)],
-        compiler_params=pltpu.CompilerParams(vmem_limit_bytes=48 * 2**20),
+        compiler_params=pltpu.CompilerParams(vmem_limit_bytes=60 * 2**20),
         cost_estimate=pl.CostEstimate(flops=2 * tok * 1152 * (width + EXTRA), bytes_accessed=16 * tok * width, transcendentals=0),
         name="finish_outputs",
     )(*chosen, *got, local, probs, d_probs, low)
@@ -579,57 +617,62 @@
     return [(i, i ^ mask) for i in range(size)]
 
 
-def pack_kernel(core_ref, mixed_ref, dlow_ref, act_ref, far_ref, dq_ref, dk_ref, dv_ref, dkf_ref, dvf_ref, local_ref, gain_ref, router_ref, mine_ref, theirs_ref, mixed_t, act_t, far_t):
-    core = core_ref[0]
-    width = mixed_ref.shape[1]
-    half, piece = width // 2, width // 8
-
-    @pl.when(pl.program_id(0) == 0)
-    def _():
-        mixed_t[...] = mixed_ref[...].T
-        act_t[...] = act_ref[...].T
-        far_t[...] = far_ref[...].T
-
+def store_halves(core, turned_terms, at, mine_ref, theirs_ref):
+    half = mine_ref.shape[0]
+    columns = turned_terms[0][1].shape[1]
     for out_ref, which in ((theirs_ref, 1 - core), (mine_ref, core)):
         rows = pl.ds(pl.multiple_of(which * half, half), half)
-        parts = [
-            dot_nn(mixed_t[rows, :], dlow_ref[...]),
-            dot_nn(act_t[rows, :], dq_ref[...]),
-            dot_nn(act_t[rows, :], dk_ref[...]) + dot_nn(far_t[rows, :], dkf_ref[...]),
-            dot_nn(act_t[rows, :], dv_ref[...]) + dot_nn(far_t[rows, :], dvf_ref[...]),
-        ]
-        for j, part in enumerate(parts):
-            for k in range(4):
-                out_ref[j, k, 0:piece, :] = part[k * piece : (k + 1) * piece].astype(bf16)
-                small = jnp.zeros((SMALL, part.shape[1]), f32)
-                if j == 0:
-                    small = (local_ref[...], gain_ref[...], router_ref[0:SMALL, :], router_ref[SMALL : 2 * SMALL, :])[k]
-                    small = jnp.where(which == 0, small, 0.0)
-                out_ref[j, k, piece : piece + SMALL, :] = small.astype(bf16)
-
-
-def pack(core, mixed, dlow, act, far, dq, dk, dv, dkf, dvf, local, gain, router):
-    tok, width = mixed.shape
-    remote = far.shape[0]
-    tile = 256
-    whole = lambda n: pl.BlockSpec((n, width), lambda i: (0, 0))
-    column = lambda n: pl.BlockSpec((n, tile), lambda i: (0, i))
-    out = pl.BlockSpec((4, 4, width // 8 + SMALL, tile), lambda i: (0, 0, 0, i))
-    return pl.pallas_call(
-        pack_kernel,
-        grid=(width // tile,),
-        in_specs=[
-            pl.BlockSpec(memory_space=pltpu.SMEM), whole(tok), column(tok), whole(tok), whole(remote),
-            column(tok), column(tok), column(tok), column(remote), column(remote),
-            column(SMALL), column(SMALL), column(2 * SMALL),
-        ],
-        out_specs=[out, out],
-        out_shape=[jax.ShapeDtypeStruct((4, 4, width // 8 + SMALL, width), bf16)] * 2,
-        scratch_shapes=[pltpu.VMEM((width, tok), bf16), pltpu.VMEM((width, tok), bf16), pltpu.VMEM((width, remote), bf16)],
-        compiler_params=pltpu.CompilerParams(vmem_limit_bytes=48 * 2**20),
-        cost_estimate=pl.CostEstimate(flops=2 * width * width * (4 * tok + 2 * remote), bytes_accessed=2 * width * (6 * tok + 3 * remote + 4 * width), transcendentals=0),
-        name="pack_gradients",
-    )(core, mixed, dlow, act, far, dq, dk, dv, dkf, dvf, local, gain, router)
+        total = None
+        for left, right in turned_terms:
+            part = dot_nn(left[rows, :], right[...])
+            total = part if total is None else total + part
+        out_ref[:, at : at + columns] = total.astype(bf16)
+
+
+def pack_first_kernel(core_ref, act_ref, far_ref, dq_ref, dk_ref, dv_ref, dkf_ref, dvf_ref, mixed_ref, dlow_ref, mine_ref, theirs_ref, act_t, far_t, mixed_t):
+    core = core_ref[0]
+    width, n = mixed_ref.shape[1], dq_ref.shape[1]
+    mixed_t[...] = mixed_ref[...].T
+    act_t[...] = act_ref[...].T
+    far_t[...] = far_ref[...].T
+    store_halves(core, [(mixed_t, dlow_ref)], 0, mine_ref, theirs_ref)
+    store_halves(core, [(act_t, dq_ref)], width, mine_ref, theirs_ref)
+    store_halves(core, [(act_t, dk_ref), (far_t, dkf_ref)], width + n, mine_ref, theirs_ref)
+    store_halves(core, [(act_t, dv_ref), (far_t, dvf_ref)], width + 2 * n, mine_ref, theirs_ref)
+
+
+def pack_second_kernel(core_ref, act_ref, far_ref, dq_ref, dk_ref, dv_ref, dkf_ref, dvf_ref, local_ref, gain_ref, router_ref, mine_ref, theirs_ref, act_t, far_t, small_t):
+    core = core_ref[0]
+    n = dq_ref.shape[1]
+    half = mine_ref.shape[0]
+    act_t[...] = act_ref[...].T
+    far_t[...] = far_ref[...].T
+    store_halves(core, [(act_t, dq_ref)], 0, mine_ref, theirs_ref)
+    store_halves(core, [(act_t, dk_ref), (far_t, dkf_ref)], n, mine_ref, theirs_ref)
+    store_halves(core, [(act_t, dv_ref), (far_t, dvf_ref)], 2 * n, mine_ref, theirs_ref)
+    rows = [router_ref[...], local_ref[...], gain_ref[...]]
+    rows.append(jnp.zeros((EXTRA - sum(r.shape[0] for r in rows), act_ref.shape[1]), f32))
+    small_t[...] = jnp.concatenate(rows, axis=0).T
+    for out_ref, which in ((theirs_ref, 1 - core), (mine_ref, core)):
+        out_ref[:, 3 * n : 3 * n + EXTRA] = small_t[pl.ds(pl.multiple_of(which * half, half), half), :].astype(bf16)
+
+
+def pack(core, act, far, grads, others, first):
+    tok, width = act.shape
+    n = grads[0].shape[1]
+    columns = (width if first else EXTRA) + 3 * n
+    arrays = [act, far, *grads, *others]
+    extra = pltpu.VMEM((width, tok), bf16) if first else pltpu.VMEM((width, EXTRA), f32)
+    return pl.pallas_call(
+        pack_first_kernel if first else pack_second_kernel,
+        in_specs=[SCALARS] + [ANYWHERE] * len(arrays),
+        out_specs=[ANYWHERE] * 2,
+        out_shape=[jax.ShapeDtypeStruct((width // 2, columns), bf16)] * 2,
+        scratch_shapes=[pltpu.VMEM((width, tok), bf16), pltpu.VMEM((width, far.shape[0]), bf16), extra],
+        compiler_params=pltpu.CompilerParams(vmem_limit_bytes=60 * 2**20),
+        cost_estimate=pl.CostEstimate(flops=2 * width * columns * tok, bytes_accessed=2 * width * (5 * tok + columns), transcendentals=0),
+        name="pack_first" if first else "pack_second",
+    )(core, *arrays)
 
 
 def sum_kernel(terms, index_ref, *refs):
@@ -644,69 +687,111 @@
 
 def sum_pieces(index, arrays):
     n, shape = arrays[0].shape[0], arrays[0].shape[1:]
-    zeros = (0,) * len(shape)
-    views = [pl.BlockSpec((1,) + shape, functools.partial(lambda k, i, s: (s[0] ^ k,) + zeros, k)) for k in range(n)]
+    views = [pl.BlockSpec((1,) + shape, functools.partial(lambda k, i, s: (s[0] ^ k if n > 1 else 0, 0, 0), k)) for k in range(n)]
     return pl.pallas_call(
         functools.partial(sum_kernel, len(arrays)),
         grid_spec=pltpu.PrefetchScalarGridSpec(
             num_scalar_prefetch=1,
             grid=(1,),
             in_specs=views * len(arrays),
-            out_specs=[pl.BlockSpec((1,) + shape, lambda i, s: (0,) + zeros)] * n,
+            out_specs=[pl.BlockSpec((1,) + shape, lambda i, s: (0, 0, 0))] * n,
         ),
         out_shape=[jax.ShapeDtypeStruct((1,) + shape, bf16)] * n,
-        compiler_params=pltpu.CompilerParams(vmem_limit_bytes=48 * 2**20),
+        compiler_params=pltpu.CompilerParams(vmem_limit_bytes=60 * 2**20),
         cost_estimate=pl.CostEstimate(flops=0, bytes_accessed=2 * n * math.prod(shape) * (len(arrays) + 1), transcendentals=0),
         name="sum_pieces",
     )(index, *[a for a in arrays for _ in range(n)])
 
 
-def unpack_kernel(index_ref, own_ref, other_ref, out_ref):
-    piece = out_ref.shape[0] // 8
-    for c in range(2):
-        mine = index_ref[0] == c
-        for k in range(4):
-            at = k ^ index_ref[2]
-            value = jnp.where(mine, own_ref[0, at, 0:piece, :].astype(f32), other_ref[0, at, 0:piece, :].astype(f32))
-            out_ref[(c * 4 + k) * piece : (c * 4 + k + 1) * piece, :] = value
-
-
-def unpack(index, own, other, first, count):
-    width = own.shape[3]
-    source = pl.BlockSpec((1,) + own.shape[1:], lambda j, s: ((j + first) ^ s[1], 0, 0, 0))
+def quarters(value):
+    return value.reshape(4, -1, value.shape[-1])
+
+
+def swap(pieces, along):
+    axis, size, unit = along
+    return [pieces[0]] + [lax.ppermute(pieces[k], axis, xor_pairs(size, unit * k)) for k in range(1, 4)]
+
+
+def spread(value, along):
+    return swap([value] * 4, along)
+
+
+def stack_kernel(*refs):
+    n = len(refs) - 1
+    size = refs[0].shape[0]
+    for k in range(n):
+        refs[n][k * size : (k + 1) * size] = refs[k][...]
+
+
+def stack_pieces(pieces):
+    shape = (len(pieces) * pieces[0].shape[0],) + pieces[0].shape[1:]
+    return pl.pallas_call(
+        stack_kernel,
+        in_specs=[ANYWHERE] * len(pieces),
+        out_specs=ANYWHERE,
+        out_shape=jax.ShapeDtypeStruct(shape, bf16),
+        compiler_params=pltpu.CompilerParams(vmem_limit_bytes=60 * 2**20),
+        cost_estimate=pl.CostEstimate(flops=0, bytes_accessed=4 * math.prod(shape), transcendentals=0),
+        name="stack_pieces",
+    )(*pieces)
+
+
+def unpack_kernel(index_ref, own1_ref, other1_ref, own2_ref, other2_ref, w_ref, out_ref, qkv_ref, small_ref):
+    width = out_ref.shape[1]
+    n = width // 2
+    piece = own1_ref.shape[2]
+    mine = pl.program_id(0) == index_ref[0]
+    lane = lax.broadcasted_iota(jnp.int32, (1, EXTRA), 1)
+    for k in range(4):
+        rows = slice(k * piece, (k + 1) * piece)
+        at_ctx, at_z = k ^ index_ref[1], k ^ index_ref[2]
+        first = jnp.where(mine, own1_ref[at_ctx, 0, :, :], other1_ref[at_ctx, 0, :, :]).astype(f32)
+        second = jnp.where(mine, own2_ref[0, at_z, :, :], other2_ref[0, at_z, :, :]).astype(f32)
+        out_ref[rows, :] = first[:, 0:width]
+        gain = None
+        for p in range(3):
+            for value, at in ((first[:, width + p * n : width + (p + 1) * n], 0), (second[:, p * n : (p + 1) * n], n)):
+                columns = slice(p * width + at, p * width + at + n)
+                qkv_ref[rows, columns] = value
+                part = value * w_ref[rows, columns].astype(f32)
+                gain = part if gain is None else gain + part
+        gain = jnp.sum(gain, axis=1, keepdims=True)
+        small_ref[rows, :] = second[:, 3 * n : 3 * n + EXTRA] + place(gain, lane, EXTRA - 1)
+
+
+def unpack(index, first, second, w_qkv):
+    width = w_qkv.shape[0]
+    piece = width // 32
+    block = 4 * piece
+    shape = lambda value: value.reshape(4, 4, piece, -1)
+    first, second = [shape(v) for v in first], [shape(v) for v in second]
+    c1, c2 = first[0].shape[3], second[0].shape[3]
+    row = lambda c, a, s: (c * 4 + a, 0)
+    source1 = pl.BlockSpec((4, 1, piece, c1), lambda c, a, s: (0, a ^ s[2], 0, 0))
+    source2 = pl.BlockSpec((1, 4, piece, c2), lambda c, a, s: (a ^ s[1], 0, 0, 0))
     return pl.pallas_call(
         unpack_kernel,
         grid_spec=pltpu.PrefetchScalarGridSpec(
             num_scalar_prefetch=1,
-            grid=(count,),
-            in_specs=[source, source],
-            out_specs=pl.BlockSpec((width, width), lambda j, s: (0, j)),
+            grid=(2, 4),
+            in_specs=[source1, source1, source2, source2, pl.BlockSpec((block, 3 * width), row)],
+            out_specs=[pl.BlockSpec((block, width), row), pl.BlockSpec((block, 3 * width), row), pl.BlockSpec((block, EXTRA), row)],
         ),
-        out_shape=jax.ShapeDtypeStruct((width, count * width), f32),
-        compiler_params=pltpu.CompilerParams(vmem_limit_bytes=32 * 2**20),
+        out_shape=[jax.ShapeDtypeStruct((width, width), f32), jax.ShapeDtypeStruct((width, 3 * width), f32), jax.ShapeDtypeStruct((width, EXTRA), f32)],
+        compiler_params=pltpu.CompilerParams(vmem_limit_bytes=60 * 2**20),
+        cost_estimate=pl.CostEstimate(flops=0, bytes_accessed=36 * width * width, transcendentals=0),
         name="unpack_sums",
-    )(index, own, other)
-
-
-def sum_everywhere(mine, theirs):
-    me_c, me_e = lax.axis_index("ctx"), lax.axis_index("exp")
-    place = lambda v: v.reshape(1)
-    got = lax.ppermute(theirs, "exp", xor_pairs(8, 1))
-    parts = sum_pieces(place(me_c), [mine, got])
-    parts = [parts[0]] + [lax.ppermute(parts[k], "ctx", xor_pairs(4, k)) for k in range(1, 4)]
-    parts = sum_pieces(place(me_e >> 1), [p[0] for p in parts])
-    parts = [parts[0]] + [lax.ppermute(parts[k], "exp", xor_pairs(8, 2 * k)) for k in range(1, 4)]
-    [piece] = sum_pieces(place(me_e * 0), parts)
-    column = jnp.concatenate([piece] + [lax.ppermute(piece, "exp", xor_pairs(8, 2 * k)) for k in range(1, 4)], axis=0)[None]
-    own = jnp.concatenate([column] + [lax.ppermute(column, "ctx", xor_pairs(4, k)) for k in range(1, 4)], axis=0)
-    other = lax.ppermute(own, "exp", xor_pairs(8, 1))
-    return own, other
+    )(index, *first, *second, w_qkv)
 
 P = jax.sharding.PartitionSpec
 
 
 def rms_inverse(tensor):
     return lax.rsqrt(jnp.mean(tensor * tensor, axis=-1, keepdims=True) + epsilon)
+
+
+def after(values, *others):
+    return lax.optimization_barrier((values, others))[0]
 
 
 def body(inputs, prev_logits, routes, attn_gain, w_qkv, w_out, moe_gain, router, const_gate, const_vec, w_gate, w_up, w_down, out_grad):
@@ -729,10 +814,10 @@
         return [value[r::split] if split > 1 else value for r in range(split)]
 
     x_low = inputs[0]
-    far_rows = jnp.concatenate([lax.ppermute(x_low[:plen], "ctx", xor_pairs(n_ctx, k)) for k in range(1, n_ctx)], axis=0)
+    x_prompt, upstream_low = lax.optimization_barrier((x_low[:plen], out_grad[0]))
+    far_rows = jnp.concatenate([lax.ppermute(x_prompt, "ctx", xor_pairs(n_ctx, k)) for k in range(1, n_ctx)], axis=0)
     flags = jnp.where((me_c ^ jnp.arange(1, n_ctx)) < me_c, 0.0, NEG).astype(f32)
 
-    upstream_low = out_grad[0]
     prev = jnp.pad(prev_logits[0], ((0, 0), (0, EXTRA - ALL_EXPERTS)))
     mix = jnp.concatenate([router, jnp.zeros((width, 4), bf16), const_gate[0], const_gate[1], jnp.zeros((width, EXTRA - 20), bf16)], axis=1)
     router_pad = jnp.pad(router, ((0, 0), (0, EXTRA - ALL_EXPERTS)))
@@ -743,17 +828,16 @@
     act_low = (tokens_in * inverse_attn * attn_gain).astype(bf16)
     projected = dot_nn(act_low, w_qkv).astype(bf16)
     early = deal(early_sent)
-    far_in = far_rows.astype(f32)
+    far_in = after(far_rows, projected).astype(f32)
     act_far = (far_in * rms_inverse(far_in) * attn_gain).astype(bf16)
     kv_far = dot_nn(act_far, w_qkv[:, width:]).astype(bf16)
 
     mixed_low, lse = attention_forward(flags, projected, kv_far, plen)
     mixed_low, early = lax.optimization_barrier((mixed_low, early))
     hidden, moe_low, sent = after_attention(mixed_low, x_low, w_out, moe_gain[None], turned)
+    local_out, d_normed_local, probs, d_probs, small_local = local_part(hidden, moe_low, upstream_low, prev, routes[0], mix, moe_gain[None], const_vec)
+    sent = [after(sent[0], local_out, d_normed_local), sent[1]]
     got = [deal(part.reshape(FFN_EXPERTS, -1, width)) for part in sent]
-
-    local_out, d_normed_local, probs, d_probs, small_local = local_part(hidden, moe_low, upstream_low, prev, routes[0], mix, moe_gain[None], const_vec)
-    got[0], local_out, d_normed_local = lax.optimization_barrier((got[0], local_out, d_normed_local))
 
     got = [part.reshape(-1, width) for part in got]
     passes = [expert_pass(group, home, r, early, router_pad, w_gate, w_up, w_down) for group, r in zip(groups, got)]
@@ -769,36 +853,86 @@
     sum_gate_up = lax.psum_scatter(gate_up_low, "ctx", scatter_dimension=1, tiled=True).astype(f32)
     sum_down = lax.psum_scatter(down_low, "ctx", scatter_dimension=0, tiled=True).astype(f32)
 
-    dq, dk, dv, dk_far, dv_far = attention_backward(flags, projected, kv_far, mixed_low, d_mixed, lse, plen)
-    dq, out_got = lax.optimization_barrier((dq, out_got))
-    mixed_out, d_logits, small_router = finish(chosen, out_got, groups, local_out, probs, d_probs, moe_low)
-
-    wq, wk, wv = (w_qkv[:, i * width : (i + 1) * width] for i in range(3))
-    d_act_far = (dot_nt(dk_far, wk) + dot_nt(dv_far, wv)).astype(bf16).reshape(n_ctx - 1, plen, width)
-    far_back = [lax.ppermute(d_act_far[k - 1], "ctx", xor_pairs(n_ctx, k)) for k in range(1, n_ctx)]
-    d_act = dot_nt(dq, wq) + dot_nt(dk, wk) + dot_nt(dv, wv)
+    pairs = width // 128
+    cut = pairs // 2
+
+    def attention(upstream, begin, count):
+        return attention_backward(flags, projected, kv_far, mixed_low, upstream, lse, plen, begin, count)
+
+    def weight_columns(part, group):
+        at = part * width + group * cut * 128
+        return w_qkv[:, at : at + grads_1[0].shape[1]]
+
+    def far_gradient(both):
+        total = sum(dot_nt(grads[p + 2], weight_columns(p, g)) for g, grads in enumerate(both) for p in (1, 2))
+        total = total.astype(bf16).reshape(n_ctx - 1, plen, width)
+        return total, [lax.ppermute(total[k - 1], "ctx", xor_pairs(n_ctx, k)) for k in range(1, n_ctx)]
+
+    def own_gradient(both):
+        return sum(dot_nt(grads[p], weight_columns(p, g)) for g, grads in enumerate(both) for p in range(3))
+
+    grads_1 = attention(d_mixed, 0, cut)
+    if n_ctx == 4 and n_exp == 8:
+        core, z = me_e & 1, me_e >> 1
+        at_core, at_ctx, at_z, at_none = (v.reshape(1) for v in (core, me_c, z, z * 0))
+        along_ctx, along_z = ("ctx", 4, 1), ("exp", 8, 2)
+        across = lambda value: lax.ppermute(value, "exp", xor_pairs(8, 1))
+        mine_1, theirs_1 = pack(at_core, act_low, act_far, grads_1, [mixed_low, d_attn_low], True)
+        got_1 = across(theirs_1)
+        grads_2 = attention(after(d_mixed, mine_1), cut, pairs - cut)
+        both = (grads_1, grads_2)
+        sums_1 = sum_pieces(at_z, [quarters(mine_1), quarters(after(got_1, grads_2[0]))])
+        parts_1 = swap(sums_1, along_z)
+        mixed_out, d_logits, small_router = finish(chosen, out_got, groups, after(local_out, sums_1[0]), probs, d_probs, moe_low)
+        mine_2, theirs_2 = pack(at_core, act_low, act_far, grads_2, [small_local, small_gain, small_router], False)
+        got_2 = across(theirs_2)
+        d_act_far, far_back = far_gradient(after(both, mine_2))
+        sums_2 = sum_pieces(at_ctx, [quarters(mine_2), quarters(after(got_2, d_act_far))])
+        parts_2 = swap(sums_2, along_ctx)
+        d_act = own_gradient(after(both, sums_2[0]))
+        sums_1 = sum_pieces(at_ctx, [quarters(p) for p in after(parts_1, d_act)])
+        parts_1 = swap(sums_1, along_ctx)
+        sums_2 = sum_pieces(at_z, [quarters(p) for p in after(parts_2, sums_1[0])])
+        parts_2 = swap(sums_2, along_z)
+        [piece_1] = sum_pieces(at_none, after(parts_1, sums_2[0]))
+        spread_1 = spread(piece_1, along_z)
+        [piece_2] = sum_pieces(at_none, after(parts_2, piece_1))
+        spread_2 = spread(piece_2, along_z)
+        column_1 = stack_pieces(after(spread_1, piece_2))
+        spread_1 = spread(column_1, along_ctx)
+        column_2 = stack_pieces(after(spread_2, column_1))
+        spread_2 = spread(column_2, along_ctx)
+        own_1 = stack_pieces(after(spread_1, column_2))
+        other_1 = across(own_1)
+        own_2 = stack_pieces(after(spread_2, own_1))
+        other_2 = across(own_2)
+    else:
+        grads_2 = attention(d_mixed, cut, pairs - cut)
+        both = (grads_1, grads_2)
+        mixed_out, d_logits, small_router = finish(chosen, out_got, groups, local_out, probs, d_probs, moe_low)
+        d_act_far, far_back = far_gradient(both)
+        d_act = own_gradient(both)
+
     d_act = jnp.concatenate([d_act[:plen] + sum(part.astype(f32) for part in far_back), d_act[plen:]], axis=0)
     scaled = d_act * attn_gain
     d_inputs = d_hidden + inverse_attn * scaled - tokens_in * inverse_attn**3 * jnp.mean(scaled * tokens_in, axis=-1, keepdims=True)
 
     if n_ctx == 4 and n_exp == 8:
-        core, z = me_e & 1, me_e >> 1
-        mine, theirs = pack(core.reshape(1), mixed_low, d_attn_low, act_low, act_far, dq, dk, dv, dk_far, dv_far, small_local, small_gain, small_router)
-        own, other = sum_everywhere(mine, theirs)
-        index = jnp.stack([core, me_c, z])
-        out_sum = unpack(index, own, other, 0, 1)
-        qkv_sum = unpack(index, own, other, 1, 3)
-        small = jnp.where(core == 0, own[:, :, -SMALL:], other[:, :, -SMALL:])
-        small = [lax.dynamic_slice(small, (me_c, k ^ z, 0, 0), (1, 1, SMALL, width)).reshape(SMALL, width).astype(f32) for k in range(4)]
+        weights = after(w_qkv, d_inputs, sum_gate_up, sum_down)
+        out_sum, qkv_sum, small = unpack(jnp.stack([core, me_c, z]), (own_1, other_1), (own_2, other_2), weights)
+        d_attn_gain = small[:, EXTRA - 1]
     else:
+        dq, dk, dv, dk_far, dv_far = (jnp.concatenate(pair, axis=1) for pair in zip(grads_1, grads_2))
         d_w_k = dot_tn(act_low, dk) + dot_tn(act_far, dk_far)
         d_w_v = dot_tn(act_low, dv) + dot_tn(act_far, dv_far)
-        parts = [dot_tn(mixed_low, d_attn_low), dot_tn(act_low, dq), d_w_k, d_w_v, small_local, small_gain, small_router]
+        parts = [dot_tn(mixed_low, d_attn_low), dot_tn(act_low, dq), d_w_k, d_w_v, small_router, small_local, small_gain]
         out_sum, q_sum, k_sum, v_sum, *small = [p.astype(f32) for p in lax.psum([p.astype(bf16) for p in parts], ("ctx", "exp"))]
         qkv_sum = jnp.concatenate([q_sum, k_sum, v_sum], axis=1)
-        small = small[:2] + [small[2][:SMALL], small[2][SMALL:]]
-    d_attn_gain = jnp.sum(qkv_sum * w_qkv.astype(f32), axis=1) / attn_gain
-    d_const_gate = jnp.stack([small[0][0:2].T, small[0][2:4].T])
+        small = jnp.concatenate(small, axis=0).T
+        d_attn_gain = jnp.sum(qkv_sum * w_qkv.astype(f32), axis=1)
+    d_attn_gain = d_attn_gain / attn_gain
+    at = 2 * SMALL
+    d_const_gate = jnp.stack([small[:, at : at + 2], small[:, at + 2 : at + 4]])
     return (
         mixed_out[None],
         d_inputs[None],
@@ -806,10 +940,10 @@
         d_attn_gain,
         qkv_sum,
         out_sum,
-        small[1][0],
-        jnp.concatenate([small[2], small[3][: ALL_EXPERTS - SMALL]], axis=0).T,
+        small[:, at + SMALL],
+        small[:, :ALL_EXPERTS],
         d_const_gate,
-        small[0][4:6],
+        small[:, at + 4 : at + 6].T,
         sum_gate_up[0][None],
         sum_gate_up[1][None],
         sum_down[None],

time: 484 us -> 448 us (0.926)
  waiting for transfers between devices: 129 us -> 64.4 us
  Pallas kernels: 170 us -> 215 us
  blocking collectives: 25.7 us -> 0 us
  local copies, waits for them, and re-layouts: 55.9 us -> 31.3 us
  starting transfers between devices: 49.9 us -> 71.2 us
  matrix products: 13.6 us -> 28.1 us
    ppermute x20 -> x34, waiting for transfers between devices: 120 us -> 52.5 us  [the longest x24 44.5 us: swap(): lax.ppermute(pieces[k], axis, xor_pairs(size, unit * k))]
    unnamed x172 -> x74, local copies, waits for them, and re-layouts: 45.7 us -> 13.4 us
    all_to_all x1 -> x0, blocking collectives: 25.7 us -> none  [deal(): return lax.all_to_all(value, 'exp', 0, 0, tiled=True)]
    pallas_call x3 -> x8, Pallas kernels: 26.4 us -> 47.2 us  [the longest x2 16.3 us: pack(): pl.pallas_call(pack_first_kernel if first else pack_second_kernel, in_spe...]
    ppermute x20 -> x34, starting transfers between devices: 24.8 us -> 40.4 us  [the longest x24 32.9 us: swap(): lax.ppermute(pieces[k], axis, xor_pairs(size, unit * k))]
    dot_general x5 -> x10, matrix products: 7.27 us -> 20.3 us  [dot_nt(): lax.dot_general(a, b, (((1,), (1,)), ((), ())), preferred_element_type=f32)]
    pallas_call x3 -> x6, Pallas kernels: 3.31 us -> 13.1 us  [sum_pieces(): pl.pallas_call(functools.partial(sum_kernel, len(arrays)), grid_spec=pltp...]
    all_to_all x2 -> x3, starting transfers between devices: 11.4 us -> 16.9 us  [deal(): return lax.all_to_all(value, 'exp', 0, 0, tiled=True)]
  transfers between devices with their start and end apart: 27 -> 42, of which waited for: 17 -> 12; matrix products, arithmetic and copies ran while one was open for 9% -> 13% of each run, Pallas kernels for 34% -> 43%
where the time goes in v2:
time: 448 us; the launch traced here: 442 us
  Pallas kernels  215 us (48%)
  starting transfers between devices  71.2 us (16%)
  waiting for transfers between devices  64.4 us (14%)
  local copies, waits for them, and re-layouts  31.3 us (7%)
  matrix products  28.1 us (6%)
  other arithmetic  17.5 us (4%)
  between operations  15 us (3%)
    ppermute x24, waiting for transfers between devices, swap(): lax.ppermute(pieces[k], axis, xor_pairs(size, unit * k))  44.5 us
    pallas_call x2, Pallas kernels, attention_backward(): pl.pallas_call(functools.partial(attention_backward_kernel, plen), grid=(...  41 us
    pallas_call x2, Pallas kernels, expert_pass(): pl.pallas_call(functools.partial(expert_kernel, group), grid=(ff // tile,...  37.8 us
    ppermute x24, starting transfers between devices, swap(): lax.ppermute(pieces[k], axis, xor_pairs(size, unit * k))  32.9 us
    pallas_call x1, Pallas kernels, attention_forward(): pl.pallas_call(functools.partial(attention_forward_kernel, plen), grid=(p...  24 us
    dot_general x10, matrix products, dot_nt(): lax.dot_general(a, b, (((1,), (1,)), ((), ())), preferred_element_type=f32)  20.3 us
    pallas_call x1, Pallas kernels, weight_gradients(): pl.pallas_call(functools.partial(weight_kernel, count), grid=(ff // tile,...  17.9 us
    all_to_all x3, starting transfers between devices, deal(): return lax.all_to_all(value, 'exp', 0, 0, tiled=True)  16.9 us
  transfers between devices with their start and end apart: 42, of which 12 were waited for; matrix products, arithmetic and copies ran while one was open for 13% of the time, Pallas kernels for 43%

profile of v2, /device:TPU:0, one launch (start us, length us, event | category | flops | bytes accessed | tf_op | source)
XLA Modules:
  0.0 442.5 jit_solution(10093416667020766664)
XLA Ops:
  12.3 6.3 %route_plan.1 = (bf16[640,768]{1,0:T(8,128)(2,1)}, bf16[512,768]{1,0:T(8,128)(2,1)}, bf16[768,640]{1,0:T(8,128)(2,1)}, bf16[768,512]{1,0:T(8,128)(2,1)}, bf16[8,144,896]{2,1,0:T(8,128)(2,1)}) custom-call(s32[1]{0:T(128)} %bitcast.home_ref, s32[2,768]{1,0:T(2,128)} %copy.51.ids_ref, bf16[768,768]{1,0:T(8,128)(2,1)} %bitcast.89, f32[768,128]{1,0:T(8,128)} %pad.8.prev_ref), custom_call_target="tpu_custom_call" | custom-call | flops 1585446912 | bytes 3538944 | tf_op jit(solution)/shard_map/route_plan/pallas_call | solution.py:262
  18.6 6.7 %all-to-all-start = ((bf16[8,144,896]{2,1,0:T(8,128)(2,1)}), bf16[8,144,896]{2,1,0:T(8,128)(2,1)}, u32[]{:S(2)}, u32[]{:S(2)}) async-start(bf16[8,144,896]{2,1,0:T(8,128)(2,1)} %get-tuple-element.146), calls=%async_computation | async-start | bytes 4128768 | tf_op jit(solution)/shard_map/all_to_all | solution.py:810
  34.4 4.3 convolution_convert_fusion.q_ref.k_ref.v_ref
  38.7 7.8 %collective-permute-done.1 = bf16[256,768]{1,0:T(8,128)(2,1)} collective-permute-done((bf16[256,768]{1,0:T(8,128)(2,1)}, bf16[256,768]{1,0:T(8,128)(2,1)}, u32[]{:S(2)}, u32[]{:S(2)}) %collective-permute-start.1) | collective-permute-done | bytes 393248 | tf_op jit(solution)/shard_map/ppermute | solution.py:818
  49.7 3.4 convolution_convert_fusion.1.kr_ref.vr_ref
  53.1 24.0 %attention_forward.1 = (bf16[768,768]{1,0:T(8,128)(2,1)}, f32[6,16,768]{2,1,0:T(8,128)}) custom-call(f32[3]{0:T(128)} %compare_select_fusion.flags_ref, bf16[768,2304]{1,0:T(8,128)(2,1)} %convolution_convert_fusion.q_ref.k_ref.v_ref, bf16[768,2304]{1,0:T(8,128)(2,1)} %convolution_convert_fusion.q_ref.k_ref.v_ref, ...), custom_call_target="tpu_custom_call" | custom-call | flops 3623878656 | bytes 7077888 | tf_op jit(solution)/shard_map/attention_forward/pallas_call | solution.py:86
  77.1 6.9 %after_attention.1 = (f32[768,768]{1,0:T(8,128)}, bf16[768,768]{1,0:T(8,128)(2,1)}, bf16[640,768]{1,0:T(8,128)(2,1)}, bf16[512,768]{1,0:T(8,128)(2,1)}) custom-call(bf16[768,768]{1,0:T(8,128)(2,1)} %get-tuple-element.147.mixed_ref.o_ref, bf16[768,768]{1,0:T(8,128)(2,1)} %bitcast.74, bf16[768,768]{1,0:T(8,128)(2,1)} %refs_8_.1, ...), custom_call_target="tpu_custom_call" | custom-call | flops 2264924160 | bytes 10616832 | tf_op jit(solution)/shard_map/after_attention/pallas_call | solution.py:419
  84.0 5.1 %all-to-all-start.3 = ((bf16[8,64,768]{2,1,0:T(8,128)(2,1)}), bf16[8,64,768]{2,1,0:T(8,128)(2,1)}, u32[]{:S(2)}, u32[]{:S(2)}) async-start(bf16[8,64,768]{2,1,0:T(8,128)(2,1)} %bitcast.107), calls=%async_computation.3 | async-start | bytes 1572864 | tf_op jit(solution)/shard_map/all_to_all | solution.py:810
  95.9 14.3 %local_part.1 = (f32[768,768]{1,0:T(8,128)}, f32[768,768]{1,0:T(8,128)}, f32[768,128]{1,0:T(8,128)}, f32[768,128]{1,0:T(8,128)}, f32[8,768]{1,0:T(8,128)}) custom-call(f32[768,768]{1,0:T(8,128)} %get-tuple-element.151.hidden_ref.refs_5_, bf16[768,768]{1,0:T(8,128)(2,1)} %get-tuple-element.152.low_ref.refs_6_, bf16[768,768]{1,0:T(8,128)(2,1)} %bitcast.90, ...), custom_call_target="tpu_custom_call" | custom-call | flops 1056964608 | bytes 9437184 | tf_op jit(solution)/shard_map/local_part/pallas_call | solution.py:499
  110.2 5.1 %all-to-all-start.1 = ((bf16[8,80,768]{2,1,0:T(8,128)(2,1)}), bf16[8,80,768]{2,1,0:T(8,128)(2,1)}, u32[]{:S(2)}, u32[]{:S(2)}) async-start(bf16[8,80,768]{2,1,0:T(8,128)(2,1)} %bitcast.102), calls=%async_computation.1 | async-start | bytes 1966080 | tf_op jit(solution)/shard_map/all_to_all | solution.py:810
  116.9 17.4 %expert_pass.3 = (bf16[512,896]{1,0:T(8,128)(2,1)}, bf16[512,768]{1,0:T(8,128)(2,1)}, bf16[512,768]{1,0:T(8,128)(2,1)}, bf16[512,2048]{1,0:T(8,128)(2,1)}, bf16[...) custom-call(s32[1]{0:T(128)} %bitcast.home_ref, bf16[512,768]{1,0:T(8,128)(2,1)} %bitcast.13.rows_ref.refs_1_, ...), custom_call_target="tpu_custom_call" | custom-call | flops 9663676416 | bytes 19660800 | tf_op jit(solution)/shard_map/expert_pass/pallas_call | solution.py:337
  134.3 6.3 %all-to-all-done.1 = bf16[8,80,768]{2,1,0:T(8,128)(2,1)} async-done(((bf16[8,80,768]{2,1,0:T(8,128)(2,1)}), bf16[8,80,768]{2,1,0:T(8,128)(2,1)}, u32[]{:S(2)}, u32[]{:S(2)}) %all-to-all-start.1) | async-done | bytes 983072 | tf_op jit(solution)/shard_map/all_to_all | solution.py:810
  140.6 4.7 %all-to-all-start.4 = ((bf16[8,64,768]{2,1,0:T(8,128)(2,1)}), bf16[8,64,768]{2,1,0:T(8,128)(2,1)}, u32[]{:S(2)}, u32[]{:S(2)}) async-start(bf16[8,64,768]{2,1,0:T(8,128)(2,1)} %bitcast.108), calls=%async_computation.4 | async-start | bytes 1572864 | tf_op jit(solution)/shard_map/all_to_all | solution.py:813
  145.3 20.5 %expert_pass.2 = (bf16[640,896]{1,0:T(8,128)(2,1)}, bf16[640,768]{1,0:T(8,128)(2,1)}, bf16[640,768]{1,0:T(8,128)(2,1)}, bf16[640,2048]{1,0:T(8,128)(2,1)}, bf16[...) custom-call(s32[1]{0:T(128)} %bitcast.home_ref, bf16[640,768]{1,0:T(8,128)(2,1)} %bitcast.10.rows_ref.refs_0_, ...), custom_call_target="tpu_custom_call" | custom-call | flops 12079595520 | bytes 22216704 | tf_op jit(solution)/shard_map/expert_pass/pallas_call | solution.py:337
  166.2 4.6 %all-to-all-start.2 = ((bf16[8,80,768]{2,1,0:T(8,128)(2,1)}), bf16[8,80,768]{2,1,0:T(8,128)(2,1)}, u32[]{:S(2)}, u32[]{:S(2)}) async-start(bf16[8,80,768]{2,1,0:T(8,128)(2,1)} %bitcast.103), calls=%async_computation.2 | async-start | bytes 1966080 | tf_op jit(solution)/shard_map/all_to_all | solution.py:813
  173.9 17.9 %weight_gradients.1 = (bf16[2,768,2048]{2,1,0:T(8,128)(2,1)}, bf16[2048,768]{1,0:T(8,128)(2,1)}) custom-call(bf16[640,768]{1,0:T(8,128)(2,1)} %bitcast.10.rows_ref.refs_0_, bf16[512,768]{1,0:T(8,128)(2,1)} %bitcast.13.rows_ref.refs_1_, bf16[640,768]{1,0:T(8,128)(2,1)} %get-tuple-element.160.refs_2_, bf16[512,768]{1,0:T(8,128)(2,1)} %get-tuple-element.161.refs_3_, ...), custom_call_target="tpu_custom_call" | custom-call | flops 10871635968 | bytes 27131904 | tf_op jit(solution)/shard_map/weight_gradients/pallas_call | solution.py:385
  191.7 4.4 all-to-all-done.2
  196.9 4.6 %all-to-all-start.5 = ((bf16[8,144,896]{2,1,0:T(8,128)(2,1)}), bf16[8,144,896]{2,1,0:T(8,128)(2,1)}, u32[]{:S(2)}, u32[]{:S(2)}) async-start(bf16[8,144,896]{2,1,0:T(8,128)(2,1)} %pad_maximum_fusion), calls=%async_computation.5 | async-start | bytes 4128768 | tf_op jit(solution)/shard_map/all_to_all | solution.py:813
  201.5 9.4 %combine_gradients.1 = (f32[768,768]{1,0:T(8,128)}, bf16[768,768]{1,0:T(8,128)(2,1)}, bf16[768,768]{1,0:T(8,128)(2,1)}, f32[8,768]{1,0:T(8,128)}) custom-call(bf16[768,640]{1,0:T(8,128)(2,1)} %get-tuple-element.141.refs_0_, bf16[768,512]{1,0:T(8,128)(2,1)} %get-tuple-element.142.refs_1_, bf16[640,768]{1,0:T(8,128)(2,1)} %bitcast.19.refs_2_, ...), custom_call_target="tpu_custom_call" | custom-call | flops 2264924160 | bytes 14155776 | tf_op jit(solution)/shard_map/combine_gradients/pallas_call | solution.py:554
  210.8 20.4 %attention_backward.2 = (bf16[768,384]{1,0:T(8,128)(2,1)}, bf16[768,384]{1,0:T(8,128)(2,1)}, bf16[768,384]{1,0:T(8,128)(2,1)}, bf16[768,384]{1,0:T(8,128)(2,1)}, bf16[768,384]{1,0:T(8,128)(2,1)}) custom-call(f32[3]{0:T(128)} %compare_select_fusion.flags_ref, bf16[768,2304]{1,0:T(8,128)(2,1)} %convolution_convert_fusion.q_ref.k_ref.v_ref, ...), custom_call_target="tpu_custom_call" | custom-call | flops 4529848320 | bytes 7077888 | tf_op jit(solution)/shard_map/attention_backward/pallas_call | solution.py:178
  231.3 8.9 %pack_first.1 = (bf16[384,1920]{1,0:T(8,128)(2,1)}, bf16[384,1920]{1,0:T(8,128)(2,1)}) custom-call(s32[1]{0:T(128)} %bitcast.18.core_ref, bf16[768,768]{1,0:T(8,128)(2,1)} %copy-done.8, bf16[768,768]{1,0:T(8,128)(2,1)} %copy-done.9, bf16[768,384]{1,0:T(8,128)(2,1)} %get-tuple-element.204.dq_ref, bf16[768,384]{1,0:T(8,128)(2,1)} %get-tuple-element.205.dk_ref, ...), custom_call_target="tpu_custom_call" | custom-call | flops 2264924160 | bytes 8847360 | tf_op jit(solution)/shard_map/pack_first/pallas_call | solution.py:666
  240.6 20.6 %attention_backward.3 = (bf16[768,384]{1,0:T(8,128)(2,1)}, bf16[768,384]{1,0:T(8,128)(2,1)}, bf16[768,384]{1,0:T(8,128)(2,1)}, bf16[768,384]{1,0:T(8,128)(2,1)}, bf16[768,384]{1,0:T(8,128)(2,1)}) custom-call(f32[3]{0:T(128)} %compare_select_fusion.flags_ref, bf16[768,2304]{1,0:T(8,128)(2,1)} %convolution_convert_fusion.q_ref.k_ref.v_ref, ...), custom_call_target="tpu_custom_call" | custom-call | flops 4529848320 | bytes 7077888 | tf_op jit(solution)/shard_map/attention_backward/pallas_call | solution.py:178
  264.2 8.5 %finish_outputs.1 = (bf16[768,768]{1,0:T(8,128)(2,1)}, f32[768,128]{1,0:T(8,128)}, f32[16,768]{1,0:T(8,128)}) custom-call(bf16[768,640]{1,0:T(8,128)(2,1)} %get-tuple-element.141.refs_0_, bf16[768,512]{1,0:T(8,128)(2,1)} %get-tuple-element.142.refs_1_, bf16[8,144,896]{2,1,0:T(8,128)(2,1)} %all-to-all-done.5.refs_2_, f32[768,768]{1,0:T(8,128)} %get-tuple-element.189.refs_3_, ...), custom_call_target="tpu_custom_call" | custom-call | flops 1585446912 | bytes 9437184 | tf_op jit(solution)/shard_map/finish_outputs/pallas_call | solution.py:604
  272.6 7.4 %pack_second.1 = (bf16[384,1280]{1,0:T(8,128)(2,1)}, bf16[384,1280]{1,0:T(8,128)(2,1)}) custom-call(s32[1]{0:T(128)} %bitcast.18.core_ref, bf16[768,768]{1,0:T(8,128)(2,1)} %copy-done.8, bf16[768,768]{1,0:T(8,128)(2,1)} %copy-done.9, bf16[768,384]{1,0:T(8,128)(2,1)} %get-tuple-element.207.dq_ref, bf16[768,384]{1,0:T(8,128)(2,1)} %get-tuple-element.208.dk_ref, ...), custom_call_target="tpu_custom_call" | custom-call | flops 1509949440 | bytes 7864320 | tf_op jit(solution)/shard_map/pack_second/pallas_call | solution.py:666
  302.7 7.6 %collective-permute-done.9 = bf16[1,96,1920]{2,1,0:T(8,128)(2,1)} collective-permute-done((bf16[1,96,1920]{2,1,0:T(8,128)(2,1)}, bf16[1,96,1920]{2,1,0:T(8,128)(2,1)}, u32[]{:S(2)}, u32[]{:S(2)}) %collective-permute-start.9) | collective-permute-done | bytes 368672 | tf_op jit(solution)/shard_map/ppermute | solution.py:712
  316.0 5.1 %collective-permute-done.16 = bf16[1,96,1280]{2,1,0:T(8,128)(2,1)} collective-permute-done((bf16[1,96,1280]{2,1,0:T(8,128)(2,1)}, bf16[1,96,1280]{2,1,0:T(8,128)(2,1)}, u32[]{:S(2)}, u32[]{:S(2)}) %collective-permute-start.16) | collective-permute-done | bytes 245792 | tf_op jit(solution)/shard_map/ppermute | solution.py:712
  339.7 5.7 %collective-permute-done.21.refs_2_ = bf16[1,24,1280]{2,1,0:T(8,128)(2,1)} collective-permute-done((bf16[1,24,1280]{2,1,0:T(8,128)(2,1)}, bf16[1,24,1280]{2,1,0:T(8,128)(2,1)}, u32[]{:S(2)}, u32[]{:S(2)}) %collective-permute-start.21) | collective-permute-done | bytes 61472 | tf_op jit(solution)/shard_map/ppermute | solution.py:712
  351.4 4.1 add_convert_fusion
  367.5 16.5 %collective-permute-done.24.refs_2_ = bf16[4,24,1920]{2,1,0:T(8,128)(2,1)S(1)} collective-permute-done((bf16[4,24,1920]{2,1,0:T(8,128)(2,1)S(1)}, bf16[4,24,1920]{2,1,0:T(8,128)(2,1)S(1)}, u32[]{:S(2)}, u32[]{:S(2)}) %collective-permute-start.24) | collective-permute-done | bytes 368672 | tf_op jit(solution)/shard_map/ppermute | solution.py:712
  395.9 3.8 collective-permute-done.30.refs_1_
  399.7 5.7 %collective-permute-done.31.refs_2_ = bf16[4,24,1280]{2,1,0:T(8,128)(2,1)S(1)} collective-permute-done((bf16[4,24,1280]{2,1,0:T(8,128)(2,1)}, bf16[4,24,1280]{2,1,0:T(8,128)(2,1)S(1)}, u32[]{:S(2)}, u32[]{:S(2)}) %collective-permute-start.31) | collective-permute-done | bytes 245792 | tf_op jit(solution)/shard_map/ppermute | solution.py:712
  414.5 11.4 %unpack_sums.1 = (f32[768,768]{1,0:T(8,128)}, f32[768,2304]{1,0:T(8,128)}, f32[768,128]{1,0:T(8,128)}) custom-call(s32[3]{0:T(128)} %pad_add_fusion.index_ref, bf16[4,4,24,1920]{3,2,1,0:T(8,128)(2,1)} %bitcast.80, bf16[4,4,24,1920]{3,2,1,0:T(8,128)(2,1)} %bitcast.38.other1_ref, bf16[4,4,24,1280]{3,2,1,0:T(8,128)(2,1)} %bitcast.92, ...), custom_call_target="tpu_custom_call" | custom-call | bytes 21233664 | tf_op jit(solution)/shard_map/unpack_sums/pallas_call | solution.py:772
  (198 shorter events, 128.4 us)
Async XLA Ops:
  18.6 58.5 %all-to-all-start = ((bf16[8,144,896]{2,1,0:T(8,128)(2,1)}), bf16[8,144,896]{2,1,0:T(8,128)(2,1)}, u32[]{:S(2)}, u32[]{:S(2)}) async-start(bf16[8,144,896]{2,1,0:T(8,128)(2,1)} %get-tuple-element.146), calls=%async_computation | async-start | bytes 4128768 | tf_op jit(solution)/shard_map/all_to_all | solution.py:810
  25.4 13.4 %collective-permute-start.2 = (bf16[256,768]{1,0:T(8,128)(2,1)}, bf16[256,768]{1,0:T(8,128)(2,1)}, u32[]{:S(2)}, u32[]{:S(2)}) collective-permute-start(bf16[256,768]{1,0:T(8,128)(2,1)} %slice_bitcast_fusion.4), channel_id=1, source_target_pairs={{0,24},{8,16},{16,8},{24,0},{1,25},{9,17},{17,9},{25,1},{2,26},{10... | collective-permute-start | bytes 1179656 | tf_op jit(solution)/shard_map/ppermute | solution.py:818
  27.9 18.7 %collective-permute-start.1 = (bf16[256,768]{1,0:T(8,128)(2,1)}, bf16[256,768]{1,0:T(8,128)(2,1)}, u32[]{:S(2)}, u32[]{:S(2)}) collective-permute-start(bf16[256,768]{1,0:T(8,128)(2,1)} %slice_bitcast_fusion.4), channel_id=1, source_target_pairs={{0,16},{8,24},{16,0},{24,8},{1,17},{9,25},{17,1},{25,9},{2,18},{10... | collective-permute-start | bytes 1179656 | tf_op jit(solution)/shard_map/ppermute | solution.py:818
  28.4 18.3 %collective-permute-start = (bf16[256,768]{1,0:T(8,128)(2,1)}, bf16[256,768]{1,0:T(8,128)(2,1)}, u32[]{:S(2)}, u32[]{:S(2)}) collective-permute-start(bf16[256,768]{1,0:T(8,128)(2,1)} %slice_bitcast_fusion.4), channel_id=1, source_target_pairs={{0,8},{8,0},{16,24},{24,16},{1,9},{9,1},{17,25},{25,17},{2,10},{10... | collective-permute-start | bytes 1179656 | tf_op jit(solution)/shard_map/ppermute | solution.py:818
  84.0 26.2 %all-to-all-start.3 = ((bf16[8,64,768]{2,1,0:T(8,128)(2,1)}), bf16[8,64,768]{2,1,0:T(8,128)(2,1)}, u32[]{:S(2)}, u32[]{:S(2)}) async-start(bf16[8,64,768]{2,1,0:T(8,128)(2,1)} %bitcast.107), calls=%async_computation.3 | async-start | bytes 1572864 | tf_op jit(solution)/shard_map/all_to_all | solution.py:810
  110.2 30.4 %all-to-all-start.1 = ((bf16[8,80,768]{2,1,0:T(8,128)(2,1)}), bf16[8,80,768]{2,1,0:T(8,128)(2,1)}, u32[]{:S(2)}, u32[]{:S(2)}) async-start(bf16[8,80,768]{2,1,0:T(8,128)(2,1)} %bitcast.102), calls=%async_computation.1 | async-start | bytes 1966080 | tf_op jit(solution)/shard_map/all_to_all | solution.py:810
  140.6 25.7 %all-to-all-start.4 = ((bf16[8,64,768]{2,1,0:T(8,128)(2,1)}), bf16[8,64,768]{2,1,0:T(8,128)(2,1)}, u32[]{:S(2)}, u32[]{:S(2)}) async-start(bf16[8,64,768]{2,1,0:T(8,128)(2,1)} %bitcast.108), calls=%async_computation.4 | async-start | bytes 1572864 | tf_op jit(solution)/shard_map/all_to_all | solution.py:813
  166.2 29.9 %all-to-all-start.2 = ((bf16[8,80,768]{2,1,0:T(8,128)(2,1)}), bf16[8,80,768]{2,1,0:T(8,128)(2,1)}, u32[]{:S(2)}, u32[]{:S(2)}) async-start(bf16[8,80,768]{2,1,0:T(8,128)(2,1)} %bitcast.103), calls=%async_computation.2 | async-start | bytes 1966080 | tf_op jit(solution)/shard_map/all_to_all | solution.py:813
  170.8 241.3 %reduce-scatter.5.cloned.1.call-start = ((), (), s32[]{:S(2)}) async-start(), calls=%async_computation.9 | async-start | bytes 3932160 | tf_op jit(solution)/shard_map/reduce_scatter | solution.py:854
  196.1 218.4 %reduce-scatter.3.cloned.1.call-start = ((), (), s32[]{:S(2)}) async-start(), calls=%async_computation.8 | async-start | bytes 7864320 | tf_op jit(solution)/shard_map/reduce_scatter | solution.py:853
  196.9 67.3 %all-to-all-start.5 = ((bf16[8,144,896]{2,1,0:T(8,128)(2,1)}), bf16[8,144,896]{2,1,0:T(8,128)(2,1)}, u32[]{:S(2)}, u32[]{:S(2)}) async-start(bf16[8,144,896]{2,1,0:T(8,128)(2,1)} %pad_maximum_fusion), calls=%async_computation.5 | async-start | bytes 4128768 | tf_op jit(solution)/shard_map/all_to_all | solution.py:813
  240.1 21.0 %collective-permute-start.3 = (bf16[384,1920]{1,0:T(8,128)(2,1)}, bf16[384,1920]{1,0:T(8,128)(2,1)}, u32[]{:S(2)}, u32[]{:S(2)}) collective-permute-start(bf16[384,1920]{1,0:T(8,128)(2,1)} %get-tuple-element.184), channel_id=1, source_target_pairs={{0,1},{1,0},{2,3},{3,2},{4,5},{5,4},{6,7},{7,6},{8,9},{9,8},{10,11... | collective-permute-start | bytes 4423688 | tf_op jit(solution)/shard_map/ppermute | solution.py:879
  280.0 18.6 %collective-permute-start.8 = (bf16[1,96,1920]{2,1,0:T(8,128)(2,1)}, bf16[1,96,1920]{2,1,0:T(8,128)(2,1)S(1)}, u32[]{:S(2)}, u32[]{:S(2)}) collective-permute-start(bf16[1,96,1920]{2,1,0:T(8,128)(2,1)} %get-tuple-element.215), channel_id=1, source_target_pairs={{0,2},{1,3},{2,0},{3,1},{4,6},{5,7},{6,4},{7,5},{8,10},{9,11},{10,... | collective-permute-start | bytes 1105928 | tf_op jit(solution)/shard_map/ppermute | solution.py:712
  281.7 28.5 %collective-permute-start.9 = (bf16[1,96,1920]{2,1,0:T(8,128)(2,1)}, bf16[1,96,1920]{2,1,0:T(8,128)(2,1)}, u32[]{:S(2)}, u32[]{:S(2)}) collective-permute-start(bf16[1,96,1920]{2,1,0:T(8,128)(2,1)} %get-tuple-element.216), channel_id=1, source_target_pairs={{0,4},{1,5},{2,6},{3,7},{4,0},{5,1},{6,2},{7,3},{8,12},{9,13},{10,... | collective-permute-start | bytes 1105928 | tf_op jit(solution)/shard_map/ppermute | solution.py:712
  284.1 26.1 %collective-permute-start.10 = (bf16[1,96,1920]{2,1,0:T(8,128)(2,1)}, bf16[1,96,1920]{2,1,0:T(8,128)(2,1)}, u32[]{:S(2)}, u32[]{:S(2)}) collective-permute-start(bf16[1,96,1920]{2,1,0:T(8,128)(2,1)} %get-tuple-element.217), channel_id=1, source_target_pairs={{0,6},{1,7},{2,4},{3,5},{4,2},{5,3},{6,0},{7,1},{8,14},{9,15},{10,... | collective-permute-start | bytes 1105928 | tf_op jit(solution)/shard_map/ppermute | solution.py:712
  295.4 19.2 %collective-permute-start.14 = (bf16[1,96,1280]{2,1,0:T(8,128)(2,1)}, bf16[1,96,1280]{2,1,0:T(8,128)(2,1)}, u32[]{:S(2)}, u32[]{:S(2)}) collective-permute-start(bf16[1,96,1280]{2,1,0:T(8,128)(2,1)} %get-tuple-element.226), channel_id=1, source_target_pairs={{0,8},{8,0},{16,24},{24,16},{1,9},{9,1},{17,25},{25,17},{2,10},{10... | collective-permute-start | bytes 737288 | tf_op jit(solution)/shard_map/ppermute | solution.py:712
  296.8 19.2 %collective-permute-start.15 = (bf16[1,96,1280]{2,1,0:T(8,128)(2,1)}, bf16[1,96,1280]{2,1,0:T(8,128)(2,1)}, u32[]{:S(2)}, u32[]{:S(2)}) collective-permute-start(bf16[1,96,1280]{2,1,0:T(8,128)(2,1)} %get-tuple-element.227), channel_id=1, source_target_pairs={{0,16},{8,24},{16,0},{24,8},{1,17},{9,25},{17,1},{25,9},{2,18},{10... | collective-permute-start | bytes 737288 | tf_op jit(solution)/shard_map/ppermute | solution.py:712
  298.7 22.4 %collective-permute-start.16 = (bf16[1,96,1280]{2,1,0:T(8,128)(2,1)}, bf16[1,96,1280]{2,1,0:T(8,128)(2,1)}, u32[]{:S(2)}, u32[]{:S(2)}) collective-permute-start(bf16[1,96,1280]{2,1,0:T(8,128)(2,1)} %get-tuple-element.228), channel_id=1, source_target_pairs={{0,24},{8,16},{16,8},{24,0},{1,25},{9,17},{17,9},{25,1},{2,26},{10... | collective-permute-start | bytes 737288 | tf_op jit(solution)/shard_map/ppermute | solution.py:712
  312.5 16.5 %collective-permute-start.11 = (bf16[1,24,1920]{2,1,0:T(8,128)(2,1)}, bf16[1,24,1920]{2,1,0:T(8,128)(2,1)}, u32[]{:S(2)}, u32[]{:S(2)}) collective-permute-start(bf16[1,24,1920]{2,1,0:T(8,128)(2,1)} %get-tuple-element.223), channel_id=1, source_target_pairs={{0,8},{8,0},{16,24},{24,16},{1,9},{9,1},{17,25},{25,17},{2,10},{10... | collective-permute-start | bytes 276488 | tf_op jit(solution)/shard_map/ppermute | solution.py:712
  313.9 15.1 %collective-permute-start.12 = (bf16[1,24,1920]{2,1,0:T(8,128)(2,1)}, bf16[1,24,1920]{2,1,0:T(8,128)(2,1)}, u32[]{:S(2)}, u32[]{:S(2)}) collective-permute-start(bf16[1,24,1920]{2,1,0:T(8,128)(2,1)} %get-tuple-element.224), channel_id=1, source_target_pairs={{0,16},{8,24},{16,0},{24,8},{1,17},{9,25},{17,1},{25,9},{2,18},{10... | collective-permute-start | bytes 276488 | tf_op jit(solution)/shard_map/ppermute | solution.py:712
  314.6 14.3 %collective-permute-start.13 = (bf16[1,24,1920]{2,1,0:T(8,128)(2,1)}, bf16[1,24,1920]{2,1,0:T(8,128)(2,1)}, u32[]{:S(2)}, u32[]{:S(2)}) collective-permute-start(bf16[1,24,1920]{2,1,0:T(8,128)(2,1)} %get-tuple-element.225), channel_id=1, source_target_pairs={{0,24},{8,16},{16,8},{24,0},{1,25},{9,17},{17,9},{25,1},{2,26},{10... | collective-permute-start | bytes 276488 | tf_op jit(solution)/shard_map/ppermute | solution.py:712
  330.7 17.5 %collective-permute-start.17 = (bf16[1,24,1920]{2,1,0:T(8,128)(2,1)}, bf16[1,24,1920]{2,1,0:T(8,128)(2,1)}, u32[]{:S(2)}, u32[]{:S(2)}) collective-permute-start(bf16[1,24,1920]{2,1,0:T(8,128)(2,1)} %sum_pieces.10.refs_0_), channel_id=1, source_target_pairs={{0,2},{1,3},{2,0},{3,1},{4,6},{5,7},{6,4},{7,5},{8,10},{9,11},{10,... | collective-permute-start | bytes 276488 | tf_op jit(solution)/shard_map/ppermute | solution.py:712
  330.8 17.5 %collective-permute-start.18 = (bf16[1,24,1920]{2,1,0:T(8,128)(2,1)}, bf16[1,24,1920]{2,1,0:T(8,128)(2,1)}, u32[]{:S(2)}, u32[]{:S(2)}) collective-permute-start(bf16[1,24,1920]{2,1,0:T(8,128)(2,1)} %sum_pieces.10.refs_0_), channel_id=1, source_target_pairs={{0,4},{1,5},{2,6},{3,7},{4,0},{5,1},{6,2},{7,3},{8,12},{9,13},{10,... | collective-permute-start | bytes 276488 | tf_op jit(solution)/shard_map/ppermute | solution.py:712
  333.6 14.6 %collective-permute-start.19 = (bf16[1,24,1920]{2,1,0:T(8,128)(2,1)}, bf16[1,24,1920]{2,1,0:T(8,128)(2,1)}, u32[]{:S(2)}, u32[]{:S(2)}) collective-permute-start(bf16[1,24,1920]{2,1,0:T(8,128)(2,1)} %sum_pieces.10.refs_0_), channel_id=1, source_target_pairs={{0,6},{1,7},{2,4},{3,5},{4,2},{5,3},{6,0},{7,1},{8,14},{9,15},{10,... | collective-permute-start | bytes 276488 | tf_op jit(solution)/shard_map/ppermute | solution.py:712
  350.0 14.5 %collective-permute-start.23 = (bf16[4,24,1920]{2,1,0:T(8,128)(2,1)}, bf16[4,24,1920]{2,1,0:T(8,128)(2,1)S(1)}, u32[]{:S(2)}, u32[]{:S(2)}) collective-permute-start(bf16[4,24,1920]{2,1,0:T(8,128)(2,1)} %stack_pieces.4.refs_0_), channel_id=1, source_target_pairs={{0,8},{8,0},{16,24},{24,16},{1,9},{9,1},{17,25},{25,17},{2,10},{10... | collective-permute-start | bytes 1105928 | tf_op jit(solution)/shard_map/ppermute | solution.py:712
  358.8 25.2 %collective-permute-start.24 = (bf16[4,24,1920]{2,1,0:T(8,128)(2,1)S(1)}, bf16[4,24,1920]{2,1,0:T(8,128)(2,1)S(1)}, u32[]{:S(2)}, u32[]{:S(2)}) collective-permute-start(bf16[4,24,1920]{2,1,0:T(8,128)(2,1)S(1)} %copy-done.7), channel_id=1, source_target_pairs={{0,16},{8,24},{16,0},{24,8},{1,17},{9,25},{17,1},{25,9},{2,18},{10... | collective-permute-start | bytes 1105928 | tf_op jit(solution)/shard_map/ppermute | solution.py:712
  359.5 24.5 %collective-permute-start.25 = (bf16[4,24,1920]{2,1,0:T(8,128)(2,1)S(1)}, bf16[4,24,1920]{2,1,0:T(8,128)(2,1)S(1)}, u32[]{:S(2)}, u32[]{:S(2)}) collective-permute-start(bf16[4,24,1920]{2,1,0:T(8,128)(2,1)S(1)} %copy-done.7), channel_id=1, source_target_pairs={{0,24},{8,16},{16,8},{24,0},{1,25},{9,17},{17,9},{25,1},{2,26},{10... | collective-permute-start | bytes 1105928 | tf_op jit(solution)/shard_map/ppermute | solution.py:712
  361.7 30.2 %collective-permute-start.7 = (bf16[256,768]{1,0:T(8,128)(2,1)}, bf16[256,768]{1,0:T(8,128)(2,1)}, u32[]{:S(2)}, u32[]{:S(2)}) collective-permute-start(bf16[256,768]{1,0:T(8,128)(2,1)} %get-tuple-element.311), channel_id=1, source_target_pairs={{0,24},{8,16},{16,8},{24,0},{1,25},{9,17},{17,9},{25,1},{2,26},{10... | collective-permute-start | bytes 1179656 | tf_op jit(solution)/shard_map/ppermute | solution.py:869
  363.3 29.6 %collective-permute-start.6 = (bf16[256,768]{1,0:T(8,128)(2,1)S(1)}, bf16[256,768]{1,0:T(8,128)(2,1)}, u32[]{:S(2)}, u32[]{:S(2)}) collective-permute-start(bf16[256,768]{1,0:T(8,128)(2,1)S(1)} %get-tuple-element.312), channel_id=1, source_target_pairs={{0,16},{8,24},{16,0},{24,8},{1,17},{9,25},{17,1},{25,9},{2,18},{10... | collective-permute-start | bytes 1179656 | tf_op jit(solution)/shard_map/ppermute | solution.py:869
  364.6 29.7 %collective-permute-start.5 = (bf16[256,768]{1,0:T(8,128)(2,1)S(1)}, bf16[256,768]{1,0:T(8,128)(2,1)}, u32[]{:S(2)}, u32[]{:S(2)}) collective-permute-start(bf16[256,768]{1,0:T(8,128)(2,1)S(1)} %get-tuple-element.310), channel_id=1, source_target_pairs={{0,8},{8,0},{16,24},{24,16},{1,9},{9,1},{17,25},{25,17},{2,10},{10... | collective-permute-start | bytes 1179656 | tf_op jit(solution)/shard_map/ppermute | solution.py:869
  388.0 26.5 %collective-permute-start.29 = (bf16[16,24,1920]{2,1,0:T(8,128)(2,1)}, bf16[16,24,1920]{2,1,0:T(8,128)(2,1)}, u32[]{:S(2)}, u32[]{:S(2)}) collective-permute-start(bf16[16,24,1920]{2,1,0:T(8,128)(2,1)} %stack_pieces.6), channel_id=1, source_target_pairs={{0,1},{1,0},{2,3},{3,2},{4,5},{5,4},{6,7},{7,6},{8,9},{9,8},{10,11... | collective-permute-start | bytes 4423688 | tf_op jit(solution)/shard_map/ppermute | solution.py:879
  391.8 13.6 %collective-permute-start.31 = (bf16[4,24,1280]{2,1,0:T(8,128)(2,1)}, bf16[4,24,1280]{2,1,0:T(8,128)(2,1)S(1)}, u32[]{:S(2)}, u32[]{:S(2)}) collective-permute-start(bf16[4,24,1280]{2,1,0:T(8,128)(2,1)} %stack_pieces.5.refs_0_), channel_id=1, source_target_pairs={{0,16},{8,24},{16,0},{24,8},{1,17},{9,25},{17,1},{25,9},{2,18},{10... | collective-permute-start | bytes 737288 | tf_op jit(solution)/shard_map/ppermute | solution.py:712
  (43 other events, 330.7 us)
Sparse Core Ops, SparseCore 0:
  196.3 42.0 reduce-scatter.4
  241.9 82.5 reduce-scatter.2

commit v3 on v2

--- a/solution.py
+++ b/solution.py
@@ -108,8 +108,13 @@
     )(flags, proj, proj, proj, kv_rem, kv_rem)
 
 
-def attention_backward_kernel(plen, flags_ref, q_ref, k_ref, v_ref, kr_ref, vr_ref, o_ref, do_ref, lse_ref,
-                              dq_ref, dk_ref, dv_ref, dkr_ref, dvr_ref, kt, krt, dka, dva, dkra, dvra):
+def attention_backward_kernel(plen, started, last, skip, flags_ref, core_ref, q_ref, k_ref, v_ref, kr_ref, vr_ref, o_ref, do_ref, lse_ref, act_ref, far_ref, wq_ref, wk_ref, wv_ref, *refs):
+    refs = refs[skip:]
+    if started:
+        start_act_ref, start_far_ref, *refs = refs
+    mine_ref, theirs_ref, dact_ref, *refs = refs
+    dfar_ref, *dfar_refs = (refs[-1:] + refs[:-9]) if last else refs[:1]
+    kt, krt, dka, dva, dkra, dvra, own_grads, weights = refs[-9:-1] if last else refs[-8:]
     tok = q_ref.shape[0]
     remote = kr_ref.shape[0]
     lane = lax.broadcasted_iota(jnp.int32, (1, 128), 1)
@@ -162,47 +167,111 @@
                 part = dot_nn(tt[head * HEAD_DIM : (head + 1) * HEAD_DIM, keys], dst)
                 total = part if total is None else total + part
             dqt.append(total)
-        dq_ref[rows, :] = (jnp.concatenate(dqt, axis=0).T * SCALE).astype(bf16)
-    dk_ref[...] = (dka[...] * SCALE).astype(bf16)
-    dv_ref[...] = dva[...].astype(bf16)
-    dkr_ref[...] = (dkra[...] * SCALE).astype(bf16)
-    dvr_ref[...] = dvra[...].astype(bf16)
-
-
-def attention_backward(flags, proj, kv_rem, mixed, d_mixed, lse, plen, begin, count):
+        own_grads[rows, 0:128] = (jnp.concatenate(dqt, axis=0).T * SCALE).astype(bf16)
+    own_grads[:, 128:256] = (dka[...] * SCALE).astype(bf16)
+    own_grads[:, 256:384] = dva[...].astype(bf16)
+    far_grads = jnp.concatenate([(dkra[...] * SCALE).astype(bf16), dvra[...].astype(bf16)], axis=1)
+    weights[:, 0:128] = wq_ref[...]
+    weights[:, 128:256] = wk_ref[...]
+    weights[:, 256:384] = wv_ref[...]
+    half = mine_ref.shape[0]
+    for out_ref, which in ((theirs_ref, 1 - core_ref[0]), (mine_ref, core_ref[0])):
+        rows = pl.ds(pl.multiple_of(which * half, half), half)
+        total = dot_nn(act_ref[rows, :], own_grads[...])
+        out_ref[:, 0:128] = total[:, 0:128].astype(bf16)
+        out_ref[:, 128:384] = (total[:, 128:384] + dot_nn(far_ref[rows, :], far_grads)).astype(bf16)
+    d_act = dot_nt(own_grads[...], weights[...])
+    d_far = dot_nt(far_grads, weights[:, 128:384])
+    step = pl.program_id(0)
+
+    @pl.when(step == 0)
+    def _():
+        dact_ref[...] = d_act + start_act_ref[...] if started else d_act
+        dfar_ref[...] = d_far + start_far_ref[...] if started else d_far
+
+    @pl.when(step > 0)
+    def _():
+        dact_ref[...] += d_act
+        dfar_ref[...] += d_far
+
+    if last:
+
+        @pl.when(step == pl.num_programs(0) - 1)
+        def _():
+            for k, ref in enumerate(dfar_refs):
+                ref[...] = dfar_ref[k * plen : (k + 1) * plen, :].astype(bf16)
+
+
+def attention_backward(flags, core, proj, kv_rem, mixed, d_mixed, lse, act_t, far_t, w_qkv, plen, begin, count, buffers, at, starts, last):
     tok, width = mixed.shape
     remote = kv_rem.shape[0]
     pairs = width // 128
     own = lambda shift: pl.BlockSpec((tok, 128), lambda i: (0, shift + i))
     far = lambda shift: pl.BlockSpec((remote, 128), lambda i: (0, shift + i))
-    return pl.pallas_call(
-        functools.partial(attention_backward_kernel, plen),
+    weight = lambda shift: pl.BlockSpec((width, 128), lambda i: (0, shift + i))
+    still = lambda shape: pl.BlockSpec(shape, lambda i: (0, 0))
+    half = pl.BlockSpec((width // 2, 384), lambda i: (0, at + i))
+    in_specs = [
+        pl.BlockSpec(memory_space=pltpu.SMEM),
+        pl.BlockSpec(memory_space=pltpu.SMEM),
+        own(begin),
+        own(pairs + begin),
+        own(2 * pairs + begin),
+        far(begin),
+        far(pairs + begin),
+        own(begin),
+        own(begin),
+        pl.BlockSpec((1, 16, tok), lambda i: (begin + i, 0, 0)),
+        still((width, tok)),
+        still((width, remote)),
+        weight(begin),
+        weight(pairs + begin),
+        weight(2 * pairs + begin),
+    ]
+    arrays = [flags, core, proj, proj, proj, kv_rem, kv_rem, mixed, d_mixed, lse, act_t, far_t, w_qkv, w_qkv, w_qkv]
+    scratch = [
+        pltpu.VMEM((128, tok), bf16),
+        pltpu.VMEM((128, remote), bf16),
+        pltpu.VMEM((tok, 128), f32),
+        pltpu.VMEM((tok, 128), f32),
+        pltpu.VMEM((remote, 128), f32),
+        pltpu.VMEM((remote, 128), f32),
+        pltpu.VMEM((tok, 384), bf16),
+        pltpu.VMEM((width, 384), bf16),
+    ]
+    sums = [jax.ShapeDtypeStruct((tok, width), f32), jax.ShapeDtypeStruct((remote, width), f32)]
+    aliases = {}
+    skip = 0
+    if not isinstance(buffers, int):
+        aliases = {len(arrays): 0, len(arrays) + 1: 1}
+        in_specs += [pl.BlockSpec(memory_space=pl.ANY)] * 2
+        arrays += list(buffers)
+        skip = 2
+        buffers = buffers[0].shape[1]
+    if starts:
+        in_specs += [still((tok, width)), still((remote, width))]
+        arrays += list(starts)
+    out_specs = [half, half, still((tok, width))]
+    out_shape = [jax.ShapeDtypeStruct((width // 2, buffers), bf16)] * 2 + sums[:1]
+    if last:
+        out_specs += [still((plen, width))] * (remote // plen)
+        out_shape += [jax.ShapeDtypeStruct((plen, width), bf16)] * (remote // plen)
+        scratch = scratch + [pltpu.VMEM((remote, width), f32)]
+    else:
+        out_specs += [still((remote, width))]
+        out_shape += sums[1:]
+    return pl.pallas_call(
+        functools.partial(attention_backward_kernel, plen, bool(starts), last, skip),
         grid=(count,),
-        in_specs=[
-            pl.BlockSpec(memory_space=pltpu.SMEM),
-            own(begin),
-            own(pairs + begin),
-            own(2 * pairs + begin),
-            far(begin),
-            far(pairs + begin),
-            own(begin),
-            own(begin),
-            pl.BlockSpec((1, 16, tok), lambda i: (begin + i, 0, 0)),
-        ],
-        out_specs=[own(0), own(0), own(0), far(0), far(0)],
-        out_shape=[jax.ShapeDtypeStruct((tok, count * 128), bf16)] * 3 + [jax.ShapeDtypeStruct((remote, count * 128), bf16)] * 2,
-        scratch_shapes=[
-            pltpu.VMEM((128, tok), bf16),
-            pltpu.VMEM((128, remote), bf16),
-            pltpu.VMEM((tok, 128), f32),
-            pltpu.VMEM((tok, 128), f32),
-            pltpu.VMEM((remote, 128), f32),
-            pltpu.VMEM((remote, 128), f32),
-        ],
-        compiler_params=pltpu.CompilerParams(vmem_limit_bytes=60 * 2**20),
-        cost_estimate=pl.CostEstimate(flops=10 * tok * (tok + remote) * count * 128, bytes_accessed=2 * (tok * 8 + remote * 4) * count * 128, transcendentals=tok * (tok + remote) * 2 * count),
+        in_specs=in_specs,
+        out_specs=out_specs,
+        out_shape=out_shape,
+        scratch_shapes=scratch,
+        input_output_aliases=aliases,
+        compiler_params=pltpu.CompilerParams(vmem_limit_bytes=60 * 2**20),
+        cost_estimate=pl.CostEstimate(flops=10 * tok * (tok + remote) * count * 128 + 20 * tok * width * count * 128, bytes_accessed=2 * (tok * 8 + remote * 4) * count * 128 + 16 * tok * width, transcendentals=tok * (tok + remote) * 2 * count),
         name="attention_backward",
-    )(flags, proj, proj, proj, kv_rem, kv_rem, mixed, d_mixed, lse)
+    )(*arrays)
 
 
 FFN_EXPERTS = 8
@@ -274,7 +343,7 @@
 
 
 def expert_kernel(group, home_ref, rows_ref, early_ref, router_ref, wg_ref, wu_ref, wd_ref,
-                  out_ref, drow_ref, dout_ref, inner_ref, dgate_ref, dup_ref, acc_out, acc_row, probs_ref):
+                  out_ref, drow_ref, dout_ref, inner_ref, dgate_ref, dup_ref, small_ref, acc_out, acc_row, probs_ref):
     width = rows_ref.shape[1]
     step, steps = pl.program_id(0), pl.num_programs(0)
     home = home_ref[0]
@@ -323,6 +392,8 @@
         out_ref[:, width : width + EXTRA] = extra.astype(bf16)
         term = d_row_gate * gate * (jnp.where(lane == home, 1.0, 0.0) - probs)
         high, rest = split_low(term, 2)
+        turned = [piece.T for piece in (high, rest)]
+        small_ref[...] = (dot_nn(turned[0], rows) + dot_nn(turned[1], rows))[0 : 2 * SMALL, :]
         drow_ref[...] = (acc_row[...] + dot_nt(high, router_ref[...]) + dot_nt(rest, router_ref[...])).astype(bf16)
 
 
@@ -346,13 +417,14 @@
             tall,
             pl.BlockSpec((1, tile, width), lambda j: (0, j, 0)),
         ],
-        out_specs=[wide, full, full, piece, piece, piece],
+        out_specs=[wide, full, full, piece, piece, piece, pl.BlockSpec((2 * SMALL, width), lambda j: (0, 0))],
         out_shape=[
             jax.ShapeDtypeStruct((count, width + EXTRA), bf16),
             jax.ShapeDtypeStruct((count, width), bf16),
             jax.ShapeDtypeStruct((count, width), bf16),
         ]
-        + [jax.ShapeDtypeStruct((count, ff), bf16)] * 3,
+        + [jax.ShapeDtypeStruct((count, ff), bf16)] * 3
+        + [jax.ShapeDtypeStruct((2 * SMALL, width), f32)],
         scratch_shapes=[pltpu.VMEM((count, width), f32), pltpu.VMEM((count, width), f32), pltpu.VMEM((count, EXTRA), f32)],
         compiler_params=pltpu.CompilerParams(vmem_limit_bytes=60 * 2**20),
         cost_estimate=pl.CostEstimate(flops=12 * count * width * ff, bytes_accessed=6 * width * ff + 2 * count * (5 * width + 3 * ff), transcendentals=count * ff),
@@ -451,7 +523,6 @@
     weight = copy_gate
     d_probs = place(dots, lane, FFN_EXPERTS + 1)
     logit_grads = jnp.zeros_like(probs)
-    mixing_terms = jnp.zeros_like(probs)
     vec_terms = jnp.zeros_like(probs)
     for c in range(2):
         vec = vec_ref[c : c + 1, :]
@@ -467,8 +538,7 @@
         mean = a0 * d0 + a1 * d1
         d0, d1 = a0 * (d0 - mean), a1 * (d1 - mean)
         logit_grads = logit_grads + place(d0, lane, at) + place(d1, lane, at + 1)
-        mixing_terms = mixing_terms + place(d0, lane, 2 * c) + place(d1, lane, 2 * c + 1)
-        vec_terms = vec_terms + place(gate * a1, lane, 4 + c)
+        vec_terms = vec_terms + place(gate * a1, lane, 20 + c)
     d_probs = jnp.where(named, d_probs, 0.0)
     logit_grads = logit_grads + probs * (d_probs - jnp.sum(probs * d_probs, axis=1, keepdims=True))
     high, rest = split_low(logit_grads, 2)
@@ -477,11 +547,11 @@
     probs_ref[...] = probs
     dprobs_ref[...] = d_probs
     sums = None
-    for terms, rows in ((mixing_terms, low), (vec_terms, grad_ref[...])):
+    for terms, rows in ((logit_grads, low), (vec_terms, grad_ref[...])):
         for piece in split_low(terms.T, 2):
             part = dot_nn(piece, rows)
             sums = part if sums is None else sums + part
-    sums = sums[0:SMALL, :]
+    sums = sums[0 : 3 * SMALL, :]
 
     @pl.when(pl.program_id(0) == 0)
     def _():
@@ -495,12 +565,12 @@
 def local_part(hidden, low, grad, prev, ids, mix, gain, vec):
     tok, width = hidden.shape
     block, tiles = row_tiles(tok)
-    shapes = [(tok, width), (tok, width), (tok, EXTRA), (tok, EXTRA), (SMALL, width)]
+    shapes = [(tok, width), (tok, width), (tok, EXTRA), (tok, EXTRA), (3 * SMALL, width)]
     return pl.pallas_call(
         local_kernel,
         grid=(tok // block,),
         in_specs=[tiles(width), tiles(width), tiles(width), tiles(EXTRA), tiles(2), fixed(mix), fixed(gain), fixed(vec)],
-        out_specs=[tiles(width), tiles(width), tiles(EXTRA), tiles(EXTRA), pl.BlockSpec((SMALL, width), lambda i: (0, 0))],
+        out_specs=[tiles(width), tiles(width), tiles(EXTRA), tiles(EXTRA), pl.BlockSpec((3 * SMALL, width), lambda i: (0, 0))],
         out_shape=[jax.ShapeDtypeStruct(s, f32) for s in shapes],
         compiler_params=pltpu.CompilerParams(vmem_limit_bytes=60 * 2**20),
         cost_estimate=pl.CostEstimate(flops=14 * tok * width * EXTRA, bytes_accessed=16 * tok * width, transcendentals=tok * EXTRA),
@@ -517,9 +587,17 @@
     return pl.BlockSpec(value.shape, lambda i: (0,) * value.ndim)
 
 
-def combine_kernel(count, parts, *refs):
-    chosen, got = refs[:count], refs[count : count * (1 + parts)]
-    local_ref, hidden_ref, gain_ref, grad_ref, w_ref, dhidden_ref, dlow_ref, dmixed_ref, small_ref = refs[count * (1 + parts) :]
+def combine_kernel(count, parts, core_ref, *refs):
+    chosen, got, refs = refs[:count], refs[count : count * (1 + parts)], refs[count * (1 + parts) :]
+    smalls, refs = refs[: count + 1], refs[count + 1 :]
+    local_ref, hidden_ref, gain_ref, grad_ref, mixed_ref, w_ref, dhidden_ref, dmixed_ref, mine_ref, theirs_ref, total_w, total_gain, small_t = refs
+    step = pl.program_id(0)
+
+    @pl.when(step == 0)
+    def _():
+        total_w[...] = jnp.zeros_like(total_w)
+        total_gain[...] = jnp.zeros_like(total_gain)
+
     d_normed = local_ref[...]
     for g in range(count):
         for r in range(parts):
@@ -531,36 +609,46 @@
     d_hidden = grad_ref[...].astype(f32) + inverse * scaled - hidden * (inverse * inverse * inverse * mean)
     low = d_hidden.astype(bf16)
     dhidden_ref[...] = d_hidden
-    dlow_ref[...] = low
     dmixed_ref[...] = dot_nt(low, w_ref[...]).astype(bf16)
-    gain = jnp.sum(d_normed * hidden * inverse, axis=0, keepdims=True)
-    row = lax.broadcasted_iota(jnp.int32, (SMALL, 1), 0)
-    gain = jnp.where(row == 0, gain, 0.0)
-
-    @pl.when(pl.program_id(0) == 0)
+    total_w[...] += dot_nn(mixed_ref[...].T, low)
+    total_gain[...] += jnp.sum(d_normed * hidden * inverse, axis=0, keepdims=True)
+
+    @pl.when(step == pl.num_programs(0) - 1)
     def _():
-        small_ref[...] = gain
-
-    @pl.when(pl.program_id(0) > 0)
-    def _():
-        small_ref[...] += gain
-
-
-def combine(chosen, got, local, hidden, gain, grad, w_out):
+        width = w_ref.shape[0]
+        half = width // 2
+        row = lax.broadcasted_iota(jnp.int32, (SMALL, 1), 0)
+        top = smalls[0][0 : 2 * SMALL, :]
+        for small in smalls[1:]:
+            top = top + small[...]
+        rest = jnp.zeros((EXTRA - 4 * SMALL, width), f32)
+        rows = [top, smalls[0][2 * SMALL : 3 * SMALL, :], jnp.where(row == 0, total_gain[...], 0.0), rest]
+        small_t[...] = jnp.concatenate(rows, axis=0).T
+        at = mine_ref.shape[1] - width - EXTRA
+        for out_ref, which in ((theirs_ref, 1 - core_ref[0]), (mine_ref, core_ref[0])):
+            place_rows = pl.ds(pl.multiple_of(which * half, half), half)
+            out_ref[:, at : at + width] = total_w[place_rows, :].astype(bf16)
+            out_ref[:, at + width : at + width + EXTRA] = small_t[place_rows, :].astype(bf16)
+
+
+def combine(core, chosen, got, smalls, local, hidden, gain, grad, mixed, w_out, columns):
     tok, width = hidden.shape
     rows = sum(c.shape[1] for c in chosen)
     arrays = [a for group in got for a in group]
     block, tiles = row_tiles(tok)
+    half = (width // 2, columns + width + EXTRA)
     return pl.pallas_call(
         functools.partial(combine_kernel, len(chosen), len(got[0])),
         grid=(tok // block,),
-        in_specs=[tiles(c.shape[1]) for c in chosen] + [fixed(a) for a in arrays] + [tiles(width), tiles(width), fixed(gain), tiles(width), fixed(w_out)],
-        out_specs=[tiles(width)] * 3 + [pl.BlockSpec((SMALL, width), lambda i: (0, 0))],
-        out_shape=[jax.ShapeDtypeStruct((tok, width), f32)] + [jax.ShapeDtypeStruct((tok, width), bf16)] * 2 + [jax.ShapeDtypeStruct((SMALL, width), f32)],
-        compiler_params=pltpu.CompilerParams(vmem_limit_bytes=60 * 2**20),
-        cost_estimate=pl.CostEstimate(flops=2 * tok * width * (rows + width), bytes_accessed=2 * width * (9 * tok + 2 * rows), transcendentals=0),
+        in_specs=[SCALARS] + [tiles(c.shape[1]) for c in chosen] + [fixed(a) for a in arrays + smalls]
+        + [tiles(width), tiles(width), fixed(gain), tiles(width), tiles(width), fixed(w_out)],
+        out_specs=[tiles(width)] * 2 + [pl.BlockSpec(half, lambda i: (0, 0))] * 2,
+        out_shape=[jax.ShapeDtypeStruct((tok, width), f32), jax.ShapeDtypeStruct((tok, width), bf16)] + [jax.ShapeDtypeStruct(half, bf16)] * 2,
+        scratch_shapes=[pltpu.VMEM((width, width), f32), pltpu.VMEM((1, width), f32), pltpu.VMEM((width, EXTRA), f32)],
+        compiler_params=pltpu.CompilerParams(vmem_limit_bytes=60 * 2**20),
+        cost_estimate=pl.CostEstimate(flops=2 * tok * width * (rows + 2 * width), bytes_accessed=2 * width * (10 * tok + 2 * rows), transcendentals=0),
         name="combine_gradients",
-    )(*chosen, *arrays, local, hidden, gain, grad, w_out)
+    )(core, *chosen, *arrays, *smalls, local, hidden, gain, grad, mixed, w_out)
 
 
 def flat_rows(value):
@@ -571,7 +659,7 @@
 
 def finish_kernel(groups, parts, *refs):
     chosen, got = refs[: len(groups)], refs[len(groups) : len(groups) + parts]
-    local_ref, probs_ref, dprobs_ref, low_ref, out_ref, dlogits_ref, small_ref = refs[len(groups) + parts :]
+    local_ref, probs_ref, dprobs_ref, out_ref, dlogits_ref = refs[len(groups) + parts :]
     width = local_ref.shape[1]
     lane = lax.broadcasted_iota(jnp.int32, (1, EXTRA), 1)
     picked = None
@@ -585,120 +673,88 @@
     d_probs = dprobs_ref[...] + jnp.where(lane < ALL_EXPERTS, extra, 0.0)
     probs = probs_ref[...]
     d_logits = probs * (d_probs - jnp.sum(probs * d_probs, axis=1, keepdims=True))
-    dlogits_ref[...] = d_logits
-    high, rest = split_low(d_logits.T, 2)
-    sums = (dot_nn(high, low_ref[...]) + dot_nn(rest, low_ref[...]))[0 : 2 * SMALL, :]
-
-    @pl.when(pl.program_id(0) == 0)
-    def _():
-        small_ref[...] = sums
-
-    @pl.when(pl.program_id(0) > 0)
-    def _():
-        small_ref[...] += sums
-
-
-def finish(chosen, got, groups, local, probs, d_probs, low):
+    dlogits_ref[...] = d_logits.T
+
+
+def finish(chosen, got, groups, local, probs, d_probs):
     tok, width = local.shape
     block, tiles = row_tiles(tok)
     return pl.pallas_call(
         functools.partial(finish_kernel, groups, len(got)),
         grid=(tok // block,),
-        in_specs=[tiles(c.shape[1]) for c in chosen] + [fixed(g) for g in got] + [tiles(width), tiles(EXTRA), tiles(EXTRA), tiles(width)],
-        out_specs=[tiles(width), tiles(EXTRA), pl.BlockSpec((2 * SMALL, width), lambda i: (0, 0))],
-        out_shape=[jax.ShapeDtypeStruct((tok, width), bf16), jax.ShapeDtypeStruct((tok, EXTRA), f32), jax.ShapeDtypeStruct((2 * SMALL, width), f32)],
+        in_specs=[tiles(c.shape[1]) for c in chosen] + [fixed(g) for g in got] + [tiles(width), tiles(EXTRA), tiles(EXTRA)],
+        out_specs=[tiles(width), pl.BlockSpec((EXTRA, block), lambda i: (0, i))],
+        out_shape=[jax.ShapeDtypeStruct((tok, width), bf16), jax.ShapeDtypeStruct((EXTRA, tok), f32)],
         compiler_params=pltpu.CompilerParams(vmem_limit_bytes=60 * 2**20),
         cost_estimate=pl.CostEstimate(flops=2 * tok * 1152 * (width + EXTRA), bytes_accessed=16 * tok * width, transcendentals=0),
         name="finish_outputs",
-    )(*chosen, *got, local, probs, d_probs, low)
+    )(*chosen, *got, local, probs, d_probs)
+
+
+def input_kernel(dact_ref, x_ref, gain_ref, dhidden_ref, *refs):
+    out_ref = refs[-1]
+    far = refs[0][...].astype(f32)
+    for ref in refs[1:-1]:
+        far = far + ref[...].astype(f32)
+    x = x_ref[...].astype(f32)
+    inverse = inverse_rms(x)
+    scaled = (dact_ref[...] + jnp.where(pl.program_id(0) == 0, far, 0.0)) * gain_ref[...]
+    mean = jnp.mean(scaled * x, axis=1, keepdims=True)
+    out_ref[...] = dhidden_ref[...] + inverse * scaled - x * (inverse * inverse * inverse * mean)
+
+
+def input_gradient(d_act, x, gain, d_hidden, far):
+    tok, width = x.shape
+    block = far[0].shape[0]
+    tiles = pl.BlockSpec((block, width), lambda i: (i, 0))
+    return pl.pallas_call(
+        input_kernel,
+        grid=(tok // block,),
+        in_specs=[tiles, tiles, fixed(gain), tiles] + [fixed(f) for f in far],
+        out_specs=tiles,
+        out_shape=jax.ShapeDtypeStruct((tok, width), f32),
+        compiler_params=pltpu.CompilerParams(vmem_limit_bytes=60 * 2**20),
+        cost_estimate=pl.CostEstimate(flops=12 * tok * width, bytes_accessed=16 * tok * width, transcendentals=0),
+        name="input_gradient",
+    )(d_act, x, gain, d_hidden, *far)
 
 
 def xor_pairs(size, mask):
     return [(i, i ^ mask) for i in range(size)]
 
 
-def store_halves(core, turned_terms, at, mine_ref, theirs_ref):
-    half = mine_ref.shape[0]
-    columns = turned_terms[0][1].shape[1]
-    for out_ref, which in ((theirs_ref, 1 - core), (mine_ref, core)):
-        rows = pl.ds(pl.multiple_of(which * half, half), half)
-        total = None
-        for left, right in turned_terms:
-            part = dot_nn(left[rows, :], right[...])
-            total = part if total is None else total + part
-        out_ref[:, at : at + columns] = total.astype(bf16)
-
-
-def pack_first_kernel(core_ref, act_ref, far_ref, dq_ref, dk_ref, dv_ref, dkf_ref, dvf_ref, mixed_ref, dlow_ref, mine_ref, theirs_ref, act_t, far_t, mixed_t):
-    core = core_ref[0]
-    width, n = mixed_ref.shape[1], dq_ref.shape[1]
-    mixed_t[...] = mixed_ref[...].T
-    act_t[...] = act_ref[...].T
-    far_t[...] = far_ref[...].T
-    store_halves(core, [(mixed_t, dlow_ref)], 0, mine_ref, theirs_ref)
-    store_halves(core, [(act_t, dq_ref)], width, mine_ref, theirs_ref)
-    store_halves(core, [(act_t, dk_ref), (far_t, dkf_ref)], width + n, mine_ref, theirs_ref)
-    store_halves(core, [(act_t, dv_ref), (far_t, dvf_ref)], width + 2 * n, mine_ref, theirs_ref)
-
-
-def pack_second_kernel(core_ref, act_ref, far_ref, dq_ref, dk_ref, dv_ref, dkf_ref, dvf_ref, local_ref, gain_ref, router_ref, mine_ref, theirs_ref, act_t, far_t, small_t):
-    core = core_ref[0]
-    n = dq_ref.shape[1]
-    half = mine_ref.shape[0]
-    act_t[...] = act_ref[...].T
-    far_t[...] = far_ref[...].T
-    store_halves(core, [(act_t, dq_ref)], 0, mine_ref, theirs_ref)
-    store_halves(core, [(act_t, dk_ref), (far_t, dkf_ref)], n, mine_ref, theirs_ref)
-    store_halves(core, [(act_t, dv_ref), (far_t, dvf_ref)], 2 * n, mine_ref, theirs_ref)
-    rows = [router_ref[...], local_ref[...], gain_ref[...]]
-    rows.append(jnp.zeros((EXTRA - sum(r.shape[0] for r in rows), act_ref.shape[1]), f32))
-    small_t[...] = jnp.concatenate(rows, axis=0).T
-    for out_ref, which in ((theirs_ref, 1 - core), (mine_ref, core)):
-        out_ref[:, 3 * n : 3 * n + EXTRA] = small_t[pl.ds(pl.multiple_of(which * half, half), half), :].astype(bf16)
-
-
-def pack(core, act, far, grads, others, first):
-    tok, width = act.shape
-    n = grads[0].shape[1]
-    columns = (width if first else EXTRA) + 3 * n
-    arrays = [act, far, *grads, *others]
-    extra = pltpu.VMEM((width, tok), bf16) if first else pltpu.VMEM((width, EXTRA), f32)
-    return pl.pallas_call(
-        pack_first_kernel if first else pack_second_kernel,
-        in_specs=[SCALARS] + [ANYWHERE] * len(arrays),
-        out_specs=[ANYWHERE] * 2,
-        out_shape=[jax.ShapeDtypeStruct((width // 2, columns), bf16)] * 2,
-        scratch_shapes=[pltpu.VMEM((width, tok), bf16), pltpu.VMEM((width, far.shape[0]), bf16), extra],
-        compiler_params=pltpu.CompilerParams(vmem_limit_bytes=60 * 2**20),
-        cost_estimate=pl.CostEstimate(flops=2 * width * columns * tok, bytes_accessed=2 * width * (5 * tok + columns), transcendentals=0),
-        name="pack_first" if first else "pack_second",
-    )(core, *arrays)
-
-
 def sum_kernel(terms, index_ref, *refs):
-    count = (len(refs)) // (terms + 1)
-    for k in range(count):
-        total = None
-        for t in range(terms):
-            value = refs[t * count + k][...].astype(f32)
-            total = value if total is None else total + value
-        refs[terms * count + k][...] = total.astype(bf16)
-
-
-def sum_pieces(index, arrays):
-    n, shape = arrays[0].shape[0], arrays[0].shape[1:]
-    views = [pl.BlockSpec((1,) + shape, functools.partial(lambda k, i, s: (s[0] ^ k if n > 1 else 0, 0, 0), k)) for k in range(n)]
-    return pl.pallas_call(
-        functools.partial(sum_kernel, len(arrays)),
+    count = len(refs) // (sum(terms) + 1)
+    outs = refs[-count:]
+    for k, out_ref in enumerate(outs):
+        at = 0
+        first = 0
+        for number in terms:
+            total = None
+            for t in range(first, first + number):
+                value = refs[t * count + k][0].astype(f32)
+                total = value if total is None else total + value
+            out_ref[0, :, at : at + total.shape[1]] = total.astype(bf16)
+            at += total.shape[1]
+            first += number
+
+
+def sum_pieces(index, groups):
+    arrays = [a for group in groups for a in group]
+    n, rows = arrays[0].shape[:2]
+    columns = sum(group[0].shape[2] for group in groups)
+    view = lambda a, k: pl.BlockSpec((1, rows, a.shape[2]), lambda i, s: (s[0] ^ k if n > 1 else 0, 0, 0))
+    return pl.pallas_call(
+        functools.partial(sum_kernel, [len(g) for g in groups]),
         grid_spec=pltpu.PrefetchScalarGridSpec(
             num_scalar_prefetch=1,
             grid=(1,),
-            in_specs=views * len(arrays),
-            out_specs=[pl.BlockSpec((1,) + shape, lambda i, s: (0, 0, 0))] * n,
+            in_specs=[view(a, k) for a in arrays for k in range(n)],
+            out_specs=[pl.BlockSpec((1, rows, columns), lambda i, s: (0, 0, 0))] * n,
         ),
-        out_shape=[jax.ShapeDtypeStruct((1,) + shape, bf16)] * n,
-        compiler_params=pltpu.CompilerParams(vmem_limit_bytes=60 * 2**20),
-        cost_estimate=pl.CostEstimate(flops=0, bytes_accessed=2 * n * math.prod(shape) * (len(arrays) + 1), transcendentals=0),
+        out_shape=[jax.ShapeDtypeStruct((1, rows, columns), bf16)] * n,
+        compiler_params=pltpu.CompilerParams(vmem_limit_bytes=60 * 2**20),
+        cost_estimate=pl.CostEstimate(flops=0, bytes_accessed=2 * n * rows * columns * 5, transcendentals=0),
         name="sum_pieces",
     )(index, *[a for a in arrays for _ in range(n)])
 
@@ -736,52 +792,55 @@
     )(*pieces)
 
 
-def unpack_kernel(index_ref, own1_ref, other1_ref, own2_ref, other2_ref, w_ref, out_ref, qkv_ref, small_ref):
+def unpack_kernel(left, index_ref, own_ref, other_ref, w_ref, out_ref, qkv_ref, turned_ref, small):
     width = out_ref.shape[1]
-    n = width // 2
-    piece = own1_ref.shape[2]
+    piece = own_ref.shape[2]
     mine = pl.program_id(0) == index_ref[0]
     lane = lax.broadcasted_iota(jnp.int32, (1, EXTRA), 1)
+    block = pl.program_id(0) * 4 + pl.program_id(1)
     for k in range(4):
         rows = slice(k * piece, (k + 1) * piece)
-        at_ctx, at_z = k ^ index_ref[1], k ^ index_ref[2]
-        first = jnp.where(mine, own1_ref[at_ctx, 0, :, :], other1_ref[at_ctx, 0, :, :]).astype(f32)
-        second = jnp.where(mine, own2_ref[0, at_z, :, :], other2_ref[0, at_z, :, :]).astype(f32)
-        out_ref[rows, :] = first[:, 0:width]
+        at_ctx = k ^ index_ref[1]
+        total = jnp.where(mine, own_ref[at_ctx, 0, :, :], other_ref[at_ctx, 0, :, :]).astype(f32)
+        out_ref[rows, :] = total[:, left : left + width]
         gain = None
         for p in range(3):
-            for value, at in ((first[:, width + p * n : width + (p + 1) * n], 0), (second[:, p * n : (p + 1) * n], n)):
-                columns = slice(p * width + at, p * width + at + n)
+            for i in range(width // 128):
+                at = i * 384 + p * 128 + (0 if i * 384 < left else width + EXTRA)
+                value = total[:, at : at + 128]
+                columns = slice(p * width + i * 128, p * width + (i + 1) * 128)
                 qkv_ref[rows, columns] = value
                 part = value * w_ref[rows, columns].astype(f32)
                 gain = part if gain is None else gain + part
         gain = jnp.sum(gain, axis=1, keepdims=True)
-        small_ref[rows, :] = second[:, 3 * n : 3 * n + EXTRA] + place(gain, lane, EXTRA - 1)
-
-
-def unpack(index, first, second, w_qkv):
+        small[pl.ds(block * 4 * piece + k * piece, piece), :] = total[:, left + width : left + width + EXTRA] + place(gain, lane, EXTRA - 1)
+
+    @pl.when(block == 7)
+    def _():
+        turned_ref[...] = small[...].T
+
+
+def unpack(index, own, other, w_qkv, left):
     width = w_qkv.shape[0]
     piece = width // 32
     block = 4 * piece
-    shape = lambda value: value.reshape(4, 4, piece, -1)
-    first, second = [shape(v) for v in first], [shape(v) for v in second]
-    c1, c2 = first[0].shape[3], second[0].shape[3]
+    own, other = own.reshape(4, 4, piece, -1), other.reshape(4, 4, piece, -1)
     row = lambda c, a, s: (c * 4 + a, 0)
-    source1 = pl.BlockSpec((4, 1, piece, c1), lambda c, a, s: (0, a ^ s[2], 0, 0))
-    source2 = pl.BlockSpec((1, 4, piece, c2), lambda c, a, s: (a ^ s[1], 0, 0, 0))
-    return pl.pallas_call(
-        unpack_kernel,
+    source = pl.BlockSpec((4, 1, piece, own.shape[3]), lambda c, a, s: (0, a ^ s[2], 0, 0))
+    return pl.pallas_call(
+        functools.partial(unpack_kernel, left),
         grid_spec=pltpu.PrefetchScalarGridSpec(
             num_scalar_prefetch=1,
             grid=(2, 4),
-            in_specs=[source1, source1, source2, source2, pl.BlockSpec((block, 3 * width), row)],
-            out_specs=[pl.BlockSpec((block, width), row), pl.BlockSpec((block, 3 * width), row), pl.BlockSpec((block, EXTRA), row)],
+            in_specs=[source, source, pl.BlockSpec((block, 3 * width), row)],
+            out_specs=[pl.BlockSpec((block, width), row), pl.BlockSpec((block, 3 * width), row), pl.BlockSpec((EXTRA, width), lambda c, a, s: (0, 0))],
+            scratch_shapes=[pltpu.VMEM((width, EXTRA), f32)],
         ),
-        out_shape=[jax.ShapeDtypeStruct((width, width), f32), jax.ShapeDtypeStruct((width, 3 * width), f32), jax.ShapeDtypeStruct((width, EXTRA), f32)],
+        out_shape=[jax.ShapeDtypeStruct((width, width), f32), jax.ShapeDtypeStruct((width, 3 * width), f32), jax.ShapeDtypeStruct((EXTRA, width), f32)],
         compiler_params=pltpu.CompilerParams(vmem_limit_bytes=60 * 2**20),
         cost_estimate=pl.CostEstimate(flops=0, bytes_accessed=36 * width * width, transcendentals=0),
         name="unpack_sums",
-    )(index, *first, *second, w_qkv)
+    )(index, own, other, w_qkv)
 
 P = jax.sharding.PartitionSpec
 
@@ -836,7 +895,8 @@
     mixed_low, early = lax.optimization_barrier((mixed_low, early))
     hidden, moe_low, sent = after_attention(mixed_low, x_low, w_out, moe_gain[None], turned)
     local_out, d_normed_local, probs, d_probs, small_local = local_part(hidden, moe_low, upstream_low, prev, routes[0], mix, moe_gain[None], const_vec)
-    sent = [after(sent[0], local_out, d_normed_local), sent[1]]
+    act_t, far_t = act_low.T, act_far.T
+    sent = [after(sent[0], local_out, d_normed_local, act_t, far_t), sent[1]]
     got = [deal(part.reshape(FFN_EXPERTS, -1, width)) for part in sent]
 
     got = [part.reshape(-1, width) for part in got]
@@ -848,105 +908,81 @@
     out_got = give_back(outs)
 
     d_got = [[part.reshape(-1, width) for part in group] for group in d_got]
-    d_hidden, d_attn_low, d_mixed, small_gain = combine(chosen, d_got, d_normed_local, hidden, moe_gain[None], upstream_low, w_out)
+    pairs = width // 128
+    cut = pairs // 3
+    core = (me_e & 1).reshape(1)
+    smalls = [small_local] + [p[6] for p in passes]
+    d_hidden, d_mixed, *buffers = combine(core, chosen, d_got, smalls, d_normed_local, hidden, moe_gain[None], upstream_low, mixed_low, w_out, cut * 384)
 
     sum_gate_up = lax.psum_scatter(gate_up_low, "ctx", scatter_dimension=1, tiled=True).astype(f32)
     sum_down = lax.psum_scatter(down_low, "ctx", scatter_dimension=0, tiled=True).astype(f32)
 
-    pairs = width // 128
-    cut = pairs // 2
-
-    def attention(upstream, begin, count):
-        return attention_backward(flags, projected, kv_far, mixed_low, upstream, lse, plen, begin, count)
-
-    def weight_columns(part, group):
-        at = part * width + group * cut * 128
-        return w_qkv[:, at : at + grads_1[0].shape[1]]
-
-    def far_gradient(both):
-        total = sum(dot_nt(grads[p + 2], weight_columns(p, g)) for g, grads in enumerate(both) for p in (1, 2))
-        total = total.astype(bf16).reshape(n_ctx - 1, plen, width)
-        return total, [lax.ppermute(total[k - 1], "ctx", xor_pairs(n_ctx, k)) for k in range(1, n_ctx)]
-
-    def own_gradient(both):
-        return sum(dot_nt(grads[p], weight_columns(p, g)) for g, grads in enumerate(both) for p in range(3))
-
-    grads_1 = attention(d_mixed, 0, cut)
-    if n_ctx == 4 and n_exp == 8:
-        core, z = me_e & 1, me_e >> 1
-        at_core, at_ctx, at_z, at_none = (v.reshape(1) for v in (core, me_c, z, z * 0))
-        along_ctx, along_z = ("ctx", 4, 1), ("exp", 8, 2)
-        across = lambda value: lax.ppermute(value, "exp", xor_pairs(8, 1))
-        mine_1, theirs_1 = pack(at_core, act_low, act_far, grads_1, [mixed_low, d_attn_low], True)
+    def attention(upstream, begin, count, buffers, at, starts, last):
+        return attention_backward(flags, core, projected, kv_far, mixed_low, upstream, lse, act_t, far_t, w_qkv, plen, begin, count, buffers, at, starts, last)
+
+    dense = n_ctx == 4 and n_exp == 8
+    left, right = cut * 384, (pairs - cut) * 384
+    z = me_e >> 1
+    at_ctx, at_z = me_c.reshape(1), z.reshape(1)
+    along_ctx, along_z = ("ctx", 4, 1), ("exp", 8, 2)
+    across = lambda value: lax.ppermute(value, "exp", xor_pairs(n_exp, 1))
+    mine_1, theirs_1, *starts = attention(d_mixed, 0, cut, buffers, 0, None, False)
+    if dense:
         got_1 = across(theirs_1)
-        grads_2 = attention(after(d_mixed, mine_1), cut, pairs - cut)
-        both = (grads_1, grads_2)
-        sums_1 = sum_pieces(at_z, [quarters(mine_1), quarters(after(got_1, grads_2[0]))])
+    mine_2, theirs_2, *starts = attention(d_mixed, cut, 1, right, 0, starts, False)
+    if dense:
+        mine_2, theirs_2, starts, got_1 = lax.optimization_barrier((mine_2, theirs_2, starts, got_1))
+        sums_1 = sum_pieces(at_z, [[quarters(mine_1), quarters(got_1)]])
         parts_1 = swap(sums_1, along_z)
-        mixed_out, d_logits, small_router = finish(chosen, out_got, groups, after(local_out, sums_1[0]), probs, d_probs, moe_low)
-        mine_2, theirs_2 = pack(at_core, act_low, act_far, grads_2, [small_local, small_gain, small_router], False)
+        mine_2 = after(mine_2, sums_1[0])
+    mine_2, theirs_2, d_act, *d_far = attention(d_mixed, cut + 1, pairs - cut - 1, (mine_2, theirs_2), 1, starts, True)
+    if dense:
+        mine_2, theirs_2, d_act, d_far, parts_1 = lax.optimization_barrier((mine_2, theirs_2, d_act, d_far, parts_1))
+    far_back = [lax.ppermute(d_far[k - 1], "ctx", xor_pairs(n_ctx, k)) for k in range(1, n_ctx)]
+    if dense:
         got_2 = across(theirs_2)
-        d_act_far, far_back = far_gradient(after(both, mine_2))
-        sums_2 = sum_pieces(at_ctx, [quarters(mine_2), quarters(after(got_2, d_act_far))])
-        parts_2 = swap(sums_2, along_ctx)
-        d_act = own_gradient(after(both, sums_2[0]))
-        sums_1 = sum_pieces(at_ctx, [quarters(p) for p in after(parts_1, d_act)])
-        parts_1 = swap(sums_1, along_ctx)
-        sums_2 = sum_pieces(at_z, [quarters(p) for p in after(parts_2, sums_1[0])])
+        mixed_out, d_logits = finish(chosen, out_got, groups, after(local_out, d_act), probs, d_probs)
+        mixed_out, d_logits, got_2 = lax.optimization_barrier((mixed_out, d_logits, got_2))
+        sums_2 = sum_pieces(at_z, [[quarters(mine_2), quarters(got_2)]])
         parts_2 = swap(sums_2, along_z)
-        [piece_1] = sum_pieces(at_none, after(parts_1, sums_2[0]))
-        spread_1 = spread(piece_1, along_z)
-        [piece_2] = sum_pieces(at_none, after(parts_2, piece_1))
-        spread_2 = spread(piece_2, along_z)
-        column_1 = stack_pieces(after(spread_1, piece_2))
-        spread_1 = spread(column_1, along_ctx)
-        column_2 = stack_pieces(after(spread_2, column_1))
-        spread_2 = spread(column_2, along_ctx)
-        own_1 = stack_pieces(after(spread_1, column_2))
-        other_1 = across(own_1)
-        own_2 = stack_pieces(after(spread_2, own_1))
-        other_2 = across(own_2)
     else:
-        grads_2 = attention(d_mixed, cut, pairs - cut)
-        both = (grads_1, grads_2)
-        mixed_out, d_logits, small_router = finish(chosen, out_got, groups, local_out, probs, d_probs, moe_low)
-        d_act_far, far_back = far_gradient(both)
-        d_act = own_gradient(both)
-
-    d_act = jnp.concatenate([d_act[:plen] + sum(part.astype(f32) for part in far_back), d_act[plen:]], axis=0)
-    scaled = d_act * attn_gain
-    d_inputs = d_hidden + inverse_attn * scaled - tokens_in * inverse_attn**3 * jnp.mean(scaled * tokens_in, axis=-1, keepdims=True)
-
-    if n_ctx == 4 and n_exp == 8:
-        weights = after(w_qkv, d_inputs, sum_gate_up, sum_down)
-        out_sum, qkv_sum, small = unpack(jnp.stack([core, me_c, z]), (own_1, other_1), (own_2, other_2), weights)
-        d_attn_gain = small[:, EXTRA - 1]
+        mixed_out, d_logits = finish(chosen, out_got, groups, local_out, probs, d_probs)
+    d_inputs = input_gradient(d_act, x_low, attn_gain[None], d_hidden, far_back)
+
+    total_gate, total_up, total_down = sum_gate_up[0][None], sum_gate_up[1][None], sum_down[None]
+    if dense:
+        parts_1, parts_2 = ([quarters(p) for p in parts] for parts in (parts_1, after(parts_2, d_inputs)))
+        parts = swap(sum_pieces(at_ctx, [parts_1, parts_2]), along_ctx)
+        [piece] = sum_pieces(at_ctx, [parts])
+        column = stack_pieces(spread(piece, along_z))
+        own = stack_pieces(after(spread(column, along_ctx), total_gate, total_up, total_down))
+        other = across(own)
+        out_sum, qkv_sum, small = unpack(jnp.stack([core[0], me_c, z]), own, other, w_qkv, left)
+        d_attn_gain = small[EXTRA - 1]
     else:
-        dq, dk, dv, dk_far, dv_far = (jnp.concatenate(pair, axis=1) for pair in zip(grads_1, grads_2))
-        d_w_k = dot_tn(act_low, dk) + dot_tn(act_far, dk_far)
-        d_w_v = dot_tn(act_low, dv) + dot_tn(act_far, dv_far)
-        parts = [dot_tn(mixed_low, d_attn_low), dot_tn(act_low, dq), d_w_k, d_w_v, small_router, small_local, small_gain]
-        out_sum, q_sum, k_sum, v_sum, *small = [p.astype(f32) for p in lax.psum([p.astype(bf16) for p in parts], ("ctx", "exp"))]
-        qkv_sum = jnp.concatenate([q_sum, k_sum, v_sum], axis=1)
-        small = jnp.concatenate(small, axis=0).T
+        whole = lambda mine, theirs: jnp.where(core == 0, jnp.concatenate([mine, theirs], axis=0), jnp.concatenate([theirs, mine], axis=0))
+        total_1, total_2 = [v.astype(f32) for v in lax.psum((whole(mine_1, theirs_1), whole(mine_2, theirs_2)), ("ctx", "exp"))]
+        columns = jnp.concatenate([total_1[:, :left], total_2], axis=1).reshape(width, pairs, 3, 128)
+        qkv_sum = columns.transpose(0, 2, 1, 3).reshape(width, 3 * width)
+        out_sum, small = total_1[:, left : left + width], total_1[:, left + width :].T
         d_attn_gain = jnp.sum(qkv_sum * w_qkv.astype(f32), axis=1)
     d_attn_gain = d_attn_gain / attn_gain
     at = 2 * SMALL
-    d_const_gate = jnp.stack([small[:, at : at + 2], small[:, at + 2 : at + 4]])
+    d_const_gate = jnp.stack([small[at : at + 2].T, small[at + 2 : at + 4].T])
     return (
         mixed_out[None],
         d_inputs[None],
-        d_logits[None, :, :ALL_EXPERTS],
+        d_logits[:ALL_EXPERTS].T[None],
         d_attn_gain,
         qkv_sum,
         out_sum,
-        small[:, at + SMALL],
-        small[:, :ALL_EXPERTS],
+        small[at + SMALL],
+        small[:ALL_EXPERTS].T,
         d_const_gate,
-        small[:, at + 4 : at + 6].T,
-        sum_gate_up[0][None],
-        sum_gate_up[1][None],
-        sum_down[None],
+        small[at + 4 : at + 6],
+        total_gate,
+        total_up,
+        total_down,
     )
 
 

time: 448 us -> 438 us (0.978)
  matrix products: 28.1 us -> 9.6 us
  Pallas kernels: 215 us -> 227 us
  starting transfers between devices: 71.2 us -> 62.4 us
  waiting for transfers between devices: 64.4 us -> 70.1 us
  other arithmetic: 17.5 us -> 12.1 us
    dot_general x10 -> x0, matrix products: 20.3 us -> none  [dot_nt(): lax.dot_general(a, b, (((1,), (1,)), ((), ())), preferred_element_type=f32)]
    pallas_call x11 -> x9, Pallas kernels: 81.8 us -> 96.2 us  [the longest x3 68.3 us: attention_backward(): pl.pallas_call(functools.partial(attention_backward_kernel, plen, bool(st...]
    ppermute x7 -> x6, waiting for transfers between devices: 0.02 us -> 13.7 us  [the longest x3 10.9 us: body(): lax.ppermute(d_far[k - 1], 'ctx', xor_pairs(n_ctx, k))]
    ppermute x24 -> x15, waiting for transfers between devices: 44.5 us -> 31.7 us  [swap(): lax.ppermute(pieces[k], axis, xor_pairs(size, unit * k))]
    ppermute x24 -> x15, starting transfers between devices: 32.9 us -> 26.6 us  [swap(): lax.ppermute(pieces[k], axis, xor_pairs(size, unit * k))]
    unnamed x74 -> x76, local copies, waits for them, and re-layouts: 13.4 us -> 15.8 us
  transfers between devices with their start and end apart: 42 -> 32, of which waited for: 12 -> 16; matrix products, arithmetic and copies ran while one was open for 13% -> 7% of each run, Pallas kernels for 43% -> 46%
where the time goes in v3:
time: 438 us; the launch traced here: 430 us
  Pallas kernels  227 us (52%)
  waiting for transfers between devices  70.1 us (16%)
  starting transfers between devices  62.4 us (14%)
  local copies, waits for them, and re-layouts  33.5 us (8%)
  between operations  14.8 us (3%)
  other arithmetic  12.1 us (3%)
  matrix products  9.6 us (2%)
    pallas_call x3, Pallas kernels, attention_backward(): pl.pallas_call(functools.partial(attention_backward_kernel, plen, bool(st...  68.3 us
    pallas_call x2, Pallas kernels, expert_pass(): pl.pallas_call(functools.partial(expert_kernel, group), grid=(ff // tile,...  38.7 us
    ppermute x15, waiting for transfers between devices, swap(): lax.ppermute(pieces[k], axis, xor_pairs(size, unit * k))  31.7 us
    ppermute x15, starting transfers between devices, swap(): lax.ppermute(pieces[k], axis, xor_pairs(size, unit * k))  26.6 us
    pallas_call x1, Pallas kernels, attention_forward(): pl.pallas_call(functools.partial(attention_forward_kernel, plen), grid=(p...  24 us
    pallas_call x1, Pallas kernels, weight_gradients(): pl.pallas_call(functools.partial(weight_kernel, count), grid=(ff // tile,...  17.9 us
    unnamed x76, local copies, waits for them, and re-layouts  15.8 us
    all_to_all x3, starting transfers between devices, deal(): return lax.all_to_all(value, 'exp', 0, 0, tiled=True)  15.6 us
  transfers between devices with their start and end apart: 32, of which 16 were waited for; matrix products, arithmetic and copies ran while one was open for 7% of the time, Pallas kernels for 46%

profile of v3, /device:TPU:0, one launch (start us, length us, event | category | flops | bytes accessed | tf_op | source)
XLA Modules:
  0.0 430.0 jit_solution(15001066626352239737)
XLA Ops:
  12.3 6.3 %route_plan.1 = (bf16[640,768]{1,0:T(8,128)(2,1)}, bf16[512,768]{1,0:T(8,128)(2,1)}, bf16[768,640]{1,0:T(8,128)(2,1)}, bf16[768,512]{1,0:T(8,128)(2,1)}, bf16[8,144,896]{2,1,0:T(8,128)(2,1)}) custom-call(s32[1]{0:T(128)} %bitcast.home_ref, s32[2,768]{1,0:T(2,128)} %copy.33.ids_ref, bf16[768,768]{1,0:T(8,128)(2,1)} %bitcast.119, f32[768,128]{1,0:T(8,128)} %pad.8.prev_ref), custom_call_target="tpu_custom_call" | custom-call | flops 1585446912 | bytes 3538944 | tf_op jit(solution)/shard_map/route_plan/pallas_call | solution.py:331
  18.6 6.8 %all-to-all-start = ((bf16[8,144,896]{2,1,0:T(8,128)(2,1)}), bf16[8,144,896]{2,1,0:T(8,128)(2,1)}, u32[]{:S(2)}, u32[]{:S(2)}) async-start(bf16[8,144,896]{2,1,0:T(8,128)(2,1)} %get-tuple-element.125), calls=%async_computation | async-start | bytes 4128768 | tf_op jit(solution)/shard_map/all_to_all | solution.py:869
  31.7 6.1 %convolution_convert_fusion.q_ref.k_ref.v_ref = bf16[768,2304]{1,0:T(8,128)(2,1)} fusion(bf16[768,2304]{1,0:T(8,128)(2,1)S(1)} %copy-done, f32[768]{0:T(1024)S(1)} %copy-done.31, f32[768]{0:T(1024)S(1)} %add_rsqrt_fusion.1, bf16[1,768,768]{2,1,0:T(8,128)(2,1)} %param.14), kind=kOutput, calls=%fused_computation | convolution fusion | flops 2722037760 | bytes 8263680 | tf_op jit(solution)/shard_map/dot_general | solution.py:22
  38.7 8.0 %collective-permute-done.1 = bf16[256,768]{1,0:T(8,128)(2,1)} collective-permute-done((bf16[256,768]{1,0:T(8,128)(2,1)}, bf16[256,768]{1,0:T(8,128)(2,1)}, u32[]{:S(2)}, u32[]{:S(2)}) %collective-permute-start.1) | collective-permute-done | bytes 393248 | tf_op jit(solution)/shard_map/ppermute | solution.py:877
  52.6 24.0 %attention_forward.1 = (bf16[768,768]{1,0:T(8,128)(2,1)}, f32[6,16,768]{2,1,0:T(8,128)}) custom-call(f32[3]{0:T(128)} %compare_select_fusion.flags_ref, bf16[768,2304]{1,0:T(8,128)(2,1)} %convolution_convert_fusion.q_ref.k_ref.v_ref, bf16[768,2304]{1,0:T(8,128)(2,1)} %convolution_convert_fusion.q_ref.k_ref.v_ref, ...), custom_call_target="tpu_custom_call" | custom-call | flops 3623878656 | bytes 7077888 | tf_op jit(solution)/shard_map/attention_forward/pallas_call | solution.py:86
  76.6 6.9 %after_attention.1 = (f32[768,768]{1,0:T(8,128)}, bf16[768,768]{1,0:T(8,128)(2,1)}, bf16[640,768]{1,0:T(8,128)(2,1)}, bf16[512,768]{1,0:T(8,128)(2,1)}) custom-call(bf16[768,768]{1,0:T(8,128)(2,1)} %get-tuple-element.126.mixed_ref.refs_11_.o_ref, bf16[768,768]{1,0:T(8,128)(2,1)} %bitcast.84, bf16[768,768]{1,0:T(8,128)(2,1)} %refs_12_.1, ...), custom_call_target="tpu_custom_call" | custom-call | flops 2264924160 | bytes 10616832 | tf_op jit(solution)/shard_map/after_attention/pallas_call | solution.py:491
  83.5 5.2 %all-to-all-start.3 = ((bf16[8,64,768]{2,1,0:T(8,128)(2,1)}), bf16[8,64,768]{2,1,0:T(8,128)(2,1)}, u32[]{:S(2)}, u32[]{:S(2)}) async-start(bf16[8,64,768]{2,1,0:T(8,128)(2,1)} %bitcast.136), calls=%async_computation.3 | async-start | bytes 1572864 | tf_op jit(solution)/shard_map/all_to_all | solution.py:869
  92.3 13.8 %local_part.1 = (f32[768,768]{1,0:T(8,128)}, f32[768,768]{1,0:T(8,128)}, f32[768,128]{1,0:T(8,128)}, f32[768,128]{1,0:T(8,128)}, f32[24,768]{1,0:T(8,128)}) custom-call(f32[768,768]{1,0:T(8,128)} %get-tuple-element.130.hidden_ref.refs_8_, bf16[768,768]{1,0:T(8,128)(2,1)} %get-tuple-element.131.low_ref, bf16[768,768]{1,0:T(8,128)(2,1)} %bitcast.120, ...), custom_call_target="tpu_custom_call" | custom-call | flops 1056964608 | bytes 9437184 | tf_op jit(solution)/shard_map/local_part/pallas_call | solution.py:569
  106.0 3.7 all-to-all-done.3
  109.7 3.6 all-to-all-start.1
  114.0 17.7 %expert_pass.3 = (bf16[512,896]{1,0:T(8,128)(2,1)}, bf16[512,768]{1,0:T(8,128)(2,1)}, bf16[512,768]{1,0:T(8,128)(2,1)}, bf16[512,2048]{1,0:T(8,128)(2,1)}, bf16[...) custom-call(s32[1]{0:T(128)} %bitcast.home_ref, bf16[512,768]{1,0:T(8,128)(2,1)} %bitcast.15.rows_ref.refs_1_, ...), custom_call_target="tpu_custom_call" | custom-call | flops 9663676416 | bytes 19660800 | tf_op jit(solution)/shard_map/expert_pass/pallas_call | solution.py:408
  131.7 6.6 %all-to-all-done.1 = bf16[8,80,768]{2,1,0:T(8,128)(2,1)S(1)} async-done(((bf16[8,80,768]{2,1,0:T(8,128)(2,1)}), bf16[8,80,768]{2,1,0:T(8,128)(2,1)S(1)}, u32[]{:S(2)}, u32[]{:S(2)}) %all-to-all-start.1) | async-done | bytes 983072 | tf_op jit(solution)/shard_map/all_to_all | solution.py:869
  138.4 4.0 all-to-all-start.4
  142.3 21.0 %expert_pass.2 = (bf16[640,896]{1,0:T(8,128)(2,1)}, bf16[640,768]{1,0:T(8,128)(2,1)}, bf16[640,768]{1,0:T(8,128)(2,1)}, bf16[640,2048]{1,0:T(8,128)(2,1)}, bf16[...) custom-call(s32[1]{0:T(128)} %bitcast.home_ref, bf16[640,768]{1,0:T(8,128)(2,1)} %bitcast.130, ...), custom_call_target="tpu_custom_call" | custom-call | flops 12079595520 | bytes 22216704 | tf_op jit(solution)/shard_map/expert_pass/pallas_call | solution.py:408
  164.3 5.1 %all-to-all-start.2 = ((bf16[8,80,768]{2,1,0:T(8,128)(2,1)}), bf16[8,80,768]{2,1,0:T(8,128)(2,1)S(1)}, u32[]{:S(2)}, u32[]{:S(2)}) async-start(bf16[8,80,768]{2,1,0:T(8,128)(2,1)} %bitcast.132), calls=%async_computation.2 | async-start | bytes 1966080 | tf_op jit(solution)/shard_map/all_to_all | solution.py:872
  172.0 17.9 %weight_gradients.1 = (bf16[2,768,2048]{2,1,0:T(8,128)(2,1)}, bf16[2048,768]{1,0:T(8,128)(2,1)}) custom-call(bf16[640,768]{1,0:T(8,128)(2,1)} %bitcast.131, bf16[512,768]{1,0:T(8,128)(2,1)} %bitcast.15.rows_ref.refs_1_, bf16[640,768]{1,0:T(8,128)(2,1)} %get-tuple-element.139.refs_2_, bf16[512,768]{1,0:T(8,128)(2,1)} %get-tuple-element.140.refs_3_, ...), custom_call_target="tpu_custom_call" | custom-call | flops 10871635968 | bytes 27131904 | tf_op jit(solution)/shard_map/weight_gradients/pallas_call | solution.py:457
  189.9 4.6 %all-to-all-done.2 = bf16[8,80,768]{2,1,0:T(8,128)(2,1)S(1)} async-done(((bf16[8,80,768]{2,1,0:T(8,128)(2,1)}), bf16[8,80,768]{2,1,0:T(8,128)(2,1)S(1)}, u32[]{:S(2)}, u32[]{:S(2)}) %all-to-all-start.2) | async-done | bytes 983072 | tf_op jit(solution)/shard_map/all_to_all | solution.py:872
  199.7 3.8 all-to-all-start.5
  203.5 11.9 %combine_gradients.1 = (f32[768,768]{1,0:T(8,128)}, bf16[768,768]{1,0:T(8,128)(2,1)}, bf16[384,1664]{1,0:T(8,128)(2,1)}, bf16[384,1664]{1,0:T(8,128)(2,1)}) custom-call(s32[1]{0:T(128)} %bitcast.19.core_ref, bf16[768,640]{1,0:T(8,128)(2,1)} %get-tuple-element.120.refs_0_, bf16[768,512]{1,0:T(8,128)(2,1)} %get-tuple-element.121.refs_1_, ...), custom_call_target="tpu_custom_call" | custom-call | flops 3170893824 | bytes 15335424 | tf_op jit(solution)/shard_map/combine_gradients/pallas_call | solution.py:640
  215.4 22.1 %attention_backward.3 = (bf16[384,1664]{1,0:T(8,128)(2,1)}, bf16[384,1664]{1,0:T(8,128)(2,1)}, f32[768,768]{1,0:T(8,128)}, f32[768,768]{1,0:T(8,128)}) custom-call(f32[3]{0:T(128)} %compare_select_fusion.flags_ref, s32[1]{0:T(128)} %bitcast.19.core_ref, ...), custom_call_target="tpu_custom_call", output_to_operand_aliasing={{0}: (15, {}), {1}: (16, {})} | custom-call | flops 6039797760 | bytes 14155776 | tf_op jit(solution)/shard_map/attention_backward/pallas_call | solution.py:263
  237.9 13.8 %attention_backward.4 = (bf16[384,1536]{1,0:T(8,128)(2,1)}, bf16[384,1536]{1,0:T(8,128)(2,1)}, f32[768,768]{1,0:T(8,128)}, f32[768,768]{1,0:T(8,128)}) custom-call(f32[3]{0:T(128)} %compare_select_fusion.flags_ref, s32[1]{0:T(128)} %bitcast.19.core_ref, bf16[768,2304]{1,0:T(8,128)(2,1)} %convolution_convert_fusion.q_ref.k_ref.v_ref, ...), custom_call_target="tpu_custom_call" | custom-call | flops 3019898880 | bytes 11796480 | tf_op jit(solution)/shard_map/attention_backward/pallas_call | solution.py:263
  259.9 32.4 %attention_backward.5 = (bf16[384,1536]{1,0:T(8,128)(2,1)}, bf16[384,1536]{1,0:T(8,128)(2,1)}, f32[768,768]{1,0:T(8,128)}, bf16[256,768]{1,0:T(8,128)(2,1)}, bf1...) custom-call(f32[3]{0:T(128)} %compare_select_fusion.flags_ref, ...), custom_call_target="tpu_custom_call", output_to_operand_aliasing={{0}: (15, {}), {1}: (16, {})} | custom-call | flops 9059696640 | bytes 16515072 | tf_op jit(solution)/shard_map/attention_backward/pallas_call | solution.py:263
  298.0 6.7 %finish_outputs.1 = (bf16[768,768]{1,0:T(8,128)(2,1)}, f32[128,768]{1,0:T(8,128)}) custom-call(bf16[768,640]{1,0:T(8,128)(2,1)} %get-tuple-element.120.refs_0_, bf16[768,512]{1,0:T(8,128)(2,1)} %get-tuple-element.121.refs_1_, bf16[8,144,896]{2,1,0:T(8,128)(2,1)} %copy-done.6, f32[768,768]{1,0:T(8,128)} %get-tuple-element.186.refs_3_, ...), custom_call_target="tpu_custom_call" | custom-call | flops 1585446912 | bytes 9437184 | tf_op jit(solution)/shard_map/finish_outputs/pallas_call | solution.py:682
  313.9 3.5 collective-permute-start.13
  318.0 9.5 %collective-permute-done.10.refs_2_ = bf16[256,768]{1,0:T(8,128)(2,1)} collective-permute-done((bf16[256,768]{1,0:T(8,128)(2,1)}, bf16[256,768]{1,0:T(8,128)(2,1)}, u32[]{:S(2)}, u32[]{:S(2)}) %collective-permute-start.10) | collective-permute-done | bytes 393248 | tf_op jit(solution)/shard_map/ppermute | solution.py:941
  327.5 6.1 %input_gradient.1 = f32[768,768]{1,0:T(8,128)} custom-call(f32[768,768]{1,0:T(8,128)} %get-tuple-element.185.dact_ref, bf16[768,768]{1,0:T(8,128)(2,1)} %bitcast.85, f32[1,768]{1,0:T(1,128)} %broadcast_in_dim.47.gain_ref, f32[768,768]{1,0:T(8,128)} %get-tuple-element.193.dhidden_ref, bf16[256,768]{1,0:T(8,128)(2,1)} %collective-permute-done.8.refs_0_, ...), custom_call_target="tpu_custom_call" | custom-call | flops 7077888 | bytes 9437184 | tf_op jit(solution)/shard_map/input_gradient/pallas_call | solution.py:710
  340.8 3.6 collective-permute-done.14.refs_1_
  349.5 4.8 %collective-permute-start.17 = (bf16[1,24,3200]{2,1,0:T(8,128)(2,1)}, bf16[1,24,3200]{2,1,0:T(8,128)(2,1)S(1)}, u32[]{:S(2)}, u32[]{:S(2)}) collective-permute-start(bf16[1,24,3200]{2,1,0:T(8,128)(2,1)} %sum_pieces.7.refs_0_), channel_id=1, source_target_pairs={{0,2},{1,3},{2,0},{3,1},{4,6},{5,7},{6,4},{7,5},{8,10},{9,11},{10,... | collective-permute-start | bytes 460808 | tf_op jit(solution)/shard_map/ppermute | solution.py:768
  358.5 7.9 %collective-permute-done.18.refs_2_ = bf16[1,24,3200]{2,1,0:T(8,128)(2,1)S(1)} collective-permute-done((bf16[1,24,3200]{2,1,0:T(8,128)(2,1)}, bf16[1,24,3200]{2,1,0:T(8,128)(2,1)S(1)}, u32[]{:S(2)}, u32[]{:S(2)}) %collective-permute-start.18) | collective-permute-done | bytes 153632 | tf_op jit(solution)/shard_map/ppermute | solution.py:768
  379.3 7.4 %collective-permute-done.20.refs_1_ = bf16[4,24,3200]{2,1,0:T(8,128)(2,1)S(1)} collective-permute-done((bf16[4,24,3200]{2,1,0:T(8,128)(2,1)}, bf16[4,24,3200]{2,1,0:T(8,128)(2,1)S(1)}, u32[]{:S(2)}, u32[]{:S(2)}) %collective-permute-start.20) | collective-permute-done | bytes 614432 | tf_op jit(solution)/shard_map/ppermute | solution.py:768
  386.7 6.7 %collective-permute-done.21.refs_2_ = bf16[4,24,3200]{2,1,0:T(8,128)(2,1)S(1)} collective-permute-done((bf16[4,24,3200]{2,1,0:T(8,128)(2,1)}, bf16[4,24,3200]{2,1,0:T(8,128)(2,1)S(1)}, u32[]{:S(2)}, u32[]{:S(2)}) %collective-permute-start.21) | collective-permute-done | bytes 614432 | tf_op jit(solution)/shard_map/ppermute | solution.py:768
  405.6 11.7 %unpack_sums.1 = (f32[768,768]{1,0:T(8,128)}, f32[768,2304]{1,0:T(8,128)}, f32[128,768]{1,0:T(8,128)}) custom-call(s32[3]{0:T(128)} %pad_add_fusion.index_ref, bf16[4,4,24,3200]{3,2,1,0:T(8,128)(2,1)} %bitcast.86, bf16[4,4,24,3200]{3,2,1,0:T(8,128)(2,1)} %bitcast.126, bf16[768,2304]{1,0:T(8,128)(2,1)} %w_ref.3), custom_call_target="tpu_custom_call" | custom-call | bytes 21233664 | tf_op jit(solution)/shard_map/unpack_sums/pallas_call | solution.py:830
  (161 shorter events, 102.2 us)
Async XLA Ops:
  18.6 57.9 %all-to-all-start = ((bf16[8,144,896]{2,1,0:T(8,128)(2,1)}), bf16[8,144,896]{2,1,0:T(8,128)(2,1)}, u32[]{:S(2)}, u32[]{:S(2)}) async-start(bf16[8,144,896]{2,1,0:T(8,128)(2,1)} %get-tuple-element.125), calls=%async_computation | async-start | bytes 4128768 | tf_op jit(solution)/shard_map/all_to_all | solution.py:869
  25.5 13.2 %collective-permute-start.2 = (bf16[256,768]{1,0:T(8,128)(2,1)}, bf16[256,768]{1,0:T(8,128)(2,1)}, u32[]{:S(2)}, u32[]{:S(2)}) collective-permute-start(bf16[256,768]{1,0:T(8,128)(2,1)} %slice_bitcast_fusion), channel_id=1, source_target_pairs={{0,24},{8,16},{16,8},{24,0},{1,25},{9,17},{17,9},{25,1},{2,26},{10... | collective-permute-start | bytes 1179656 | tf_op jit(solution)/shard_map/ppermute | solution.py:877
  28.0 18.7 %collective-permute-start.1 = (bf16[256,768]{1,0:T(8,128)(2,1)}, bf16[256,768]{1,0:T(8,128)(2,1)}, u32[]{:S(2)}, u32[]{:S(2)}) collective-permute-start(bf16[256,768]{1,0:T(8,128)(2,1)} %slice_bitcast_fusion), channel_id=1, source_target_pairs={{0,16},{8,24},{16,0},{24,8},{1,17},{9,25},{17,1},{25,9},{2,18},{10... | collective-permute-start | bytes 1179656 | tf_op jit(solution)/shard_map/ppermute | solution.py:877
  28.5 18.3 %collective-permute-start = (bf16[256,768]{1,0:T(8,128)(2,1)}, bf16[256,768]{1,0:T(8,128)(2,1)}, u32[]{:S(2)}, u32[]{:S(2)}) collective-permute-start(bf16[256,768]{1,0:T(8,128)(2,1)} %slice_bitcast_fusion), channel_id=1, source_target_pairs={{0,8},{8,0},{16,24},{24,16},{1,9},{9,1},{17,25},{25,17},{2,10},{10... | collective-permute-start | bytes 1179656 | tf_op jit(solution)/shard_map/ppermute | solution.py:877
  83.5 26.2 %all-to-all-start.3 = ((bf16[8,64,768]{2,1,0:T(8,128)(2,1)}), bf16[8,64,768]{2,1,0:T(8,128)(2,1)}, u32[]{:S(2)}, u32[]{:S(2)}) async-start(bf16[8,64,768]{2,1,0:T(8,128)(2,1)} %bitcast.136), calls=%async_computation.3 | async-start | bytes 1572864 | tf_op jit(solution)/shard_map/all_to_all | solution.py:869
  109.7 28.7 %all-to-all-start.1 = ((bf16[8,80,768]{2,1,0:T(8,128)(2,1)}), bf16[8,80,768]{2,1,0:T(8,128)(2,1)S(1)}, u32[]{:S(2)}, u32[]{:S(2)}) async-start(bf16[8,80,768]{2,1,0:T(8,128)(2,1)} %bitcast.11), calls=%async_computation.1 | async-start | bytes 1966080 | tf_op jit(solution)/shard_map/all_to_all | solution.py:869
  138.4 24.9 %all-to-all-start.4 = ((bf16[8,64,768]{2,1,0:T(8,128)(2,1)}), bf16[8,64,768]{2,1,0:T(8,128)(2,1)S(1)}, u32[]{:S(2)}, u32[]{:S(2)}) async-start(bf16[8,64,768]{2,1,0:T(8,128)(2,1)} %bitcast.137), calls=%async_computation.4 | async-start | bytes 1572864 | tf_op jit(solution)/shard_map/all_to_all | solution.py:872
  164.3 30.3 %all-to-all-start.2 = ((bf16[8,80,768]{2,1,0:T(8,128)(2,1)}), bf16[8,80,768]{2,1,0:T(8,128)(2,1)S(1)}, u32[]{:S(2)}, u32[]{:S(2)}) async-start(bf16[8,80,768]{2,1,0:T(8,128)(2,1)} %bitcast.132), calls=%async_computation.2 | async-start | bytes 1966080 | tf_op jit(solution)/shard_map/all_to_all | solution.py:872
  169.3 204.2 %reduce-scatter.5.cloned.1.call-start = ((), (), s32[]{:S(2)}) async-start(), calls=%async_computation.9 | async-start | bytes 3932160 | tf_op jit(solution)/shard_map/reduce_scatter | solution.py:918
  195.6 180.3 %reduce-scatter.3.cloned.1.call-start = ((), (), s32[]{:S(2)}) async-start(), calls=%async_computation.8 | async-start | bytes 7864320 | tf_op jit(solution)/shard_map/reduce_scatter | solution.py:917
  199.7 97.0 %all-to-all-start.5 = ((bf16[8,144,896]{2,1,0:T(8,128)(2,1)}), bf16[8,144,896]{2,1,0:T(8,128)(2,1)S(1)}, u32[]{:S(2)}, u32[]{:S(2)}) async-start(bf16[8,144,896]{2,1,0:T(8,128)(2,1)} %pad_maximum_fusion), calls=%async_computation.5 | async-start | bytes 4128768 | tf_op jit(solution)/shard_map/all_to_all | solution.py:872
  237.5 14.1 %collective-permute-start.3 = (bf16[384,1664]{1,0:T(8,128)(2,1)}, bf16[384,1664]{1,0:T(8,128)(2,1)S(1)}, u32[]{:S(2)}, u32[]{:S(2)}) collective-permute-start(bf16[384,1664]{1,0:T(8,128)(2,1)} %get-tuple-element.167), channel_id=1, source_target_pairs={{0,1},{1,0},{2,3},{3,2},{4,5},{5,4},{6,7},{7,6},{8,9},{9,8},{10,11... | collective-permute-start | bytes 3833864 | tf_op jit(solution)/shard_map/ppermute | solution.py:928
  255.5 36.8 %collective-permute-start.4 = (bf16[1,96,1664]{2,1,0:T(8,128)(2,1)}, bf16[1,96,1664]{2,1,0:T(8,128)(2,1)S(1)}, u32[]{:S(2)}, u32[]{:S(2)}) collective-permute-start(bf16[1,96,1664]{2,1,0:T(8,128)(2,1)} %get-tuple-element.182), channel_id=1, source_target_pairs={{0,2},{1,3},{2,0},{3,1},{4,6},{5,7},{6,4},{7,5},{8,10},{9,11},{10,... | collective-permute-start | bytes 958472 | tf_op jit(solution)/shard_map/ppermute | solution.py:768
  257.1 35.1 %collective-permute-start.5 = (bf16[1,96,1664]{2,1,0:T(8,128)(2,1)}, bf16[1,96,1664]{2,1,0:T(8,128)(2,1)S(1)}, u32[]{:S(2)}, u32[]{:S(2)}) collective-permute-start(bf16[1,96,1664]{2,1,0:T(8,128)(2,1)} %get-tuple-element.183), channel_id=1, source_target_pairs={{0,4},{1,5},{2,6},{3,7},{4,0},{5,1},{6,2},{7,3},{8,12},{9,13},{10,... | collective-permute-start | bytes 958472 | tf_op jit(solution)/shard_map/ppermute | solution.py:768
  259.5 32.8 %collective-permute-start.6 = (bf16[1,96,1664]{2,1,0:T(8,128)(2,1)}, bf16[1,96,1664]{2,1,0:T(8,128)(2,1)S(1)}, u32[]{:S(2)}, u32[]{:S(2)}) collective-permute-start(bf16[1,96,1664]{2,1,0:T(8,128)(2,1)} %get-tuple-element.184), channel_id=1, source_target_pairs={{0,6},{1,7},{2,4},{3,5},{4,2},{5,3},{6,0},{7,1},{8,14},{9,15},{10,... | collective-permute-start | bytes 958472 | tf_op jit(solution)/shard_map/ppermute | solution.py:768
  293.2 11.5 %collective-permute-start.7 = (bf16[384,1536]{1,0:T(8,128)(2,1)}, bf16[384,1536]{1,0:T(8,128)(2,1)S(1)}, u32[]{:S(2)}, u32[]{:S(2)}) collective-permute-start(bf16[384,1536]{1,0:T(8,128)(2,1)} %get-tuple-element.191), channel_id=1, source_target_pairs={{0,1},{1,0},{2,3},{3,2},{4,5},{5,4},{6,7},{7,6},{8,9},{9,8},{10,11... | collective-permute-start | bytes 3538952 | tf_op jit(solution)/shard_map/ppermute | solution.py:928
  293.2 20.7 %collective-permute-start.8 = (bf16[256,768]{1,0:T(8,128)(2,1)}, bf16[256,768]{1,0:T(8,128)(2,1)}, u32[]{:S(2)}, u32[]{:S(2)}) collective-permute-start(bf16[256,768]{1,0:T(8,128)(2,1)} %get-tuple-element.194), channel_id=1, source_target_pairs={{0,8},{8,0},{16,24},{24,16},{1,9},{9,1},{17,25},{25,17},{2,10},{10... | collective-permute-start | bytes 1179656 | tf_op jit(solution)/shard_map/ppermute | solution.py:941
  294.7 23.3 %collective-permute-start.9 = (bf16[256,768]{1,0:T(8,128)(2,1)}, bf16[256,768]{1,0:T(8,128)(2,1)}, u32[]{:S(2)}, u32[]{:S(2)}) collective-permute-start(bf16[256,768]{1,0:T(8,128)(2,1)} %get-tuple-element.195), channel_id=1, source_target_pairs={{0,16},{8,24},{16,0},{24,8},{1,17},{9,25},{17,1},{25,9},{2,18},{10... | collective-permute-start | bytes 1179656 | tf_op jit(solution)/shard_map/ppermute | solution.py:941
  295.0 32.5 %collective-permute-start.10 = (bf16[256,768]{1,0:T(8,128)(2,1)}, bf16[256,768]{1,0:T(8,128)(2,1)}, u32[]{:S(2)}, u32[]{:S(2)}) collective-permute-start(bf16[256,768]{1,0:T(8,128)(2,1)} %get-tuple-element.196), channel_id=1, source_target_pairs={{0,24},{8,16},{16,8},{24,0},{1,25},{9,17},{17,9},{25,1},{2,26},{10... | collective-permute-start | bytes 1179656 | tf_op jit(solution)/shard_map/ppermute | solution.py:941
  308.4 25.2 %collective-permute-start.11 = (bf16[1,96,1536]{2,1,0:T(8,128)(2,1)}, bf16[1,96,1536]{2,1,0:T(8,128)(2,1)S(1)}, u32[]{:S(2)}, u32[]{:S(2)}) collective-permute-start(bf16[1,96,1536]{2,1,0:T(8,128)(2,1)} %get-tuple-element.205), channel_id=1, source_target_pairs={{0,2},{1,3},{2,0},{3,1},{4,6},{5,7},{6,4},{7,5},{8,10},{9,11},{10,... | collective-permute-start | bytes 884744 | tf_op jit(solution)/shard_map/ppermute | solution.py:768
  309.1 24.6 %collective-permute-start.12 = (bf16[1,96,1536]{2,1,0:T(8,128)(2,1)}, bf16[1,96,1536]{2,1,0:T(8,128)(2,1)S(1)}, u32[]{:S(2)}, u32[]{:S(2)}) collective-permute-start(bf16[1,96,1536]{2,1,0:T(8,128)(2,1)} %get-tuple-element.206), channel_id=1, source_target_pairs={{0,4},{1,5},{2,6},{3,7},{4,0},{5,1},{6,2},{7,3},{8,12},{9,13},{10,... | collective-permute-start | bytes 884744 | tf_op jit(solution)/shard_map/ppermute | solution.py:768
  313.9 19.8 %collective-permute-start.13 = (bf16[1,96,1536]{2,1,0:T(8,128)(2,1)}, bf16[1,96,1536]{2,1,0:T(8,128)(2,1)S(1)}, u32[]{:S(2)}, u32[]{:S(2)}) collective-permute-start(bf16[1,96,1536]{2,1,0:T(8,128)(2,1)} %get-tuple-element.207), channel_id=1, source_target_pairs={{0,6},{1,7},{2,4},{3,5},{4,2},{5,3},{6,0},{7,1},{8,14},{9,15},{10,... | collective-permute-start | bytes 884744 | tf_op jit(solution)/shard_map/ppermute | solution.py:768
  337.2 7.1 %collective-permute-start.14 = (bf16[1,24,3200]{2,1,0:T(8,128)(2,1)}, bf16[1,24,3200]{2,1,0:T(8,128)(2,1)S(1)}, u32[]{:S(2)}, u32[]{:S(2)}) collective-permute-start(bf16[1,24,3200]{2,1,0:T(8,128)(2,1)} %get-tuple-element.213), channel_id=1, source_target_pairs={{0,8},{8,0},{16,24},{24,16},{1,9},{9,1},{17,25},{25,17},{2,10},{10... | collective-permute-start | bytes 460808 | tf_op jit(solution)/shard_map/ppermute | solution.py:768
  338.3 8.7 %collective-permute-start.15 = (bf16[1,24,3200]{2,1,0:T(8,128)(2,1)}, bf16[1,24,3200]{2,1,0:T(8,128)(2,1)S(1)}, u32[]{:S(2)}, u32[]{:S(2)}) collective-permute-start(bf16[1,24,3200]{2,1,0:T(8,128)(2,1)} %get-tuple-element.214), channel_id=1, source_target_pairs={{0,16},{8,24},{16,0},{24,8},{1,17},{9,25},{17,1},{25,9},{2,18},{10... | collective-permute-start | bytes 460808 | tf_op jit(solution)/shard_map/ppermute | solution.py:768
  338.7 8.3 %collective-permute-start.16 = (bf16[1,24,3200]{2,1,0:T(8,128)(2,1)}, bf16[1,24,3200]{2,1,0:T(8,128)(2,1)S(1)}, u32[]{:S(2)}, u32[]{:S(2)}) collective-permute-start(bf16[1,24,3200]{2,1,0:T(8,128)(2,1)} %get-tuple-element.215), channel_id=1, source_target_pairs={{0,24},{8,16},{16,8},{24,0},{1,25},{9,17},{17,9},{25,1},{2,26},{10... | collective-permute-start | bytes 460808 | tf_op jit(solution)/shard_map/ppermute | solution.py:768
  349.5 9.0 %collective-permute-start.17 = (bf16[1,24,3200]{2,1,0:T(8,128)(2,1)}, bf16[1,24,3200]{2,1,0:T(8,128)(2,1)S(1)}, u32[]{:S(2)}, u32[]{:S(2)}) collective-permute-start(bf16[1,24,3200]{2,1,0:T(8,128)(2,1)} %sum_pieces.7.refs_0_), channel_id=1, source_target_pairs={{0,2},{1,3},{2,0},{3,1},{4,6},{5,7},{6,4},{7,5},{8,10},{9,11},{10,... | collective-permute-start | bytes 460808 | tf_op jit(solution)/shard_map/ppermute | solution.py:768
  354.3 12.0 %collective-permute-start.18 = (bf16[1,24,3200]{2,1,0:T(8,128)(2,1)}, bf16[1,24,3200]{2,1,0:T(8,128)(2,1)S(1)}, u32[]{:S(2)}, u32[]{:S(2)}) collective-permute-start(bf16[1,24,3200]{2,1,0:T(8,128)(2,1)} %sum_pieces.7.refs_0_), channel_id=1, source_target_pairs={{0,4},{1,5},{2,6},{3,7},{4,0},{5,1},{6,2},{7,3},{8,12},{9,13},{10,... | collective-permute-start | bytes 460808 | tf_op jit(solution)/shard_map/ppermute | solution.py:768
  355.2 11.1 %collective-permute-start.19 = (bf16[1,24,3200]{2,1,0:T(8,128)(2,1)}, bf16[1,24,3200]{2,1,0:T(8,128)(2,1)S(1)}, u32[]{:S(2)}, u32[]{:S(2)}) collective-permute-start(bf16[1,24,3200]{2,1,0:T(8,128)(2,1)} %sum_pieces.7.refs_0_), channel_id=1, source_target_pairs={{0,6},{1,7},{2,4},{3,5},{4,2},{5,3},{6,0},{7,1},{8,14},{9,15},{10,... | collective-permute-start | bytes 460808 | tf_op jit(solution)/shard_map/ppermute | solution.py:768
  369.7 17.0 %collective-permute-start.20 = (bf16[4,24,3200]{2,1,0:T(8,128)(2,1)}, bf16[4,24,3200]{2,1,0:T(8,128)(2,1)S(1)}, u32[]{:S(2)}, u32[]{:S(2)}) collective-permute-start(bf16[4,24,3200]{2,1,0:T(8,128)(2,1)} %stack_pieces.2.refs_0_), channel_id=1, source_target_pairs={{0,8},{8,0},{16,24},{24,16},{1,9},{9,1},{17,25},{25,17},{2,10},{10... | collective-permute-start | bytes 1843208 | tf_op jit(solution)/shard_map/ppermute | solution.py:768
  371.7 21.7 %collective-permute-start.21 = (bf16[4,24,3200]{2,1,0:T(8,128)(2,1)}, bf16[4,24,3200]{2,1,0:T(8,128)(2,1)S(1)}, u32[]{:S(2)}, u32[]{:S(2)}) collective-permute-start(bf16[4,24,3200]{2,1,0:T(8,128)(2,1)} %stack_pieces.2.refs_0_), channel_id=1, source_target_pairs={{0,16},{8,24},{16,0},{24,8},{1,17},{9,25},{17,1},{25,9},{2,18},{10... | collective-permute-start | bytes 1843208 | tf_op jit(solution)/shard_map/ppermute | solution.py:768
  372.1 23.2 %collective-permute-start.22 = (bf16[4,24,3200]{2,1,0:T(8,128)(2,1)}, bf16[4,24,3200]{2,1,0:T(8,128)(2,1)S(1)}, u32[]{:S(2)}, u32[]{:S(2)}) collective-permute-start(bf16[4,24,3200]{2,1,0:T(8,128)(2,1)} %stack_pieces.2.refs_0_), channel_id=1, source_target_pairs={{0,24},{8,16},{16,8},{24,0},{1,25},{9,17},{17,9},{25,1},{2,26},{10... | collective-permute-start | bytes 1843208 | tf_op jit(solution)/shard_map/ppermute | solution.py:768
  399.3 4.9 %collective-permute-start.23 = (bf16[16,24,3200]{2,1,0:T(8,128)(2,1)}, bf16[16,24,3200]{2,1,0:T(8,128)(2,1)S(1)}, u32[]{:S(2)}, u32[]{:S(2)}) collective-permute-start(bf16[16,24,3200]{2,1,0:T(8,128)(2,1)} %stack_pieces.3), channel_id=1, source_target_pairs={{0,1},{1,0},{2,3},{3,2},{4,5},{5,4},{6,7},{7,6},{8,9},{9,8},{10,11... | collective-permute-start | bytes 7372808 | tf_op jit(solution)/shard_map/ppermute | solution.py:928
  (35 other events, 157.9 us)
Sparse Core Ops, SparseCore 0:
  195.7 42.0 reduce-scatter.4
  241.3 83.2 reduce-scatter.2

commit v4 on v3

--- a/solution.py
+++ b/solution.py
@@ -30,51 +30,70 @@
     return tiles
 
 
-def attention_forward_kernel(plen, flags_ref, q_ref, k_ref, v_ref, kr_ref, vr_ref, o_ref, lse_ref):
+def split_high(value):
+    high = value.astype(bf16)
+    return high, (value - high.astype(f32)).astype(bf16)
+
+
+def both_halves(value, head, low_half):
+    turned = pltpu.roll(value, HEAD_DIM, 1)
+    return jnp.where(low_half, value, turned) if head == 0 else jnp.where(low_half, turned, value)
+
+
+def scaled_queries(value, head, low_half):
+    high, rest = split_high(value.astype(f32) * (SCALE * LOG2E))
+    rest = pltpu.roll(rest, HEAD_DIM, 1)
+    return jnp.where(low_half, high, rest) if head == 0 else jnp.where(low_half, rest, high)
+
+
+def attention_forward_kernel(plen, flags_ref, q_ref, k_ref, v_ref, kr_ref, vr_ref, o_ref, lse_ref, kd, krd, vd, vrd):
     tok = q_ref.shape[0]
     remote = kr_ref.shape[0]
-    lane = lax.broadcasted_iota(jnp.int32, (1, 128), 1)
-    low_half = lane < HEAD_DIM
-    c = SCALE * LOG2E
+    low_half = lax.broadcasted_iota(jnp.int32, (1, 128), 1) < HEAD_DIM
     one = jnp.ones((), bf16)
-    zero = jnp.zeros((), bf16)
+    for head in range(2):
+        mine = low_half if head == 0 else ~low_half
+        kd[head] = both_halves(k_ref[...], head, low_half)
+        krd[head] = both_halves(kr_ref[...], head, low_half)
+        vd[head] = jnp.where(mine, v_ref[...], one)
+        vrd[head] = jnp.where(mine, vr_ref[...], one)
     for start, size, is_prompt in query_tiles(tok, plen):
-        accs, peaks = [], []
+        row = lax.broadcasted_iota(jnp.int32, (size, size), 0)
+        col = lax.broadcasted_iota(jnp.int32, (size, size), 1)
+        queries = q_ref[start : start + size, :]
+        units = []
         for head in range(2):
-            mine = low_half if head == 0 else ~low_half
-            qh = jnp.where(mine, q_ref[start : start + size, :], zero)
+            qh = scaled_queries(queries, head, low_half)
             pieces = []
-            row = lax.broadcasted_iota(jnp.int32, (size, size), 0)
-            col = lax.broadcasted_iota(jnp.int32, (size, size), 1)
-            diag = dot_nt(qh, k_ref[start : start + size, :])
-            pieces.append((jnp.where(col <= row, diag, NEG), v_ref, start, size))
+            diag = dot_nt(qh, kd[head, start : start + size, :])
+            pieces.append((jnp.where(col <= row, diag, NEG), vd, start, size))
             if is_prompt:
                 for j in range(remote // plen):
-                    s = dot_nt(qh, kr_ref[j * plen : (j + 1) * plen, :])
-                    pieces.append((s + flags_ref[j], vr_ref, j * plen, plen))
+                    s = dot_nt(qh, krd[head, j * plen : (j + 1) * plen, :])
+                    pieces.append((s + flags_ref[j], vrd, j * plen, plen))
             else:
-                s = dot_nt(qh, k_ref[0:start, :])
-                pieces.append((s, v_ref, 0, start))
-                s = dot_nt(qh, kr_ref[...])
-                pieces.append((s, vr_ref, 0, remote))
+                s = dot_nt(qh, kd[head, 0:start, :])
+                pieces.append((s, vd, 0, start))
+                s = dot_nt(qh, krd[head])
+                pieces.append((s, vrd, 0, remote))
+            units.append(pieces)
+        accs, peaks = [], []
+        for head, pieces in enumerate(units):
             peak = None
             for s, _, _, _ in pieces:
                 m = jnp.max(s, axis=1, keepdims=True)
                 peak = m if peak is None else jnp.maximum(peak, m)
-            shift = peak * c
             acc = None
             for s, ref, at, n in pieces:
-                p = jnp.exp2(s * c - shift).astype(bf16)
-                vh = jnp.where(mine, ref[at : at + n, :], one)
-                part = dot_nn(p, vh)
+                p = jnp.exp2(s - peak).astype(bf16)
+                part = dot_nn(p, ref[head, at : at + n, :])
                 acc = part if acc is None else acc + part
             accs.append(acc)
-            peaks.append(shift)
+            peaks.append(peak)
         num = jnp.where(low_half, accs[0], accs[1])
         den = pltpu.roll(jnp.where(low_half, accs[1], accs[0]), HEAD_DIM, 1)
         o_ref[start : start + size, :] = (num / den).astype(bf16)
-        logs = jnp.where(low_half, peaks[0], peaks[1]) + jnp.log2(den)
-        turned = logs.T
+        turned = (jnp.where(low_half, peaks[0], peaks[1]) + jnp.log2(den)).T
         lse_ref[0, 0:8, start : start + size] = turned[0:8, :]
         lse_ref[0, 8:16, start : start + size] = turned[HEAD_DIM : HEAD_DIM + 8, :]
 
@@ -102,6 +121,7 @@
             jax.ShapeDtypeStruct((tok, width), bf16),
             jax.ShapeDtypeStruct((pairs, 16, tok), f32),
         ],
+        scratch_shapes=[pltpu.VMEM((2, n, 128), bf16) for n in (tok, remote, tok, remote)],
         compiler_params=pltpu.CompilerParams(vmem_limit_bytes=60 * 2**20),
         cost_estimate=pl.CostEstimate(flops=4 * tok * (tok + remote) * width, bytes_accessed=2 * (tok * 4 + remote * 2) * width, transcendentals=tok * (tok + remote) * HEADS),
         name="attention_forward",
@@ -113,14 +133,17 @@
     if started:
         start_act_ref, start_far_ref, *refs = refs
     mine_ref, theirs_ref, dact_ref, *refs = refs
-    dfar_ref, *dfar_refs = (refs[-1:] + refs[:-9]) if last else refs[:1]
-    kt, krt, dka, dva, dkra, dvra, own_grads, weights = refs[-9:-1] if last else refs[-8:]
+    dfar_ref, *dfar_refs = (refs[-1:] + refs[:-11]) if last else refs[:1]
+    kt, krt, dka, dva, dkra, dvra, own_grads, weights, kd, krd = refs[-11:-1] if last else refs[-10:]
     tok = q_ref.shape[0]
     remote = kr_ref.shape[0]
     lane = lax.broadcasted_iota(jnp.int32, (1, 128), 1)
     low_half = lane < HEAD_DIM
     c = SCALE * LOG2E
     zero = jnp.zeros((), bf16)
+    for head in range(2):
+        kd[head] = both_halves(k_ref[...], head, low_half)
+        krd[head] = both_halves(kr_ref[...], head, low_half)
     kt[...] = k_ref[...].T
     krt[...] = kr_ref[...].T
     dka[...] = jnp.zeros_like(dka)
@@ -135,24 +158,25 @@
         high = product.astype(bf16)
         rest = (product - high.astype(f32)).astype(bf16)
         delta = dot_nt(pick, high) + dot_nt(pick, rest)
-        dqt = []
-        for head in range(2):
-            mine = low_half if head == 0 else ~low_half
-            qh = jnp.where(mine, q_ref[rows, :], zero)
-            doh = jnp.where(mine, do_ref[rows, :], zero)
-            lse_row = lse_ref[0, 8 * head : 8 * head + 1, rows]
-            delta_row = delta[8 * head : 8 * head + 1, :]
-            segments = [(k_ref, v_ref, kt, dka, dva, start, size, "diag")]
-            if is_prompt:
-                for j in range(remote // plen):
-                    segments.append((kr_ref, vr_ref, krt, dkra, dvra, j * plen, plen, j))
-            else:
-                segments.append((k_ref, v_ref, kt, dka, dva, 0, start, None))
-                segments.append((kr_ref, vr_ref, krt, dkra, dvra, 0, remote, None))
-            total = None
-            for kk, vv, tt, dk_acc, dv_acc, at, n, mode in segments:
-                keys = slice(at, at + n)
-                st = dot_nt(kk[keys, :], qh) * c - lse_row
+        totals = [None, None]
+        masks = [low_half, ~low_half]
+        qh = [jnp.where(m, q_ref[rows, :], zero) for m in masks]
+        qs = [scaled_queries(q_ref[rows, :], head, low_half) for head in range(2)]
+        doh = [jnp.where(m, do_ref[rows, :], zero) for m in masks]
+        segments = [(kd, v_ref, kt, dka, dva, start, size, "diag")]
+        if is_prompt:
+            for j in range(remote // plen):
+                segments.append((krd, vr_ref, krt, dkra, dvra, j * plen, plen, j))
+        else:
+            segments.append((kd, v_ref, kt, dka, dva, 0, start, None))
+            segments.append((krd, vr_ref, krt, dkra, dvra, 0, remote, None))
+        for kk, vv, tt, dk_acc, dv_acc, at, n, mode in segments:
+            keys = slice(at, at + n)
+            scores = [dot_nt(kk[head, keys, :], qs[head]) for head in range(2)]
+            d_probs = [dot_nt(vv[keys, :], doh[head]) for head in range(2)]
+            low_p, low_d = [], []
+            for head in range(2):
+                st = scores[head] - lse_ref[0, 8 * head : 8 * head + 1, rows]
                 if mode == "diag":
                     key = lax.broadcasted_iota(jnp.int32, (n, size), 0)
                     query = lax.broadcasted_iota(jnp.int32, (n, size), 1)
@@ -160,13 +184,14 @@
                 elif mode is not None:
                     st = st + flags_ref[mode]
                 pt = jnp.exp2(st)
-                dpt = dot_nt(vv[keys, :], doh)
-                dst = (pt * (dpt - delta_row)).astype(bf16)
-                dv_acc[keys, :] += dot_nn(pt.astype(bf16), doh)
-                dk_acc[keys, :] += dot_nn(dst, qh)
-                part = dot_nn(tt[head * HEAD_DIM : (head + 1) * HEAD_DIM, keys], dst)
-                total = part if total is None else total + part
-            dqt.append(total)
+                low_p.append(pt.astype(bf16))
+                low_d.append((pt * (d_probs[head] - delta[8 * head : 8 * head + 1, :])).astype(bf16))
+            dv_acc[keys, :] += dot_nn(low_p[0], doh[0]) + dot_nn(low_p[1], doh[1])
+            dk_acc[keys, :] += dot_nn(low_d[0], qh[0]) + dot_nn(low_d[1], qh[1])
+            for head in range(2):
+                part = dot_nn(tt[head * HEAD_DIM : (head + 1) * HEAD_DIM, keys], low_d[head])
+                totals[head] = part if totals[head] is None else totals[head] + part
+        dqt = totals
         own_grads[rows, 0:128] = (jnp.concatenate(dqt, axis=0).T * SCALE).astype(bf16)
     own_grads[:, 128:256] = (dka[...] * SCALE).astype(bf16)
     own_grads[:, 256:384] = dva[...].astype(bf16)
@@ -238,6 +263,8 @@
         pltpu.VMEM((remote, 128), f32),
         pltpu.VMEM((tok, 384), bf16),
         pltpu.VMEM((width, 384), bf16),
+        pltpu.VMEM((2, tok, 128), bf16),
+        pltpu.VMEM((2, remote, 128), bf16),
     ]
     sums = [jax.ShapeDtypeStruct((tok, width), f32), jax.ShapeDtypeStruct((remote, width), f32)]
     aliases = {}
@@ -299,20 +326,21 @@
     count = len(groups)
     turned_refs, chosen_refs, early_ref = out_refs[:count], out_refs[count : 2 * count], out_refs[2 * count]
     expert = lax.broadcasted_iota(jnp.int32, (16, tok), 0)
-    names = [ids_ref[k : k + 1, :] == expert for k in range(2)]
+    ids = jnp.concatenate([ids_ref[...].astype(f32), jnp.zeros((tok, EXTRA - 2), f32)], axis=1).T.astype(jnp.int32)
+    ids = [ids[k : k + 1, :] for k in range(2)]
+    names = [row == expert for row in ids]
     both = jnp.where(names[0] | names[1], 1.0, 0.0).astype(bf16)
     earlier = lax.broadcasted_iota(jnp.int32, (tok, tok), 0) < lax.broadcasted_iota(jnp.int32, (tok, tok), 1)
     before = dot_nn(both, jnp.where(earlier, 1.0, 0.0).astype(bf16))
-    pieces = [piece.astype(f32) for piece in split_low(prev_ref[...], 3)]
+    pieces = [piece.astype(f32) for piece in split_low(jnp.concatenate([prev_ref[...], jnp.zeros((tok, EXTRA - ALL_EXPERTS), f32)], axis=1), 3)]
     extra = (pieces[0] + pltpu.roll(pieces[1], 16, 1) + pltpu.roll(pieces[2], 32, 1)).astype(bf16)
     slot = [jnp.sum(jnp.where(n, before, 0.0), axis=0, keepdims=True).astype(jnp.int32) for n in names]
     for (first, size), turned_ref, chosen_ref in zip(groups, turned_refs, chosen_refs):
         spots = lax.broadcasted_iota(jnp.int32, (FFN_EXPERTS * size, tok), 0)
         hit = None
         for k in range(2):
-            ids = ids_ref[k : k + 1, :]
-            inside = (ids < FFN_EXPERTS) & (slot[k] >= first) & (slot[k] < first + size)
-            place = jnp.where(inside, ids * size + slot[k] - first, -1)
+            inside = (ids[k] < FFN_EXPERTS) & (slot[k] >= first) & (slot[k] < first + size)
+            place = jnp.where(inside, ids[k] * size + slot[k] - first, -1)
             hit = spots == place if hit is None else hit | (spots == place)
         turned = jnp.where(hit, 1.0, 0.0).astype(bf16)
         turned_ref[...] = turned
@@ -476,29 +504,66 @@
 
 
 def after_attention_kernel(count, mixed_ref, x_ref, w_ref, gain_ref, *refs):
-    turned, (hidden_ref, low_ref), sent = refs[:count], refs[count : count + 2], refs[count + 2 :]
+    turned, (hidden_ref, low_ref), sent = refs[:count], refs[count : count + 2], refs[count + 2 : 2 * count + 2]
+    kept, local, sems = refs[2 * count + 2], refs[2 * count + 3 : 3 * count + 3], refs[-1]
+    step = pl.program_id(0)
+    copies = [pltpu.make_async_copy(t, s, sems.at[g]) for g, (t, s) in enumerate(zip(turned, local))]
+
+    @pl.when(step == 0)
+    def _():
+        for copy in copies:
+            copy.start()
+
     hidden = x_ref[...].astype(f32) + dot_nn(mixed_ref[...], w_ref[...])
     low = (hidden * inverse_rms(hidden) * gain_ref[...]).astype(bf16)
     hidden_ref[...] = hidden
     low_ref[...] = low
-    for t, s in zip(turned, sent):
-        s[...] = dot_nn(t[...], low).astype(bf16)
+    block = low.shape[0]
+    kept[pl.ds(pl.multiple_of(step * block, block), block), :] = low
+
+    @pl.when(step == pl.num_programs(0) - 1)
+    def _():
+        for copy, t, s in zip(copies, local, sent):
+            copy.wait()
+            s[...] = dot_nn(t[...], kept[...]).astype(bf16)
 
 
 def after_attention(mixed, x, w_out, gain, turned):
     tok, width = x.shape
     rows = sum(t.shape[0] for t in turned)
+    block, tiles = row_tiles(tok)
     out = pl.pallas_call(
         functools.partial(after_attention_kernel, len(turned)),
-        in_specs=[ANYWHERE] * (4 + len(turned)),
-        out_specs=[ANYWHERE] * (2 + len(turned)),
+        grid=(tok // block,),
+        in_specs=[tiles(width), tiles(width), fixed(w_out), fixed(gain)] + [pl.BlockSpec(memory_space=pl.ANY)] * len(turned),
+        out_specs=[tiles(width)] * 2 + [pl.BlockSpec((t.shape[0], width), lambda i: (0, 0)) for t in turned],
         out_shape=[jax.ShapeDtypeStruct((tok, width), f32), jax.ShapeDtypeStruct((tok, width), bf16)]
         + [jax.ShapeDtypeStruct((t.shape[0], width), bf16) for t in turned],
+        scratch_shapes=[pltpu.VMEM((tok, width), bf16)] + [pltpu.VMEM(t.shape, bf16) for t in turned] + [pltpu.SemaphoreType.DMA((len(turned),))],
         compiler_params=pltpu.CompilerParams(vmem_limit_bytes=60 * 2**20),
         cost_estimate=pl.CostEstimate(flops=2 * tok * width * (width + rows), bytes_accessed=2 * width * (6 * tok + 2 * rows), transcendentals=0),
         name="after_attention",
     )(mixed, x, w_out, gain, *turned)
     return out[0], out[1], out[2:]
+
+
+def turn_kernel(in_ref, out_ref):
+    out_ref[...] = in_ref[...].T
+
+
+def turn(value):
+    rows, columns = value.shape
+    block = 256 if rows % 256 == 0 else 128
+    return pl.pallas_call(
+        turn_kernel,
+        grid=(rows // block,),
+        in_specs=[pl.BlockSpec((block, columns), lambda i: (i, 0))],
+        out_specs=pl.BlockSpec((columns, block), lambda i: (0, i)),
+        out_shape=jax.ShapeDtypeStruct((columns, rows), value.dtype),
+        compiler_params=pltpu.CompilerParams(vmem_limit_bytes=60 * 2**20),
+        cost_estimate=pl.CostEstimate(flops=0, bytes_accessed=4 * rows * columns, transcendentals=0),
+        name="turn",
+    )(value)
 
 
 def place(value, lane, at):
@@ -512,7 +577,8 @@
     low = low_ref[...]
     grad = grad_ref[...].astype(f32)
     raw = dot_nn(low, mix_ref[...])
-    logits = jnp.where(lane < ALL_EXPERTS, raw + prev_ref[...], NEG)
+    prev = jnp.concatenate([prev_ref[...], jnp.zeros((raw.shape[0], EXTRA - ALL_EXPERTS), f32)], axis=1)
+    logits = jnp.where(lane < ALL_EXPERTS, raw + prev, NEG)
     unnormed = jnp.exp(logits - jnp.max(logits, axis=1, keepdims=True))
     probs = unnormed / jnp.sum(unnormed, axis=1, keepdims=True)
     named = (ids_ref[:, 0:1] == lane) | (ids_ref[:, 1:2] == lane)
@@ -569,7 +635,7 @@
     return pl.pallas_call(
         local_kernel,
         grid=(tok // block,),
-        in_specs=[tiles(width), tiles(width), tiles(width), tiles(EXTRA), tiles(2), fixed(mix), fixed(gain), fixed(vec)],
+        in_specs=[tiles(width), tiles(width), tiles(width), tiles(ALL_EXPERTS), tiles(2), fixed(mix), fixed(gain), fixed(vec)],
         out_specs=[tiles(width), tiles(width), tiles(EXTRA), tiles(EXTRA), pl.BlockSpec((3 * SMALL, width), lambda i: (0, 0))],
         out_shape=[jax.ShapeDtypeStruct(s, f32) for s in shapes],
         compiler_params=pltpu.CompilerParams(vmem_limit_bytes=60 * 2**20),
@@ -635,7 +701,7 @@
     tok, width = hidden.shape
     rows = sum(c.shape[1] for c in chosen)
     arrays = [a for group in got for a in group]
-    block, tiles = row_tiles(tok)
+    block, tiles = 128, lambda columns: pl.BlockSpec((128, columns), lambda i: (i, 0))
     half = (width // 2, columns + width + EXTRA)
     return pl.pallas_call(
         functools.partial(combine_kernel, len(chosen), len(got[0])),
@@ -792,7 +858,7 @@
     )(*pieces)
 
 
-def unpack_kernel(left, index_ref, own_ref, other_ref, w_ref, out_ref, qkv_ref, turned_ref, small):
+def unpack_kernel(left, index_ref, own_ref, other_ref, w_ref, scale_ref, out_ref, qkv_ref, router_ref, mixing_ref, vec_ref, gain_ref, attn_ref, small):
     width = out_ref.shape[1]
     piece = own_ref.shape[2]
     mine = pl.program_id(0) == index_ref[0]
@@ -817,30 +883,44 @@
 
     @pl.when(block == 7)
     def _():
-        turned_ref[...] = small[...].T
-
-
-def unpack(index, own, other, w_qkv, left):
+        turned = small[...].T
+        router_ref[...] = turned[0:ALL_EXPERTS]
+        mixing_ref[...] = turned[16:20]
+        vec_ref[...] = turned[20:22]
+        gain_ref[...] = turned[24:25]
+        attn_ref[...] = turned[EXTRA - 1 : EXTRA] / scale_ref[...]
+
+
+def unpack(index, own, other, w_qkv, scale, left):
     width = w_qkv.shape[0]
     piece = width // 32
     block = 4 * piece
     own, other = own.reshape(4, 4, piece, -1), other.reshape(4, 4, piece, -1)
     row = lambda c, a, s: (c * 4 + a, 0)
-    source = pl.BlockSpec((4, 1, piece, own.shape[3]), lambda c, a, s: (0, a ^ s[2], 0, 0))
+
+    def source(core_of):
+        def at(c, a, s):
+            core = core_of(s[0])
+            return 0, jnp.where(c == core, a, jnp.where(c < core, 0, 3)) ^ s[2], 0, 0
+
+        return pl.BlockSpec((4, 1, piece, own.shape[3]), at)
+
+    whole = lambda n: pl.BlockSpec((n, width), lambda c, a, s: (0, 0))
+    counts = (ALL_EXPERTS, 4, 2, 1, 1)
     return pl.pallas_call(
         functools.partial(unpack_kernel, left),
         grid_spec=pltpu.PrefetchScalarGridSpec(
             num_scalar_prefetch=1,
             grid=(2, 4),
-            in_specs=[source, source, pl.BlockSpec((block, 3 * width), row)],
-            out_specs=[pl.BlockSpec((block, width), row), pl.BlockSpec((block, 3 * width), row), pl.BlockSpec((EXTRA, width), lambda c, a, s: (0, 0))],
+            in_specs=[source(lambda core: core), source(lambda core: 1 - core), pl.BlockSpec((block, 3 * width), row), whole(1)],
+            out_specs=[pl.BlockSpec((block, width), row), pl.BlockSpec((block, 3 * width), row), *[whole(n) for n in counts]],
             scratch_shapes=[pltpu.VMEM((width, EXTRA), f32)],
         ),
-        out_shape=[jax.ShapeDtypeStruct((width, width), f32), jax.ShapeDtypeStruct((width, 3 * width), f32), jax.ShapeDtypeStruct((EXTRA, width), f32)],
+        out_shape=[jax.ShapeDtypeStruct((width, width), f32), jax.ShapeDtypeStruct((width, 3 * width), f32), *[jax.ShapeDtypeStruct((n, width), f32) for n in counts]],
         compiler_params=pltpu.CompilerParams(vmem_limit_bytes=60 * 2**20),
         cost_estimate=pl.CostEstimate(flops=0, bytes_accessed=36 * width * width, transcendentals=0),
         name="unpack_sums",
-    )(index, own, other, w_qkv)
+    )(index, own, other, w_qkv, scale)
 
 P = jax.sharding.PartitionSpec
 
@@ -873,14 +953,14 @@
         return [value[r::split] if split > 1 else value for r in range(split)]
 
     x_low = inputs[0]
-    x_prompt, upstream_low = lax.optimization_barrier((x_low[:plen], out_grad[0]))
-    far_rows = jnp.concatenate([lax.ppermute(x_prompt, "ctx", xor_pairs(n_ctx, k)) for k in range(1, n_ctx)], axis=0)
+    upstream_low = out_grad[0]
+    far_rows = jnp.concatenate([lax.ppermute(x_low[:plen], "ctx", xor_pairs(n_ctx, k)) for k in range(1, n_ctx)], axis=0)
     flags = jnp.where((me_c ^ jnp.arange(1, n_ctx)) < me_c, 0.0, NEG).astype(f32)
 
-    prev = jnp.pad(prev_logits[0], ((0, 0), (0, EXTRA - ALL_EXPERTS)))
+    prev = prev_logits[0]
     mix = jnp.concatenate([router, jnp.zeros((width, 4), bf16), const_gate[0], const_gate[1], jnp.zeros((width, EXTRA - 20), bf16)], axis=1)
     router_pad = jnp.pad(router, ((0, 0), (0, EXTRA - ALL_EXPERTS)))
-    turned, chosen, early_sent = route_plan(home, routes[0].T, upstream_low, prev, groups)
+    turned, chosen, early_sent = route_plan(home, routes[0], upstream_low, prev, groups)
 
     tokens_in = x_low.astype(f32)
     inverse_attn = rms_inverse(tokens_in)
@@ -895,7 +975,7 @@
     mixed_low, early = lax.optimization_barrier((mixed_low, early))
     hidden, moe_low, sent = after_attention(mixed_low, x_low, w_out, moe_gain[None], turned)
     local_out, d_normed_local, probs, d_probs, small_local = local_part(hidden, moe_low, upstream_low, prev, routes[0], mix, moe_gain[None], const_vec)
-    act_t, far_t = act_low.T, act_far.T
+    act_t, far_t = turn(act_low), turn(act_far)
     sent = [after(sent[0], local_out, d_normed_local, act_t, far_t), sent[1]]
     got = [deal(part.reshape(FFN_EXPERTS, -1, width)) for part in sent]
 
@@ -940,11 +1020,10 @@
         mine_2, theirs_2, d_act, d_far, parts_1 = lax.optimization_barrier((mine_2, theirs_2, d_act, d_far, parts_1))
     far_back = [lax.ppermute(d_far[k - 1], "ctx", xor_pairs(n_ctx, k)) for k in range(1, n_ctx)]
     if dense:
-        got_2 = across(theirs_2)
-        mixed_out, d_logits = finish(chosen, out_got, groups, after(local_out, d_act), probs, d_probs)
-        mixed_out, d_logits, got_2 = lax.optimization_barrier((mixed_out, d_logits, got_2))
-        sums_2 = sum_pieces(at_z, [[quarters(mine_2), quarters(got_2)]])
+        sums_2 = sum_pieces(at_z, [[quarters(mine_2), quarters(across(theirs_2))]])
         parts_2 = swap(sums_2, along_z)
+        mixed_out, d_logits = finish(chosen, out_got, groups, after(local_out, sums_2[0]), probs, d_probs)
+        mixed_out, d_logits, far_back = lax.optimization_barrier((mixed_out, d_logits, far_back))
     else:
         mixed_out, d_logits = finish(chosen, out_got, groups, local_out, probs, d_probs)
     d_inputs = input_gradient(d_act, x_low, attn_gain[None], d_hidden, far_back)
@@ -957,29 +1036,28 @@
         column = stack_pieces(spread(piece, along_z))
         own = stack_pieces(after(spread(column, along_ctx), total_gate, total_up, total_down))
         other = across(own)
-        out_sum, qkv_sum, small = unpack(jnp.stack([core[0], me_c, z]), own, other, w_qkv, left)
-        d_attn_gain = small[EXTRA - 1]
+        out_sum, qkv_sum, d_router, d_mixing, d_const_vec, d_moe_gain, d_attn_gain = unpack(
+            jnp.stack([core[0], me_c, z]), own, other, w_qkv, attn_gain[None], left
+        )
     else:
         whole = lambda mine, theirs: jnp.where(core == 0, jnp.concatenate([mine, theirs], axis=0), jnp.concatenate([theirs, mine], axis=0))
         total_1, total_2 = [v.astype(f32) for v in lax.psum((whole(mine_1, theirs_1), whole(mine_2, theirs_2)), ("ctx", "exp"))]
         columns = jnp.concatenate([total_1[:, :left], total_2], axis=1).reshape(width, pairs, 3, 128)
         qkv_sum = columns.transpose(0, 2, 1, 3).reshape(width, 3 * width)
         out_sum, small = total_1[:, left : left + width], total_1[:, left + width :].T
-        d_attn_gain = jnp.sum(qkv_sum * w_qkv.astype(f32), axis=1)
-    d_attn_gain = d_attn_gain / attn_gain
-    at = 2 * SMALL
-    d_const_gate = jnp.stack([small[at : at + 2].T, small[at + 2 : at + 4].T])
+        d_attn_gain = (jnp.sum(qkv_sum * w_qkv.astype(f32), axis=1) / attn_gain)[None]
+        d_router, d_mixing, d_const_vec, d_moe_gain = small[:ALL_EXPERTS], small[16:20], small[20:22], small[24:25]
     return (
         mixed_out[None],
         d_inputs[None],
         d_logits[:ALL_EXPERTS].T[None],
-        d_attn_gain,
+        d_attn_gain[0],
         qkv_sum,
         out_sum,
-        small[at + SMALL],
-        small[:ALL_EXPERTS].T,
-        d_const_gate,
-        small[at + 4 : at + 6],
+        d_moe_gain[0],
+        d_router.T,
+        d_mixing.reshape(2, 2, width).transpose(0, 2, 1),
+        d_const_vec,
         total_gate,
         total_up,
         total_down,

time: 438 us -> 426 us (0.973)
  local copies, waits for them, and re-layouts: 33.5 us -> 25.8 us
    pallas_call x1 -> x3, Pallas kernels: 6.9 us -> 15.1 us  [the longest x1 8.25 us: after_attention(): pl.pallas_call(functools.partial(after_attention_kernel, len(turned)), gr...]
    transpose x4 -> x0, local copies, waits for them, and re-layouts: 5.08 us -> none  [the longest x2 2.9 us: body(): act_t, far_t = (act_low.T, act_far.T)]
    pallas_call x1, Pallas kernels: 24 us -> 19 us  [attention_forward(): pl.pallas_call(functools.partial(attention_forward_kernel, plen), grid=(p...]
    unnamed x76 -> x68, local copies, waits for them, and re-layouts: 15.8 us -> 15.2 us
  transfers between devices with their start and end apart: 32 -> 32, of which waited for: 16 -> 15; matrix products, arithmetic and copies ran while one was open for 7% -> 7% of each run, Pallas kernels for 46% -> 48%
where the time goes in v4:
time: 426 us; the launch traced here: 419 us
  Pallas kernels  227 us (53%)
  waiting for transfers between devices  69 us (16%)
  starting transfers between devices  60.5 us (14%)
  local copies, waits for them, and re-layouts  25.8 us (6%)
  between operations  14.7 us (3%)
  other arithmetic  13.8 us (3%)
  matrix products  7.74 us (2%)
    pallas_call x3, Pallas kernels, attention_backward(): pl.pallas_call(functools.partial(attention_backward_kernel, plen, bool(st...  64.5 us
    pallas_call x2, Pallas kernels, expert_pass(): pl.pallas_call(functools.partial(expert_kernel, group), grid=(ff // tile,...  38.7 us
    ppermute x15, waiting for transfers between devices, swap(): lax.ppermute(pieces[k], axis, xor_pairs(size, unit * k))  31.4 us
    ppermute x15, starting transfers between devices, swap(): lax.ppermute(pieces[k], axis, xor_pairs(size, unit * k))  22.9 us
    pallas_call x1, Pallas kernels, attention_forward(): pl.pallas_call(functools.partial(attention_forward_kernel, plen), grid=(p...  19 us
    pallas_call x1, Pallas kernels, weight_gradients(): pl.pallas_call(functools.partial(weight_kernel, count), grid=(ff // tile,...  17.9 us
    all_to_all x3, starting transfers between devices, deal(): return lax.all_to_all(value, 'exp', 0, 0, tiled=True)  17.2 us
    unnamed x68, local copies, waits for them, and re-layouts  15.2 us
  transfers between devices with their start and end apart: 32, of which 15 were waited for; matrix products, arithmetic and copies ran while one was open for 7% of the time, Pallas kernels for 48%

profile of v4, /device:TPU:0, one launch (start us, length us, event | category | flops | bytes accessed | tf_op | source)
XLA Modules:
  0.0 418.5 jit_solution(7725804663364935470)
XLA Ops:
  10.5 6.4 %route_plan.1 = (bf16[640,768]{1,0:T(8,128)(2,1)}, bf16[512,768]{1,0:T(8,128)(2,1)}, bf16[768,640]{1,0:T(8,128)(2,1)}, bf16[768,512]{1,0:T(8,128)(2,1)}, bf16[8,144,896]{2,1,0:T(8,128)(2,1)}) custom-call(s32[1]{0:T(128)} %bitcast.home_ref, s32[768,2]{1,0:T(8,128)} %bitcast.110, bf16[768,768]{1,0:T(8,128)(2,1)} %bitcast.103, f32[768,12]{1,0:T(8,128)} %bitcast.112), custom_call_target="tpu_custom_call" | custom-call | flops 1585446912 | bytes 3538944 | tf_op jit(solution)/shard_map/route_plan/pallas_call | solution.py:359
  17.0 7.1 %all-to-all-start = ((bf16[8,144,896]{2,1,0:T(8,128)(2,1)}), bf16[8,144,896]{2,1,0:T(8,128)(2,1)}, u32[]{:S(2)}, u32[]{:S(2)}) async-start(bf16[8,144,896]{2,1,0:T(8,128)(2,1)} %get-tuple-element.127), calls=%async_computation | async-start | bytes 4128768 | tf_op jit(solution)/shard_map/all_to_all | solution.py:949
  33.8 4.3 %convolution_convert_fusion.q_ref.k_ref.v_ref = bf16[768,2304]{1,0:T(8,128)(2,1)} fusion(bf16[768,768]{1,0:T(8,128)(2,1)S(1)} %fusion.2.in_ref, bf16[768,2304]{1,0:T(8,128)(2,1)S(1)} %copy-done), kind=kOutput, calls=%fused_computation | convolution fusion | flops 2719678464 | bytes 8257536 | tf_op jit(solution)/shard_map/dot_general | solution.py:22
  39.2 8.0 %collective-permute-done.1 = bf16[256,768]{1,0:T(8,128)(2,1)} collective-permute-done((bf16[256,768]{1,0:T(8,128)(2,1)}, bf16[256,768]{1,0:T(8,128)(2,1)}, u32[]{:S(2)}, u32[]{:S(2)}) %collective-permute-start.1) | collective-permute-done | bytes 393248 | tf_op jit(solution)/shard_map/ppermute | solution.py:957
  53.7 19.0 %attention_forward.1 = (bf16[768,768]{1,0:T(8,128)(2,1)}, f32[6,16,768]{2,1,0:T(8,128)}) custom-call(f32[3]{0:T(128)} %compare_select_fusion.flags_ref, bf16[768,2304]{1,0:T(8,128)(2,1)} %convolution_convert_fusion.q_ref.k_ref.v_ref, bf16[768,2304]{1,0:T(8,128)(2,1)} %convolution_convert_fusion.q_ref.k_ref.v_ref, ...), custom_call_target="tpu_custom_call" | custom-call | flops 3623878656 | bytes 7077888 | tf_op jit(solution)/shard_map/attention_forward/pallas_call | solution.py:105
  72.7 8.2 %after_attention.1 = (f32[768,768]{1,0:T(8,128)}, bf16[768,768]{1,0:T(8,128)(2,1)}, bf16[640,768]{1,0:T(8,128)(2,1)}, bf16[512,768]{1,0:T(8,128)(2,1)}) custom-call(bf16[768,768]{1,0:T(8,128)(2,1)} %get-tuple-element.128.mixed_ref.refs_11_.o_ref, bf16[768,768]{1,0:T(8,128)(2,1)} %bitcast.68, bf16[768,768]{1,0:T(8,128)(2,1)} %refs_12_.1, ...), custom_call_target="tpu_custom_call" | custom-call | flops 2264924160 | bytes 10616832 | tf_op jit(solution)/shard_map/after_attention/pallas_call | solution.py:535
  81.0 4.9 %all-to-all-start.3 = ((bf16[8,64,768]{2,1,0:T(8,128)(2,1)}), bf16[8,64,768]{2,1,0:T(8,128)(2,1)S(1)}, u32[]{:S(2)}, u32[]{:S(2)}) async-start(bf16[8,64,768]{2,1,0:T(8,128)(2,1)} %bitcast.123), calls=%async_computation.3 | async-start | bytes 1572864 | tf_op jit(solution)/shard_map/all_to_all | solution.py:949
  85.9 3.5 turn.2.act_ref
  94.6 13.8 %local_part.1 = (f32[768,768]{1,0:T(8,128)}, f32[768,768]{1,0:T(8,128)}, f32[768,128]{1,0:T(8,128)}, f32[768,128]{1,0:T(8,128)}, f32[24,768]{1,0:T(8,128)}) custom-call(f32[768,768]{1,0:T(8,128)} %get-tuple-element.132.hidden_ref.refs_8_, bf16[768,768]{1,0:T(8,128)(2,1)} %get-tuple-element.133.low_ref, bf16[768,768]{1,0:T(8,128)(2,1)} %bitcast.104, ...), custom_call_target="tpu_custom_call" | custom-call | flops 1056964608 | bytes 9437184 | tf_op jit(solution)/shard_map/local_part/pallas_call | solution.py:635
  108.4 5.1 %all-to-all-start.1 = ((bf16[8,80,768]{2,1,0:T(8,128)(2,1)}), bf16[8,80,768]{2,1,0:T(8,128)(2,1)S(1)}, u32[]{:S(2)}, u32[]{:S(2)}) async-start(bf16[8,80,768]{2,1,0:T(8,128)(2,1)} %bitcast.8), calls=%async_computation.1 | async-start | bytes 1966080 | tf_op jit(solution)/shard_map/all_to_all | solution.py:949
  114.2 17.7 %expert_pass.3 = (bf16[512,896]{1,0:T(8,128)(2,1)}, bf16[512,768]{1,0:T(8,128)(2,1)}, bf16[512,768]{1,0:T(8,128)(2,1)}, bf16[512,2048]{1,0:T(8,128)(2,1)}, bf16[...) custom-call(s32[1]{0:T(128)} %bitcast.home_ref, bf16[512,768]{1,0:T(8,128)(2,1)} %bitcast.121, ...), custom_call_target="tpu_custom_call" | custom-call | flops 9663676416 | bytes 19660800 | tf_op jit(solution)/shard_map/expert_pass/pallas_call | solution.py:436
  132.0 6.7 %all-to-all-done.1 = bf16[8,80,768]{2,1,0:T(8,128)(2,1)S(1)} async-done(((bf16[8,80,768]{2,1,0:T(8,128)(2,1)}), bf16[8,80,768]{2,1,0:T(8,128)(2,1)S(1)}, u32[]{:S(2)}, u32[]{:S(2)}) %all-to-all-start.1) | async-done | bytes 983072 | tf_op jit(solution)/shard_map/all_to_all | solution.py:949
  138.7 3.8 all-to-all-start.4
  142.5 21.0 %expert_pass.2 = (bf16[640,896]{1,0:T(8,128)(2,1)}, bf16[640,768]{1,0:T(8,128)(2,1)}, bf16[640,768]{1,0:T(8,128)(2,1)}, bf16[640,2048]{1,0:T(8,128)(2,1)}, bf16[...) custom-call(s32[1]{0:T(128)} %bitcast.home_ref, bf16[640,768]{1,0:T(8,128)(2,1)} %bitcast.115, ...), custom_call_target="tpu_custom_call" | custom-call | flops 12079595520 | bytes 22216704 | tf_op jit(solution)/shard_map/expert_pass/pallas_call | solution.py:436
  163.4 5.2 %all-to-all-start.2 = ((bf16[8,80,768]{2,1,0:T(8,128)(2,1)}), bf16[8,80,768]{2,1,0:T(8,128)(2,1)S(1)}, u32[]{:S(2)}, u32[]{:S(2)}) async-start(bf16[8,80,768]{2,1,0:T(8,128)(2,1)} %bitcast.117), calls=%async_computation.2 | async-start | bytes 1966080 | tf_op jit(solution)/shard_map/all_to_all | solution.py:952
  171.4 17.9 %weight_gradients.1 = (bf16[2,768,2048]{2,1,0:T(8,128)(2,1)}, bf16[2048,768]{1,0:T(8,128)(2,1)}) custom-call(bf16[640,768]{1,0:T(8,128)(2,1)} %bitcast.116, bf16[512,768]{1,0:T(8,128)(2,1)} %bitcast.122, bf16[640,768]{1,0:T(8,128)(2,1)} %get-tuple-element.141.refs_2_, bf16[512,768]{1,0:T(8,128)(2,1)} %get-tuple-element.142.refs_3_, ...), custom_call_target="tpu_custom_call" | custom-call | flops 10871635968 | bytes 27131904 | tf_op jit(solution)/shard_map/weight_gradients/pallas_call | solution.py:485
  189.2 4.6 %all-to-all-done.2 = bf16[8,80,768]{2,1,0:T(8,128)(2,1)S(1)} async-done(((bf16[8,80,768]{2,1,0:T(8,128)(2,1)}), bf16[8,80,768]{2,1,0:T(8,128)(2,1)S(1)}, u32[]{:S(2)}, u32[]{:S(2)}) %all-to-all-start.2) | async-done | bytes 983072 | tf_op jit(solution)/shard_map/all_to_all | solution.py:952
  194.8 3.9 all-to-all-start.5
  198.7 13.6 %combine_gradients.1 = (f32[768,768]{1,0:T(8,128)}, bf16[768,768]{1,0:T(8,128)(2,1)}, bf16[384,1664]{1,0:T(8,128)(2,1)}, bf16[384,1664]{1,0:T(8,128)(2,1)}) custom-call(s32[1]{0:T(128)} %bitcast.17.core_ref, bf16[768,640]{1,0:T(8,128)(2,1)} %get-tuple-element.123.refs_0_, bf16[768,512]{1,0:T(8,128)(2,1)} %get-tuple-element.124.refs_1_, ...), custom_call_target="tpu_custom_call" | custom-call | flops 3170893824 | bytes 15335424 | tf_op jit(solution)/shard_map/combine_gradients/pallas_call | solution.py:706
  212.3 20.9 %attention_backward.3 = (bf16[384,1664]{1,0:T(8,128)(2,1)}, bf16[384,1664]{1,0:T(8,128)(2,1)}, f32[768,768]{1,0:T(8,128)}, f32[768,768]{1,0:T(8,128)}) custom-call(f32[3]{0:T(128)} %compare_select_fusion.flags_ref, s32[1]{0:T(128)} %bitcast.17.core_ref, ...), custom_call_target="tpu_custom_call", output_to_operand_aliasing={{0}: (15, {}), {1}: (16, {})} | custom-call | flops 6039797760 | bytes 14155776 | tf_op jit(solution)/shard_map/attention_backward/pallas_call | solution.py:290
  233.7 13.6 %attention_backward.4 = (bf16[384,1536]{1,0:T(8,128)(2,1)}, bf16[384,1536]{1,0:T(8,128)(2,1)}, f32[768,768]{1,0:T(8,128)}, f32[768,768]{1,0:T(8,128)}) custom-call(f32[3]{0:T(128)} %compare_select_fusion.flags_ref, s32[1]{0:T(128)} %bitcast.17.core_ref, bf16[768,2304]{1,0:T(8,128)(2,1)} %convolution_convert_fusion.q_ref.k_ref.v_ref, ...), custom_call_target="tpu_custom_call" | custom-call | flops 3019898880 | bytes 11796480 | tf_op jit(solution)/shard_map/attention_backward/pallas_call | solution.py:290
  255.5 30.1 %attention_backward.5 = (bf16[384,1536]{1,0:T(8,128)(2,1)}, bf16[384,1536]{1,0:T(8,128)(2,1)}, f32[768,768]{1,0:T(8,128)}, bf16[256,768]{1,0:T(8,128)(2,1)}, bf1...) custom-call(f32[3]{0:T(128)} %compare_select_fusion.flags_ref, ...), custom_call_target="tpu_custom_call", output_to_operand_aliasing={{0}: (15, {}), {1}: (16, {})} | custom-call | flops 9059696640 | bytes 16515072 | tf_op jit(solution)/shard_map/attention_backward/pallas_call | solution.py:290
  297.5 8.8 %collective-permute-done.8.refs_0_ = bf16[256,768]{1,0:T(8,128)(2,1)} collective-permute-done((bf16[256,768]{1,0:T(8,128)(2,1)}, bf16[256,768]{1,0:T(8,128)(2,1)}, u32[]{:S(2)}, u32[]{:S(2)}) %collective-permute-start.8) | collective-permute-done | bytes 393248 | tf_op jit(solution)/shard_map/ppermute | solution.py:1021
  311.3 6.5 %finish_outputs.1 = (bf16[768,768]{1,0:T(8,128)(2,1)}, f32[128,768]{1,0:T(8,128)}) custom-call(bf16[768,640]{1,0:T(8,128)(2,1)} %get-tuple-element.123.refs_0_, bf16[768,512]{1,0:T(8,128)(2,1)} %get-tuple-element.124.refs_1_, bf16[8,144,896]{2,1,0:T(8,128)(2,1)} %copy-done.3, f32[768,768]{1,0:T(8,128)} %get-tuple-element.190.refs_3_, ...), custom_call_target="tpu_custom_call" | custom-call | flops 1585446912 | bytes 9437184 | tf_op jit(solution)/shard_map/finish_outputs/pallas_call | solution.py:748
  317.9 4.8 %collective-permute-done.10.refs_2_ = bf16[256,768]{1,0:T(8,128)(2,1)} collective-permute-done((bf16[256,768]{1,0:T(8,128)(2,1)}, bf16[256,768]{1,0:T(8,128)(2,1)}, u32[]{:S(2)}, u32[]{:S(2)}) %collective-permute-start.10) | collective-permute-done | bytes 393248 | tf_op jit(solution)/shard_map/ppermute | solution.py:1021
  322.7 6.1 %input_gradient.1 = f32[768,768]{1,0:T(8,128)} custom-call(f32[768,768]{1,0:T(8,128)} %get-tuple-element.199.dact_ref, bf16[768,768]{1,0:T(8,128)(2,1)} %bitcast.69, f32[1,768]{1,0:T(1,128)} %broadcast_in_dim.48.gain_ref.scale_ref, f32[768,768]{1,0:T(8,128)} %get-tuple-element.200.dhidden_ref, bf16[256,768]{1,0:T(8,128)(2,1)} %collective-permute-done.8.refs_0_, ...), custom_call_target="tpu_custom_call" | custom-call | flops 7077888 | bytes 9437184 | tf_op jit(solution)/shard_map/input_gradient/pallas_call | solution.py:776
  338.7 4.2 %collective-permute-done.15.refs_2_ = bf16[1,24,3200]{2,1,0:T(8,128)(2,1)S(1)} collective-permute-done((bf16[1,24,3200]{2,1,0:T(8,128)(2,1)}, bf16[1,24,3200]{2,1,0:T(8,128)(2,1)S(1)}, u32[]{:S(2)}, u32[]{:S(2)}) %collective-permute-start.15) | collective-permute-done | bytes 153632 | tf_op jit(solution)/shard_map/ppermute | solution.py:834
  345.5 4.0 collective-permute-start.18
  351.0 8.4 %collective-permute-done.18.refs_2_ = bf16[1,24,3200]{2,1,0:T(8,128)(2,1)S(1)} collective-permute-done((bf16[1,24,3200]{2,1,0:T(8,128)(2,1)}, bf16[1,24,3200]{2,1,0:T(8,128)(2,1)S(1)}, u32[]{:S(2)}, u32[]{:S(2)}) %collective-permute-start.18) | collective-permute-done | bytes 153632 | tf_op jit(solution)/shard_map/ppermute | solution.py:834
  372.0 7.4 %collective-permute-done.20.refs_1_ = bf16[4,24,3200]{2,1,0:T(8,128)(2,1)S(1)} collective-permute-done((bf16[4,24,3200]{2,1,0:T(8,128)(2,1)}, bf16[4,24,3200]{2,1,0:T(8,128)(2,1)S(1)}, u32[]{:S(2)}, u32[]{:S(2)}) %collective-permute-start.20) | collective-permute-done | bytes 614432 | tf_op jit(solution)/shard_map/ppermute | solution.py:834
  380.4 6.6 %collective-permute-done.22.refs_3_ = bf16[4,24,3200]{2,1,0:T(8,128)(2,1)S(1)} collective-permute-done((bf16[4,24,3200]{2,1,0:T(8,128)(2,1)}, bf16[4,24,3200]{2,1,0:T(8,128)(2,1)S(1)}, u32[]{:S(2)}, u32[]{:S(2)}) %collective-permute-start.22) | collective-permute-done | bytes 614432 | tf_op jit(solution)/shard_map/ppermute | solution.py:834
  397.3 10.2 %unpack_sums.1 = (f32[768,768]{1,0:T(8,128)}, f32[768,2304]{1,0:T(8,128)}, f32[12,768]{1,0:T(8,128)}, f32[4,768]{1,0:T(4,128)}, f32[2,768]{1,0:T(2,128)}, /*index=5*/f32[1,768]{1,0:T(1,128)}, f32[1,768]{1,0:T(1,128)}) custom-call(s32[3]{0:T(128)} %pad_add_fusion.index_ref, bf16[4,4,24,3200]{3,2,1,0:T(8,128)(2,1)} %bitcast.70, ...), custom_call_target="tpu_custom_call" | custom-call | bytes 21233664 | tf_op jit(solution)/shard_map/unpack_sums/pallas_call | solution.py:910
  (150 shorter events, 97.6 us)
Async XLA Ops:
  17.0 55.7 %all-to-all-start = ((bf16[8,144,896]{2,1,0:T(8,128)(2,1)}), bf16[8,144,896]{2,1,0:T(8,128)(2,1)}, u32[]{:S(2)}, u32[]{:S(2)}) async-start(bf16[8,144,896]{2,1,0:T(8,128)(2,1)} %get-tuple-element.127), calls=%async_computation | async-start | bytes 4128768 | tf_op jit(solution)/shard_map/all_to_all | solution.py:949
  26.0 13.2 %collective-permute-start.2 = (bf16[256,768]{1,0:T(8,128)(2,1)}, bf16[256,768]{1,0:T(8,128)(2,1)}, u32[]{:S(2)}, u32[]{:S(2)}) collective-permute-start(bf16[256,768]{1,0:T(8,128)(2,1)} %slice_bitcast_fusion), channel_id=1, source_target_pairs={{0,24},{8,16},{16,8},{24,0},{1,25},{9,17},{17,9},{25,1},{2,26},{10... | collective-permute-start | bytes 1179656 | tf_op jit(solution)/shard_map/ppermute | solution.py:957
  28.5 18.7 %collective-permute-start.1 = (bf16[256,768]{1,0:T(8,128)(2,1)}, bf16[256,768]{1,0:T(8,128)(2,1)}, u32[]{:S(2)}, u32[]{:S(2)}) collective-permute-start(bf16[256,768]{1,0:T(8,128)(2,1)} %slice_bitcast_fusion), channel_id=1, source_target_pairs={{0,16},{8,24},{16,0},{24,8},{1,17},{9,25},{17,1},{25,9},{2,18},{10... | collective-permute-start | bytes 1179656 | tf_op jit(solution)/shard_map/ppermute | solution.py:957
  29.0 18.3 %collective-permute-start = (bf16[256,768]{1,0:T(8,128)(2,1)}, bf16[256,768]{1,0:T(8,128)(2,1)}, u32[]{:S(2)}, u32[]{:S(2)}) collective-permute-start(bf16[256,768]{1,0:T(8,128)(2,1)} %slice_bitcast_fusion), channel_id=1, source_target_pairs={{0,8},{8,0},{16,24},{24,16},{1,9},{9,1},{17,25},{25,17},{2,10},{10... | collective-permute-start | bytes 1179656 | tf_op jit(solution)/shard_map/ppermute | solution.py:957
  81.0 27.4 %all-to-all-start.3 = ((bf16[8,64,768]{2,1,0:T(8,128)(2,1)}), bf16[8,64,768]{2,1,0:T(8,128)(2,1)S(1)}, u32[]{:S(2)}, u32[]{:S(2)}) async-start(bf16[8,64,768]{2,1,0:T(8,128)(2,1)} %bitcast.123), calls=%async_computation.3 | async-start | bytes 1572864 | tf_op jit(solution)/shard_map/all_to_all | solution.py:949
  108.4 30.3 %all-to-all-start.1 = ((bf16[8,80,768]{2,1,0:T(8,128)(2,1)}), bf16[8,80,768]{2,1,0:T(8,128)(2,1)S(1)}, u32[]{:S(2)}, u32[]{:S(2)}) async-start(bf16[8,80,768]{2,1,0:T(8,128)(2,1)} %bitcast.8), calls=%async_computation.1 | async-start | bytes 1966080 | tf_op jit(solution)/shard_map/all_to_all | solution.py:949
  138.7 24.7 %all-to-all-start.4 = ((bf16[8,64,768]{2,1,0:T(8,128)(2,1)}), bf16[8,64,768]{2,1,0:T(8,128)(2,1)S(1)}, u32[]{:S(2)}, u32[]{:S(2)}) async-start(bf16[8,64,768]{2,1,0:T(8,128)(2,1)} %bitcast.124), calls=%async_computation.4 | async-start | bytes 1572864 | tf_op jit(solution)/shard_map/all_to_all | solution.py:952
  163.4 30.4 %all-to-all-start.2 = ((bf16[8,80,768]{2,1,0:T(8,128)(2,1)}), bf16[8,80,768]{2,1,0:T(8,128)(2,1)S(1)}, u32[]{:S(2)}, u32[]{:S(2)}) async-start(bf16[8,80,768]{2,1,0:T(8,128)(2,1)} %bitcast.117), calls=%async_computation.2 | async-start | bytes 1966080 | tf_op jit(solution)/shard_map/all_to_all | solution.py:952
  168.7 197.6 %reduce-scatter.5.cloned.1.call-start = ((), (), s32[]{:S(2)}) async-start(), calls=%async_computation.9 | async-start | bytes 3932160 | tf_op jit(solution)/shard_map/reduce_scatter | solution.py:998
  193.9 174.7 %reduce-scatter.3.cloned.1.call-start = ((), (), s32[]{:S(2)}) async-start(), calls=%async_computation.8 | async-start | bytes 7864320 | tf_op jit(solution)/shard_map/reduce_scatter | solution.py:997
  194.8 115.2 %all-to-all-start.5 = ((bf16[8,144,896]{2,1,0:T(8,128)(2,1)}), bf16[8,144,896]{2,1,0:T(8,128)(2,1)S(1)}, u32[]{:S(2)}, u32[]{:S(2)}) async-start(bf16[8,144,896]{2,1,0:T(8,128)(2,1)} %pad_maximum_fusion), calls=%async_computation.5 | async-start | bytes 4128768 | tf_op jit(solution)/shard_map/all_to_all | solution.py:952
  233.1 14.1 %collective-permute-start.3 = (bf16[384,1664]{1,0:T(8,128)(2,1)}, bf16[384,1664]{1,0:T(8,128)(2,1)S(1)}, u32[]{:S(2)}, u32[]{:S(2)}) collective-permute-start(bf16[384,1664]{1,0:T(8,128)(2,1)} %get-tuple-element.169), channel_id=1, source_target_pairs={{0,1},{1,0},{2,3},{3,2},{4,5},{5,4},{6,7},{7,6},{8,9},{9,8},{10,11... | collective-permute-start | bytes 3833864 | tf_op jit(solution)/shard_map/ppermute | solution.py:1008
  251.1 34.5 %collective-permute-start.4 = (bf16[1,96,1664]{2,1,0:T(8,128)(2,1)}, bf16[1,96,1664]{2,1,0:T(8,128)(2,1)S(1)}, u32[]{:S(2)}, u32[]{:S(2)}) collective-permute-start(bf16[1,96,1664]{2,1,0:T(8,128)(2,1)} %get-tuple-element.184), channel_id=1, source_target_pairs={{0,2},{1,3},{2,0},{3,1},{4,6},{5,7},{6,4},{7,5},{8,10},{9,11},{10,... | collective-permute-start | bytes 958472 | tf_op jit(solution)/shard_map/ppermute | solution.py:834
  252.6 33.0 %collective-permute-start.5 = (bf16[1,96,1664]{2,1,0:T(8,128)(2,1)}, bf16[1,96,1664]{2,1,0:T(8,128)(2,1)S(1)}, u32[]{:S(2)}, u32[]{:S(2)}) collective-permute-start(bf16[1,96,1664]{2,1,0:T(8,128)(2,1)} %get-tuple-element.185), channel_id=1, source_target_pairs={{0,4},{1,5},{2,6},{3,7},{4,0},{5,1},{6,2},{7,3},{8,12},{9,13},{10,... | collective-permute-start | bytes 958472 | tf_op jit(solution)/shard_map/ppermute | solution.py:834
  254.9 30.7 %collective-permute-start.6 = (bf16[1,96,1664]{2,1,0:T(8,128)(2,1)}, bf16[1,96,1664]{2,1,0:T(8,128)(2,1)S(1)}, u32[]{:S(2)}, u32[]{:S(2)}) collective-permute-start(bf16[1,96,1664]{2,1,0:T(8,128)(2,1)} %get-tuple-element.186), channel_id=1, source_target_pairs={{0,6},{1,7},{2,4},{3,5},{4,2},{5,3},{6,0},{7,1},{8,14},{9,15},{10,... | collective-permute-start | bytes 958472 | tf_op jit(solution)/shard_map/ppermute | solution.py:834
  286.5 3.5 collective-permute-start.7
  286.5 19.8 %collective-permute-start.8 = (bf16[256,768]{1,0:T(8,128)(2,1)}, bf16[256,768]{1,0:T(8,128)(2,1)}, u32[]{:S(2)}, u32[]{:S(2)}) collective-permute-start(bf16[256,768]{1,0:T(8,128)(2,1)} %get-tuple-element.195), channel_id=1, source_target_pairs={{0,8},{8,0},{16,24},{24,16},{1,9},{9,1},{17,25},{25,17},{2,10},{10... | collective-permute-start | bytes 1179656 | tf_op jit(solution)/shard_map/ppermute | solution.py:1021
  287.6 30.3 %collective-permute-start.9 = (bf16[256,768]{1,0:T(8,128)(2,1)}, bf16[256,768]{1,0:T(8,128)(2,1)}, u32[]{:S(2)}, u32[]{:S(2)}) collective-permute-start(bf16[256,768]{1,0:T(8,128)(2,1)} %get-tuple-element.196), channel_id=1, source_target_pairs={{0,16},{8,24},{16,0},{24,8},{1,17},{9,25},{17,1},{25,9},{2,18},{10... | collective-permute-start | bytes 1179656 | tf_op jit(solution)/shard_map/ppermute | solution.py:1021
  288.7 34.0 %collective-permute-start.10 = (bf16[256,768]{1,0:T(8,128)(2,1)}, bf16[256,768]{1,0:T(8,128)(2,1)}, u32[]{:S(2)}, u32[]{:S(2)}) collective-permute-start(bf16[256,768]{1,0:T(8,128)(2,1)} %get-tuple-element.197), channel_id=1, source_target_pairs={{0,24},{8,16},{16,8},{24,0},{1,25},{9,17},{17,9},{25,1},{2,26},{10... | collective-permute-start | bytes 1179656 | tf_op jit(solution)/shard_map/ppermute | solution.py:1021
  293.7 35.0 %collective-permute-start.11 = (bf16[1,96,1536]{2,1,0:T(8,128)(2,1)}, bf16[1,96,1536]{2,1,0:T(8,128)(2,1)S(1)}, u32[]{:S(2)}, u32[]{:S(2)}) collective-permute-start(bf16[1,96,1536]{2,1,0:T(8,128)(2,1)} %get-tuple-element.209), channel_id=1, source_target_pairs={{0,2},{1,3},{2,0},{3,1},{4,6},{5,7},{6,4},{7,5},{8,10},{9,11},{10,... | collective-permute-start | bytes 884744 | tf_op jit(solution)/shard_map/ppermute | solution.py:834
  294.2 34.5 %collective-permute-start.12 = (bf16[1,96,1536]{2,1,0:T(8,128)(2,1)}, bf16[1,96,1536]{2,1,0:T(8,128)(2,1)S(1)}, u32[]{:S(2)}, u32[]{:S(2)}) collective-permute-start(bf16[1,96,1536]{2,1,0:T(8,128)(2,1)} %get-tuple-element.210), channel_id=1, source_target_pairs={{0,4},{1,5},{2,6},{3,7},{4,0},{5,1},{6,2},{7,3},{8,12},{9,13},{10,... | collective-permute-start | bytes 884744 | tf_op jit(solution)/shard_map/ppermute | solution.py:834
  306.3 22.5 %collective-permute-start.13 = (bf16[1,96,1536]{2,1,0:T(8,128)(2,1)}, bf16[1,96,1536]{2,1,0:T(8,128)(2,1)S(1)}, u32[]{:S(2)}, u32[]{:S(2)}) collective-permute-start(bf16[1,96,1536]{2,1,0:T(8,128)(2,1)} %get-tuple-element.211), channel_id=1, source_target_pairs={{0,6},{1,7},{2,4},{3,5},{4,2},{5,3},{6,0},{7,1},{8,14},{9,15},{10,... | collective-permute-start | bytes 884744 | tf_op jit(solution)/shard_map/ppermute | solution.py:834
  332.3 6.4 %collective-permute-start.14 = (bf16[1,24,3200]{2,1,0:T(8,128)(2,1)}, bf16[1,24,3200]{2,1,0:T(8,128)(2,1)S(1)}, u32[]{:S(2)}, u32[]{:S(2)}) collective-permute-start(bf16[1,24,3200]{2,1,0:T(8,128)(2,1)} %get-tuple-element.217), channel_id=1, source_target_pairs={{0,8},{8,0},{16,24},{24,16},{1,9},{9,1},{17,25},{25,17},{2,10},{10... | collective-permute-start | bytes 460808 | tf_op jit(solution)/shard_map/ppermute | solution.py:834
  334.3 8.7 %collective-permute-start.15 = (bf16[1,24,3200]{2,1,0:T(8,128)(2,1)}, bf16[1,24,3200]{2,1,0:T(8,128)(2,1)S(1)}, u32[]{:S(2)}, u32[]{:S(2)}) collective-permute-start(bf16[1,24,3200]{2,1,0:T(8,128)(2,1)} %get-tuple-element.218), channel_id=1, source_target_pairs={{0,16},{8,24},{16,0},{24,8},{1,17},{9,25},{17,1},{25,9},{2,18},{10... | collective-permute-start | bytes 460808 | tf_op jit(solution)/shard_map/ppermute | solution.py:834
  336.0 7.0 %collective-permute-start.16 = (bf16[1,24,3200]{2,1,0:T(8,128)(2,1)}, bf16[1,24,3200]{2,1,0:T(8,128)(2,1)S(1)}, u32[]{:S(2)}, u32[]{:S(2)}) collective-permute-start(bf16[1,24,3200]{2,1,0:T(8,128)(2,1)} %get-tuple-element.219), channel_id=1, source_target_pairs={{0,24},{8,16},{16,8},{24,0},{1,25},{9,17},{17,9},{25,1},{2,26},{10... | collective-permute-start | bytes 460808 | tf_op jit(solution)/shard_map/ppermute | solution.py:834
  345.5 5.5 %collective-permute-start.17 = (bf16[1,24,3200]{2,1,0:T(8,128)(2,1)}, bf16[1,24,3200]{2,1,0:T(8,128)(2,1)S(1)}, u32[]{:S(2)}, u32[]{:S(2)}) collective-permute-start(bf16[1,24,3200]{2,1,0:T(8,128)(2,1)} %sum_pieces.7.refs_0_), channel_id=1, source_target_pairs={{0,2},{1,3},{2,0},{3,1},{4,6},{5,7},{6,4},{7,5},{8,10},{9,11},{10,... | collective-permute-start | bytes 460808 | tf_op jit(solution)/shard_map/ppermute | solution.py:834
  345.5 13.9 %collective-permute-start.18 = (bf16[1,24,3200]{2,1,0:T(8,128)(2,1)}, bf16[1,24,3200]{2,1,0:T(8,128)(2,1)S(1)}, u32[]{:S(2)}, u32[]{:S(2)}) collective-permute-start(bf16[1,24,3200]{2,1,0:T(8,128)(2,1)} %sum_pieces.7.refs_0_), channel_id=1, source_target_pairs={{0,4},{1,5},{2,6},{3,7},{4,0},{5,1},{6,2},{7,3},{8,12},{9,13},{10,... | collective-permute-start | bytes 460808 | tf_op jit(solution)/shard_map/ppermute | solution.py:834
  349.6 9.8 %collective-permute-start.19 = (bf16[1,24,3200]{2,1,0:T(8,128)(2,1)}, bf16[1,24,3200]{2,1,0:T(8,128)(2,1)S(1)}, u32[]{:S(2)}, u32[]{:S(2)}) collective-permute-start(bf16[1,24,3200]{2,1,0:T(8,128)(2,1)} %sum_pieces.7.refs_0_), channel_id=1, source_target_pairs={{0,6},{1,7},{2,4},{3,5},{4,2},{5,3},{6,0},{7,1},{8,14},{9,15},{10,... | collective-permute-start | bytes 460808 | tf_op jit(solution)/shard_map/ppermute | solution.py:834
  362.7 16.7 %collective-permute-start.20 = (bf16[4,24,3200]{2,1,0:T(8,128)(2,1)}, bf16[4,24,3200]{2,1,0:T(8,128)(2,1)S(1)}, u32[]{:S(2)}, u32[]{:S(2)}) collective-permute-start(bf16[4,24,3200]{2,1,0:T(8,128)(2,1)} %stack_pieces.2.refs_0_), channel_id=1, source_target_pairs={{0,8},{8,0},{16,24},{24,16},{1,9},{9,1},{17,25},{25,17},{2,10},{10... | collective-permute-start | bytes 1843208 | tf_op jit(solution)/shard_map/ppermute | solution.py:834
  363.7 16.6 %collective-permute-start.21 = (bf16[4,24,3200]{2,1,0:T(8,128)(2,1)}, bf16[4,24,3200]{2,1,0:T(8,128)(2,1)S(1)}, u32[]{:S(2)}, u32[]{:S(2)}) collective-permute-start(bf16[4,24,3200]{2,1,0:T(8,128)(2,1)} %stack_pieces.2.refs_0_), channel_id=1, source_target_pairs={{0,16},{8,24},{16,0},{24,8},{1,17},{9,25},{17,1},{25,9},{2,18},{10... | collective-permute-start | bytes 1843208 | tf_op jit(solution)/shard_map/ppermute | solution.py:834
  364.1 22.9 %collective-permute-start.22 = (bf16[4,24,3200]{2,1,0:T(8,128)(2,1)}, bf16[4,24,3200]{2,1,0:T(8,128)(2,1)S(1)}, u32[]{:S(2)}, u32[]{:S(2)}) collective-permute-start(bf16[4,24,3200]{2,1,0:T(8,128)(2,1)} %stack_pieces.2.refs_0_), channel_id=1, source_target_pairs={{0,24},{8,16},{16,8},{24,0},{1,25},{9,17},{17,9},{25,1},{2,26},{10... | collective-permute-start | bytes 1843208 | tf_op jit(solution)/shard_map/ppermute | solution.py:834
  391.0 4.9 %collective-permute-start.23 = (bf16[16,24,3200]{2,1,0:T(8,128)(2,1)}, bf16[16,24,3200]{2,1,0:T(8,128)(2,1)S(1)}, u32[]{:S(2)}, u32[]{:S(2)}) collective-permute-start(bf16[16,24,3200]{2,1,0:T(8,128)(2,1)} %stack_pieces.3), channel_id=1, source_target_pairs={{0,1},{1,0},{2,3},{3,2},{4,5},{5,4},{6,7},{7,6},{8,9},{9,8},{10,11... | collective-permute-start | bytes 7372808 | tf_op jit(solution)/shard_map/ppermute | solution.py:1008
  (31 other events, 147.2 us)
Sparse Core Ops, SparseCore 0:
  194.0 42.0 reduce-scatter.4
  239.6 86.4 reduce-scatter.2

commit v5 on v4

--- a/solution.py
+++ b/solution.py
@@ -128,13 +128,13 @@
     )(flags, proj, proj, proj, kv_rem, kv_rem)
 
 
-def attention_backward_kernel(plen, started, last, skip, flags_ref, core_ref, q_ref, k_ref, v_ref, kr_ref, vr_ref, o_ref, do_ref, lse_ref, act_ref, far_ref, wq_ref, wk_ref, wv_ref, *refs):
+def attention_backward_kernel(plen, started, last, skip, flags_ref, core_ref, q_ref, k_ref, v_ref, kr_ref, vr_ref, o_ref, do_ref, lse_ref, act_ref, far_ref, wk_ref, wv_ref, *refs):
     refs = refs[skip:]
     if started:
-        start_act_ref, start_far_ref, *refs = refs
-    mine_ref, theirs_ref, dact_ref, *refs = refs
-    dfar_ref, *dfar_refs = (refs[-1:] + refs[:-11]) if last else refs[:1]
-    kt, krt, dka, dva, dkra, dvra, own_grads, weights, kd, krd = refs[-11:-1] if last else refs[-10:]
+        start_far_ref, *refs = refs
+    mine_ref, theirs_ref, own_grads, *refs = refs
+    dfar_ref, *dfar_refs = (refs[-1:] + refs[:-10]) if last else refs[:1]
+    kt, krt, dka, dva, dkra, dvra, weights, kd, krd = refs[-10:-1] if last else refs[-9:]
     tok = q_ref.shape[0]
     remote = kr_ref.shape[0]
     lane = lax.broadcasted_iota(jnp.int32, (1, 128), 1)
@@ -196,27 +196,23 @@
     own_grads[:, 128:256] = (dka[...] * SCALE).astype(bf16)
     own_grads[:, 256:384] = dva[...].astype(bf16)
     far_grads = jnp.concatenate([(dkra[...] * SCALE).astype(bf16), dvra[...].astype(bf16)], axis=1)
-    weights[:, 0:128] = wq_ref[...]
-    weights[:, 128:256] = wk_ref[...]
-    weights[:, 256:384] = wv_ref[...]
+    weights[:, 0:128] = wk_ref[...]
+    weights[:, 128:256] = wv_ref[...]
     half = mine_ref.shape[0]
     for out_ref, which in ((theirs_ref, 1 - core_ref[0]), (mine_ref, core_ref[0])):
         rows = pl.ds(pl.multiple_of(which * half, half), half)
         total = dot_nn(act_ref[rows, :], own_grads[...])
         out_ref[:, 0:128] = total[:, 0:128].astype(bf16)
         out_ref[:, 128:384] = (total[:, 128:384] + dot_nn(far_ref[rows, :], far_grads)).astype(bf16)
-    d_act = dot_nt(own_grads[...], weights[...])
-    d_far = dot_nt(far_grads, weights[:, 128:384])
+    d_far = dot_nt(far_grads, weights[...])
     step = pl.program_id(0)
 
     @pl.when(step == 0)
     def _():
-        dact_ref[...] = d_act + start_act_ref[...] if started else d_act
         dfar_ref[...] = d_far + start_far_ref[...] if started else d_far
 
     @pl.when(step > 0)
     def _():
-        dact_ref[...] += d_act
         dfar_ref[...] += d_far
 
     if last:
@@ -249,11 +245,10 @@
         pl.BlockSpec((1, 16, tok), lambda i: (begin + i, 0, 0)),
         still((width, tok)),
         still((width, remote)),
-        weight(begin),
         weight(pairs + begin),
         weight(2 * pairs + begin),
     ]
-    arrays = [flags, core, proj, proj, proj, kv_rem, kv_rem, mixed, d_mixed, lse, act_t, far_t, w_qkv, w_qkv, w_qkv]
+    arrays = [flags, core, proj, proj, proj, kv_rem, kv_rem, mixed, d_mixed, lse, act_t, far_t, w_qkv, w_qkv]
     scratch = [
         pltpu.VMEM((128, tok), bf16),
         pltpu.VMEM((128, remote), bf16),
@@ -261,12 +256,10 @@
         pltpu.VMEM((tok, 128), f32),
         pltpu.VMEM((remote, 128), f32),
         pltpu.VMEM((remote, 128), f32),
-        pltpu.VMEM((tok, 384), bf16),
-        pltpu.VMEM((width, 384), bf16),
+        pltpu.VMEM((width, 256), bf16),
         pltpu.VMEM((2, tok, 128), bf16),
         pltpu.VMEM((2, remote, 128), bf16),
     ]
-    sums = [jax.ShapeDtypeStruct((tok, width), f32), jax.ShapeDtypeStruct((remote, width), f32)]
     aliases = {}
     skip = 0
     if not isinstance(buffers, int):
@@ -276,17 +269,17 @@
         skip = 2
         buffers = buffers[0].shape[1]
     if starts:
-        in_specs += [still((tok, width)), still((remote, width))]
+        in_specs += [still((remote, width))]
         arrays += list(starts)
-    out_specs = [half, half, still((tok, width))]
-    out_shape = [jax.ShapeDtypeStruct((width // 2, buffers), bf16)] * 2 + sums[:1]
+    out_specs = [half, half, pl.BlockSpec((tok, 384), lambda i: (0, i))]
+    out_shape = [jax.ShapeDtypeStruct((width // 2, buffers), bf16)] * 2 + [jax.ShapeDtypeStruct((tok, count * 384), bf16)]
     if last:
         out_specs += [still((plen, width))] * (remote // plen)
         out_shape += [jax.ShapeDtypeStruct((plen, width), bf16)] * (remote // plen)
         scratch = scratch + [pltpu.VMEM((remote, width), f32)]
     else:
         out_specs += [still((remote, width))]
-        out_shape += sums[1:]
+        out_shape += [jax.ShapeDtypeStruct((remote, width), f32)]
     return pl.pallas_call(
         functools.partial(attention_backward_kernel, plen, bool(starts), last, skip),
         grid=(count,),
@@ -504,42 +497,24 @@
 
 
 def after_attention_kernel(count, mixed_ref, x_ref, w_ref, gain_ref, *refs):
-    turned, (hidden_ref, low_ref), sent = refs[:count], refs[count : count + 2], refs[count + 2 : 2 * count + 2]
-    kept, local, sems = refs[2 * count + 2], refs[2 * count + 3 : 3 * count + 3], refs[-1]
-    step = pl.program_id(0)
-    copies = [pltpu.make_async_copy(t, s, sems.at[g]) for g, (t, s) in enumerate(zip(turned, local))]
-
-    @pl.when(step == 0)
-    def _():
-        for copy in copies:
-            copy.start()
-
+    turned, (hidden_ref, low_ref), sent = refs[:count], refs[count : count + 2], refs[count + 2 :]
     hidden = x_ref[...].astype(f32) + dot_nn(mixed_ref[...], w_ref[...])
     low = (hidden * inverse_rms(hidden) * gain_ref[...]).astype(bf16)
     hidden_ref[...] = hidden
     low_ref[...] = low
-    block = low.shape[0]
-    kept[pl.ds(pl.multiple_of(step * block, block), block), :] = low
-
-    @pl.when(step == pl.num_programs(0) - 1)
-    def _():
-        for copy, t, s in zip(copies, local, sent):
-            copy.wait()
-            s[...] = dot_nn(t[...], kept[...]).astype(bf16)
+    for t, s in zip(turned, sent):
+        s[...] = dot_nn(t[...], low).astype(bf16)
 
 
 def after_attention(mixed, x, w_out, gain, turned):
     tok, width = x.shape
     rows = sum(t.shape[0] for t in turned)
-    block, tiles = row_tiles(tok)
     out = pl.pallas_call(
         functools.partial(after_attention_kernel, len(turned)),
-        grid=(tok // block,),
-        in_specs=[tiles(width), tiles(width), fixed(w_out), fixed(gain)] + [pl.BlockSpec(memory_space=pl.ANY)] * len(turned),
-        out_specs=[tiles(width)] * 2 + [pl.BlockSpec((t.shape[0], width), lambda i: (0, 0)) for t in turned],
+        in_specs=[ANYWHERE] * (4 + len(turned)),
+        out_specs=[ANYWHERE] * (2 + len(turned)),
         out_shape=[jax.ShapeDtypeStruct((tok, width), f32), jax.ShapeDtypeStruct((tok, width), bf16)]
         + [jax.ShapeDtypeStruct((t.shape[0], width), bf16) for t in turned],
-        scratch_shapes=[pltpu.VMEM((tok, width), bf16)] + [pltpu.VMEM(t.shape, bf16) for t in turned] + [pltpu.SemaphoreType.DMA((len(turned),))],
         compiler_params=pltpu.CompilerParams(vmem_limit_bytes=60 * 2**20),
         cost_estimate=pl.CostEstimate(flops=2 * tok * width * (width + rows), bytes_accessed=2 * width * (6 * tok + 2 * rows), transcendentals=0),
         name="after_attention",
@@ -701,7 +676,7 @@
     tok, width = hidden.shape
     rows = sum(c.shape[1] for c in chosen)
     arrays = [a for group in got for a in group]
-    block, tiles = 128, lambda columns: pl.BlockSpec((128, columns), lambda i: (i, 0))
+    block, tiles = row_tiles(tok)
     half = (width // 2, columns + width + EXTRA)
     return pl.pallas_call(
         functools.partial(combine_kernel, len(chosen), len(got[0])),
@@ -757,32 +732,47 @@
     )(*chosen, *got, local, probs, d_probs)
 
 
-def input_kernel(dact_ref, x_ref, gain_ref, dhidden_ref, *refs):
-    out_ref = refs[-1]
-    far = refs[0][...].astype(f32)
-    for ref in refs[1:-1]:
-        far = far + ref[...].astype(f32)
+def input_kernel(count, x_ref, gain_ref, dhidden_ref, w_ref, *refs):
+    grads, far, (out_ref, weights) = refs[:count], refs[count:-2], refs[-2:]
+    width = x_ref.shape[1]
+
+    @pl.when(pl.program_id(0) == 0)
+    def _():
+        for i in range(width // 128):
+            for p in range(3):
+                weights[:, i * 384 + p * 128 : i * 384 + (p + 1) * 128] = w_ref[:, p * width + i * 128 : p * width + (i + 1) * 128]
+
+    total = None
+    for ref in far:
+        total = ref[...].astype(f32) if total is None else total + ref[...].astype(f32)
+    d_act = jnp.where(pl.program_id(0) == 0, total, 0.0)
+    at = 0
+    for ref in grads:
+        columns = ref.shape[1]
+        d_act = d_act + dot_nt(ref[...], weights[:, at : at + columns])
+        at += columns
     x = x_ref[...].astype(f32)
     inverse = inverse_rms(x)
-    scaled = (dact_ref[...] + jnp.where(pl.program_id(0) == 0, far, 0.0)) * gain_ref[...]
+    scaled = d_act * gain_ref[...]
     mean = jnp.mean(scaled * x, axis=1, keepdims=True)
     out_ref[...] = dhidden_ref[...] + inverse * scaled - x * (inverse * inverse * inverse * mean)
 
 
-def input_gradient(d_act, x, gain, d_hidden, far):
+def input_gradient(grads, x, gain, d_hidden, w_qkv, far):
     tok, width = x.shape
     block = far[0].shape[0]
-    tiles = pl.BlockSpec((block, width), lambda i: (i, 0))
-    return pl.pallas_call(
-        input_kernel,
+    tiles = lambda columns: pl.BlockSpec((block, columns), lambda i: (i, 0))
+    return pl.pallas_call(
+        functools.partial(input_kernel, len(grads)),
         grid=(tok // block,),
-        in_specs=[tiles, tiles, fixed(gain), tiles] + [fixed(f) for f in far],
-        out_specs=tiles,
+        in_specs=[tiles(width), fixed(gain), tiles(width), fixed(w_qkv)] + [tiles(g.shape[1]) for g in grads] + [fixed(f) for f in far],
+        out_specs=tiles(width),
         out_shape=jax.ShapeDtypeStruct((tok, width), f32),
-        compiler_params=pltpu.CompilerParams(vmem_limit_bytes=60 * 2**20),
-        cost_estimate=pl.CostEstimate(flops=12 * tok * width, bytes_accessed=16 * tok * width, transcendentals=0),
+        scratch_shapes=[pltpu.VMEM((width, 3 * width), bf16)],
+        compiler_params=pltpu.CompilerParams(vmem_limit_bytes=60 * 2**20),
+        cost_estimate=pl.CostEstimate(flops=6 * tok * width * width, bytes_accessed=22 * tok * width, transcendentals=0),
         name="input_gradient",
-    )(d_act, x, gain, d_hidden, *far)
+    )(x, gain, d_hidden, w_qkv, *grads, *far)
 
 
 def xor_pairs(size, mask):
@@ -885,10 +875,11 @@
     def _():
         turned = small[...].T
         router_ref[...] = turned[0:ALL_EXPERTS]
-        mixing_ref[...] = turned[16:20]
+        mixing_ref[0] = turned[16:18]
+        mixing_ref[1] = turned[18:20]
         vec_ref[...] = turned[20:22]
-        gain_ref[...] = turned[24:25]
-        attn_ref[...] = turned[EXTRA - 1 : EXTRA] / scale_ref[...]
+        gain_ref[...] = turned[24]
+        attn_ref[...] = (turned[EXTRA - 1 : EXTRA] / scale_ref[...])[0]
 
 
 def unpack(index, own, other, w_qkv, scale, left):
@@ -905,18 +896,18 @@
 
         return pl.BlockSpec((4, 1, piece, own.shape[3]), at)
 
-    whole = lambda n: pl.BlockSpec((n, width), lambda c, a, s: (0, 0))
-    counts = (ALL_EXPERTS, 4, 2, 1, 1)
+    whole = lambda shape: pl.BlockSpec(shape, lambda c, a, s: (0,) * len(shape))
+    shapes = ((ALL_EXPERTS, width), (2, 2, width), (2, width), (width,), (width,))
     return pl.pallas_call(
         functools.partial(unpack_kernel, left),
         grid_spec=pltpu.PrefetchScalarGridSpec(
             num_scalar_prefetch=1,
             grid=(2, 4),
-            in_specs=[source(lambda core: core), source(lambda core: 1 - core), pl.BlockSpec((block, 3 * width), row), whole(1)],
-            out_specs=[pl.BlockSpec((block, width), row), pl.BlockSpec((block, 3 * width), row), *[whole(n) for n in counts]],
+            in_specs=[source(lambda core: core), source(lambda core: 1 - core), pl.BlockSpec((block, 3 * width), row), whole((1, width))],
+            out_specs=[pl.BlockSpec((block, width), row), pl.BlockSpec((block, 3 * width), row), *[whole(s) for s in shapes]],
             scratch_shapes=[pltpu.VMEM((width, EXTRA), f32)],
         ),
-        out_shape=[jax.ShapeDtypeStruct((width, width), f32), jax.ShapeDtypeStruct((width, 3 * width), f32), *[jax.ShapeDtypeStruct((n, width), f32) for n in counts]],
+        out_shape=[jax.ShapeDtypeStruct((width, width), f32), jax.ShapeDtypeStruct((width, 3 * width), f32), *[jax.ShapeDtypeStruct(s, f32) for s in shapes]],
         compiler_params=pltpu.CompilerParams(vmem_limit_bytes=60 * 2**20),
         cost_estimate=pl.CostEstimate(flops=0, bytes_accessed=36 * width * width, transcendentals=0),
         name="unpack_sums",
@@ -1006,34 +997,40 @@
     at_ctx, at_z = me_c.reshape(1), z.reshape(1)
     along_ctx, along_z = ("ctx", 4, 1), ("exp", 8, 2)
     across = lambda value: lax.ppermute(value, "exp", xor_pairs(n_exp, 1))
-    mine_1, theirs_1, *starts = attention(d_mixed, 0, cut, buffers, 0, None, False)
+    mine_1, theirs_1, grads_1, *starts = attention(d_mixed, 0, cut, buffers, 0, None, False)
     if dense:
         got_1 = across(theirs_1)
-    mine_2, theirs_2, *starts = attention(d_mixed, cut, 1, right, 0, starts, False)
+    mine_2, theirs_2, grads_2, *starts = attention(d_mixed, cut, 1, right, 0, starts, False)
     if dense:
         mine_2, theirs_2, starts, got_1 = lax.optimization_barrier((mine_2, theirs_2, starts, got_1))
         sums_1 = sum_pieces(at_z, [[quarters(mine_1), quarters(got_1)]])
         parts_1 = swap(sums_1, along_z)
         mine_2 = after(mine_2, sums_1[0])
-    mine_2, theirs_2, d_act, *d_far = attention(d_mixed, cut + 1, pairs - cut - 1, (mine_2, theirs_2), 1, starts, True)
+    mine_2, theirs_2, grads_3, *d_far = attention(d_mixed, cut + 1, pairs - cut - 1, (mine_2, theirs_2), 1, starts, True)
     if dense:
-        mine_2, theirs_2, d_act, d_far, parts_1 = lax.optimization_barrier((mine_2, theirs_2, d_act, d_far, parts_1))
-    far_back = [lax.ppermute(d_far[k - 1], "ctx", xor_pairs(n_ctx, k)) for k in range(1, n_ctx)]
+        mine_2, theirs_2, grads_3, d_far, parts_1 = lax.optimization_barrier((mine_2, theirs_2, grads_3, d_far, parts_1))
+    send_far = lambda k: lax.ppermute(d_far[k - 1], "ctx", xor_pairs(n_ctx, k))
+    far_back = [send_far(k) for k in range(1, n_ctx - 1)]
     if dense:
         sums_2 = sum_pieces(at_z, [[quarters(mine_2), quarters(across(theirs_2))]])
         parts_2 = swap(sums_2, along_z)
         mixed_out, d_logits = finish(chosen, out_got, groups, after(local_out, sums_2[0]), probs, d_probs)
-        mixed_out, d_logits, far_back = lax.optimization_barrier((mixed_out, d_logits, far_back))
+        mixed_out, d_logits, far_back, d_far = lax.optimization_barrier((mixed_out, d_logits, far_back, d_far))
+        far_back = far_back + [send_far(n_ctx - 1)]
+        mixed_out, parts_2 = lax.optimization_barrier((mixed_out, parts_2))
+        parts_1, parts_2 = ([quarters(p) for p in parts] for parts in (parts_1, parts_2))
+        parts = swap(sum_pieces(at_ctx, [parts_1, parts_2]), along_ctx)
+        [piece] = sum_pieces(at_ctx, [parts])
+        spread_z = spread(piece, along_z)
     else:
         mixed_out, d_logits = finish(chosen, out_got, groups, local_out, probs, d_probs)
-    d_inputs = input_gradient(d_act, x_low, attn_gain[None], d_hidden, far_back)
+        far_back = far_back + [send_far(n_ctx - 1)]
+    d_inputs = input_gradient([grads_1, grads_2, grads_3], x_low, attn_gain[None], d_hidden, w_qkv, far_back)
 
     total_gate, total_up, total_down = sum_gate_up[0][None], sum_gate_up[1][None], sum_down[None]
     if dense:
-        parts_1, parts_2 = ([quarters(p) for p in parts] for parts in (parts_1, after(parts_2, d_inputs)))
-        parts = swap(sum_pieces(at_ctx, [parts_1, parts_2]), along_ctx)
-        [piece] = sum_pieces(at_ctx, [parts])
-        column = stack_pieces(spread(piece, along_z))
+        d_inputs, spread_z = lax.optimization_barrier((d_inputs, spread_z))
+        column = stack_pieces(spread_z)
         own = stack_pieces(after(spread(column, along_ctx), total_gate, total_up, total_down))
         other = across(own)
         out_sum, qkv_sum, d_router, d_mixing, d_const_vec, d_moe_gain, d_attn_gain = unpack(
@@ -1045,18 +1042,18 @@
         columns = jnp.concatenate([total_1[:, :left], total_2], axis=1).reshape(width, pairs, 3, 128)
         qkv_sum = columns.transpose(0, 2, 1, 3).reshape(width, 3 * width)
         out_sum, small = total_1[:, left : left + width], total_1[:, left + width :].T
-        d_attn_gain = (jnp.sum(qkv_sum * w_qkv.astype(f32), axis=1) / attn_gain)[None]
-        d_router, d_mixing, d_const_vec, d_moe_gain = small[:ALL_EXPERTS], small[16:20], small[20:22], small[24:25]
+        d_attn_gain = (jnp.sum(qkv_sum * w_qkv.astype(f32), axis=1) / attn_gain)
+        d_router, d_mixing, d_const_vec, d_moe_gain = small[:ALL_EXPERTS], small[16:20].reshape(2, 2, width), small[20:22], small[24]
     return (
         mixed_out[None],
         d_inputs[None],
         d_logits[:ALL_EXPERTS].T[None],
-        d_attn_gain[0],
+        d_attn_gain,
         qkv_sum,
         out_sum,
-        d_moe_gain[0],
+        d_moe_gain,
         d_router.T,
-        d_mixing.reshape(2, 2, width).transpose(0, 2, 1),
+        d_mixing.transpose(0, 2, 1),
         d_const_vec,
         total_gate,
         total_up,

time: 426 us -> 407 us (0.955)
  Pallas kernels: 227 us -> 218 us
  waiting for transfers between devices: 69 us -> 64.3 us
    ppermute x3, waiting for transfers between devices: 13.5 us -> 0.01 us  [body(): send_far = lambda k: lax.ppermute(d_far[k - 1], 'ctx', xor_pairs(n_ctx, k))]
    pallas_call x3, Pallas kernels: 64.5 us -> 55.4 us  [attention_backward(): pl.pallas_call(functools.partial(attention_backward_kernel, plen, bool(st...]
    ppermute x15, waiting for transfers between devices: 31.4 us -> 39.9 us  [swap(): lax.ppermute(pieces[k], axis, xor_pairs(size, unit * k))]
    unnamed x68 -> x72, local copies, waits for them, and re-layouts: 15.2 us -> 16 us
  transfers between devices with their start and end apart: 32 -> 32, of which waited for: 15 -> 13; matrix products, arithmetic and copies ran while one was open for 7% -> 7% of each run, Pallas kernels for 48% -> 48%
where the time goes in v5:
time: 407 us; the launch traced here: 402 us
  Pallas kernels  218 us (54%)
  waiting for transfers between devices  64.3 us (16%)
  starting transfers between devices  60.8 us (15%)
  local copies, waits for them, and re-layouts  25.2 us (6%)
  between operations  14.6 us (4%)
  other arithmetic  11.3 us (3%)
  matrix products  7.75 us (2%)
    pallas_call x3, Pallas kernels, attention_backward(): pl.pallas_call(functools.partial(attention_backward_kernel, plen, bool(st...  55.4 us
    ppermute x15, waiting for transfers between devices, swap(): lax.ppermute(pieces[k], axis, xor_pairs(size, unit * k))  39.9 us
    pallas_call x2, Pallas kernels, expert_pass(): pl.pallas_call(functools.partial(expert_kernel, group), grid=(ff // tile,...  38.7 us
    ppermute x15, starting transfers between devices, swap(): lax.ppermute(pieces[k], axis, xor_pairs(size, unit * k))  21.2 us
    pallas_call x1, Pallas kernels, attention_forward(): pl.pallas_call(functools.partial(attention_forward_kernel, plen), grid=(p...  19 us
    pallas_call x1, Pallas kernels, weight_gradients(): pl.pallas_call(functools.partial(weight_kernel, count), grid=(ff // tile,...  17.9 us
    all_to_all x3, starting transfers between devices, deal(): return lax.all_to_all(value, 'exp', 0, 0, tiled=True)  17.2 us
    unnamed x72, local copies, waits for them, and re-layouts  16 us
  transfers between devices with their start and end apart: 32, of which 13 were waited for; matrix products, arithmetic and copies ran while one was open for 7% of the time, Pallas kernels for 48%

profile of v5, /device:TPU:0, one launch (start us, length us, event | category | flops | bytes accessed | tf_op | source)
XLA Modules:
  0.0 402.1 jit_solution(16593044733071792676)
XLA Ops:
  10.5 6.5 %route_plan.1 = (bf16[640,768]{1,0:T(8,128)(2,1)}, bf16[512,768]{1,0:T(8,128)(2,1)}, bf16[768,640]{1,0:T(8,128)(2,1)}, bf16[768,512]{1,0:T(8,128)(2,1)}, bf16[8,144,896]{2,1,0:T(8,128)(2,1)}) custom-call(s32[1]{0:T(128)} %bitcast.home_ref, s32[768,2]{1,0:T(8,128)} %bitcast.110, bf16[768,768]{1,0:T(8,128)(2,1)} %bitcast.103, f32[768,12]{1,0:T(8,128)} %bitcast.112), custom_call_target="tpu_custom_call" | custom-call | flops 1585446912 | bytes 3538944 | tf_op jit(solution)/shard_map/route_plan/pallas_call | solution.py:352
  17.0 7.0 %all-to-all-start = ((bf16[8,144,896]{2,1,0:T(8,128)(2,1)}), bf16[8,144,896]{2,1,0:T(8,128)(2,1)}, u32[]{:S(2)}, u32[]{:S(2)}) async-start(bf16[8,144,896]{2,1,0:T(8,128)(2,1)} %get-tuple-element.132), calls=%async_computation | async-start | bytes 4128768 | tf_op jit(solution)/shard_map/all_to_all | solution.py:940
  33.8 4.3 %convolution_convert_fusion.q_ref.k_ref.v_ref = bf16[768,2304]{1,0:T(8,128)(2,1)} fusion(bf16[768,768]{1,0:T(8,128)(2,1)S(1)} %fusion.2.in_ref, bf16[768,2304]{1,0:T(8,128)(2,1)S(1)} %copy-done), kind=kOutput, calls=%fused_computation | convolution fusion | flops 2719678464 | bytes 8257536 | tf_op jit(solution)/shard_map/dot_general | solution.py:22
  39.1 8.0 %collective-permute-done.1 = bf16[256,768]{1,0:T(8,128)(2,1)} collective-permute-done((bf16[256,768]{1,0:T(8,128)(2,1)}, bf16[256,768]{1,0:T(8,128)(2,1)}, u32[]{:S(2)}, u32[]{:S(2)}) %collective-permute-start.1) | collective-permute-done | bytes 393248 | tf_op jit(solution)/shard_map/ppermute | solution.py:948
  50.2 3.4 convolution_convert_fusion.1.kr_ref.vr_ref
  53.6 19.0 %attention_forward.1 = (bf16[768,768]{1,0:T(8,128)(2,1)}, f32[6,16,768]{2,1,0:T(8,128)}) custom-call(f32[3]{0:T(128)} %compare_select_fusion.flags_ref, bf16[768,2304]{1,0:T(8,128)(2,1)} %convolution_convert_fusion.q_ref.k_ref.v_ref, bf16[768,2304]{1,0:T(8,128)(2,1)} %convolution_convert_fusion.q_ref.k_ref.v_ref, ...), custom_call_target="tpu_custom_call" | custom-call | flops 3623878656 | bytes 7077888 | tf_op jit(solution)/shard_map/attention_forward/pallas_call | solution.py:105
  72.6 6.9 %after_attention.1 = (f32[768,768]{1,0:T(8,128)}, bf16[768,768]{1,0:T(8,128)(2,1)}, bf16[640,768]{1,0:T(8,128)(2,1)}, bf16[512,768]{1,0:T(8,128)(2,1)}) custom-call(bf16[768,768]{1,0:T(8,128)(2,1)} %get-tuple-element.133.mixed_ref.refs_11_.o_ref, bf16[768,768]{1,0:T(8,128)(2,1)} %bitcast.68, bf16[768,768]{1,0:T(8,128)(2,1)} %refs_12_.1, ...), custom_call_target="tpu_custom_call" | custom-call | flops 2264924160 | bytes 10616832 | tf_op jit(solution)/shard_map/after_attention/pallas_call | solution.py:512
  79.5 5.1 %all-to-all-start.3 = ((bf16[8,64,768]{2,1,0:T(8,128)(2,1)}), bf16[8,64,768]{2,1,0:T(8,128)(2,1)S(1)}, u32[]{:S(2)}, u32[]{:S(2)}) async-start(bf16[8,64,768]{2,1,0:T(8,128)(2,1)} %bitcast.123), calls=%async_computation.3 | async-start | bytes 1572864 | tf_op jit(solution)/shard_map/all_to_all | solution.py:940
  89.8 3.4 turn.3.far_ref
  93.2 13.7 %local_part.1 = (f32[768,768]{1,0:T(8,128)}, f32[768,768]{1,0:T(8,128)}, f32[768,128]{1,0:T(8,128)}, f32[768,128]{1,0:T(8,128)}, f32[24,768]{1,0:T(8,128)}) custom-call(f32[768,768]{1,0:T(8,128)} %get-tuple-element.137.hidden_ref.refs_8_, bf16[768,768]{1,0:T(8,128)(2,1)} %get-tuple-element.138.low_ref, bf16[768,768]{1,0:T(8,128)(2,1)} %bitcast.104, ...), custom_call_target="tpu_custom_call" | custom-call | flops 1056964608 | bytes 9437184 | tf_op jit(solution)/shard_map/local_part/pallas_call | solution.py:610
  107.0 5.1 %all-to-all-start.1 = ((bf16[8,80,768]{2,1,0:T(8,128)(2,1)}), bf16[8,80,768]{2,1,0:T(8,128)(2,1)S(1)}, u32[]{:S(2)}, u32[]{:S(2)}) async-start(bf16[8,80,768]{2,1,0:T(8,128)(2,1)} %bitcast.8), calls=%async_computation.1 | async-start | bytes 1966080 | tf_op jit(solution)/shard_map/all_to_all | solution.py:940
  112.8 17.8 %expert_pass.3 = (bf16[512,896]{1,0:T(8,128)(2,1)}, bf16[512,768]{1,0:T(8,128)(2,1)}, bf16[512,768]{1,0:T(8,128)(2,1)}, bf16[512,2048]{1,0:T(8,128)(2,1)}, bf16[...) custom-call(s32[1]{0:T(128)} %bitcast.home_ref, bf16[512,768]{1,0:T(8,128)(2,1)} %bitcast.121, ...), custom_call_target="tpu_custom_call" | custom-call | flops 9663676416 | bytes 19660800 | tf_op jit(solution)/shard_map/expert_pass/pallas_call | solution.py:429
  130.5 6.7 %all-to-all-done.1 = bf16[8,80,768]{2,1,0:T(8,128)(2,1)S(1)} async-done(((bf16[8,80,768]{2,1,0:T(8,128)(2,1)}), bf16[8,80,768]{2,1,0:T(8,128)(2,1)S(1)}, u32[]{:S(2)}, u32[]{:S(2)}) %all-to-all-start.1) | async-done | bytes 983072 | tf_op jit(solution)/shard_map/all_to_all | solution.py:940
  137.3 3.8 all-to-all-start.4
  141.0 20.9 %expert_pass.2 = (bf16[640,896]{1,0:T(8,128)(2,1)}, bf16[640,768]{1,0:T(8,128)(2,1)}, bf16[640,768]{1,0:T(8,128)(2,1)}, bf16[640,2048]{1,0:T(8,128)(2,1)}, bf16[...) custom-call(s32[1]{0:T(128)} %bitcast.home_ref, bf16[640,768]{1,0:T(8,128)(2,1)} %bitcast.115, ...), custom_call_target="tpu_custom_call" | custom-call | flops 12079595520 | bytes 22216704 | tf_op jit(solution)/shard_map/expert_pass/pallas_call | solution.py:429
  162.0 5.2 %all-to-all-start.2 = ((bf16[8,80,768]{2,1,0:T(8,128)(2,1)}), bf16[8,80,768]{2,1,0:T(8,128)(2,1)S(1)}, u32[]{:S(2)}, u32[]{:S(2)}) async-start(bf16[8,80,768]{2,1,0:T(8,128)(2,1)} %bitcast.117), calls=%async_computation.2 | async-start | bytes 1966080 | tf_op jit(solution)/shard_map/all_to_all | solution.py:943
  169.9 17.9 %weight_gradients.1 = (bf16[2,768,2048]{2,1,0:T(8,128)(2,1)}, bf16[2048,768]{1,0:T(8,128)(2,1)}) custom-call(bf16[640,768]{1,0:T(8,128)(2,1)} %bitcast.116, bf16[512,768]{1,0:T(8,128)(2,1)} %bitcast.122, bf16[640,768]{1,0:T(8,128)(2,1)} %get-tuple-element.146.refs_2_, bf16[512,768]{1,0:T(8,128)(2,1)} %get-tuple-element.147.refs_3_, ...), custom_call_target="tpu_custom_call" | custom-call | flops 10871635968 | bytes 27131904 | tf_op jit(solution)/shard_map/weight_gradients/pallas_call | solution.py:478
  187.8 4.6 %all-to-all-done.2 = bf16[8,80,768]{2,1,0:T(8,128)(2,1)S(1)} async-done(((bf16[8,80,768]{2,1,0:T(8,128)(2,1)}), bf16[8,80,768]{2,1,0:T(8,128)(2,1)S(1)}, u32[]{:S(2)}, u32[]{:S(2)}) %all-to-all-start.2) | async-done | bytes 983072 | tf_op jit(solution)/shard_map/all_to_all | solution.py:943
  193.4 3.9 all-to-all-start.5
  197.2 11.6 %combine_gradients.1 = (f32[768,768]{1,0:T(8,128)}, bf16[768,768]{1,0:T(8,128)(2,1)}, bf16[384,1664]{1,0:T(8,128)(2,1)}, bf16[384,1664]{1,0:T(8,128)(2,1)}) custom-call(s32[1]{0:T(128)} %bitcast.17.core_ref, bf16[768,640]{1,0:T(8,128)(2,1)} %get-tuple-element.128.refs_0_, bf16[768,512]{1,0:T(8,128)(2,1)} %get-tuple-element.129.refs_1_, ...), custom_call_target="tpu_custom_call" | custom-call | flops 3170893824 | bytes 15335424 | tf_op jit(solution)/shard_map/combine_gradients/pallas_call | solution.py:681
  208.8 18.6 %attention_backward.3 = (bf16[384,1664]{1,0:T(8,128)(2,1)}, bf16[384,1664]{1,0:T(8,128)(2,1)}, bf16[768,768]{1,0:T(8,128)(2,1)}, f32[768,768]{1,0:T(8,128)}) custom-call(f32[3]{0:T(128)} %compare_select_fusion.flags_ref, s32[1]{0:T(128)} %bitcast.17.core_ref, ...), custom_call_target="tpu_custom_call", output_to_operand_aliasing={{0}: (14, {}), {1}: (15, {})} | custom-call | flops 6039797760 | bytes 14155776 | tf_op jit(solution)/shard_map/attention_backward/pallas_call | solution.py:283
  227.9 11.2 %attention_backward.4 = (bf16[384,1536]{1,0:T(8,128)(2,1)}, bf16[384,1536]{1,0:T(8,128)(2,1)}, bf16[768,384]{1,0:T(8,128)(2,1)}, f32[768,768]{1,0:T(8,128)}) custom-call(f32[3]{0:T(128)} %compare_select_fusion.flags_ref, s32[1]{0:T(128)} %bitcast.17.core_ref, bf16[768,2304]{1,0:T(8,128)(2,1)} %convolution_convert_fusion.q_ref.k_ref.v_ref, ...), custom_call_target="tpu_custom_call" | custom-call | flops 3019898880 | bytes 11796480 | tf_op jit(solution)/shard_map/attention_backward/pallas_call | solution.py:283
  247.3 25.7 %attention_backward.5 = (bf16[384,1536]{1,0:T(8,128)(2,1)}, bf16[384,1536]{1,0:T(8,128)(2,1)}, bf16[768,1152]{1,0:T(8,128)(2,1)}, bf16[256,768]{1,0:T(8,128)(2,1...) custom-call(f32[3]{0:T(128)} %compare_select_fusion.flags_ref, ...), custom_call_target="tpu_custom_call", output_to_operand_aliasing={{0}: (14, {}), {1}: (15, {})} | custom-call | flops 9059696640 | bytes 16515072 | tf_op jit(solution)/shard_map/attention_backward/pallas_call | solution.py:283
  287.5 6.8 %finish_outputs.1 = (bf16[768,768]{1,0:T(8,128)(2,1)}, f32[128,768]{1,0:T(8,128)}) custom-call(bf16[768,640]{1,0:T(8,128)(2,1)} %get-tuple-element.128.refs_0_, bf16[768,512]{1,0:T(8,128)(2,1)} %get-tuple-element.129.refs_1_, bf16[8,144,896]{2,1,0:T(8,128)(2,1)} %copy-done.3, f32[768,768]{1,0:T(8,128)} %get-tuple-element.192.refs_3_, ...), custom_call_target="tpu_custom_call" | custom-call | flops 1585446912 | bytes 9437184 | tf_op jit(solution)/shard_map/finish_outputs/pallas_call | solution.py:723
  297.0 10.4 %collective-permute-done.11 = bf16[1,96,1536]{2,1,0:T(8,128)(2,1)S(1)} collective-permute-done((bf16[1,96,1536]{2,1,0:T(8,128)(2,1)}, bf16[1,96,1536]{2,1,0:T(8,128)(2,1)S(1)}, u32[]{:S(2)}, u32[]{:S(2)}) %collective-permute-start.11) | collective-permute-done | bytes 294944 | tf_op jit(solution)/shard_map/ppermute | solution.py:824
  315.0 6.7 %collective-permute-done.14.refs_1_ = bf16[1,24,3200]{2,1,0:T(8,128)(2,1)S(1)} collective-permute-done((bf16[1,24,3200]{2,1,0:T(8,128)(2,1)}, bf16[1,24,3200]{2,1,0:T(8,128)(2,1)S(1)}, u32[]{:S(2)}, u32[]{:S(2)}) %collective-permute-start.14) | collective-permute-done | bytes 153632 | tf_op jit(solution)/shard_map/ppermute | solution.py:824
  321.7 3.8 collective-permute-done.16.refs_3_
  333.2 9.4 %input_gradient.1 = f32[768,768]{1,0:T(8,128)} custom-call(bf16[768,768]{1,0:T(8,128)(2,1)} %bitcast.69, f32[1,768]{1,0:T(1,128)} %broadcast_in_dim.48.gain_ref.scale_ref, f32[768,768]{1,0:T(8,128)} %get-tuple-element.205.dhidden_ref, bf16[768,2304]{1,0:T(8,128)(2,1)} %w_ref.5, bf16[768,768]{1,0:T(8,128)(2,1)} %get-tuple-element.206.refs_0_, ...), custom_call_target="tpu_custom_call" | custom-call | flops 2717908992 | bytes 12976128 | tf_op jit(solution)/shard_map/input_gradient/pallas_call | solution.py:765
  352.9 3.4 fusion.7
  356.3 7.7 %collective-permute-done.20.refs_1_ = bf16[4,24,3200]{2,1,0:T(8,128)(2,1)S(1)} collective-permute-done((bf16[4,24,3200]{2,1,0:T(8,128)(2,1)}, bf16[4,24,3200]{2,1,0:T(8,128)(2,1)S(1)}, u32[]{:S(2)}, u32[]{:S(2)}) %collective-permute-start.20) | collective-permute-done | bytes 614432 | tf_op jit(solution)/shard_map/ppermute | solution.py:824
  364.0 10.2 %collective-permute-done.21.refs_2_ = bf16[4,24,3200]{2,1,0:T(8,128)(2,1)S(1)} collective-permute-done((bf16[4,24,3200]{2,1,0:T(8,128)(2,1)}, bf16[4,24,3200]{2,1,0:T(8,128)(2,1)S(1)}, u32[]{:S(2)}, u32[]{:S(2)}) %collective-permute-start.21) | collective-permute-done | bytes 614432 | tf_op jit(solution)/shard_map/ppermute | solution.py:824
  384.8 10.2 %unpack_sums.1 = (f32[768,768]{1,0:T(8,128)}, f32[768,2304]{1,0:T(8,128)}, f32[12,768]{1,0:T(8,128)}, f32[2,2,768]{2,1,0:T(2,128)}, f32[2,768]{1,0:T(2,128)}, /*index=5*/f32[768]{0:T(1024)}, f32[768]{0:T(1024)}) custom-call(s32[3]{0:T(128)} %pad_add_fusion.index_ref, bf16[4,4,24,3200]{3,2,1,0:T(8,128)(2,1)} %bitcast.70, bf16[4,4,24,3200]{3,2,1,0:T(8,128)(2,1)} %bitcast.108, ...), custom_call_target="tpu_custom_call" | custom-call | bytes 21233664 | tf_op jit(solution)/shard_map/unpack_sums/pallas_call | solution.py:901
  (151 shorter events, 88.6 us)
Async XLA Ops:
  17.0 55.6 %all-to-all-start = ((bf16[8,144,896]{2,1,0:T(8,128)(2,1)}), bf16[8,144,896]{2,1,0:T(8,128)(2,1)}, u32[]{:S(2)}, u32[]{:S(2)}) async-start(bf16[8,144,896]{2,1,0:T(8,128)(2,1)} %get-tuple-element.132), calls=%async_computation | async-start | bytes 4128768 | tf_op jit(solution)/shard_map/all_to_all | solution.py:940
  25.9 13.2 %collective-permute-start.2 = (bf16[256,768]{1,0:T(8,128)(2,1)}, bf16[256,768]{1,0:T(8,128)(2,1)}, u32[]{:S(2)}, u32[]{:S(2)}) collective-permute-start(bf16[256,768]{1,0:T(8,128)(2,1)} %slice_bitcast_fusion), channel_id=1, source_target_pairs={{0,24},{8,16},{16,8},{24,0},{1,25},{9,17},{17,9},{25,1},{2,26},{10... | collective-permute-start | bytes 1179656 | tf_op jit(solution)/shard_map/ppermute | solution.py:948
  28.4 18.7 %collective-permute-start.1 = (bf16[256,768]{1,0:T(8,128)(2,1)}, bf16[256,768]{1,0:T(8,128)(2,1)}, u32[]{:S(2)}, u32[]{:S(2)}) collective-permute-start(bf16[256,768]{1,0:T(8,128)(2,1)} %slice_bitcast_fusion), channel_id=1, source_target_pairs={{0,16},{8,24},{16,0},{24,8},{1,17},{9,25},{17,1},{25,9},{2,18},{10... | collective-permute-start | bytes 1179656 | tf_op jit(solution)/shard_map/ppermute | solution.py:948
  28.9 18.3 %collective-permute-start = (bf16[256,768]{1,0:T(8,128)(2,1)}, bf16[256,768]{1,0:T(8,128)(2,1)}, u32[]{:S(2)}, u32[]{:S(2)}) collective-permute-start(bf16[256,768]{1,0:T(8,128)(2,1)} %slice_bitcast_fusion), channel_id=1, source_target_pairs={{0,8},{8,0},{16,24},{24,16},{1,9},{9,1},{17,25},{25,17},{2,10},{10... | collective-permute-start | bytes 1179656 | tf_op jit(solution)/shard_map/ppermute | solution.py:948
  79.5 27.4 %all-to-all-start.3 = ((bf16[8,64,768]{2,1,0:T(8,128)(2,1)}), bf16[8,64,768]{2,1,0:T(8,128)(2,1)S(1)}, u32[]{:S(2)}, u32[]{:S(2)}) async-start(bf16[8,64,768]{2,1,0:T(8,128)(2,1)} %bitcast.123), calls=%async_computation.3 | async-start | bytes 1572864 | tf_op jit(solution)/shard_map/all_to_all | solution.py:940
  107.0 30.3 %all-to-all-start.1 = ((bf16[8,80,768]{2,1,0:T(8,128)(2,1)}), bf16[8,80,768]{2,1,0:T(8,128)(2,1)S(1)}, u32[]{:S(2)}, u32[]{:S(2)}) async-start(bf16[8,80,768]{2,1,0:T(8,128)(2,1)} %bitcast.8), calls=%async_computation.1 | async-start | bytes 1966080 | tf_op jit(solution)/shard_map/all_to_all | solution.py:940
  137.3 24.7 %all-to-all-start.4 = ((bf16[8,64,768]{2,1,0:T(8,128)(2,1)}), bf16[8,64,768]{2,1,0:T(8,128)(2,1)S(1)}, u32[]{:S(2)}, u32[]{:S(2)}) async-start(bf16[8,64,768]{2,1,0:T(8,128)(2,1)} %bitcast.124), calls=%async_computation.4 | async-start | bytes 1572864 | tf_op jit(solution)/shard_map/all_to_all | solution.py:943
  162.0 30.4 %all-to-all-start.2 = ((bf16[8,80,768]{2,1,0:T(8,128)(2,1)}), bf16[8,80,768]{2,1,0:T(8,128)(2,1)S(1)}, u32[]{:S(2)}, u32[]{:S(2)}) async-start(bf16[8,80,768]{2,1,0:T(8,128)(2,1)} %bitcast.117), calls=%async_computation.2 | async-start | bytes 1966080 | tf_op jit(solution)/shard_map/all_to_all | solution.py:943
  167.2 183.3 %reduce-scatter.5.cloned.1.call-start = ((), (), s32[]{:S(2)}) async-start(), calls=%async_computation.9 | async-start | bytes 3932160 | tf_op jit(solution)/shard_map/reduce_scatter | solution.py:989
  192.4 160.4 %reduce-scatter.3.cloned.1.call-start = ((), (), s32[]{:S(2)}) async-start(), calls=%async_computation.8 | async-start | bytes 7864320 | tf_op jit(solution)/shard_map/reduce_scatter | solution.py:988
  193.4 92.8 %all-to-all-start.5 = ((bf16[8,144,896]{2,1,0:T(8,128)(2,1)}), bf16[8,144,896]{2,1,0:T(8,128)(2,1)S(1)}, u32[]{:S(2)}, u32[]{:S(2)}) async-start(bf16[8,144,896]{2,1,0:T(8,128)(2,1)} %pad_maximum_fusion), calls=%async_computation.5 | async-start | bytes 4128768 | tf_op jit(solution)/shard_map/all_to_all | solution.py:943
  227.4 11.7 %collective-permute-start.3 = (bf16[384,1664]{1,0:T(8,128)(2,1)}, bf16[384,1664]{1,0:T(8,128)(2,1)S(1)}, u32[]{:S(2)}, u32[]{:S(2)}) collective-permute-start(bf16[384,1664]{1,0:T(8,128)(2,1)} %get-tuple-element.172), channel_id=1, source_target_pairs={{0,1},{1,0},{2,3},{3,2},{4,5},{5,4},{6,7},{7,6},{8,9},{9,8},{10,11... | collective-permute-start | bytes 3833864 | tf_op jit(solution)/shard_map/ppermute | solution.py:999
  242.9 30.1 %collective-permute-start.4 = (bf16[1,96,1664]{2,1,0:T(8,128)(2,1)}, bf16[1,96,1664]{2,1,0:T(8,128)(2,1)S(1)}, u32[]{:S(2)}, u32[]{:S(2)}) collective-permute-start(bf16[1,96,1664]{2,1,0:T(8,128)(2,1)} %get-tuple-element.186), channel_id=1, source_target_pairs={{0,2},{1,3},{2,0},{3,1},{4,6},{5,7},{6,4},{7,5},{8,10},{9,11},{10,... | collective-permute-start | bytes 958472 | tf_op jit(solution)/shard_map/ppermute | solution.py:824
  244.7 28.3 %collective-permute-start.5 = (bf16[1,96,1664]{2,1,0:T(8,128)(2,1)}, bf16[1,96,1664]{2,1,0:T(8,128)(2,1)S(1)}, u32[]{:S(2)}, u32[]{:S(2)}) collective-permute-start(bf16[1,96,1664]{2,1,0:T(8,128)(2,1)} %get-tuple-element.187), channel_id=1, source_target_pairs={{0,4},{1,5},{2,6},{3,7},{4,0},{5,1},{6,2},{7,3},{8,12},{9,13},{10,... | collective-permute-start | bytes 958472 | tf_op jit(solution)/shard_map/ppermute | solution.py:824
  247.1 26.0 %collective-permute-start.6 = (bf16[1,96,1664]{2,1,0:T(8,128)(2,1)}, bf16[1,96,1664]{2,1,0:T(8,128)(2,1)S(1)}, u32[]{:S(2)}, u32[]{:S(2)}) collective-permute-start(bf16[1,96,1664]{2,1,0:T(8,128)(2,1)} %get-tuple-element.188), channel_id=1, source_target_pairs={{0,6},{1,7},{2,4},{3,5},{4,2},{5,3},{6,0},{7,1},{8,14},{9,15},{10,... | collective-permute-start | bytes 958472 | tf_op jit(solution)/shard_map/ppermute | solution.py:824
  273.9 3.1 collective-permute-start.7
  273.9 20.3 %collective-permute-start.8 = (bf16[256,768]{1,0:T(8,128)(2,1)}, bf16[256,768]{1,0:T(8,128)(2,1)}, u32[]{:S(2)}, u32[]{:S(2)}) collective-permute-start(bf16[256,768]{1,0:T(8,128)(2,1)} %get-tuple-element.197), channel_id=1, source_target_pairs={{0,8},{8,0},{16,24},{24,16},{1,9},{9,1},{17,25},{25,17},{2,10},{10... | collective-permute-start | bytes 1179656 | tf_op jit(solution)/shard_map/ppermute | solution.py:1012
  275.5 18.8 %collective-permute-start.9 = (bf16[256,768]{1,0:T(8,128)(2,1)}, bf16[256,768]{1,0:T(8,128)(2,1)}, u32[]{:S(2)}, u32[]{:S(2)}) collective-permute-start(bf16[256,768]{1,0:T(8,128)(2,1)} %get-tuple-element.198), channel_id=1, source_target_pairs={{0,16},{8,24},{16,0},{24,8},{1,17},{9,25},{17,1},{25,9},{2,18},{10... | collective-permute-start | bytes 1179656 | tf_op jit(solution)/shard_map/ppermute | solution.py:1012
  280.7 16.2 %collective-permute-start.10 = (bf16[1,96,1536]{2,1,0:T(8,128)(2,1)}, bf16[1,96,1536]{2,1,0:T(8,128)(2,1)S(1)}, u32[]{:S(2)}, u32[]{:S(2)}) collective-permute-start(bf16[1,96,1536]{2,1,0:T(8,128)(2,1)} %get-tuple-element.201), channel_id=1, source_target_pairs={{0,2},{1,3},{2,0},{3,1},{4,6},{5,7},{6,4},{7,5},{8,10},{9,11},{10,... | collective-permute-start | bytes 884744 | tf_op jit(solution)/shard_map/ppermute | solution.py:824
  283.8 23.6 %collective-permute-start.11 = (bf16[1,96,1536]{2,1,0:T(8,128)(2,1)}, bf16[1,96,1536]{2,1,0:T(8,128)(2,1)S(1)}, u32[]{:S(2)}, u32[]{:S(2)}) collective-permute-start(bf16[1,96,1536]{2,1,0:T(8,128)(2,1)} %get-tuple-element.202), channel_id=1, source_target_pairs={{0,4},{1,5},{2,6},{3,7},{4,0},{5,1},{6,2},{7,3},{8,12},{9,13},{10,... | collective-permute-start | bytes 884744 | tf_op jit(solution)/shard_map/ppermute | solution.py:824
  284.8 22.6 %collective-permute-start.12 = (bf16[1,96,1536]{2,1,0:T(8,128)(2,1)}, bf16[1,96,1536]{2,1,0:T(8,128)(2,1)S(1)}, u32[]{:S(2)}, u32[]{:S(2)}) collective-permute-start(bf16[1,96,1536]{2,1,0:T(8,128)(2,1)} %get-tuple-element.203), channel_id=1, source_target_pairs={{0,6},{1,7},{2,4},{3,5},{4,2},{5,3},{6,0},{7,1},{8,14},{9,15},{10,... | collective-permute-start | bytes 884744 | tf_op jit(solution)/shard_map/ppermute | solution.py:824
  294.3 38.1 %collective-permute-start.13 = (bf16[256,768]{1,0:T(8,128)(2,1)S(1)}, bf16[256,768]{1,0:T(8,128)(2,1)S(1)}, u32[]{:S(2)}, u32[]{:S(2)}) collective-permute-start(bf16[256,768]{1,0:T(8,128)(2,1)S(1)} %copy-done.32), channel_id=1, source_target_pairs={{0,24},{8,16},{16,8},{24,0},{1,25},{9,17},{17,9},{25,1},{2,26},{10... | collective-permute-start | bytes 1179656 | tf_op jit(solution)/shard_map/ppermute | solution.py:1012
  310.9 10.8 %collective-permute-start.14 = (bf16[1,24,3200]{2,1,0:T(8,128)(2,1)}, bf16[1,24,3200]{2,1,0:T(8,128)(2,1)S(1)}, u32[]{:S(2)}, u32[]{:S(2)}) collective-permute-start(bf16[1,24,3200]{2,1,0:T(8,128)(2,1)} %get-tuple-element.221), channel_id=1, source_target_pairs={{0,8},{8,0},{16,24},{24,16},{1,9},{9,1},{17,25},{25,17},{2,10},{10... | collective-permute-start | bytes 460808 | tf_op jit(solution)/shard_map/ppermute | solution.py:824
  312.5 9.2 %collective-permute-start.15 = (bf16[1,24,3200]{2,1,0:T(8,128)(2,1)}, bf16[1,24,3200]{2,1,0:T(8,128)(2,1)S(1)}, u32[]{:S(2)}, u32[]{:S(2)}) collective-permute-start(bf16[1,24,3200]{2,1,0:T(8,128)(2,1)} %get-tuple-element.222), channel_id=1, source_target_pairs={{0,16},{8,24},{16,0},{24,8},{1,17},{9,25},{17,1},{25,9},{2,18},{10... | collective-permute-start | bytes 460808 | tf_op jit(solution)/shard_map/ppermute | solution.py:824
  313.7 11.8 %collective-permute-start.16 = (bf16[1,24,3200]{2,1,0:T(8,128)(2,1)}, bf16[1,24,3200]{2,1,0:T(8,128)(2,1)S(1)}, u32[]{:S(2)}, u32[]{:S(2)}) collective-permute-start(bf16[1,24,3200]{2,1,0:T(8,128)(2,1)} %get-tuple-element.223), channel_id=1, source_target_pairs={{0,24},{8,16},{16,8},{24,0},{1,25},{9,17},{17,9},{25,1},{2,26},{10... | collective-permute-start | bytes 460808 | tf_op jit(solution)/shard_map/ppermute | solution.py:824
  328.0 14.6 %collective-permute-start.17 = (bf16[1,24,3200]{2,1,0:T(8,128)(2,1)}, bf16[1,24,3200]{2,1,0:T(8,128)(2,1)S(1)}, u32[]{:S(2)}, u32[]{:S(2)}) collective-permute-start(bf16[1,24,3200]{2,1,0:T(8,128)(2,1)} %sum_pieces.7.refs_0_), channel_id=1, source_target_pairs={{0,2},{1,3},{2,0},{3,1},{4,6},{5,7},{6,4},{7,5},{8,10},{9,11},{10,... | collective-permute-start | bytes 460808 | tf_op jit(solution)/shard_map/ppermute | solution.py:824
  329.5 14.1 %collective-permute-start.18 = (bf16[1,24,3200]{2,1,0:T(8,128)(2,1)}, bf16[1,24,3200]{2,1,0:T(8,128)(2,1)S(1)}, u32[]{:S(2)}, u32[]{:S(2)}) collective-permute-start(bf16[1,24,3200]{2,1,0:T(8,128)(2,1)} %sum_pieces.7.refs_0_), channel_id=1, source_target_pairs={{0,4},{1,5},{2,6},{3,7},{4,0},{5,1},{6,2},{7,3},{8,12},{9,13},{10,... | collective-permute-start | bytes 460808 | tf_op jit(solution)/shard_map/ppermute | solution.py:824
  331.9 11.7 %collective-permute-start.19 = (bf16[1,24,3200]{2,1,0:T(8,128)(2,1)}, bf16[1,24,3200]{2,1,0:T(8,128)(2,1)S(1)}, u32[]{:S(2)}, u32[]{:S(2)}) collective-permute-start(bf16[1,24,3200]{2,1,0:T(8,128)(2,1)} %sum_pieces.7.refs_0_), channel_id=1, source_target_pairs={{0,6},{1,7},{2,4},{3,5},{4,2},{5,3},{6,0},{7,1},{8,14},{9,15},{10,... | collective-permute-start | bytes 460808 | tf_op jit(solution)/shard_map/ppermute | solution.py:824
  347.0 17.0 %collective-permute-start.20 = (bf16[4,24,3200]{2,1,0:T(8,128)(2,1)}, bf16[4,24,3200]{2,1,0:T(8,128)(2,1)S(1)}, u32[]{:S(2)}, u32[]{:S(2)}) collective-permute-start(bf16[4,24,3200]{2,1,0:T(8,128)(2,1)} %stack_pieces.2.refs_0_), channel_id=1, source_target_pairs={{0,8},{8,0},{16,24},{24,16},{1,9},{9,1},{17,25},{25,17},{2,10},{10... | collective-permute-start | bytes 1843208 | tf_op jit(solution)/shard_map/ppermute | solution.py:824
  347.5 26.7 %collective-permute-start.21 = (bf16[4,24,3200]{2,1,0:T(8,128)(2,1)}, bf16[4,24,3200]{2,1,0:T(8,128)(2,1)S(1)}, u32[]{:S(2)}, u32[]{:S(2)}) collective-permute-start(bf16[4,24,3200]{2,1,0:T(8,128)(2,1)} %stack_pieces.2.refs_0_), channel_id=1, source_target_pairs={{0,16},{8,24},{16,0},{24,8},{1,17},{9,25},{17,1},{25,9},{2,18},{10... | collective-permute-start | bytes 1843208 | tf_op jit(solution)/shard_map/ppermute | solution.py:824
  348.3 25.9 %collective-permute-start.22 = (bf16[4,24,3200]{2,1,0:T(8,128)(2,1)}, bf16[4,24,3200]{2,1,0:T(8,128)(2,1)S(1)}, u32[]{:S(2)}, u32[]{:S(2)}) collective-permute-start(bf16[4,24,3200]{2,1,0:T(8,128)(2,1)} %stack_pieces.2.refs_0_), channel_id=1, source_target_pairs={{0,24},{8,16},{16,8},{24,0},{1,25},{9,17},{17,9},{25,1},{2,26},{10... | collective-permute-start | bytes 1843208 | tf_op jit(solution)/shard_map/ppermute | solution.py:824
  378.5 4.9 %collective-permute-start.23 = (bf16[16,24,3200]{2,1,0:T(8,128)(2,1)}, bf16[16,24,3200]{2,1,0:T(8,128)(2,1)S(1)}, u32[]{:S(2)}, u32[]{:S(2)}) collective-permute-start(bf16[16,24,3200]{2,1,0:T(8,128)(2,1)} %stack_pieces.3), channel_id=1, source_target_pairs={{0,1},{1,0},{2,3},{3,2},{4,5},{5,4},{6,7},{7,6},{8,9},{9,8},{10,11... | collective-permute-start | bytes 7372808 | tf_op jit(solution)/shard_map/ppermute | solution.py:999
  (33 other events, 144.2 us)
Sparse Core Ops, SparseCore 0:
  192.6 42.0 reduce-scatter.4
  238.2 84.6 reduce-scatter.2

commit v6 on v5

--- a/solution.py
+++ b/solution.py
@@ -318,16 +318,17 @@
     tok, width = grad_ref.shape
     count = len(groups)
     turned_refs, chosen_refs, early_ref = out_refs[:count], out_refs[count : 2 * count], out_refs[2 * count]
+    capacity = early_ref.shape[1] - SMALL
     expert = lax.broadcasted_iota(jnp.int32, (16, tok), 0)
-    ids = jnp.concatenate([ids_ref[...].astype(f32), jnp.zeros((tok, EXTRA - 2), f32)], axis=1).T.astype(jnp.int32)
-    ids = [ids[k : k + 1, :] for k in range(2)]
+    ids = [ids_ref[k : k + 1, :] for k in range(2)]
     names = [row == expert for row in ids]
     both = jnp.where(names[0] | names[1], 1.0, 0.0).astype(bf16)
     earlier = lax.broadcasted_iota(jnp.int32, (tok, tok), 0) < lax.broadcasted_iota(jnp.int32, (tok, tok), 1)
     before = dot_nn(both, jnp.where(earlier, 1.0, 0.0).astype(bf16))
-    pieces = [piece.astype(f32) for piece in split_low(jnp.concatenate([prev_ref[...], jnp.zeros((tok, EXTRA - ALL_EXPERTS), f32)], axis=1), 3)]
-    extra = (pieces[0] + pltpu.roll(pieces[1], 16, 1) + pltpu.roll(pieces[2], 32, 1)).astype(bf16)
+    pieces = [piece.astype(f32) for piece in split_low(prev_ref[...], 3)]
+    extra = jnp.concatenate(pieces + [jnp.zeros((EXTRA - 3 * ALL_EXPERTS, tok), f32)], axis=0).T.astype(bf16)
     slot = [jnp.sum(jnp.where(n, before, 0.0), axis=0, keepdims=True).astype(jnp.int32) for n in names]
+    extras = []
     for (first, size), turned_ref, chosen_ref in zip(groups, turned_refs, chosen_refs):
         spots = lax.broadcasted_iota(jnp.int32, (FFN_EXPERTS * size, tok), 0)
         hit = None
@@ -339,28 +340,48 @@
         turned_ref[...] = turned
         chosen_ref[...] = turned.T
         grads = dot_nn(turned, grad_ref[...]).astype(bf16)
-        extras = dot_nn(turned, extra).astype(bf16)
+        extras.append(dot_nn(turned, extra))
         for e in range(FFN_EXPERTS):
-            early_ref[e, first : first + size, 0:width] = grads[e * size : (e + 1) * size]
-            early_ref[e, first : first + size, width : width + EXTRA] = extras[e * size : (e + 1) * size]
+            early_ref[e, first : first + size, :] = grads[e * size : (e + 1) * size]
+    third = capacity // 3
+    for e in range(FFN_EXPERTS):
+        rows = jnp.concatenate([x[e * size : (e + 1) * size] for x, (_, size) in zip(extras, groups)], axis=0)
+        rows = rows[0:third] + pltpu.roll(rows[third : 2 * third], 40, 1) + pltpu.roll(rows[2 * third : capacity], 80, 1)
+        early_ref[e, capacity : capacity + SMALL, :] = jnp.zeros((SMALL, width), bf16)
+        for g in range(third // SMALL):
+            early_ref[e, capacity : capacity + SMALL, g * EXTRA : (g + 1) * EXTRA] = rows[g * SMALL : (g + 1) * SMALL].astype(bf16)
 
 
 def route_plan(home, ids, grad, prev, groups):
     tok, width = grad.shape
     counts = [FFN_EXPERTS * size for _, size in groups]
     whole = pl.BlockSpec(memory_space=pltpu.VMEM)
+    early = (FFN_EXPERTS, sum(counts) // FFN_EXPERTS + SMALL, width)
     out = pl.pallas_call(
         functools.partial(route_kernel, groups),
         in_specs=[pl.BlockSpec(memory_space=pltpu.SMEM), whole, whole, whole],
         out_specs=[whole] * (2 * len(groups) + 1),
         out_shape=[jax.ShapeDtypeStruct((n, tok), bf16) for n in counts]
         + [jax.ShapeDtypeStruct((tok, n), bf16) for n in counts]
-        + [jax.ShapeDtypeStruct((FFN_EXPERTS, sum(counts) // FFN_EXPERTS, width + EXTRA), bf16)],
+        + [jax.ShapeDtypeStruct(early, bf16)],
         compiler_params=pltpu.CompilerParams(vmem_limit_bytes=60 * 2**20),
         cost_estimate=pl.CostEstimate(flops=2 * sum(counts) * tok * (width + EXTRA), bytes_accessed=4 * sum(counts) * width, transcendentals=0),
         name="route_plan",
     )(home, ids, grad, prev)
     return out[: len(groups)], out[len(groups) : -1], out[-1]
+
+
+def router_inputs(early_ref, slots):
+    capacity = early_ref.shape[1] - SMALL
+    groups = capacity // 3 // SMALL
+    rows = []
+    for sender in range(early_ref.shape[0]):
+        packed = early_ref[sender, capacity : capacity + SMALL, :].astype(f32)
+        third = jnp.concatenate([packed[:, g * EXTRA : (g + 1) * EXTRA] for g in range(groups)], axis=0)
+        every = jnp.concatenate([third, pltpu.roll(third, EXTRA - 40, 1), pltpu.roll(third, EXTRA - 80, 1)], axis=0)
+        rows.append(every[slots])
+    rows = jnp.concatenate(rows, axis=0)
+    return rows + pltpu.roll(rows, EXTRA - ALL_EXPERTS, 1) + pltpu.roll(rows, EXTRA - 2 * ALL_EXPERTS, 1)
 
 
 def expert_kernel(group, home_ref, rows_ref, early_ref, router_ref, wg_ref, wu_ref, wd_ref,
@@ -373,9 +394,7 @@
 
     @pl.when(step == 0)
     def _():
-        extra = early_ref[:, slots, width : width + EXTRA].astype(f32).reshape(-1, EXTRA)
-        logits = extra + pltpu.roll(extra, EXTRA - 16, 1) + pltpu.roll(extra, EXTRA - 32, 1)
-        logits = logits + dot_nn(rows_ref[...], router_ref[...])
+        logits = router_inputs(early_ref, slots) + dot_nn(rows_ref[...], router_ref[...])
         logits = jnp.where(lane < ALL_EXPERTS, logits, NEG)
         unnormed = jnp.exp(logits - jnp.max(logits, axis=1, keepdims=True))
         probs = unnormed / jnp.sum(unnormed, axis=1, keepdims=True)
@@ -775,6 +794,35 @@
     )(x, gain, d_hidden, w_qkv, *grads, *far)
 
 
+def far_kernel(count, gain_ref, wk_ref, wv_ref, *refs):
+    far, (act_ref, kv_ref) = refs[:count], refs[count:]
+    width = wk_ref.shape[0]
+    for k, ref in enumerate(far):
+
+        @pl.when(pl.program_id(0) == k)
+        def _():
+            x = ref[...].astype(f32)
+            act = (x * inverse_rms(x) * gain_ref[...]).astype(bf16)
+            act_ref[...] = act
+            kv_ref[:, 0:width] = dot_nn(act, wk_ref[...]).astype(bf16)
+            kv_ref[:, width : 2 * width] = dot_nn(act, wv_ref[...]).astype(bf16)
+
+
+def far_projection(far, gain, w_qkv):
+    rows, width = far[0].shape
+    count = len(far)
+    return pl.pallas_call(
+        functools.partial(far_kernel, count),
+        grid=(count,),
+        in_specs=[fixed(gain), pl.BlockSpec((width, width), lambda i: (0, 1)), pl.BlockSpec((width, width), lambda i: (0, 2))] + [fixed(f) for f in far],
+        out_specs=[pl.BlockSpec((rows, width), lambda i: (i, 0)), pl.BlockSpec((rows, 2 * width), lambda i: (i, 0))],
+        out_shape=[jax.ShapeDtypeStruct((count * rows, width), bf16), jax.ShapeDtypeStruct((count * rows, 2 * width), bf16)],
+        compiler_params=pltpu.CompilerParams(vmem_limit_bytes=60 * 2**20),
+        cost_estimate=pl.CostEstimate(flops=4 * count * rows * width * width, bytes_accessed=2 * width * (4 * count * rows + 2 * width), transcendentals=0),
+        name="far_projection",
+    )(gain, w_qkv, w_qkv, *far)
+
+
 def xor_pairs(size, mask):
     return [(i, i ^ mask) for i in range(size)]
 
@@ -848,16 +896,22 @@
     )(*pieces)
 
 
-def unpack_kernel(left, index_ref, own_ref, other_ref, w_ref, scale_ref, out_ref, qkv_ref, router_ref, mixing_ref, vec_ref, gain_ref, attn_ref, small):
+def unpack_kernel(left, last, index_ref, *refs):
+    pieces, (w_ref, *refs) = refs[:4], refs[4:]
+    if last:
+        scale_ref, first_ref, _, _, out_ref, qkv_ref, router_ref, mixing_ref, vec_ref, gain_ref, attn_ref, small = refs
+    else:
+        out_ref, qkv_ref, small = refs
     width = out_ref.shape[1]
-    piece = own_ref.shape[2]
-    mine = pl.program_id(0) == index_ref[0]
+    size = pieces[0].shape[1]
     lane = lax.broadcasted_iota(jnp.int32, (1, EXTRA), 1)
-    block = pl.program_id(0) * 4 + pl.program_id(1)
+    step = pl.program_id(0)
+    half = index_ref[0]
+    base = (half * width // 2 if last else 0) + step * 4 * size
     for k in range(4):
-        rows = slice(k * piece, (k + 1) * piece)
-        at_ctx = k ^ index_ref[1]
-        total = jnp.where(mine, own_ref[at_ctx, 0, :, :], other_ref[at_ctx, 0, :, :]).astype(f32)
+        at_ctx = pl.multiple_of((k ^ index_ref[1]) * size, size)
+        rows = pl.ds(at_ctx, size)
+        total = pieces[k][0].astype(f32)
         out_ref[rows, :] = total[:, left : left + width]
         gain = None
         for p in range(3):
@@ -869,49 +923,57 @@
                 part = value * w_ref[rows, columns].astype(f32)
                 gain = part if gain is None else gain + part
         gain = jnp.sum(gain, axis=1, keepdims=True)
-        small[pl.ds(block * 4 * piece + k * piece, piece), :] = total[:, left + width : left + width + EXTRA] + place(gain, lane, EXTRA - 1)
-
-    @pl.when(block == 7)
-    def _():
-        turned = small[...].T
-        router_ref[...] = turned[0:ALL_EXPERTS]
-        mixing_ref[0] = turned[16:18]
-        mixing_ref[1] = turned[18:20]
-        vec_ref[...] = turned[20:22]
-        gain_ref[...] = turned[24]
-        attn_ref[...] = (turned[EXTRA - 1 : EXTRA] / scale_ref[...])[0]
-
-
-def unpack(index, own, other, w_qkv, scale, left):
+        small[pl.ds(pl.multiple_of(base + at_ctx, size), size), :] = total[:, left + width : left + width + EXTRA] + place(gain, lane, EXTRA - 1)
+    if last:
+
+        @pl.when(step == 3)
+        def _():
+            small[pl.ds(pl.multiple_of((1 - half) * (width // 2), width // 2), width // 2), :] = first_ref[...]
+            turned = small[...].T
+            router_ref[...] = turned[0:ALL_EXPERTS]
+            mixing_ref[0] = turned[16:18]
+            mixing_ref[1] = turned[18:20]
+            vec_ref[...] = turned[20:22]
+            gain_ref[...] = turned[24]
+            attn_ref[...] = (turned[EXTRA - 1 : EXTRA] / scale_ref[...])[0]
+
+
+def unpack_half(index, pieces, w_qkv, left, scale, before):
     width = w_qkv.shape[0]
-    piece = width // 32
-    block = 4 * piece
-    own, other = own.reshape(4, 4, piece, -1), other.reshape(4, 4, piece, -1)
-    row = lambda c, a, s: (c * 4 + a, 0)
-
-    def source(core_of):
-        def at(c, a, s):
-            core = core_of(s[0])
-            return 0, jnp.where(c == core, a, jnp.where(c < core, 0, 3)) ^ s[2], 0, 0
-
-        return pl.BlockSpec((4, 1, piece, own.shape[3]), at)
-
-    whole = lambda shape: pl.BlockSpec(shape, lambda c, a, s: (0,) * len(shape))
-    shapes = ((ALL_EXPERTS, width), (2, 2, width), (2, width), (width,), (width,))
-    return pl.pallas_call(
-        functools.partial(unpack_kernel, left),
+    size = width // 32
+    last = before is not None
+    row = lambda a, s: (s[0] * 4 + a, 0)
+    source = pl.BlockSpec((1, size, pieces[0].shape[2]), lambda a, s: (a ^ s[2], 0, 0))
+    whole = lambda shape: pl.BlockSpec(shape, lambda a, s: (0,) * len(shape))
+    in_specs = [source] * 4 + [pl.BlockSpec((4 * size, 3 * width), row)]
+    out_specs = [pl.BlockSpec((4 * size, width), row), pl.BlockSpec((4 * size, 3 * width), row)]
+    out_shape = [jax.ShapeDtypeStruct((width, width), f32), jax.ShapeDtypeStruct((width, 3 * width), f32)]
+    arrays = [*pieces, w_qkv]
+    if last:
+        shapes = ((ALL_EXPERTS, width), (2, 2, width), (2, width), (width,), (width,))
+        in_specs += [whole((1, width)), whole((width // 2, EXTRA))] + [pl.BlockSpec(memory_space=pl.ANY)] * 2
+        arrays += [scale, before[2], before[0], before[1]]
+        scratch = [pltpu.VMEM((width, EXTRA), f32)]
+        aliases = {len(arrays) - 1: 0, len(arrays): 1}
+    else:
+        shapes = ((width // 2, EXTRA),)
+        scratch = []
+        aliases = {}
+    return pl.pallas_call(
+        functools.partial(unpack_kernel, left, last),
         grid_spec=pltpu.PrefetchScalarGridSpec(
             num_scalar_prefetch=1,
-            grid=(2, 4),
-            in_specs=[source(lambda core: core), source(lambda core: 1 - core), pl.BlockSpec((block, 3 * width), row), whole((1, width))],
-            out_specs=[pl.BlockSpec((block, width), row), pl.BlockSpec((block, 3 * width), row), *[whole(s) for s in shapes]],
-            scratch_shapes=[pltpu.VMEM((width, EXTRA), f32)],
+            grid=(4,),
+            in_specs=in_specs,
+            out_specs=out_specs + [whole(s) for s in shapes],
+            scratch_shapes=scratch,
         ),
-        out_shape=[jax.ShapeDtypeStruct((width, width), f32), jax.ShapeDtypeStruct((width, 3 * width), f32), *[jax.ShapeDtypeStruct(s, f32) for s in shapes]],
-        compiler_params=pltpu.CompilerParams(vmem_limit_bytes=60 * 2**20),
-        cost_estimate=pl.CostEstimate(flops=0, bytes_accessed=36 * width * width, transcendentals=0),
-        name="unpack_sums",
-    )(index, own, other, w_qkv, scale)
+        out_shape=out_shape + [jax.ShapeDtypeStruct(s, f32) for s in shapes],
+        input_output_aliases=aliases,
+        compiler_params=pltpu.CompilerParams(vmem_limit_bytes=60 * 2**20),
+        cost_estimate=pl.CostEstimate(flops=0, bytes_accessed=14 * width * width, transcendentals=0),
+        name="unpack_half",
+    )(index, *arrays)
 
 P = jax.sharding.PartitionSpec
 
@@ -945,29 +1007,28 @@
 
     x_low = inputs[0]
     upstream_low = out_grad[0]
-    far_rows = jnp.concatenate([lax.ppermute(x_low[:plen], "ctx", xor_pairs(n_ctx, k)) for k in range(1, n_ctx)], axis=0)
     flags = jnp.where((me_c ^ jnp.arange(1, n_ctx)) < me_c, 0.0, NEG).astype(f32)
 
     prev = prev_logits[0]
     mix = jnp.concatenate([router, jnp.zeros((width, 4), bf16), const_gate[0], const_gate[1], jnp.zeros((width, EXTRA - 20), bf16)], axis=1)
     router_pad = jnp.pad(router, ((0, 0), (0, EXTRA - ALL_EXPERTS)))
-    turned, chosen, early_sent = route_plan(home, routes[0], upstream_low, prev, groups)
+    turned, chosen, early_sent = route_plan(home, routes[0].T, upstream_low, prev.T, groups)
+    far = [lax.ppermute(x_low[:plen], "ctx", xor_pairs(n_ctx, k)) for k in range(1, n_ctx)]
 
     tokens_in = x_low.astype(f32)
     inverse_attn = rms_inverse(tokens_in)
     act_low = (tokens_in * inverse_attn * attn_gain).astype(bf16)
     projected = dot_nn(act_low, w_qkv).astype(bf16)
     early = deal(early_sent)
-    far_in = after(far_rows, projected).astype(f32)
-    act_far = (far_in * rms_inverse(far_in) * attn_gain).astype(bf16)
-    kv_far = dot_nn(act_far, w_qkv[:, width:]).astype(bf16)
+    act_t = turn(act_low)
+    act_far, kv_far = far_projection(after(far, projected, act_t), attn_gain[None], w_qkv)
 
     mixed_low, lse = attention_forward(flags, projected, kv_far, plen)
     mixed_low, early = lax.optimization_barrier((mixed_low, early))
     hidden, moe_low, sent = after_attention(mixed_low, x_low, w_out, moe_gain[None], turned)
     local_out, d_normed_local, probs, d_probs, small_local = local_part(hidden, moe_low, upstream_low, prev, routes[0], mix, moe_gain[None], const_vec)
-    act_t, far_t = turn(act_low), turn(act_far)
-    sent = [after(sent[0], local_out, d_normed_local, act_t, far_t), sent[1]]
+    far_t = turn(act_far)
+    sent = [after(sent[0], local_out, d_normed_local, far_t), sent[1]]
     got = [deal(part.reshape(FFN_EXPERTS, -1, width)) for part in sent]
 
     got = [part.reshape(-1, width) for part in got]
@@ -1027,15 +1088,17 @@
         far_back = far_back + [send_far(n_ctx - 1)]
     d_inputs = input_gradient([grads_1, grads_2, grads_3], x_low, attn_gain[None], d_hidden, w_qkv, far_back)
 
+    d_prev = d_logits[:ALL_EXPERTS].T[None]
     total_gate, total_up, total_down = sum_gate_up[0][None], sum_gate_up[1][None], sum_down[None]
     if dense:
         d_inputs, spread_z = lax.optimization_barrier((d_inputs, spread_z))
         column = stack_pieces(spread_z)
-        own = stack_pieces(after(spread(column, along_ctx), total_gate, total_up, total_down))
-        other = across(own)
-        out_sum, qkv_sum, d_router, d_mixing, d_const_vec, d_moe_gain, d_attn_gain = unpack(
-            jnp.stack([core[0], me_c, z]), own, other, w_qkv, attn_gain[None], left
-        )
+        own = after(spread(column, along_ctx), total_gate, total_up, total_down, d_prev)
+        other = [across(piece) for piece in own]
+        place_of = lambda half: jnp.stack([half, me_c, z])
+        first = unpack_half(place_of(core[0]), own, w_qkv, left, None, None)
+        first, other = lax.optimization_barrier((first, other))
+        out_sum, qkv_sum, d_router, d_mixing, d_const_vec, d_moe_gain, d_attn_gain = unpack_half(place_of(1 - core[0]), other, w_qkv, left, attn_gain[None], first)
     else:
         whole = lambda mine, theirs: jnp.where(core == 0, jnp.concatenate([mine, theirs], axis=0), jnp.concatenate([theirs, mine], axis=0))
         total_1, total_2 = [v.astype(f32) for v in lax.psum((whole(mine_1, theirs_1), whole(mine_2, theirs_2)), ("ctx", "exp"))]
@@ -1047,7 +1110,7 @@
     return (
         mixed_out[None],
         d_inputs[None],
-        d_logits[:ALL_EXPERTS].T[None],
+        d_prev,
         d_attn_gain,
         qkv_sum,
         out_sum,

time: 407 us -> 397 us (0.975)
  waiting for transfers between devices: 64.3 us -> 57.1 us
    pallas_call x1 -> x3, Pallas kernels: 10.2 us -> 18 us  [the longest x2 12.2 us: unpack_half(): pl.pallas_call(functools.partial(unpack_kernel, left, last), grid_spec=pl...]
    ppermute x3, waiting for transfers between devices: 9.1 us -> 3.67 us  [body(): lax.ppermute(x_low[:plen], 'ctx', xor_pairs(n_ctx, k))]
    unnamed x72 -> x80, local copies, waits for them, and re-layouts: 16 us -> 13.2 us
  transfers between devices with their start and end apart: 32 -> 35, of which waited for: 13 -> 12; matrix products, arithmetic and copies ran while one was open for 7% -> 6% of each run, Pallas kernels for 48% -> 52%
where the time goes in v6:
time: 397 us; the launch traced here: 393 us
  Pallas kernels  222 us (56%)
  starting transfers between devices  60.6 us (15%)
  waiting for transfers between devices  57.1 us (14%)
  local copies, waits for them, and re-layouts  23.5 us (6%)
  between operations  14.7 us (4%)
  other arithmetic  9.19 us (2%)
  matrix products  5.98 us (2%)
    pallas_call x3, Pallas kernels, attention_backward(): pl.pallas_call(functools.partial(attention_backward_kernel, plen, bool(st...  55.4 us
    ppermute x15, waiting for transfers between devices, swap(): lax.ppermute(pieces[k], axis, xor_pairs(size, unit * k))  39.6 us
    pallas_call x2, Pallas kernels, expert_pass(): pl.pallas_call(functools.partial(expert_kernel, group), grid=(ff // tile,...  38.6 us
    ppermute x15, starting transfers between devices, swap(): lax.ppermute(pieces[k], axis, xor_pairs(size, unit * k))  21.3 us
    pallas_call x1, Pallas kernels, attention_forward(): pl.pallas_call(functools.partial(attention_forward_kernel, plen), grid=(p...  19 us
    pallas_call x1, Pallas kernels, weight_gradients(): pl.pallas_call(functools.partial(weight_kernel, count), grid=(ff // tile,...  17.9 us
    all_to_all x3, starting transfers between devices, deal(): return lax.all_to_all(value, 'exp', 0, 0, tiled=True)  16.2 us
    pallas_call x1, Pallas kernels, local_part(): pl.pallas_call(local_kernel, grid=(tok // block,), in_specs=[tiles(width)...  13.8 us
  transfers between devices with their start and end apart: 35, of which 12 were waited for; matrix products, arithmetic and copies ran while one was open for 6% of the time, Pallas kernels for 52%

profile of v6, /device:TPU:0, one launch (start us, length us, event | category | flops | bytes accessed | tf_op | source)
XLA Modules:
  0.0 392.7 jit_solution(18083308212368151677)
XLA Ops:
  10.2 5.7 %route_plan.1 = (bf16[640,768]{1,0:T(8,128)(2,1)}, bf16[512,768]{1,0:T(8,128)(2,1)}, bf16[768,640]{1,0:T(8,128)(2,1)}, bf16[768,512]{1,0:T(8,128)(2,1)}, bf16[8,152,768]{2,1,0:T(8,128)(2,1)}) custom-call(s32[1]{0:T(128)} %bitcast.home_ref, s32[2,768]{1,0:T(2,128)} %copy.35.ids_ref, bf16[768,768]{1,0:T(8,128)(2,1)} %bitcast.106, f32[12,768]{1,0:T(8,128)} %bitcast.126), custom_call_target="tpu_custom_call" | custom-call | flops 1585446912 | bytes 3538944 | tf_op jit(solution)/shard_map/route_plan/pallas_call | solution.py:360
  15.9 7.1 %all-to-all-start = ((bf16[8,152,768]{2,1,0:T(8,128)(2,1)}), bf16[8,152,768]{2,1,0:T(8,128)(2,1)}, u32[]{:S(2)}, u32[]{:S(2)}) async-start(bf16[8,152,768]{2,1,0:T(8,128)(2,1)} %get-tuple-element.149), calls=%async_computation | async-start | bytes 3735552 | tf_op jit(solution)/shard_map/all_to_all | solution.py:1002
  30.9 3.5 turn.2.act_ref
  35.6 6.0 %convolution_convert_fusion.q_ref.k_ref.v_ref = bf16[768,2304]{1,0:T(8,128)(2,1)} fusion(bf16[768,768]{1,0:T(8,128)(2,1)} %fusion.2.in_ref, bf16[768,2304]{1,0:T(8,128)(2,1)S(1)} %copy-done), kind=kOutput, calls=%fused_computation | convolution fusion | flops 2719678464 | bytes 8257536 | tf_op jit(solution)/shard_map/dot_general | solution.py:22
  41.5 3.7 collective-permute-done.1.refs_1_
  45.2 5.7 %far_projection.1 = (bf16[768,768]{1,0:T(8,128)(2,1)}, bf16[768,1536]{1,0:T(8,128)(2,1)}) custom-call(f32[1,768]{1,0:T(1,128)} %broadcast_in_dim.43.gain_ref.refs_5_, bf16[768,2304]{1,0:T(8,128)(2,1)} %refs_4_.3, bf16[768,2304]{1,0:T(8,128)(2,1)} %refs_4_.3, bf16[256,768]{1,0:T(8,128)(2,1)} %copy-done.23, bf16[256,768]{1,0:T(8,128)(2,1)} %collective-permute-done.1.refs_1_, ...), custom_call_target="tpu_custom_call" | custom-call | flops 1811939328 | bytes 7077888 | tf_op jit(solution)/shard_map/far_projection/pallas_call | solution.py:814
  51.0 19.0 %attention_forward.1 = (bf16[768,768]{1,0:T(8,128)(2,1)}, f32[6,16,768]{2,1,0:T(8,128)}) custom-call(f32[3]{0:T(128)} %compare_select_fusion.flags_ref, bf16[768,2304]{1,0:T(8,128)(2,1)} %convolution_convert_fusion.q_ref.k_ref.v_ref, bf16[768,2304]{1,0:T(8,128)(2,1)} %convolution_convert_fusion.q_ref.k_ref.v_ref, ...), custom_call_target="tpu_custom_call" | custom-call | flops 3623878656 | bytes 7077888 | tf_op jit(solution)/shard_map/attention_forward/pallas_call | solution.py:105
  70.0 6.9 %after_attention.1 = (f32[768,768]{1,0:T(8,128)}, bf16[768,768]{1,0:T(8,128)(2,1)}, bf16[640,768]{1,0:T(8,128)(2,1)}, bf16[512,768]{1,0:T(8,128)(2,1)}) custom-call(bf16[768,768]{1,0:T(8,128)(2,1)} %get-tuple-element.150.mixed_ref.refs_11_.o_ref, bf16[768,768]{1,0:T(8,128)(2,1)} %bitcast.72, bf16[768,768]{1,0:T(8,128)(2,1)} %refs_12_.1, ...), custom_call_target="tpu_custom_call" | custom-call | flops 2264924160 | bytes 10616832 | tf_op jit(solution)/shard_map/after_attention/pallas_call | solution.py:531
  76.9 5.1 %all-to-all-start.3 = ((bf16[8,64,768]{2,1,0:T(8,128)(2,1)}), bf16[8,64,768]{2,1,0:T(8,128)(2,1)S(1)}, u32[]{:S(2)}, u32[]{:S(2)}) async-start(bf16[8,64,768]{2,1,0:T(8,128)(2,1)} %bitcast.124), calls=%async_computation.3 | async-start | bytes 1572864 | tf_op jit(solution)/shard_map/all_to_all | solution.py:1002
  88.1 13.8 %local_part.1 = (f32[768,768]{1,0:T(8,128)}, f32[768,768]{1,0:T(8,128)}, f32[768,128]{1,0:T(8,128)}, f32[768,128]{1,0:T(8,128)}, f32[24,768]{1,0:T(8,128)}) custom-call(f32[768,768]{1,0:T(8,128)} %get-tuple-element.154.hidden_ref.refs_8_, bf16[768,768]{1,0:T(8,128)(2,1)} %get-tuple-element.155.low_ref, bf16[768,768]{1,0:T(8,128)(2,1)} %bitcast.107, ...), custom_call_target="tpu_custom_call" | custom-call | flops 1056964608 | bytes 9437184 | tf_op jit(solution)/shard_map/local_part/pallas_call | solution.py:629
  102.9 4.1 %all-to-all-start.1 = ((bf16[8,80,768]{2,1,0:T(8,128)(2,1)}), bf16[8,80,768]{2,1,0:T(8,128)(2,1)S(1)}, u32[]{:S(2)}, u32[]{:S(2)}) async-start(bf16[8,80,768]{2,1,0:T(8,128)(2,1)} %bitcast.11), calls=%async_computation.1 | async-start | bytes 1966080 | tf_op jit(solution)/shard_map/all_to_all | solution.py:1002
  107.8 17.7 %expert_pass.3 = (bf16[512,896]{1,0:T(8,128)(2,1)}, bf16[512,768]{1,0:T(8,128)(2,1)}, bf16[512,768]{1,0:T(8,128)(2,1)}, bf16[512,2048]{1,0:T(8,128)(2,1)}, bf16[...) custom-call(s32[1]{0:T(128)} %bitcast.home_ref, bf16[512,768]{1,0:T(8,128)(2,1)} %bitcast.122, ...), custom_call_target="tpu_custom_call" | custom-call | flops 9663676416 | bytes 19660800 | tf_op jit(solution)/shard_map/expert_pass/pallas_call | solution.py:448
  125.4 6.8 %all-to-all-done.1 = bf16[8,80,768]{2,1,0:T(8,128)(2,1)S(1)} async-done(((bf16[8,80,768]{2,1,0:T(8,128)(2,1)}), bf16[8,80,768]{2,1,0:T(8,128)(2,1)S(1)}, u32[]{:S(2)}, u32[]{:S(2)}) %all-to-all-start.1) | async-done | bytes 983072 | tf_op jit(solution)/shard_map/all_to_all | solution.py:1002
  132.2 3.8 all-to-all-start.4
  136.0 20.9 %expert_pass.2 = (bf16[640,896]{1,0:T(8,128)(2,1)}, bf16[640,768]{1,0:T(8,128)(2,1)}, bf16[640,768]{1,0:T(8,128)(2,1)}, bf16[640,2048]{1,0:T(8,128)(2,1)}, bf16[...) custom-call(s32[1]{0:T(128)} %bitcast.home_ref, bf16[640,768]{1,0:T(8,128)(2,1)} %bitcast.116, ...), custom_call_target="tpu_custom_call" | custom-call | flops 12079595520 | bytes 22216704 | tf_op jit(solution)/shard_map/expert_pass/pallas_call | solution.py:448
  156.9 5.2 %all-to-all-start.2 = ((bf16[8,80,768]{2,1,0:T(8,128)(2,1)}), bf16[8,80,768]{2,1,0:T(8,128)(2,1)S(1)}, u32[]{:S(2)}, u32[]{:S(2)}) async-start(bf16[8,80,768]{2,1,0:T(8,128)(2,1)} %bitcast.118), calls=%async_computation.2 | async-start | bytes 1966080 | tf_op jit(solution)/shard_map/all_to_all | solution.py:1005
  164.8 17.9 %weight_gradients.1 = (bf16[2,768,2048]{2,1,0:T(8,128)(2,1)}, bf16[2048,768]{1,0:T(8,128)(2,1)}) custom-call(bf16[640,768]{1,0:T(8,128)(2,1)} %bitcast.117, bf16[512,768]{1,0:T(8,128)(2,1)} %bitcast.123, bf16[640,768]{1,0:T(8,128)(2,1)} %get-tuple-element.164.refs_2_, bf16[512,768]{1,0:T(8,128)(2,1)} %get-tuple-element.165.refs_3_, ...), custom_call_target="tpu_custom_call" | custom-call | flops 10871635968 | bytes 27131904 | tf_op jit(solution)/shard_map/weight_gradients/pallas_call | solution.py:497
  182.7 4.6 %all-to-all-done.2 = bf16[8,80,768]{2,1,0:T(8,128)(2,1)S(1)} async-done(((bf16[8,80,768]{2,1,0:T(8,128)(2,1)}), bf16[8,80,768]{2,1,0:T(8,128)(2,1)S(1)}, u32[]{:S(2)}, u32[]{:S(2)}) %all-to-all-start.2) | async-done | bytes 983072 | tf_op jit(solution)/shard_map/all_to_all | solution.py:1005
  188.3 3.9 all-to-all-start.5
  192.2 11.5 %combine_gradients.1 = (f32[768,768]{1,0:T(8,128)}, bf16[768,768]{1,0:T(8,128)(2,1)}, bf16[384,1664]{1,0:T(8,128)(2,1)}, bf16[384,1664]{1,0:T(8,128)(2,1)}) custom-call(s32[1]{0:T(128)} %bitcast.20.core_ref, bf16[768,640]{1,0:T(8,128)(2,1)} %get-tuple-element.142.refs_0_, bf16[768,512]{1,0:T(8,128)(2,1)} %get-tuple-element.143.refs_1_, ...), custom_call_target="tpu_custom_call" | custom-call | flops 3170893824 | bytes 15335424 | tf_op jit(solution)/shard_map/combine_gradients/pallas_call | solution.py:700
  203.7 18.5 %attention_backward.3 = (bf16[384,1664]{1,0:T(8,128)(2,1)}, bf16[384,1664]{1,0:T(8,128)(2,1)}, bf16[768,768]{1,0:T(8,128)(2,1)}, f32[768,768]{1,0:T(8,128)}) custom-call(f32[3]{0:T(128)} %compare_select_fusion.flags_ref, s32[1]{0:T(128)} %bitcast.20.core_ref, ...), custom_call_target="tpu_custom_call", output_to_operand_aliasing={{0}: (14, {}), {1}: (15, {})} | custom-call | flops 6039797760 | bytes 14155776 | tf_op jit(solution)/shard_map/attention_backward/pallas_call | solution.py:283
  222.9 11.2 %attention_backward.4 = (bf16[384,1536]{1,0:T(8,128)(2,1)}, bf16[384,1536]{1,0:T(8,128)(2,1)}, bf16[768,384]{1,0:T(8,128)(2,1)}, f32[768,768]{1,0:T(8,128)}) custom-call(f32[3]{0:T(128)} %compare_select_fusion.flags_ref, s32[1]{0:T(128)} %bitcast.20.core_ref, bf16[768,2304]{1,0:T(8,128)(2,1)} %convolution_convert_fusion.q_ref.k_ref.v_ref, ...), custom_call_target="tpu_custom_call" | custom-call | flops 3019898880 | bytes 11796480 | tf_op jit(solution)/shard_map/attention_backward/pallas_call | solution.py:283
  242.3 25.7 %attention_backward.5 = (bf16[384,1536]{1,0:T(8,128)(2,1)}, bf16[384,1536]{1,0:T(8,128)(2,1)}, bf16[768,1152]{1,0:T(8,128)(2,1)}, bf16[256,768]{1,0:T(8,128)(2,1...) custom-call(f32[3]{0:T(128)} %compare_select_fusion.flags_ref, ...), custom_call_target="tpu_custom_call", output_to_operand_aliasing={{0}: (14, {}), {1}: (15, {})} | custom-call | flops 9059696640 | bytes 16515072 | tf_op jit(solution)/shard_map/attention_backward/pallas_call | solution.py:283
  282.4 6.6 %finish_outputs.1 = (bf16[768,768]{1,0:T(8,128)(2,1)}, f32[128,768]{1,0:T(8,128)}) custom-call(bf16[768,640]{1,0:T(8,128)(2,1)} %get-tuple-element.142.refs_0_, bf16[768,512]{1,0:T(8,128)(2,1)} %get-tuple-element.143.refs_1_, bf16[8,144,896]{2,1,0:T(8,128)(2,1)} %copy-done.4, f32[768,768]{1,0:T(8,128)} %get-tuple-element.210.refs_3_, ...), custom_call_target="tpu_custom_call" | custom-call | flops 1585446912 | bytes 9437184 | tf_op jit(solution)/shard_map/finish_outputs/pallas_call | solution.py:742
  291.9 10.4 %collective-permute-done.11 = bf16[1,96,1536]{2,1,0:T(8,128)(2,1)S(1)} collective-permute-done((bf16[1,96,1536]{2,1,0:T(8,128)(2,1)}, bf16[1,96,1536]{2,1,0:T(8,128)(2,1)S(1)}, u32[]{:S(2)}, u32[]{:S(2)}) %collective-permute-start.11) | collective-permute-done | bytes 294944 | tf_op jit(solution)/shard_map/ppermute | solution.py:872
  310.2 5.9 %collective-permute-done.14.refs_1_ = bf16[1,24,3200]{2,1,0:T(8,128)(2,1)S(1)} collective-permute-done((bf16[1,24,3200]{2,1,0:T(8,128)(2,1)}, bf16[1,24,3200]{2,1,0:T(8,128)(2,1)S(1)}, u32[]{:S(2)}, u32[]{:S(2)}) %collective-permute-start.14) | collective-permute-done | bytes 153632 | tf_op jit(solution)/shard_map/ppermute | solution.py:872
  316.1 3.9 collective-permute-done.16.refs_3_
  327.7 9.4 %input_gradient.1 = f32[768,768]{1,0:T(8,128)} custom-call(bf16[768,768]{1,0:T(8,128)(2,1)} %bitcast.73, f32[1,768]{1,0:T(1,128)} %broadcast_in_dim.43.gain_ref.refs_5_, f32[768,768]{1,0:T(8,128)} %get-tuple-element.223.dhidden_ref, bf16[768,2304]{1,0:T(8,128)(2,1)} %refs_4_.3, bf16[768,768]{1,0:T(8,128)(2,1)} %get-tuple-element.224.refs_0_, ...), custom_call_target="tpu_custom_call" | custom-call | flops 2717908992 | bytes 12976128 | tf_op jit(solution)/shard_map/input_gradient/pallas_call | solution.py:784
  350.9 7.8 %collective-permute-done.20.refs_1_ = bf16[4,24,3200]{2,1,0:T(8,128)(2,1)} collective-permute-done((bf16[4,24,3200]{2,1,0:T(8,128)(2,1)}, bf16[4,24,3200]{2,1,0:T(8,128)(2,1)}, u32[]{:S(2)}, u32[]{:S(2)}) %collective-permute-start.20) | collective-permute-done | bytes 614432 | tf_op jit(solution)/shard_map/ppermute | solution.py:872
  358.7 10.2 %collective-permute-done.21.refs_2_ = bf16[4,24,3200]{2,1,0:T(8,128)(2,1)} collective-permute-done((bf16[4,24,3200]{2,1,0:T(8,128)(2,1)}, bf16[4,24,3200]{2,1,0:T(8,128)(2,1)}, u32[]{:S(2)}, u32[]{:S(2)}) %collective-permute-start.21) | collective-permute-done | bytes 614432 | tf_op jit(solution)/shard_map/ppermute | solution.py:872
  372.0 5.9 %unpack_half.2 = (f32[768,768]{1,0:T(8,128)}, f32[768,2304]{1,0:T(8,128)}, f32[384,128]{1,0:T(8,128)}) custom-call(s32[3]{0:T(128)} %get-tuple-element.289.index_ref, bf16[4,24,3200]{2,1,0:T(8,128)(2,1)} %stack_pieces.1.refs_0_, bf16[4,24,3200]{2,1,0:T(8,128)(2,1)} %collective-permute-done.20.refs_1_, bf16[4,24,3200]{2,1,0:T(8,128)(2,1)} %collective-permute-done.21.refs_2_, ...), custom_call_target="tpu_custom_call" | custom-call | bytes 8257536 | tf_op jit(solution)/shard_map/unpack_half/pallas_call | solution.py:962
  379.3 6.4 %unpack_half.3 = (f32[768,768]{1,0:T(8,128)}, f32[768,2304]{1,0:T(8,128)}, f32[12,768]{1,0:T(8,128)}, f32[2,2,768]{2,1,0:T(2,128)}, f32[2,768]{1,0:T(2,128)}, /*index=5*/f32[768]{0:T(1024)}, f32[768]{0:T(1024)}) custom-call(s32[3]{0:T(128)} %get-tuple-element.288.index_ref, ...), custom_call_target="tpu_custom_call", output_to_operand_aliasing={{0}: (8, {}), {1}: (9, {})} | custom-call | bytes 8257536 | tf_op jit(solution)/shard_map/unpack_half/pallas_call | solution.py:962
  (163 shorter events, 83.4 us)
Async XLA Ops:
  15.9 54.1 %all-to-all-start = ((bf16[8,152,768]{2,1,0:T(8,128)(2,1)}), bf16[8,152,768]{2,1,0:T(8,128)(2,1)}, u32[]{:S(2)}, u32[]{:S(2)}) async-start(bf16[8,152,768]{2,1,0:T(8,128)(2,1)} %get-tuple-element.149), calls=%async_computation | async-start | bytes 3735552 | tf_op jit(solution)/shard_map/all_to_all | solution.py:1002
  23.7 17.8 %collective-permute-start = (bf16[256,768]{1,0:T(8,128)(2,1)}, bf16[256,768]{1,0:T(8,128)(2,1)S(1)}, u32[]{:S(2)}, u32[]{:S(2)}) collective-permute-start(bf16[256,768]{1,0:T(8,128)(2,1)} %slice_bitcast_fusion), channel_id=1, source_target_pairs={{0,8},{8,0},{16,24},{24,16},{1,9},{9,1},{17,25},{25,17},{2,10},{10... | collective-permute-start | bytes 1179656 | tf_op jit(solution)/shard_map/ppermute | solution.py:1016
  25.2 20.0 %collective-permute-start.1 = (bf16[256,768]{1,0:T(8,128)(2,1)}, bf16[256,768]{1,0:T(8,128)(2,1)}, u32[]{:S(2)}, u32[]{:S(2)}) collective-permute-start(bf16[256,768]{1,0:T(8,128)(2,1)} %slice_bitcast_fusion), channel_id=1, source_target_pairs={{0,16},{8,24},{16,0},{24,8},{1,17},{9,25},{17,1},{25,9},{2,18},{10... | collective-permute-start | bytes 1179656 | tf_op jit(solution)/shard_map/ppermute | solution.py:1016
  26.7 18.5 %collective-permute-start.2 = (bf16[256,768]{1,0:T(8,128)(2,1)}, bf16[256,768]{1,0:T(8,128)(2,1)}, u32[]{:S(2)}, u32[]{:S(2)}) collective-permute-start(bf16[256,768]{1,0:T(8,128)(2,1)} %slice_bitcast_fusion), channel_id=1, source_target_pairs={{0,24},{8,16},{16,8},{24,0},{1,25},{9,17},{17,9},{25,1},{2,26},{10... | collective-permute-start | bytes 1179656 | tf_op jit(solution)/shard_map/ppermute | solution.py:1016
  76.9 26.0 %all-to-all-start.3 = ((bf16[8,64,768]{2,1,0:T(8,128)(2,1)}), bf16[8,64,768]{2,1,0:T(8,128)(2,1)S(1)}, u32[]{:S(2)}, u32[]{:S(2)}) async-start(bf16[8,64,768]{2,1,0:T(8,128)(2,1)} %bitcast.124), calls=%async_computation.3 | async-start | bytes 1572864 | tf_op jit(solution)/shard_map/all_to_all | solution.py:1002
  102.9 29.3 %all-to-all-start.1 = ((bf16[8,80,768]{2,1,0:T(8,128)(2,1)}), bf16[8,80,768]{2,1,0:T(8,128)(2,1)S(1)}, u32[]{:S(2)}, u32[]{:S(2)}) async-start(bf16[8,80,768]{2,1,0:T(8,128)(2,1)} %bitcast.11), calls=%async_computation.1 | async-start | bytes 1966080 | tf_op jit(solution)/shard_map/all_to_all | solution.py:1002
  132.2 24.7 %all-to-all-start.4 = ((bf16[8,64,768]{2,1,0:T(8,128)(2,1)}), bf16[8,64,768]{2,1,0:T(8,128)(2,1)S(1)}, u32[]{:S(2)}, u32[]{:S(2)}) async-start(bf16[8,64,768]{2,1,0:T(8,128)(2,1)} %bitcast.125), calls=%async_computation.4 | async-start | bytes 1572864 | tf_op jit(solution)/shard_map/all_to_all | solution.py:1005
  156.9 30.4 %all-to-all-start.2 = ((bf16[8,80,768]{2,1,0:T(8,128)(2,1)}), bf16[8,80,768]{2,1,0:T(8,128)(2,1)S(1)}, u32[]{:S(2)}, u32[]{:S(2)}) async-start(bf16[8,80,768]{2,1,0:T(8,128)(2,1)} %bitcast.118), calls=%async_computation.2 | async-start | bytes 1966080 | tf_op jit(solution)/shard_map/all_to_all | solution.py:1005
  162.1 182.9 %reduce-scatter.5.cloned.1.call-start = ((), (), s32[]{:S(2)}) async-start(), calls=%async_computation.9 | async-start | bytes 3932160 | tf_op jit(solution)/shard_map/reduce_scatter | solution.py:1050
  187.4 160.1 %reduce-scatter.3.cloned.1.call-start = ((), (), s32[]{:S(2)}) async-start(), calls=%async_computation.8 | async-start | bytes 7864320 | tf_op jit(solution)/shard_map/reduce_scatter | solution.py:1049
  188.3 92.8 %all-to-all-start.5 = ((bf16[8,144,896]{2,1,0:T(8,128)(2,1)}), bf16[8,144,896]{2,1,0:T(8,128)(2,1)S(1)}, u32[]{:S(2)}, u32[]{:S(2)}) async-start(bf16[8,144,896]{2,1,0:T(8,128)(2,1)} %pad_maximum_fusion), calls=%async_computation.5 | async-start | bytes 4128768 | tf_op jit(solution)/shard_map/all_to_all | solution.py:1005
  222.3 11.8 %collective-permute-start.3 = (bf16[384,1664]{1,0:T(8,128)(2,1)}, bf16[384,1664]{1,0:T(8,128)(2,1)S(1)}, u32[]{:S(2)}, u32[]{:S(2)}) collective-permute-start(bf16[384,1664]{1,0:T(8,128)(2,1)} %get-tuple-element.190), channel_id=1, source_target_pairs={{0,1},{1,0},{2,3},{3,2},{4,5},{5,4},{6,7},{7,6},{8,9},{9,8},{10,11... | collective-permute-start | bytes 3833864 | tf_op jit(solution)/shard_map/ppermute | solution.py:1060
  237.9 30.1 %collective-permute-start.4 = (bf16[1,96,1664]{2,1,0:T(8,128)(2,1)}, bf16[1,96,1664]{2,1,0:T(8,128)(2,1)S(1)}, u32[]{:S(2)}, u32[]{:S(2)}) collective-permute-start(bf16[1,96,1664]{2,1,0:T(8,128)(2,1)} %get-tuple-element.204), channel_id=1, source_target_pairs={{0,2},{1,3},{2,0},{3,1},{4,6},{5,7},{6,4},{7,5},{8,10},{9,11},{10,... | collective-permute-start | bytes 958472 | tf_op jit(solution)/shard_map/ppermute | solution.py:872
  239.6 28.4 %collective-permute-start.5 = (bf16[1,96,1664]{2,1,0:T(8,128)(2,1)}, bf16[1,96,1664]{2,1,0:T(8,128)(2,1)S(1)}, u32[]{:S(2)}, u32[]{:S(2)}) collective-permute-start(bf16[1,96,1664]{2,1,0:T(8,128)(2,1)} %get-tuple-element.205), channel_id=1, source_target_pairs={{0,4},{1,5},{2,6},{3,7},{4,0},{5,1},{6,2},{7,3},{8,12},{9,13},{10,... | collective-permute-start | bytes 958472 | tf_op jit(solution)/shard_map/ppermute | solution.py:872
  242.0 26.0 %collective-permute-start.6 = (bf16[1,96,1664]{2,1,0:T(8,128)(2,1)}, bf16[1,96,1664]{2,1,0:T(8,128)(2,1)S(1)}, u32[]{:S(2)}, u32[]{:S(2)}) collective-permute-start(bf16[1,96,1664]{2,1,0:T(8,128)(2,1)} %get-tuple-element.206), channel_id=1, source_target_pairs={{0,6},{1,7},{2,4},{3,5},{4,2},{5,3},{6,0},{7,1},{8,14},{9,15},{10,... | collective-permute-start | bytes 958472 | tf_op jit(solution)/shard_map/ppermute | solution.py:872
  268.9 20.1 %collective-permute-start.8 = (bf16[256,768]{1,0:T(8,128)(2,1)}, bf16[256,768]{1,0:T(8,128)(2,1)}, u32[]{:S(2)}, u32[]{:S(2)}) collective-permute-start(bf16[256,768]{1,0:T(8,128)(2,1)} %get-tuple-element.215), channel_id=1, source_target_pairs={{0,8},{8,0},{16,24},{24,16},{1,9},{9,1},{17,25},{25,17},{2,10},{10... | collective-permute-start | bytes 1179656 | tf_op jit(solution)/shard_map/ppermute | solution.py:1073
  270.1 18.9 %collective-permute-start.9 = (bf16[256,768]{1,0:T(8,128)(2,1)}, bf16[256,768]{1,0:T(8,128)(2,1)}, u32[]{:S(2)}, u32[]{:S(2)}) collective-permute-start(bf16[256,768]{1,0:T(8,128)(2,1)} %get-tuple-element.216), channel_id=1, source_target_pairs={{0,16},{8,24},{16,0},{24,8},{1,17},{9,25},{17,1},{25,9},{2,18},{10... | collective-permute-start | bytes 1179656 | tf_op jit(solution)/shard_map/ppermute | solution.py:1073
  275.7 16.2 %collective-permute-start.10 = (bf16[1,96,1536]{2,1,0:T(8,128)(2,1)}, bf16[1,96,1536]{2,1,0:T(8,128)(2,1)S(1)}, u32[]{:S(2)}, u32[]{:S(2)}) collective-permute-start(bf16[1,96,1536]{2,1,0:T(8,128)(2,1)} %get-tuple-element.219), channel_id=1, source_target_pairs={{0,2},{1,3},{2,0},{3,1},{4,6},{5,7},{6,4},{7,5},{8,10},{9,11},{10,... | collective-permute-start | bytes 884744 | tf_op jit(solution)/shard_map/ppermute | solution.py:872
  278.7 23.6 %collective-permute-start.11 = (bf16[1,96,1536]{2,1,0:T(8,128)(2,1)}, bf16[1,96,1536]{2,1,0:T(8,128)(2,1)S(1)}, u32[]{:S(2)}, u32[]{:S(2)}) collective-permute-start(bf16[1,96,1536]{2,1,0:T(8,128)(2,1)} %get-tuple-element.220), channel_id=1, source_target_pairs={{0,4},{1,5},{2,6},{3,7},{4,0},{5,1},{6,2},{7,3},{8,12},{9,13},{10,... | collective-permute-start | bytes 884744 | tf_op jit(solution)/shard_map/ppermute | solution.py:872
  279.8 22.6 %collective-permute-start.12 = (bf16[1,96,1536]{2,1,0:T(8,128)(2,1)}, bf16[1,96,1536]{2,1,0:T(8,128)(2,1)S(1)}, u32[]{:S(2)}, u32[]{:S(2)}) collective-permute-start(bf16[1,96,1536]{2,1,0:T(8,128)(2,1)} %get-tuple-element.221), channel_id=1, source_target_pairs={{0,6},{1,7},{2,4},{3,5},{4,2},{5,3},{6,0},{7,1},{8,14},{9,15},{10,... | collective-permute-start | bytes 884744 | tf_op jit(solution)/shard_map/ppermute | solution.py:872
  289.1 37.9 %collective-permute-start.13 = (bf16[256,768]{1,0:T(8,128)(2,1)S(1)}, bf16[256,768]{1,0:T(8,128)(2,1)S(1)}, u32[]{:S(2)}, u32[]{:S(2)}) collective-permute-start(bf16[256,768]{1,0:T(8,128)(2,1)S(1)} %copy-done.36), channel_id=1, source_target_pairs={{0,24},{8,16},{16,8},{24,0},{1,25},{9,17},{17,9},{25,1},{2,26},{10... | collective-permute-start | bytes 1179656 | tf_op jit(solution)/shard_map/ppermute | solution.py:1073
  305.9 10.2 %collective-permute-start.14 = (bf16[1,24,3200]{2,1,0:T(8,128)(2,1)}, bf16[1,24,3200]{2,1,0:T(8,128)(2,1)S(1)}, u32[]{:S(2)}, u32[]{:S(2)}) collective-permute-start(bf16[1,24,3200]{2,1,0:T(8,128)(2,1)} %get-tuple-element.239), channel_id=1, source_target_pairs={{0,8},{8,0},{16,24},{24,16},{1,9},{9,1},{17,25},{25,17},{2,10},{10... | collective-permute-start | bytes 460808 | tf_op jit(solution)/shard_map/ppermute | solution.py:872
  307.1 9.0 %collective-permute-start.15 = (bf16[1,24,3200]{2,1,0:T(8,128)(2,1)}, bf16[1,24,3200]{2,1,0:T(8,128)(2,1)S(1)}, u32[]{:S(2)}, u32[]{:S(2)}) collective-permute-start(bf16[1,24,3200]{2,1,0:T(8,128)(2,1)} %get-tuple-element.240), channel_id=1, source_target_pairs={{0,16},{8,24},{16,0},{24,8},{1,17},{9,25},{17,1},{25,9},{2,18},{10... | collective-permute-start | bytes 460808 | tf_op jit(solution)/shard_map/ppermute | solution.py:872
  308.4 11.6 %collective-permute-start.16 = (bf16[1,24,3200]{2,1,0:T(8,128)(2,1)}, bf16[1,24,3200]{2,1,0:T(8,128)(2,1)S(1)}, u32[]{:S(2)}, u32[]{:S(2)}) collective-permute-start(bf16[1,24,3200]{2,1,0:T(8,128)(2,1)} %get-tuple-element.241), channel_id=1, source_target_pairs={{0,24},{8,16},{16,8},{24,0},{1,25},{9,17},{17,9},{25,1},{2,26},{10... | collective-permute-start | bytes 460808 | tf_op jit(solution)/shard_map/ppermute | solution.py:872
  322.5 14.6 %collective-permute-start.17 = (bf16[1,24,3200]{2,1,0:T(8,128)(2,1)}, bf16[1,24,3200]{2,1,0:T(8,128)(2,1)S(1)}, u32[]{:S(2)}, u32[]{:S(2)}) collective-permute-start(bf16[1,24,3200]{2,1,0:T(8,128)(2,1)} %sum_pieces.7.refs_0_), channel_id=1, source_target_pairs={{0,2},{1,3},{2,0},{3,1},{4,6},{5,7},{6,4},{7,5},{8,10},{9,11},{10,... | collective-permute-start | bytes 460808 | tf_op jit(solution)/shard_map/ppermute | solution.py:872
  324.0 14.2 %collective-permute-start.18 = (bf16[1,24,3200]{2,1,0:T(8,128)(2,1)}, bf16[1,24,3200]{2,1,0:T(8,128)(2,1)S(1)}, u32[]{:S(2)}, u32[]{:S(2)}) collective-permute-start(bf16[1,24,3200]{2,1,0:T(8,128)(2,1)} %sum_pieces.7.refs_0_), channel_id=1, source_target_pairs={{0,4},{1,5},{2,6},{3,7},{4,0},{5,1},{6,2},{7,3},{8,12},{9,13},{10,... | collective-permute-start | bytes 460808 | tf_op jit(solution)/shard_map/ppermute | solution.py:872
  326.4 11.8 %collective-permute-start.19 = (bf16[1,24,3200]{2,1,0:T(8,128)(2,1)}, bf16[1,24,3200]{2,1,0:T(8,128)(2,1)S(1)}, u32[]{:S(2)}, u32[]{:S(2)}) collective-permute-start(bf16[1,24,3200]{2,1,0:T(8,128)(2,1)} %sum_pieces.7.refs_0_), channel_id=1, source_target_pairs={{0,6},{1,7},{2,4},{3,5},{4,2},{5,3},{6,0},{7,1},{8,14},{9,15},{10,... | collective-permute-start | bytes 460808 | tf_op jit(solution)/shard_map/ppermute | solution.py:872
  341.6 17.1 %collective-permute-start.20 = (bf16[4,24,3200]{2,1,0:T(8,128)(2,1)}, bf16[4,24,3200]{2,1,0:T(8,128)(2,1)}, u32[]{:S(2)}, u32[]{:S(2)}) collective-permute-start(bf16[4,24,3200]{2,1,0:T(8,128)(2,1)} %stack_pieces.1.refs_0_), channel_id=1, source_target_pairs={{0,8},{8,0},{16,24},{24,16},{1,9},{9,1},{17,25},{25,17},{2,10},{10... | collective-permute-start | bytes 1843208 | tf_op jit(solution)/shard_map/ppermute | solution.py:872
  342.1 26.8 %collective-permute-start.21 = (bf16[4,24,3200]{2,1,0:T(8,128)(2,1)}, bf16[4,24,3200]{2,1,0:T(8,128)(2,1)}, u32[]{:S(2)}, u32[]{:S(2)}) collective-permute-start(bf16[4,24,3200]{2,1,0:T(8,128)(2,1)} %stack_pieces.1.refs_0_), channel_id=1, source_target_pairs={{0,16},{8,24},{16,0},{24,8},{1,17},{9,25},{17,1},{25,9},{2,18},{10... | collective-permute-start | bytes 1843208 | tf_op jit(solution)/shard_map/ppermute | solution.py:872
  342.8 26.1 %collective-permute-start.22 = (bf16[4,24,3200]{2,1,0:T(8,128)(2,1)}, bf16[4,24,3200]{2,1,0:T(8,128)(2,1)S(1)}, u32[]{:S(2)}, u32[]{:S(2)}) collective-permute-start(bf16[4,24,3200]{2,1,0:T(8,128)(2,1)} %stack_pieces.1.refs_0_), channel_id=1, source_target_pairs={{0,24},{8,16},{16,8},{24,0},{1,25},{9,17},{17,9},{25,1},{2,26},{10... | collective-permute-start | bytes 1843208 | tf_op jit(solution)/shard_map/ppermute | solution.py:872
  369.7 8.1 %collective-permute-start.23 = (bf16[4,24,3200]{2,1,0:T(8,128)(2,1)S(1)}, bf16[4,24,3200]{2,1,0:T(8,128)(2,1)S(1)}, u32[]{:S(2)}, u32[]{:S(2)}) collective-permute-start(bf16[4,24,3200]{2,1,0:T(8,128)(2,1)S(1)} %copy-done.14), channel_id=1, source_target_pairs={{0,1},{1,0},{2,3},{3,2},{4,5},{5,4},{6,7},{7,6},{8,9},{9,8},{10,11... | collective-permute-start | bytes 1843208 | tf_op jit(solution)/shard_map/ppermute | solution.py:1060
  369.7 8.2 %collective-permute-start.24 = (bf16[4,24,3200]{2,1,0:T(8,128)(2,1)}, bf16[4,24,3200]{2,1,0:T(8,128)(2,1)S(1)}, u32[]{:S(2)}, u32[]{:S(2)}) collective-permute-start(bf16[4,24,3200]{2,1,0:T(8,128)(2,1)} %collective-permute-done.20.refs_1_), channel_id=1, source_target_pairs={{0,1},{1,0},{2,3},{3,2},{4,5},{5,4},{6,7},{7,6},{8,9},{9,8},{10,11... | collective-permute-start | bytes 1843208 | tf_op jit(solution)/shard_map/ppermute | solution.py:1060
  (40 other events, 190.5 us)
Sparse Core Ops, SparseCore 0:
  187.5 41.9 reduce-scatter.4
  233.0 84.1 reduce-scatter.2

commit v7 on v6

--- a/solution.py
+++ b/solution.py
@@ -12,6 +12,7 @@
 bf16 = jnp.bfloat16
 f32 = jnp.float32
 NEG = -1e30
+epsilon = 1e-06
 
 
 def dot_nt(a, b):
@@ -46,7 +47,17 @@
     return jnp.where(low_half, high, rest) if head == 0 else jnp.where(low_half, rest, high)
 
 
-def attention_forward_kernel(plen, flags_ref, q_ref, k_ref, v_ref, kr_ref, vr_ref, o_ref, lse_ref, kd, krd, vd, vrd):
+def attention_forward_kernel(plen, count, flags_ref, q_ref, k_ref, v_ref, kr_ref, vr_ref, gain_ref, x_any, w_any, *refs):
+    turned_any, (o_ref, lse_ref, hidden_ref, low_ref), sent = refs[:count], refs[count : count + 4], refs[count + 4 : 2 * count + 4]
+    kd, krd, vd, vrd, mixed, x_ref, w_ref, *select, sems = refs[2 * count + 4 :]
+    step = pl.program_id(0)
+    copies = [pltpu.make_async_copy(a, r, sems.at[i]) for i, (a, r) in enumerate(zip((x_any, w_any, *turned_any), (x_ref, w_ref, *select)))]
+
+    @pl.when(step == 0)
+    def _():
+        for copy in copies:
+            copy.start()
+
     tok = q_ref.shape[0]
     remote = kr_ref.shape[0]
     low_half = lax.broadcasted_iota(jnp.int32, (1, 128), 1) < HEAD_DIM
@@ -92,18 +103,36 @@
             peaks.append(peak)
         num = jnp.where(low_half, accs[0], accs[1])
         den = pltpu.roll(jnp.where(low_half, accs[1], accs[0]), HEAD_DIM, 1)
-        o_ref[start : start + size, :] = (num / den).astype(bf16)
+        value = (num / den).astype(bf16)
+        o_ref[start : start + size, :] = value
+        mixed[step, start : start + size, :] = value
         turned = (jnp.where(low_half, peaks[0], peaks[1]) + jnp.log2(den)).T
         lse_ref[0, 0:8, start : start + size] = turned[0:8, :]
         lse_ref[0, 8:16, start : start + size] = turned[HEAD_DIM : HEAD_DIM + 8, :]
 
 
-def attention_forward(flags, proj, kv_rem, plen):
+    @pl.when(step == pl.num_programs(0) - 1)
+    def _():
+        for copy in copies:
+            copy.wait()
+        joined = jnp.concatenate([mixed[i] for i in range(mixed.shape[0])], axis=1)
+        hidden = x_ref[...].astype(f32) + dot_nn(joined, w_ref[...])
+        inverse = lax.rsqrt(jnp.mean(hidden * hidden, axis=1, keepdims=True) + epsilon)
+        low = (hidden * inverse * gain_ref[...]).astype(bf16)
+        hidden_ref[...] = hidden
+        low_ref[...] = low
+        for rows_ref, s in zip(select, sent):
+            s[...] = dot_nn(rows_ref[...], low).astype(bf16)
+
+
+def attention_forward(flags, proj, kv_rem, plen, x, w_out, gain, turned):
     tok, width = proj.shape[0], proj.shape[1] // 3
     remote = kv_rem.shape[0]
     pairs = width // 128
-    return pl.pallas_call(
-        functools.partial(attention_forward_kernel, plen),
+    still = lambda shape: pl.BlockSpec(shape, lambda i: (0, 0))
+    sent = [(r.shape[0], width) for r in turned]
+    out = pl.pallas_call(
+        functools.partial(attention_forward_kernel, plen, len(turned)),
         grid=(pairs,),
         in_specs=[
             pl.BlockSpec(memory_space=pltpu.SMEM),
@@ -112,20 +141,32 @@
             pl.BlockSpec((tok, 128), lambda i: (0, 2 * pairs + i)),
             pl.BlockSpec((remote, 128), lambda i: (0, i)),
             pl.BlockSpec((remote, 128), lambda i: (0, pairs + i)),
-        ],
+            still((1, width)),
+        ]
+        + [pl.BlockSpec(memory_space=pl.ANY)] * (2 + len(turned)),
         out_specs=[
             pl.BlockSpec((tok, 128), lambda i: (0, i)),
             pl.BlockSpec((1, 16, tok), lambda i: (i, 0, 0)),
-        ],
+            still((tok, width)),
+            still((tok, width)),
+        ]
+        + [still(s) for s in sent],
         out_shape=[
             jax.ShapeDtypeStruct((tok, width), bf16),
             jax.ShapeDtypeStruct((pairs, 16, tok), f32),
-        ],
-        scratch_shapes=[pltpu.VMEM((2, n, 128), bf16) for n in (tok, remote, tok, remote)],
-        compiler_params=pltpu.CompilerParams(vmem_limit_bytes=60 * 2**20),
-        cost_estimate=pl.CostEstimate(flops=4 * tok * (tok + remote) * width, bytes_accessed=2 * (tok * 4 + remote * 2) * width, transcendentals=tok * (tok + remote) * HEADS),
+            jax.ShapeDtypeStruct((tok, width), f32),
+            jax.ShapeDtypeStruct((tok, width), bf16),
+        ]
+        + [jax.ShapeDtypeStruct(s, bf16) for s in sent],
+        scratch_shapes=[pltpu.VMEM((2, n, 128), bf16) for n in (tok, remote, tok, remote)]
+        + [pltpu.VMEM((pairs, tok, 128), bf16)]
+        + [pltpu.VMEM(a.shape, bf16) for a in (x, w_out, *turned)]
+        + [pltpu.SemaphoreType.DMA((2 + len(turned),))],
+        compiler_params=pltpu.CompilerParams(vmem_limit_bytes=60 * 2**20),
+        cost_estimate=pl.CostEstimate(flops=4 * tok * (tok + remote) * width + 4 * tok * width * width, bytes_accessed=2 * (tok * 10 + remote * 2) * width, transcendentals=tok * (tok + remote) * HEADS),
         name="attention_forward",
-    )(flags, proj, proj, proj, kv_rem, kv_rem)
+    )(flags, proj, proj, proj, kv_rem, kv_rem, gain, x, w_out, *turned)
+    return out[0], out[1], out[2], out[3], out[4:]
 
 
 def attention_backward_kernel(plen, started, last, skip, flags_ref, core_ref, q_ref, k_ref, v_ref, kr_ref, vr_ref, o_ref, do_ref, lse_ref, act_ref, far_ref, wk_ref, wv_ref, *refs):
@@ -298,7 +339,6 @@
 ALL_EXPERTS = 12
 EXTRA = 128
 SMALL = 8
-epsilon = 1e-06
 
 
 def dot_tn(a, b):
@@ -314,10 +354,11 @@
     return pieces
 
 
-def route_kernel(groups, home_ref, ids_ref, grad_ref, prev_ref, *out_refs):
+def route_kernel(groups, home_ref, ids_ref, grad_ref, prev_ref, x_ref, *out_refs):
     tok, width = grad_ref.shape
     count = len(groups)
-    turned_refs, chosen_refs, early_ref = out_refs[:count], out_refs[count : 2 * count], out_refs[2 * count]
+    turned_refs, chosen_refs, (early_ref, prompt_ref) = out_refs[:count], out_refs[count : 2 * count], out_refs[2 * count :]
+    prompt_ref[...] = x_ref[0 : prompt_ref.shape[0], :]
     capacity = early_ref.shape[1] - SMALL
     expert = lax.broadcasted_iota(jnp.int32, (16, tok), 0)
     ids = [ids_ref[k : k + 1, :] for k in range(2)]
@@ -352,23 +393,23 @@
             early_ref[e, capacity : capacity + SMALL, g * EXTRA : (g + 1) * EXTRA] = rows[g * SMALL : (g + 1) * SMALL].astype(bf16)
 
 
-def route_plan(home, ids, grad, prev, groups):
+def route_plan(home, ids, grad, prev, x, plen, groups):
     tok, width = grad.shape
     counts = [FFN_EXPERTS * size for _, size in groups]
     whole = pl.BlockSpec(memory_space=pltpu.VMEM)
     early = (FFN_EXPERTS, sum(counts) // FFN_EXPERTS + SMALL, width)
     out = pl.pallas_call(
         functools.partial(route_kernel, groups),
-        in_specs=[pl.BlockSpec(memory_space=pltpu.SMEM), whole, whole, whole],
-        out_specs=[whole] * (2 * len(groups) + 1),
+        in_specs=[pl.BlockSpec(memory_space=pltpu.SMEM), whole, whole, whole, whole],
+        out_specs=[whole] * (2 * len(groups) + 2),
         out_shape=[jax.ShapeDtypeStruct((n, tok), bf16) for n in counts]
         + [jax.ShapeDtypeStruct((tok, n), bf16) for n in counts]
-        + [jax.ShapeDtypeStruct(early, bf16)],
+        + [jax.ShapeDtypeStruct(early, bf16), jax.ShapeDtypeStruct((plen, width), bf16)],
         compiler_params=pltpu.CompilerParams(vmem_limit_bytes=60 * 2**20),
         cost_estimate=pl.CostEstimate(flops=2 * sum(counts) * tok * (width + EXTRA), bytes_accessed=4 * sum(counts) * width, transcendentals=0),
         name="route_plan",
-    )(home, ids, grad, prev)
-    return out[: len(groups)], out[len(groups) : -1], out[-1]
+    )(home, ids, grad, prev, x)
+    return out[: len(groups)], out[len(groups) : -2], out[-2], out[-1]
 
 
 def router_inputs(early_ref, slots):
@@ -513,32 +554,6 @@
 
 def inverse_rms(value):
     return lax.rsqrt(jnp.mean(value * value, axis=1, keepdims=True) + epsilon)
-
-
-def after_attention_kernel(count, mixed_ref, x_ref, w_ref, gain_ref, *refs):
-    turned, (hidden_ref, low_ref), sent = refs[:count], refs[count : count + 2], refs[count + 2 :]
-    hidden = x_ref[...].astype(f32) + dot_nn(mixed_ref[...], w_ref[...])
-    low = (hidden * inverse_rms(hidden) * gain_ref[...]).astype(bf16)
-    hidden_ref[...] = hidden
-    low_ref[...] = low
-    for t, s in zip(turned, sent):
-        s[...] = dot_nn(t[...], low).astype(bf16)
-
-
-def after_attention(mixed, x, w_out, gain, turned):
-    tok, width = x.shape
-    rows = sum(t.shape[0] for t in turned)
-    out = pl.pallas_call(
-        functools.partial(after_attention_kernel, len(turned)),
-        in_specs=[ANYWHERE] * (4 + len(turned)),
-        out_specs=[ANYWHERE] * (2 + len(turned)),
-        out_shape=[jax.ShapeDtypeStruct((tok, width), f32), jax.ShapeDtypeStruct((tok, width), bf16)]
-        + [jax.ShapeDtypeStruct((t.shape[0], width), bf16) for t in turned],
-        compiler_params=pltpu.CompilerParams(vmem_limit_bytes=60 * 2**20),
-        cost_estimate=pl.CostEstimate(flops=2 * tok * width * (width + rows), bytes_accessed=2 * width * (6 * tok + 2 * rows), transcendentals=0),
-        name="after_attention",
-    )(mixed, x, w_out, gain, *turned)
-    return out[0], out[1], out[2:]
 
 
 def turn_kernel(in_ref, out_ref):
@@ -1012,8 +1027,8 @@
     prev = prev_logits[0]
     mix = jnp.concatenate([router, jnp.zeros((width, 4), bf16), const_gate[0], const_gate[1], jnp.zeros((width, EXTRA - 20), bf16)], axis=1)
     router_pad = jnp.pad(router, ((0, 0), (0, EXTRA - ALL_EXPERTS)))
-    turned, chosen, early_sent = route_plan(home, routes[0].T, upstream_low, prev.T, groups)
-    far = [lax.ppermute(x_low[:plen], "ctx", xor_pairs(n_ctx, k)) for k in range(1, n_ctx)]
+    turned, chosen, early_sent, x_prompt = route_plan(home, routes[0].T, upstream_low, prev.T, x_low, plen, groups)
+    far = [lax.ppermute(x_prompt, "ctx", xor_pairs(n_ctx, k)) for k in range(1, n_ctx)]
 
     tokens_in = x_low.astype(f32)
     inverse_attn = rms_inverse(tokens_in)
@@ -1023,9 +1038,9 @@
     act_t = turn(act_low)
     act_far, kv_far = far_projection(after(far, projected, act_t), attn_gain[None], w_qkv)
 
-    mixed_low, lse = attention_forward(flags, projected, kv_far, plen)
-    mixed_low, early = lax.optimization_barrier((mixed_low, early))
-    hidden, moe_low, sent = after_attention(mixed_low, x_low, w_out, moe_gain[None], turned)
+    mixed_low, lse, hidden, moe_low, sent = attention_forward(flags, projected, kv_far, plen, x_low, w_out, moe_gain[None], turned)
+    sent, hidden, early = lax.optimization_barrier((sent, hidden, early))
+
     local_out, d_normed_local, probs, d_probs, small_local = local_part(hidden, moe_low, upstream_low, prev, routes[0], mix, moe_gain[None], const_vec)
     far_t = turn(act_far)
     sent = [after(sent[0], local_out, d_normed_local, far_t), sent[1]]

time: 397 us -> 395 us (level)
    pallas_call x2 -> x1, Pallas kernels: 25.9 us -> 24.5 us  [attention_forward(): pl.pallas_call(functools.partial(attention_forward_kernel, plen, len(turn...]
  transfers between devices with their start and end apart: 35 -> 35, of which waited for: 12 -> 12; matrix products, arithmetic and copies ran while one was open for 6% -> 6% of each run, Pallas kernels for 52% -> 53%
where the time goes in v7:
time: 395 us; the launch traced here: 391 us
  Pallas kernels  220 us (56%)
  starting transfers between devices  60.5 us (15%)
  waiting for transfers between devices  57.3 us (15%)
  local copies, waits for them, and re-layouts  22.7 us (6%)
  between operations  14.7 us (4%)
  other arithmetic  9.27 us (2%)
  matrix products  5.96 us (2%)
    pallas_call x3, Pallas kernels, attention_backward(): pl.pallas_call(functools.partial(attention_backward_kernel, plen, bool(st...  55.4 us
    ppermute x15, waiting for transfers between devices, swap(): lax.ppermute(pieces[k], axis, xor_pairs(size, unit * k))  39.6 us
    pallas_call x2, Pallas kernels, expert_pass(): pl.pallas_call(functools.partial(expert_kernel, group), grid=(ff // tile,...  38.6 us
    pallas_call x1, Pallas kernels, attention_forward(): pl.pallas_call(functools.partial(attention_forward_kernel, plen, len(turn...  24.5 us
    ppermute x15, starting transfers between devices, swap(): lax.ppermute(pieces[k], axis, xor_pairs(size, unit * k))  21.2 us
    pallas_call x1, Pallas kernels, weight_gradients(): pl.pallas_call(functools.partial(weight_kernel, count), grid=(ff // tile,...  17.9 us
    all_to_all x3, starting transfers between devices, deal(): return lax.all_to_all(value, 'exp', 0, 0, tiled=True)  16.1 us
    pallas_call x1, Pallas kernels, local_part(): pl.pallas_call(local_kernel, grid=(tok // block,), in_specs=[tiles(width)...  13.7 us
  transfers between devices with their start and end apart: 35, of which 12 were waited for; matrix products, arithmetic and copies ran while one was open for 6% of the time, Pallas kernels for 53%

profile of v7, /device:TPU:0, one launch (start us, length us, event | category | flops | bytes accessed | tf_op | source)
XLA Modules:
  0.0 391.0 jit_solution(11507260331530401279)
XLA Ops:
  10.2 6.1 %route_plan.1 = (bf16[640,768]{1,0:T(8,128)(2,1)}, bf16[512,768]{1,0:T(8,128)(2,1)}, bf16[768,640]{1,0:T(8,128)(2,1)}, bf16[768,512]{1,0:T(8,128)(2,1)}, bf16[8,...) custom-call(s32[1]{0:T(128)} %bitcast.home_ref, s32[2,768]{1,0:T(2,128)} %copy.35.ids_ref, bf16[768,768]{1,0:T(8,128)(2,1)} %bitcast.105, ...), custom_call_target="tpu_custom_call" | custom-call | flops 1585446912 | bytes 3538944 | tf_op jit(solution)/shard_map/route_plan/pallas_call | solution.py:401
  16.4 7.0 %all-to-all-start = ((bf16[8,152,768]{2,1,0:T(8,128)(2,1)}), bf16[8,152,768]{2,1,0:T(8,128)(2,1)}, u32[]{:S(2)}, u32[]{:S(2)}) async-start(bf16[8,152,768]{2,1,0:T(8,128)(2,1)} %get-tuple-element.157), calls=%async_computation | async-start | bytes 3735552 | tf_op jit(solution)/shard_map/all_to_all | solution.py:1017
  35.2 6.0 %convolution_convert_fusion.q_ref.k_ref.v_ref = bf16[768,2304]{1,0:T(8,128)(2,1)} fusion(bf16[768,768]{1,0:T(8,128)(2,1)} %fusion.2.in_ref, bf16[768,2304]{1,0:T(8,128)(2,1)S(1)} %copy-done), kind=kOutput, calls=%fused_computation | convolution fusion | flops 2719678464 | bytes 8257536 | tf_op jit(solution)/shard_map/dot_general | solution.py:23
  41.1 3.8 collective-permute-done.1.refs_1_
  45.0 5.7 %far_projection.1 = (bf16[768,768]{1,0:T(8,128)(2,1)}, bf16[768,1536]{1,0:T(8,128)(2,1)}) custom-call(f32[1,768]{1,0:T(1,128)} %broadcast_in_dim.43.gain_ref.refs_5_, bf16[768,2304]{1,0:T(8,128)(2,1)} %refs_4_.3, bf16[768,2304]{1,0:T(8,128)(2,1)} %refs_4_.3, bf16[256,768]{1,0:T(8,128)(2,1)} %copy-done.23, bf16[256,768]{1,0:T(8,128)(2,1)} %collective-permute-done.1.refs_1_, ...), custom_call_target="tpu_custom_call" | custom-call | flops 1811939328 | bytes 7077888 | tf_op jit(solution)/shard_map/far_projection/pallas_call | solution.py:829
  50.7 24.5 %attention_forward.1 = (bf16[768,768]{1,0:T(8,128)(2,1)}, f32[6,16,768]{2,1,0:T(8,128)}, f32[768,768]{1,0:T(8,128)}, bf16[768,768]{1,0:T(8,128)(2,1)}, bf16[640,...) custom-call(f32[3]{0:T(128)} %compare_select_fusion.flags_ref, bf16[768,2304]{1,0:T(8,128)(2,1)} %convolution_convert_fusion.q_ref.k_ref.v_ref, ...), custom_call_target="tpu_custom_call" | custom-call | flops 5435817984 | bytes 14155776 | tf_op jit(solution)/shard_map/attention_forward/pallas_call | solution.py:134
  75.2 5.0 %all-to-all-start.3 = ((bf16[8,64,768]{2,1,0:T(8,128)(2,1)}), bf16[8,64,768]{2,1,0:T(8,128)(2,1)S(1)}, u32[]{:S(2)}, u32[]{:S(2)}) async-start(bf16[8,64,768]{2,1,0:T(8,128)(2,1)} %bitcast.123), calls=%async_computation.3 | async-start | bytes 1572864 | tf_op jit(solution)/shard_map/all_to_all | solution.py:1017
  82.9 3.4 turn.3.far_ref
  86.3 13.7 %local_part.1 = (f32[768,768]{1,0:T(8,128)}, f32[768,768]{1,0:T(8,128)}, f32[768,128]{1,0:T(8,128)}, f32[768,128]{1,0:T(8,128)}, f32[24,768]{1,0:T(8,128)}) custom-call(f32[768,768]{1,0:T(8,128)} %get-tuple-element.159.hidden_ref.refs_8_, bf16[768,768]{1,0:T(8,128)(2,1)} %get-tuple-element.160.low_ref, bf16[768,768]{1,0:T(8,128)(2,1)} %bitcast.106, ...), custom_call_target="tpu_custom_call" | custom-call | flops 1056964608 | bytes 9437184 | tf_op jit(solution)/shard_map/local_part/pallas_call | solution.py:644
  101.1 4.1 %all-to-all-start.1 = ((bf16[8,80,768]{2,1,0:T(8,128)(2,1)}), bf16[8,80,768]{2,1,0:T(8,128)(2,1)S(1)}, u32[]{:S(2)}, u32[]{:S(2)}) async-start(bf16[8,80,768]{2,1,0:T(8,128)(2,1)} %bitcast.10), calls=%async_computation.1 | async-start | bytes 1966080 | tf_op jit(solution)/shard_map/all_to_all | solution.py:1017
  106.0 17.7 %expert_pass.3 = (bf16[512,896]{1,0:T(8,128)(2,1)}, bf16[512,768]{1,0:T(8,128)(2,1)}, bf16[512,768]{1,0:T(8,128)(2,1)}, bf16[512,2048]{1,0:T(8,128)(2,1)}, bf16[...) custom-call(s32[1]{0:T(128)} %bitcast.home_ref, bf16[512,768]{1,0:T(8,128)(2,1)} %bitcast.121, ...), custom_call_target="tpu_custom_call" | custom-call | flops 9663676416 | bytes 19660800 | tf_op jit(solution)/shard_map/expert_pass/pallas_call | solution.py:489
  123.6 6.8 %all-to-all-done.1 = bf16[8,80,768]{2,1,0:T(8,128)(2,1)S(1)} async-done(((bf16[8,80,768]{2,1,0:T(8,128)(2,1)}), bf16[8,80,768]{2,1,0:T(8,128)(2,1)S(1)}, u32[]{:S(2)}, u32[]{:S(2)}) %all-to-all-start.1) | async-done | bytes 983072 | tf_op jit(solution)/shard_map/all_to_all | solution.py:1017
  130.4 3.8 all-to-all-start.4
  134.2 20.9 %expert_pass.2 = (bf16[640,896]{1,0:T(8,128)(2,1)}, bf16[640,768]{1,0:T(8,128)(2,1)}, bf16[640,768]{1,0:T(8,128)(2,1)}, bf16[640,2048]{1,0:T(8,128)(2,1)}, bf16[...) custom-call(s32[1]{0:T(128)} %bitcast.home_ref, bf16[640,768]{1,0:T(8,128)(2,1)} %bitcast.115, ...), custom_call_target="tpu_custom_call" | custom-call | flops 12079595520 | bytes 22216704 | tf_op jit(solution)/shard_map/expert_pass/pallas_call | solution.py:489
  155.1 5.2 %all-to-all-start.2 = ((bf16[8,80,768]{2,1,0:T(8,128)(2,1)}), bf16[8,80,768]{2,1,0:T(8,128)(2,1)S(1)}, u32[]{:S(2)}, u32[]{:S(2)}) async-start(bf16[8,80,768]{2,1,0:T(8,128)(2,1)} %bitcast.117), calls=%async_computation.2 | async-start | bytes 1966080 | tf_op jit(solution)/shard_map/all_to_all | solution.py:1020
  163.0 17.9 %weight_gradients.1 = (bf16[2,768,2048]{2,1,0:T(8,128)(2,1)}, bf16[2048,768]{1,0:T(8,128)(2,1)}) custom-call(bf16[640,768]{1,0:T(8,128)(2,1)} %bitcast.116, bf16[512,768]{1,0:T(8,128)(2,1)} %bitcast.122, bf16[640,768]{1,0:T(8,128)(2,1)} %get-tuple-element.169.refs_2_, bf16[512,768]{1,0:T(8,128)(2,1)} %get-tuple-element.170.refs_3_, ...), custom_call_target="tpu_custom_call" | custom-call | flops 10871635968 | bytes 27131904 | tf_op jit(solution)/shard_map/weight_gradients/pallas_call | solution.py:538
  180.9 4.6 %all-to-all-done.2 = bf16[8,80,768]{2,1,0:T(8,128)(2,1)S(1)} async-done(((bf16[8,80,768]{2,1,0:T(8,128)(2,1)}), bf16[8,80,768]{2,1,0:T(8,128)(2,1)S(1)}, u32[]{:S(2)}, u32[]{:S(2)}) %all-to-all-start.2) | async-done | bytes 983072 | tf_op jit(solution)/shard_map/all_to_all | solution.py:1020
  186.5 3.9 all-to-all-start.5
  190.4 11.5 %combine_gradients.1 = (f32[768,768]{1,0:T(8,128)}, bf16[768,768]{1,0:T(8,128)(2,1)}, bf16[384,1664]{1,0:T(8,128)(2,1)}, bf16[384,1664]{1,0:T(8,128)(2,1)}) custom-call(s32[1]{0:T(128)} %bitcast.19.core_ref, bf16[768,640]{1,0:T(8,128)(2,1)} %get-tuple-element.145.refs_0_, bf16[768,512]{1,0:T(8,128)(2,1)} %get-tuple-element.146.refs_1_, ...), custom_call_target="tpu_custom_call" | custom-call | flops 3170893824 | bytes 15335424 | tf_op jit(solution)/shard_map/combine_gradients/pallas_call | solution.py:715
  201.9 18.5 %attention_backward.3 = (bf16[384,1664]{1,0:T(8,128)(2,1)}, bf16[384,1664]{1,0:T(8,128)(2,1)}, bf16[768,768]{1,0:T(8,128)(2,1)}, f32[768,768]{1,0:T(8,128)}) custom-call(f32[3]{0:T(128)} %compare_select_fusion.flags_ref, s32[1]{0:T(128)} %bitcast.19.core_ref, ...), custom_call_target="tpu_custom_call", output_to_operand_aliasing={{0}: (14, {}), {1}: (15, {})} | custom-call | flops 6039797760 | bytes 14155776 | tf_op jit(solution)/shard_map/attention_backward/pallas_call | solution.py:324
  221.1 11.2 %attention_backward.4 = (bf16[384,1536]{1,0:T(8,128)(2,1)}, bf16[384,1536]{1,0:T(8,128)(2,1)}, bf16[768,384]{1,0:T(8,128)(2,1)}, f32[768,768]{1,0:T(8,128)}) custom-call(f32[3]{0:T(128)} %compare_select_fusion.flags_ref, s32[1]{0:T(128)} %bitcast.19.core_ref, bf16[768,2304]{1,0:T(8,128)(2,1)} %convolution_convert_fusion.q_ref.k_ref.v_ref, ...), custom_call_target="tpu_custom_call" | custom-call | flops 3019898880 | bytes 11796480 | tf_op jit(solution)/shard_map/attention_backward/pallas_call | solution.py:324
  240.5 25.7 %attention_backward.5 = (bf16[384,1536]{1,0:T(8,128)(2,1)}, bf16[384,1536]{1,0:T(8,128)(2,1)}, bf16[768,1152]{1,0:T(8,128)(2,1)}, bf16[256,768]{1,0:T(8,128)(2,1...) custom-call(f32[3]{0:T(128)} %compare_select_fusion.flags_ref, ...), custom_call_target="tpu_custom_call", output_to_operand_aliasing={{0}: (14, {}), {1}: (15, {})} | custom-call | flops 9059696640 | bytes 16515072 | tf_op jit(solution)/shard_map/attention_backward/pallas_call | solution.py:324
  280.6 6.6 %finish_outputs.1 = (bf16[768,768]{1,0:T(8,128)(2,1)}, f32[128,768]{1,0:T(8,128)}) custom-call(bf16[768,640]{1,0:T(8,128)(2,1)} %get-tuple-element.145.refs_0_, bf16[768,512]{1,0:T(8,128)(2,1)} %get-tuple-element.146.refs_1_, bf16[8,144,896]{2,1,0:T(8,128)(2,1)} %copy-done.4, f32[768,768]{1,0:T(8,128)} %get-tuple-element.216.refs_3_, ...), custom_call_target="tpu_custom_call" | custom-call | flops 1585446912 | bytes 9437184 | tf_op jit(solution)/shard_map/finish_outputs/pallas_call | solution.py:757
  290.1 10.4 %collective-permute-done.11 = bf16[1,96,1536]{2,1,0:T(8,128)(2,1)S(1)} collective-permute-done((bf16[1,96,1536]{2,1,0:T(8,128)(2,1)}, bf16[1,96,1536]{2,1,0:T(8,128)(2,1)S(1)}, u32[]{:S(2)}, u32[]{:S(2)}) %collective-permute-start.11) | collective-permute-done | bytes 294944 | tf_op jit(solution)/shard_map/ppermute | solution.py:887
  308.4 6.0 %collective-permute-done.14.refs_1_ = bf16[1,24,3200]{2,1,0:T(8,128)(2,1)S(1)} collective-permute-done((bf16[1,24,3200]{2,1,0:T(8,128)(2,1)}, bf16[1,24,3200]{2,1,0:T(8,128)(2,1)S(1)}, u32[]{:S(2)}, u32[]{:S(2)}) %collective-permute-start.14) | collective-permute-done | bytes 153632 | tf_op jit(solution)/shard_map/ppermute | solution.py:887
  314.3 3.9 collective-permute-done.16.refs_3_
  325.9 9.4 %input_gradient.1 = f32[768,768]{1,0:T(8,128)} custom-call(bf16[768,768]{1,0:T(8,128)(2,1)} %bitcast.72, f32[1,768]{1,0:T(1,128)} %broadcast_in_dim.43.gain_ref.refs_5_, f32[768,768]{1,0:T(8,128)} %get-tuple-element.229.dhidden_ref, bf16[768,2304]{1,0:T(8,128)(2,1)} %refs_4_.3, bf16[768,768]{1,0:T(8,128)(2,1)} %get-tuple-element.230.refs_0_, ...), custom_call_target="tpu_custom_call" | custom-call | flops 2717908992 | bytes 12976128 | tf_op jit(solution)/shard_map/input_gradient/pallas_call | solution.py:799
  345.7 3.5 fusion.3
  349.1 7.8 %collective-permute-done.20.refs_1_ = bf16[4,24,3200]{2,1,0:T(8,128)(2,1)} collective-permute-done((bf16[4,24,3200]{2,1,0:T(8,128)(2,1)}, bf16[4,24,3200]{2,1,0:T(8,128)(2,1)}, u32[]{:S(2)}, u32[]{:S(2)}) %collective-permute-start.20) | collective-permute-done | bytes 614432 | tf_op jit(solution)/shard_map/ppermute | solution.py:887
  356.9 10.2 %collective-permute-done.21.refs_2_ = bf16[4,24,3200]{2,1,0:T(8,128)(2,1)} collective-permute-done((bf16[4,24,3200]{2,1,0:T(8,128)(2,1)}, bf16[4,24,3200]{2,1,0:T(8,128)(2,1)}, u32[]{:S(2)}, u32[]{:S(2)}) %collective-permute-start.21) | collective-permute-done | bytes 614432 | tf_op jit(solution)/shard_map/ppermute | solution.py:887
  370.3 5.9 %unpack_half.2 = (f32[768,768]{1,0:T(8,128)}, f32[768,2304]{1,0:T(8,128)}, f32[384,128]{1,0:T(8,128)}) custom-call(s32[3]{0:T(128)} %get-tuple-element.295.index_ref, bf16[4,24,3200]{2,1,0:T(8,128)(2,1)} %stack_pieces.1.refs_0_, bf16[4,24,3200]{2,1,0:T(8,128)(2,1)} %collective-permute-done.20.refs_1_, bf16[4,24,3200]{2,1,0:T(8,128)(2,1)} %collective-permute-done.21.refs_2_, ...), custom_call_target="tpu_custom_call" | custom-call | bytes 8257536 | tf_op jit(solution)/shard_map/unpack_half/pallas_call | solution.py:977
  377.6 6.4 %unpack_half.3 = (f32[768,768]{1,0:T(8,128)}, f32[768,2304]{1,0:T(8,128)}, f32[12,768]{1,0:T(8,128)}, f32[2,2,768]{2,1,0:T(2,128)}, f32[2,768]{1,0:T(2,128)}, /*index=5*/f32[768]{0:T(1024)}, f32[768]{0:T(1024)}) custom-call(s32[3]{0:T(128)} %get-tuple-element.294.index_ref, ...), custom_call_target="tpu_custom_call", output_to_operand_aliasing={{0}: (8, {}), {1}: (9, {})} | custom-call | bytes 8257536 | tf_op jit(solution)/shard_map/unpack_half/pallas_call | solution.py:977
  (161 shorter events, 79.3 us)
Async XLA Ops:
  16.4 58.8 %all-to-all-start = ((bf16[8,152,768]{2,1,0:T(8,128)(2,1)}), bf16[8,152,768]{2,1,0:T(8,128)(2,1)}, u32[]{:S(2)}, u32[]{:S(2)}) async-start(bf16[8,152,768]{2,1,0:T(8,128)(2,1)} %get-tuple-element.157), calls=%async_computation | async-start | bytes 3735552 | tf_op jit(solution)/shard_map/all_to_all | solution.py:1017
  23.4 17.7 %collective-permute-start = (bf16[256,768]{1,0:T(8,128)(2,1)}, bf16[256,768]{1,0:T(8,128)(2,1)S(1)}, u32[]{:S(2)}, u32[]{:S(2)}) collective-permute-start(bf16[256,768]{1,0:T(8,128)(2,1)} %get-tuple-element.147), channel_id=1, source_target_pairs={{0,8},{8,0},{16,24},{24,16},{1,9},{9,1},{17,25},{25,17},{2,10},{10... | collective-permute-start | bytes 1179656 | tf_op jit(solution)/shard_map/ppermute | solution.py:1031
  25.0 20.0 %collective-permute-start.1 = (bf16[256,768]{1,0:T(8,128)(2,1)}, bf16[256,768]{1,0:T(8,128)(2,1)}, u32[]{:S(2)}, u32[]{:S(2)}) collective-permute-start(bf16[256,768]{1,0:T(8,128)(2,1)} %get-tuple-element.147), channel_id=1, source_target_pairs={{0,16},{8,24},{16,0},{24,8},{1,17},{9,25},{17,1},{25,9},{2,18},{10... | collective-permute-start | bytes 1179656 | tf_op jit(solution)/shard_map/ppermute | solution.py:1031
  26.5 18.5 %collective-permute-start.2 = (bf16[256,768]{1,0:T(8,128)(2,1)}, bf16[256,768]{1,0:T(8,128)(2,1)}, u32[]{:S(2)}, u32[]{:S(2)}) collective-permute-start(bf16[256,768]{1,0:T(8,128)(2,1)} %get-tuple-element.147), channel_id=1, source_target_pairs={{0,24},{8,16},{16,8},{24,0},{1,25},{9,17},{17,9},{25,1},{2,26},{10... | collective-permute-start | bytes 1179656 | tf_op jit(solution)/shard_map/ppermute | solution.py:1031
  75.2 25.9 %all-to-all-start.3 = ((bf16[8,64,768]{2,1,0:T(8,128)(2,1)}), bf16[8,64,768]{2,1,0:T(8,128)(2,1)S(1)}, u32[]{:S(2)}, u32[]{:S(2)}) async-start(bf16[8,64,768]{2,1,0:T(8,128)(2,1)} %bitcast.123), calls=%async_computation.3 | async-start | bytes 1572864 | tf_op jit(solution)/shard_map/all_to_all | solution.py:1017
  101.1 29.3 %all-to-all-start.1 = ((bf16[8,80,768]{2,1,0:T(8,128)(2,1)}), bf16[8,80,768]{2,1,0:T(8,128)(2,1)S(1)}, u32[]{:S(2)}, u32[]{:S(2)}) async-start(bf16[8,80,768]{2,1,0:T(8,128)(2,1)} %bitcast.10), calls=%async_computation.1 | async-start | bytes 1966080 | tf_op jit(solution)/shard_map/all_to_all | solution.py:1017
  130.4 24.7 %all-to-all-start.4 = ((bf16[8,64,768]{2,1,0:T(8,128)(2,1)}), bf16[8,64,768]{2,1,0:T(8,128)(2,1)S(1)}, u32[]{:S(2)}, u32[]{:S(2)}) async-start(bf16[8,64,768]{2,1,0:T(8,128)(2,1)} %bitcast.124), calls=%async_computation.4 | async-start | bytes 1572864 | tf_op jit(solution)/shard_map/all_to_all | solution.py:1020
  155.1 30.4 %all-to-all-start.2 = ((bf16[8,80,768]{2,1,0:T(8,128)(2,1)}), bf16[8,80,768]{2,1,0:T(8,128)(2,1)S(1)}, u32[]{:S(2)}, u32[]{:S(2)}) async-start(bf16[8,80,768]{2,1,0:T(8,128)(2,1)} %bitcast.117), calls=%async_computation.2 | async-start | bytes 1966080 | tf_op jit(solution)/shard_map/all_to_all | solution.py:1020
  160.3 182.9 %reduce-scatter.5.cloned.1.call-start = ((), (), s32[]{:S(2)}) async-start(), calls=%async_computation.9 | async-start | bytes 3932160 | tf_op jit(solution)/shard_map/reduce_scatter | solution.py:1065
  185.5 160.1 %reduce-scatter.3.cloned.1.call-start = ((), (), s32[]{:S(2)}) async-start(), calls=%async_computation.8 | async-start | bytes 7864320 | tf_op jit(solution)/shard_map/reduce_scatter | solution.py:1064
  186.5 92.8 %all-to-all-start.5 = ((bf16[8,144,896]{2,1,0:T(8,128)(2,1)}), bf16[8,144,896]{2,1,0:T(8,128)(2,1)S(1)}, u32[]{:S(2)}, u32[]{:S(2)}) async-start(bf16[8,144,896]{2,1,0:T(8,128)(2,1)} %pad_maximum_fusion), calls=%async_computation.5 | async-start | bytes 4128768 | tf_op jit(solution)/shard_map/all_to_all | solution.py:1020
  220.4 11.8 %collective-permute-start.3 = (bf16[384,1664]{1,0:T(8,128)(2,1)}, bf16[384,1664]{1,0:T(8,128)(2,1)S(1)}, u32[]{:S(2)}, u32[]{:S(2)}) collective-permute-start(bf16[384,1664]{1,0:T(8,128)(2,1)} %get-tuple-element.196), channel_id=1, source_target_pairs={{0,1},{1,0},{2,3},{3,2},{4,5},{5,4},{6,7},{7,6},{8,9},{9,8},{10,11... | collective-permute-start | bytes 3833864 | tf_op jit(solution)/shard_map/ppermute | solution.py:1075
  236.1 30.1 %collective-permute-start.4 = (bf16[1,96,1664]{2,1,0:T(8,128)(2,1)}, bf16[1,96,1664]{2,1,0:T(8,128)(2,1)S(1)}, u32[]{:S(2)}, u32[]{:S(2)}) collective-permute-start(bf16[1,96,1664]{2,1,0:T(8,128)(2,1)} %get-tuple-element.210), channel_id=1, source_target_pairs={{0,2},{1,3},{2,0},{3,1},{4,6},{5,7},{6,4},{7,5},{8,10},{9,11},{10,... | collective-permute-start | bytes 958472 | tf_op jit(solution)/shard_map/ppermute | solution.py:887
  237.8 28.4 %collective-permute-start.5 = (bf16[1,96,1664]{2,1,0:T(8,128)(2,1)}, bf16[1,96,1664]{2,1,0:T(8,128)(2,1)S(1)}, u32[]{:S(2)}, u32[]{:S(2)}) collective-permute-start(bf16[1,96,1664]{2,1,0:T(8,128)(2,1)} %get-tuple-element.211), channel_id=1, source_target_pairs={{0,4},{1,5},{2,6},{3,7},{4,0},{5,1},{6,2},{7,3},{8,12},{9,13},{10,... | collective-permute-start | bytes 958472 | tf_op jit(solution)/shard_map/ppermute | solution.py:887
  240.2 26.0 %collective-permute-start.6 = (bf16[1,96,1664]{2,1,0:T(8,128)(2,1)}, bf16[1,96,1664]{2,1,0:T(8,128)(2,1)S(1)}, u32[]{:S(2)}, u32[]{:S(2)}) collective-permute-start(bf16[1,96,1664]{2,1,0:T(8,128)(2,1)} %get-tuple-element.212), channel_id=1, source_target_pairs={{0,6},{1,7},{2,4},{3,5},{4,2},{5,3},{6,0},{7,1},{8,14},{9,15},{10,... | collective-permute-start | bytes 958472 | tf_op jit(solution)/shard_map/ppermute | solution.py:887
  267.1 20.1 %collective-permute-start.8 = (bf16[256,768]{1,0:T(8,128)(2,1)}, bf16[256,768]{1,0:T(8,128)(2,1)}, u32[]{:S(2)}, u32[]{:S(2)}) collective-permute-start(bf16[256,768]{1,0:T(8,128)(2,1)} %get-tuple-element.221), channel_id=1, source_target_pairs={{0,8},{8,0},{16,24},{24,16},{1,9},{9,1},{17,25},{25,17},{2,10},{10... | collective-permute-start | bytes 1179656 | tf_op jit(solution)/shard_map/ppermute | solution.py:1088
  268.3 18.9 %collective-permute-start.9 = (bf16[256,768]{1,0:T(8,128)(2,1)}, bf16[256,768]{1,0:T(8,128)(2,1)}, u32[]{:S(2)}, u32[]{:S(2)}) collective-permute-start(bf16[256,768]{1,0:T(8,128)(2,1)} %get-tuple-element.222), channel_id=1, source_target_pairs={{0,16},{8,24},{16,0},{24,8},{1,17},{9,25},{17,1},{25,9},{2,18},{10... | collective-permute-start | bytes 1179656 | tf_op jit(solution)/shard_map/ppermute | solution.py:1088
  273.8 16.2 %collective-permute-start.10 = (bf16[1,96,1536]{2,1,0:T(8,128)(2,1)}, bf16[1,96,1536]{2,1,0:T(8,128)(2,1)S(1)}, u32[]{:S(2)}, u32[]{:S(2)}) collective-permute-start(bf16[1,96,1536]{2,1,0:T(8,128)(2,1)} %get-tuple-element.225), channel_id=1, source_target_pairs={{0,2},{1,3},{2,0},{3,1},{4,6},{5,7},{6,4},{7,5},{8,10},{9,11},{10,... | collective-permute-start | bytes 884744 | tf_op jit(solution)/shard_map/ppermute | solution.py:887
  276.9 23.6 %collective-permute-start.11 = (bf16[1,96,1536]{2,1,0:T(8,128)(2,1)}, bf16[1,96,1536]{2,1,0:T(8,128)(2,1)S(1)}, u32[]{:S(2)}, u32[]{:S(2)}) collective-permute-start(bf16[1,96,1536]{2,1,0:T(8,128)(2,1)} %get-tuple-element.226), channel_id=1, source_target_pairs={{0,4},{1,5},{2,6},{3,7},{4,0},{5,1},{6,2},{7,3},{8,12},{9,13},{10,... | collective-permute-start | bytes 884744 | tf_op jit(solution)/shard_map/ppermute | solution.py:887
  277.9 22.6 %collective-permute-start.12 = (bf16[1,96,1536]{2,1,0:T(8,128)(2,1)}, bf16[1,96,1536]{2,1,0:T(8,128)(2,1)S(1)}, u32[]{:S(2)}, u32[]{:S(2)}) collective-permute-start(bf16[1,96,1536]{2,1,0:T(8,128)(2,1)} %get-tuple-element.227), channel_id=1, source_target_pairs={{0,6},{1,7},{2,4},{3,5},{4,2},{5,3},{6,0},{7,1},{8,14},{9,15},{10,... | collective-permute-start | bytes 884744 | tf_op jit(solution)/shard_map/ppermute | solution.py:887
  287.2 37.9 %collective-permute-start.13 = (bf16[256,768]{1,0:T(8,128)(2,1)S(1)}, bf16[256,768]{1,0:T(8,128)(2,1)S(1)}, u32[]{:S(2)}, u32[]{:S(2)}) collective-permute-start(bf16[256,768]{1,0:T(8,128)(2,1)S(1)} %copy-done.36), channel_id=1, source_target_pairs={{0,24},{8,16},{16,8},{24,0},{1,25},{9,17},{17,9},{25,1},{2,26},{10... | collective-permute-start | bytes 1179656 | tf_op jit(solution)/shard_map/ppermute | solution.py:1088
  304.0 10.3 %collective-permute-start.14 = (bf16[1,24,3200]{2,1,0:T(8,128)(2,1)}, bf16[1,24,3200]{2,1,0:T(8,128)(2,1)S(1)}, u32[]{:S(2)}, u32[]{:S(2)}) collective-permute-start(bf16[1,24,3200]{2,1,0:T(8,128)(2,1)} %get-tuple-element.245), channel_id=1, source_target_pairs={{0,8},{8,0},{16,24},{24,16},{1,9},{9,1},{17,25},{25,17},{2,10},{10... | collective-permute-start | bytes 460808 | tf_op jit(solution)/shard_map/ppermute | solution.py:887
  305.2 9.1 %collective-permute-start.15 = (bf16[1,24,3200]{2,1,0:T(8,128)(2,1)}, bf16[1,24,3200]{2,1,0:T(8,128)(2,1)S(1)}, u32[]{:S(2)}, u32[]{:S(2)}) collective-permute-start(bf16[1,24,3200]{2,1,0:T(8,128)(2,1)} %get-tuple-element.246), channel_id=1, source_target_pairs={{0,16},{8,24},{16,0},{24,8},{1,17},{9,25},{17,1},{25,9},{2,18},{10... | collective-permute-start | bytes 460808 | tf_op jit(solution)/shard_map/ppermute | solution.py:887
  306.6 11.7 %collective-permute-start.16 = (bf16[1,24,3200]{2,1,0:T(8,128)(2,1)}, bf16[1,24,3200]{2,1,0:T(8,128)(2,1)S(1)}, u32[]{:S(2)}, u32[]{:S(2)}) collective-permute-start(bf16[1,24,3200]{2,1,0:T(8,128)(2,1)} %get-tuple-element.247), channel_id=1, source_target_pairs={{0,24},{8,16},{16,8},{24,0},{1,25},{9,17},{17,9},{25,1},{2,26},{10... | collective-permute-start | bytes 460808 | tf_op jit(solution)/shard_map/ppermute | solution.py:887
  320.8 14.6 %collective-permute-start.17 = (bf16[1,24,3200]{2,1,0:T(8,128)(2,1)}, bf16[1,24,3200]{2,1,0:T(8,128)(2,1)S(1)}, u32[]{:S(2)}, u32[]{:S(2)}) collective-permute-start(bf16[1,24,3200]{2,1,0:T(8,128)(2,1)} %sum_pieces.7.refs_0_), channel_id=1, source_target_pairs={{0,2},{1,3},{2,0},{3,1},{4,6},{5,7},{6,4},{7,5},{8,10},{9,11},{10,... | collective-permute-start | bytes 460808 | tf_op jit(solution)/shard_map/ppermute | solution.py:887
  322.3 14.2 %collective-permute-start.18 = (bf16[1,24,3200]{2,1,0:T(8,128)(2,1)}, bf16[1,24,3200]{2,1,0:T(8,128)(2,1)S(1)}, u32[]{:S(2)}, u32[]{:S(2)}) collective-permute-start(bf16[1,24,3200]{2,1,0:T(8,128)(2,1)} %sum_pieces.7.refs_0_), channel_id=1, source_target_pairs={{0,4},{1,5},{2,6},{3,7},{4,0},{5,1},{6,2},{7,3},{8,12},{9,13},{10,... | collective-permute-start | bytes 460808 | tf_op jit(solution)/shard_map/ppermute | solution.py:887
  324.7 11.8 %collective-permute-start.19 = (bf16[1,24,3200]{2,1,0:T(8,128)(2,1)}, bf16[1,24,3200]{2,1,0:T(8,128)(2,1)S(1)}, u32[]{:S(2)}, u32[]{:S(2)}) collective-permute-start(bf16[1,24,3200]{2,1,0:T(8,128)(2,1)} %sum_pieces.7.refs_0_), channel_id=1, source_target_pairs={{0,6},{1,7},{2,4},{3,5},{4,2},{5,3},{6,0},{7,1},{8,14},{9,15},{10,... | collective-permute-start | bytes 460808 | tf_op jit(solution)/shard_map/ppermute | solution.py:887
  339.8 17.1 %collective-permute-start.20 = (bf16[4,24,3200]{2,1,0:T(8,128)(2,1)}, bf16[4,24,3200]{2,1,0:T(8,128)(2,1)}, u32[]{:S(2)}, u32[]{:S(2)}) collective-permute-start(bf16[4,24,3200]{2,1,0:T(8,128)(2,1)} %stack_pieces.1.refs_0_), channel_id=1, source_target_pairs={{0,8},{8,0},{16,24},{24,16},{1,9},{9,1},{17,25},{25,17},{2,10},{10... | collective-permute-start | bytes 1843208 | tf_op jit(solution)/shard_map/ppermute | solution.py:887
  340.3 26.8 %collective-permute-start.21 = (bf16[4,24,3200]{2,1,0:T(8,128)(2,1)}, bf16[4,24,3200]{2,1,0:T(8,128)(2,1)}, u32[]{:S(2)}, u32[]{:S(2)}) collective-permute-start(bf16[4,24,3200]{2,1,0:T(8,128)(2,1)} %stack_pieces.1.refs_0_), channel_id=1, source_target_pairs={{0,16},{8,24},{16,0},{24,8},{1,17},{9,25},{17,1},{25,9},{2,18},{10... | collective-permute-start | bytes 1843208 | tf_op jit(solution)/shard_map/ppermute | solution.py:887
  341.0 26.1 %collective-permute-start.22 = (bf16[4,24,3200]{2,1,0:T(8,128)(2,1)}, bf16[4,24,3200]{2,1,0:T(8,128)(2,1)S(1)}, u32[]{:S(2)}, u32[]{:S(2)}) collective-permute-start(bf16[4,24,3200]{2,1,0:T(8,128)(2,1)} %stack_pieces.1.refs_0_), channel_id=1, source_target_pairs={{0,24},{8,16},{16,8},{24,0},{1,25},{9,17},{17,9},{25,1},{2,26},{10... | collective-permute-start | bytes 1843208 | tf_op jit(solution)/shard_map/ppermute | solution.py:887
  367.9 8.2 %collective-permute-start.23 = (bf16[4,24,3200]{2,1,0:T(8,128)(2,1)S(1)}, bf16[4,24,3200]{2,1,0:T(8,128)(2,1)S(1)}, u32[]{:S(2)}, u32[]{:S(2)}) collective-permute-start(bf16[4,24,3200]{2,1,0:T(8,128)(2,1)S(1)} %copy-done.14), channel_id=1, source_target_pairs={{0,1},{1,0},{2,3},{3,2},{4,5},{5,4},{6,7},{7,6},{8,9},{9,8},{10,11... | collective-permute-start | bytes 1843208 | tf_op jit(solution)/shard_map/ppermute | solution.py:1075
  367.9 8.2 %collective-permute-start.24 = (bf16[4,24,3200]{2,1,0:T(8,128)(2,1)}, bf16[4,24,3200]{2,1,0:T(8,128)(2,1)S(1)}, u32[]{:S(2)}, u32[]{:S(2)}) collective-permute-start(bf16[4,24,3200]{2,1,0:T(8,128)(2,1)} %collective-permute-done.20.refs_1_), channel_id=1, source_target_pairs={{0,1},{1,0},{2,3},{3,2},{4,5},{5,4},{6,7},{7,6},{8,9},{9,8},{10,11... | collective-permute-start | bytes 1843208 | tf_op jit(solution)/shard_map/ppermute | solution.py:1075
  (40 other events, 229.3 us)
Sparse Core Ops, SparseCore 0:
  185.7 41.9 reduce-scatter.4
  231.2 84.2 reduce-scatter.2

commit v8 on v7

--- a/solution.py
+++ b/solution.py
@@ -366,7 +366,7 @@
     both = jnp.where(names[0] | names[1], 1.0, 0.0).astype(bf16)
     earlier = lax.broadcasted_iota(jnp.int32, (tok, tok), 0) < lax.broadcasted_iota(jnp.int32, (tok, tok), 1)
     before = dot_nn(both, jnp.where(earlier, 1.0, 0.0).astype(bf16))
-    pieces = [piece.astype(f32) for piece in split_low(prev_ref[...], 3)]
+    pieces = [piece.astype(f32) for piece in split_low(prev_ref[:, 0, :], 3)]
     extra = jnp.concatenate(pieces + [jnp.zeros((EXTRA - 3 * ALL_EXPERTS, tok), f32)], axis=0).T.astype(bf16)
     slot = [jnp.sum(jnp.where(n, before, 0.0), axis=0, keepdims=True).astype(jnp.int32) for n in names]
     extras = []
@@ -586,11 +586,13 @@
     low = low_ref[...]
     grad = grad_ref[...].astype(f32)
     raw = dot_nn(low, mix_ref[...])
-    prev = jnp.concatenate([prev_ref[...], jnp.zeros((raw.shape[0], EXTRA - ALL_EXPERTS), f32)], axis=1)
+    block = raw.shape[0]
+    prev = jnp.concatenate([prev_ref[:, 0, :], jnp.zeros((EXTRA - ALL_EXPERTS, block), f32)], axis=0).T
     logits = jnp.where(lane < ALL_EXPERTS, raw + prev, NEG)
     unnormed = jnp.exp(logits - jnp.max(logits, axis=1, keepdims=True))
     probs = unnormed / jnp.sum(unnormed, axis=1, keepdims=True)
-    named = (ids_ref[:, 0:1] == lane) | (ids_ref[:, 1:2] == lane)
+    ids = jnp.concatenate([ids_ref[...].astype(f32), jnp.zeros((SMALL - 2, block), f32)], axis=0).T
+    named = (ids[:, 0:1] == lane.astype(f32)) | (ids[:, 1:2] == lane.astype(f32))
     gates = jnp.where(named, probs, 0.0)
     copy_gate = gates[:, FFN_EXPERTS + 1 : FFN_EXPERTS + 2]
     dots = jnp.sum(grad * normed, axis=1, keepdims=True)
@@ -644,7 +646,7 @@
     return pl.pallas_call(
         local_kernel,
         grid=(tok // block,),
-        in_specs=[tiles(width), tiles(width), tiles(width), tiles(ALL_EXPERTS), tiles(2), fixed(mix), fixed(gain), fixed(vec)],
+        in_specs=[tiles(width), tiles(width), tiles(width), pl.BlockSpec((ALL_EXPERTS, 1, block), lambda i: (0, 0, i)), pl.BlockSpec((2, block), lambda i: (0, i)), fixed(mix), fixed(gain), fixed(vec)],
         out_specs=[tiles(width), tiles(width), tiles(EXTRA), tiles(EXTRA), pl.BlockSpec((3 * SMALL, width), lambda i: (0, 0))],
         out_shape=[jax.ShapeDtypeStruct(s, f32) for s in shapes],
         compiler_params=pltpu.CompilerParams(vmem_limit_bytes=60 * 2**20),
@@ -1024,10 +1026,11 @@
     upstream_low = out_grad[0]
     flags = jnp.where((me_c ^ jnp.arange(1, n_ctx)) < me_c, 0.0, NEG).astype(f32)
 
-    prev = prev_logits[0]
+    prev = prev_logits.transpose(2, 0, 1)
+    ids = routes.transpose(0, 2, 1)[0]
     mix = jnp.concatenate([router, jnp.zeros((width, 4), bf16), const_gate[0], const_gate[1], jnp.zeros((width, EXTRA - 20), bf16)], axis=1)
     router_pad = jnp.pad(router, ((0, 0), (0, EXTRA - ALL_EXPERTS)))
-    turned, chosen, early_sent, x_prompt = route_plan(home, routes[0].T, upstream_low, prev.T, x_low, plen, groups)
+    turned, chosen, early_sent, x_prompt = route_plan(home, ids, upstream_low, prev, x_low, plen, groups)
     far = [lax.ppermute(x_prompt, "ctx", xor_pairs(n_ctx, k)) for k in range(1, n_ctx)]
 
     tokens_in = x_low.astype(f32)
@@ -1041,7 +1044,7 @@
     mixed_low, lse, hidden, moe_low, sent = attention_forward(flags, projected, kv_far, plen, x_low, w_out, moe_gain[None], turned)
     sent, hidden, early = lax.optimization_barrier((sent, hidden, early))
 
-    local_out, d_normed_local, probs, d_probs, small_local = local_part(hidden, moe_low, upstream_low, prev, routes[0], mix, moe_gain[None], const_vec)
+    local_out, d_normed_local, probs, d_probs, small_local = local_part(hidden, moe_low, upstream_low, prev, ids, mix, moe_gain[None], const_vec)
     far_t = turn(act_far)
     sent = [after(sent[0], local_out, d_normed_local, far_t), sent[1]]
     got = [deal(part.reshape(FFN_EXPERTS, -1, width)) for part in sent]

time: 395 us -> 392 us (level)
    unnamed x80 -> x74, local copies, waits for them, and re-layouts: 13.2 us -> 11.4 us
where the time goes in v8:
time: 392 us; the launch traced here: 387 us
  Pallas kernels  220 us (56%)
  starting transfers between devices  59.9 us (15%)
  waiting for transfers between devices  59.1 us (15%)
  local copies, waits for them, and re-layouts  18.8 us (5%)
  between operations  14.7 us (4%)
  other arithmetic  9.21 us (2%)
  matrix products  5.98 us (2%)
    pallas_call x3, Pallas kernels, attention_backward(): pl.pallas_call(functools.partial(attention_backward_kernel, plen, bool(st...  55.4 us
    ppermute x15, waiting for transfers between devices, swap(): lax.ppermute(pieces[k], axis, xor_pairs(size, unit * k))  39.6 us
    pallas_call x2, Pallas kernels, expert_pass(): pl.pallas_call(functools.partial(expert_kernel, group), grid=(ff // tile,...  38.6 us
    pallas_call x1, Pallas kernels, attention_forward(): pl.pallas_call(functools.partial(attention_forward_kernel, plen, len(turn...  24.5 us
    ppermute x15, starting transfers between devices, swap(): lax.ppermute(pieces[k], axis, xor_pairs(size, unit * k))  21.2 us
    pallas_call x1, Pallas kernels, weight_gradients(): pl.pallas_call(functools.partial(weight_kernel, count), grid=(ff // tile,...  17.9 us
    all_to_all x3, starting transfers between devices, deal(): return lax.all_to_all(value, 'exp', 0, 0, tiled=True)  15.6 us
    all_to_all x3, starting transfers between devices, give_back(): value = lax.all_to_all(value, 'exp', 0, 0, tiled=True)  12.8 us
  transfers between devices with their start and end apart: 35, of which 12 were waited for; matrix products, arithmetic and copies ran while one was open for 6% of the time, Pallas kernels for 53%

profile of v8, /device:TPU:0, one launch (start us, length us, event | category | flops | bytes accessed | tf_op | source)
XLA Modules:
  0.0 387.3 jit_solution(352973620465815442)
XLA Ops:
  7.2 6.2 %route_plan.1 = (bf16[640,768]{1,0:T(8,128)(2,1)}, bf16[512,768]{1,0:T(8,128)(2,1)}, bf16[768,640]{1,0:T(8,128)(2,1)}, bf16[768,512]{1,0:T(8,128)(2,1)}, bf16[8,...) custom-call(s32[1]{0:T(128)} %bitcast.home_ref, s32[2,768]{1,0:T(2,128)} %bitcast.120, bf16[768,768]{1,0:T(8,128)(2,1)} %bitcast.101, ...), custom_call_target="tpu_custom_call" | custom-call | flops 1585446912 | bytes 3538944 | tf_op jit(solution)/shard_map/route_plan/pallas_call | solution.py:401
  13.4 7.0 %all-to-all-start = ((bf16[8,152,768]{2,1,0:T(8,128)(2,1)}), bf16[8,152,768]{2,1,0:T(8,128)(2,1)}, u32[]{:S(2)}, u32[]{:S(2)}) async-start(bf16[8,152,768]{2,1,0:T(8,128)(2,1)} %get-tuple-element.157), calls=%async_computation | async-start | bytes 3735552 | tf_op jit(solution)/shard_map/all_to_all | solution.py:1019
  27.7 3.5 turn.2.act_ref
  32.3 6.0 %convolution_convert_fusion.q_ref.k_ref.v_ref = bf16[768,2304]{1,0:T(8,128)(2,1)} fusion(bf16[768,768]{1,0:T(8,128)(2,1)} %fusion.2.in_ref, bf16[768,2304]{1,0:T(8,128)(2,1)S(1)} %copy-done), kind=kOutput, calls=%fused_computation | convolution fusion | flops 2719678464 | bytes 8257536 | tf_op jit(solution)/shard_map/dot_general | solution.py:23
  38.3 3.7 collective-permute-done.1.refs_1_
  42.0 5.7 %far_projection.1 = (bf16[768,768]{1,0:T(8,128)(2,1)}, bf16[768,1536]{1,0:T(8,128)(2,1)}) custom-call(f32[1,768]{1,0:T(1,128)} %broadcast_in_dim.43.gain_ref.refs_5_, bf16[768,2304]{1,0:T(8,128)(2,1)} %refs_4_.3, bf16[768,2304]{1,0:T(8,128)(2,1)} %refs_4_.3, bf16[256,768]{1,0:T(8,128)(2,1)} %copy-done.22, bf16[256,768]{1,0:T(8,128)(2,1)} %collective-permute-done.1.refs_1_, ...), custom_call_target="tpu_custom_call" | custom-call | flops 1811939328 | bytes 7077888 | tf_op jit(solution)/shard_map/far_projection/pallas_call | solution.py:831
  47.7 24.5 %attention_forward.1 = (bf16[768,768]{1,0:T(8,128)(2,1)}, f32[6,16,768]{2,1,0:T(8,128)}, f32[768,768]{1,0:T(8,128)}, bf16[768,768]{1,0:T(8,128)(2,1)}, bf16[640,...) custom-call(f32[3]{0:T(128)} %compare_select_fusion.flags_ref, bf16[768,2304]{1,0:T(8,128)(2,1)} %convolution_convert_fusion.q_ref.k_ref.v_ref, ...), custom_call_target="tpu_custom_call" | custom-call | flops 5435817984 | bytes 14155776 | tf_op jit(solution)/shard_map/attention_forward/pallas_call | solution.py:134
  72.2 5.0 %all-to-all-start.3 = ((bf16[8,64,768]{2,1,0:T(8,128)(2,1)}), bf16[8,64,768]{2,1,0:T(8,128)(2,1)S(1)}, u32[]{:S(2)}, u32[]{:S(2)}) async-start(bf16[8,64,768]{2,1,0:T(8,128)(2,1)} %bitcast.116), calls=%async_computation.3 | async-start | bytes 1572864 | tf_op jit(solution)/shard_map/all_to_all | solution.py:1019
  82.4 12.6 %local_part.1 = (f32[768,768]{1,0:T(8,128)}, f32[768,768]{1,0:T(8,128)}, f32[768,128]{1,0:T(8,128)}, f32[768,128]{1,0:T(8,128)}, f32[24,768]{1,0:T(8,128)}) custom-call(f32[768,768]{1,0:T(8,128)} %get-tuple-element.159.hidden_ref.refs_8_, bf16[768,768]{1,0:T(8,128)(2,1)} %get-tuple-element.160.low_ref, bf16[768,768]{1,0:T(8,128)(2,1)} %bitcast.102, ...), custom_call_target="tpu_custom_call" | custom-call | flops 1056964608 | bytes 9437184 | tf_op jit(solution)/shard_map/local_part/pallas_call | solution.py:646
  98.1 3.6 all-to-all-start.1
  102.4 17.7 %expert_pass.3 = (bf16[512,896]{1,0:T(8,128)(2,1)}, bf16[512,768]{1,0:T(8,128)(2,1)}, bf16[512,768]{1,0:T(8,128)(2,1)}, bf16[512,2048]{1,0:T(8,128)(2,1)}, bf16[...) custom-call(s32[1]{0:T(128)} %bitcast.home_ref, bf16[512,768]{1,0:T(8,128)(2,1)} %bitcast.114, ...), custom_call_target="tpu_custom_call" | custom-call | flops 9663676416 | bytes 19660800 | tf_op jit(solution)/shard_map/expert_pass/pallas_call | solution.py:489
  120.1 6.7 %all-to-all-done.1 = bf16[8,80,768]{2,1,0:T(8,128)(2,1)S(1)} async-done(((bf16[8,80,768]{2,1,0:T(8,128)(2,1)}), bf16[8,80,768]{2,1,0:T(8,128)(2,1)S(1)}, u32[]{:S(2)}, u32[]{:S(2)}) %all-to-all-start.1) | async-done | bytes 983072 | tf_op jit(solution)/shard_map/all_to_all | solution.py:1019
  126.8 3.8 all-to-all-start.4
  130.6 20.9 %expert_pass.2 = (bf16[640,896]{1,0:T(8,128)(2,1)}, bf16[640,768]{1,0:T(8,128)(2,1)}, bf16[640,768]{1,0:T(8,128)(2,1)}, bf16[640,2048]{1,0:T(8,128)(2,1)}, bf16[...) custom-call(s32[1]{0:T(128)} %bitcast.home_ref, bf16[640,768]{1,0:T(8,128)(2,1)} %bitcast.108, ...), custom_call_target="tpu_custom_call" | custom-call | flops 12079595520 | bytes 22216704 | tf_op jit(solution)/shard_map/expert_pass/pallas_call | solution.py:489
  151.5 5.2 %all-to-all-start.2 = ((bf16[8,80,768]{2,1,0:T(8,128)(2,1)}), bf16[8,80,768]{2,1,0:T(8,128)(2,1)S(1)}, u32[]{:S(2)}, u32[]{:S(2)}) async-start(bf16[8,80,768]{2,1,0:T(8,128)(2,1)} %bitcast.110), calls=%async_computation.2 | async-start | bytes 1966080 | tf_op jit(solution)/shard_map/all_to_all | solution.py:1022
  159.4 17.9 %weight_gradients.1 = (bf16[2,768,2048]{2,1,0:T(8,128)(2,1)}, bf16[2048,768]{1,0:T(8,128)(2,1)}) custom-call(bf16[640,768]{1,0:T(8,128)(2,1)} %bitcast.109, bf16[512,768]{1,0:T(8,128)(2,1)} %bitcast.115, bf16[640,768]{1,0:T(8,128)(2,1)} %get-tuple-element.169.refs_2_, bf16[512,768]{1,0:T(8,128)(2,1)} %get-tuple-element.170.refs_3_, ...), custom_call_target="tpu_custom_call" | custom-call | flops 10871635968 | bytes 27131904 | tf_op jit(solution)/shard_map/weight_gradients/pallas_call | solution.py:538
  177.3 4.6 %all-to-all-done.2 = bf16[8,80,768]{2,1,0:T(8,128)(2,1)S(1)} async-done(((bf16[8,80,768]{2,1,0:T(8,128)(2,1)}), bf16[8,80,768]{2,1,0:T(8,128)(2,1)S(1)}, u32[]{:S(2)}, u32[]{:S(2)}) %all-to-all-start.2) | async-done | bytes 983072 | tf_op jit(solution)/shard_map/all_to_all | solution.py:1022
  182.9 3.9 all-to-all-start.5
  186.7 11.5 %combine_gradients.1 = (f32[768,768]{1,0:T(8,128)}, bf16[768,768]{1,0:T(8,128)(2,1)}, bf16[384,1664]{1,0:T(8,128)(2,1)}, bf16[384,1664]{1,0:T(8,128)(2,1)}) custom-call(s32[1]{0:T(128)} %bitcast.18.core_ref, bf16[768,640]{1,0:T(8,128)(2,1)} %get-tuple-element.145.refs_0_, bf16[768,512]{1,0:T(8,128)(2,1)} %get-tuple-element.146.refs_1_, ...), custom_call_target="tpu_custom_call" | custom-call | flops 3170893824 | bytes 15335424 | tf_op jit(solution)/shard_map/combine_gradients/pallas_call | solution.py:717
  198.3 18.5 %attention_backward.3 = (bf16[384,1664]{1,0:T(8,128)(2,1)}, bf16[384,1664]{1,0:T(8,128)(2,1)}, bf16[768,768]{1,0:T(8,128)(2,1)}, f32[768,768]{1,0:T(8,128)}) custom-call(f32[3]{0:T(128)} %compare_select_fusion.flags_ref, s32[1]{0:T(128)} %bitcast.18.core_ref, ...), custom_call_target="tpu_custom_call", output_to_operand_aliasing={{0}: (14, {}), {1}: (15, {})} | custom-call | flops 6039797760 | bytes 14155776 | tf_op jit(solution)/shard_map/attention_backward/pallas_call | solution.py:324
  217.5 11.2 %attention_backward.4 = (bf16[384,1536]{1,0:T(8,128)(2,1)}, bf16[384,1536]{1,0:T(8,128)(2,1)}, bf16[768,384]{1,0:T(8,128)(2,1)}, f32[768,768]{1,0:T(8,128)}) custom-call(f32[3]{0:T(128)} %compare_select_fusion.flags_ref, s32[1]{0:T(128)} %bitcast.18.core_ref, bf16[768,2304]{1,0:T(8,128)(2,1)} %convolution_convert_fusion.q_ref.k_ref.v_ref, ...), custom_call_target="tpu_custom_call" | custom-call | flops 3019898880 | bytes 11796480 | tf_op jit(solution)/shard_map/attention_backward/pallas_call | solution.py:324
  236.9 25.7 %attention_backward.5 = (bf16[384,1536]{1,0:T(8,128)(2,1)}, bf16[384,1536]{1,0:T(8,128)(2,1)}, bf16[768,1152]{1,0:T(8,128)(2,1)}, bf16[256,768]{1,0:T(8,128)(2,1...) custom-call(f32[3]{0:T(128)} %compare_select_fusion.flags_ref, ...), custom_call_target="tpu_custom_call", output_to_operand_aliasing={{0}: (14, {}), {1}: (15, {})} | custom-call | flops 9059696640 | bytes 16515072 | tf_op jit(solution)/shard_map/attention_backward/pallas_call | solution.py:324
  277.0 6.6 %finish_outputs.1 = (bf16[768,768]{1,0:T(8,128)(2,1)}, f32[128,768]{1,0:T(8,128)}) custom-call(bf16[768,640]{1,0:T(8,128)(2,1)} %get-tuple-element.145.refs_0_, bf16[768,512]{1,0:T(8,128)(2,1)} %get-tuple-element.146.refs_1_, bf16[8,144,896]{2,1,0:T(8,128)(2,1)} %copy-done.4, f32[768,768]{1,0:T(8,128)} %get-tuple-element.216.refs_3_, ...), custom_call_target="tpu_custom_call" | custom-call | flops 1585446912 | bytes 9437184 | tf_op jit(solution)/shard_map/finish_outputs/pallas_call | solution.py:759
  286.5 10.4 %collective-permute-done.11 = bf16[1,96,1536]{2,1,0:T(8,128)(2,1)S(1)} collective-permute-done((bf16[1,96,1536]{2,1,0:T(8,128)(2,1)}, bf16[1,96,1536]{2,1,0:T(8,128)(2,1)S(1)}, u32[]{:S(2)}, u32[]{:S(2)}) %collective-permute-start.11) | collective-permute-done | bytes 294944 | tf_op jit(solution)/shard_map/ppermute | solution.py:889
  304.8 5.9 %collective-permute-done.14.refs_1_ = bf16[1,24,3200]{2,1,0:T(8,128)(2,1)S(1)} collective-permute-done((bf16[1,24,3200]{2,1,0:T(8,128)(2,1)}, bf16[1,24,3200]{2,1,0:T(8,128)(2,1)S(1)}, u32[]{:S(2)}, u32[]{:S(2)}) %collective-permute-start.14) | collective-permute-done | bytes 153632 | tf_op jit(solution)/shard_map/ppermute | solution.py:889
  310.6 3.9 %collective-permute-done.16.refs_3_ = bf16[1,24,3200]{2,1,0:T(8,128)(2,1)S(1)} collective-permute-done((bf16[1,24,3200]{2,1,0:T(8,128)(2,1)}, bf16[1,24,3200]{2,1,0:T(8,128)(2,1)S(1)}, u32[]{:S(2)}, u32[]{:S(2)}) %collective-permute-start.16) | collective-permute-done | bytes 153632 | tf_op jit(solution)/shard_map/ppermute | solution.py:889
  322.2 9.4 %input_gradient.1 = f32[768,768]{1,0:T(8,128)} custom-call(bf16[768,768]{1,0:T(8,128)(2,1)} %bitcast.68, f32[1,768]{1,0:T(1,128)} %broadcast_in_dim.43.gain_ref.refs_5_, f32[768,768]{1,0:T(8,128)} %get-tuple-element.229.dhidden_ref, bf16[768,2304]{1,0:T(8,128)(2,1)} %refs_4_.3, bf16[768,768]{1,0:T(8,128)(2,1)} %get-tuple-element.230.refs_0_, ...), custom_call_target="tpu_custom_call" | custom-call | flops 2717908992 | bytes 12976128 | tf_op jit(solution)/shard_map/input_gradient/pallas_call | solution.py:801
  342.0 3.5 fusion.3
  345.5 7.8 %collective-permute-done.20.refs_1_ = bf16[4,24,3200]{2,1,0:T(8,128)(2,1)} collective-permute-done((bf16[4,24,3200]{2,1,0:T(8,128)(2,1)}, bf16[4,24,3200]{2,1,0:T(8,128)(2,1)}, u32[]{:S(2)}, u32[]{:S(2)}) %collective-permute-start.20) | collective-permute-done | bytes 614432 | tf_op jit(solution)/shard_map/ppermute | solution.py:889
  353.2 10.2 %collective-permute-done.21.refs_2_ = bf16[4,24,3200]{2,1,0:T(8,128)(2,1)} collective-permute-done((bf16[4,24,3200]{2,1,0:T(8,128)(2,1)}, bf16[4,24,3200]{2,1,0:T(8,128)(2,1)}, u32[]{:S(2)}, u32[]{:S(2)}) %collective-permute-start.21) | collective-permute-done | bytes 614432 | tf_op jit(solution)/shard_map/ppermute | solution.py:889
  366.6 5.9 %unpack_half.2 = (f32[768,768]{1,0:T(8,128)}, f32[768,2304]{1,0:T(8,128)}, f32[384,128]{1,0:T(8,128)}) custom-call(s32[3]{0:T(128)} %get-tuple-element.295.index_ref, bf16[4,24,3200]{2,1,0:T(8,128)(2,1)} %stack_pieces.1.refs_0_, bf16[4,24,3200]{2,1,0:T(8,128)(2,1)} %collective-permute-done.20.refs_1_, bf16[4,24,3200]{2,1,0:T(8,128)(2,1)} %collective-permute-done.21.refs_2_, ...), custom_call_target="tpu_custom_call" | custom-call | bytes 8257536 | tf_op jit(solution)/shard_map/unpack_half/pallas_call | solution.py:979
  373.9 6.4 %unpack_half.3 = (f32[768,768]{1,0:T(8,128)}, f32[768,2304]{1,0:T(8,128)}, f32[12,768]{1,0:T(8,128)}, f32[2,2,768]{2,1,0:T(2,128)}, f32[2,768]{1,0:T(2,128)}, /*index=5*/f32[768]{0:T(1024)}, f32[768]{0:T(1024)}) custom-call(s32[3]{0:T(128)} %get-tuple-element.294.index_ref, ...), custom_call_target="tpu_custom_call", output_to_operand_aliasing={{0}: (8, {}), {1}: (9, {})} | custom-call | bytes 8257536 | tf_op jit(solution)/shard_map/unpack_half/pallas_call | solution.py:979
  (153 shorter events, 77.4 us)
Async XLA Ops:
  13.4 58.8 %all-to-all-start = ((bf16[8,152,768]{2,1,0:T(8,128)(2,1)}), bf16[8,152,768]{2,1,0:T(8,128)(2,1)}, u32[]{:S(2)}, u32[]{:S(2)}) async-start(bf16[8,152,768]{2,1,0:T(8,128)(2,1)} %get-tuple-element.157), calls=%async_computation | async-start | bytes 3735552 | tf_op jit(solution)/shard_map/all_to_all | solution.py:1019
  20.4 17.9 %collective-permute-start = (bf16[256,768]{1,0:T(8,128)(2,1)}, bf16[256,768]{1,0:T(8,128)(2,1)S(1)}, u32[]{:S(2)}, u32[]{:S(2)}) collective-permute-start(bf16[256,768]{1,0:T(8,128)(2,1)} %get-tuple-element.147), channel_id=1, source_target_pairs={{0,8},{8,0},{16,24},{24,16},{1,9},{9,1},{17,25},{25,17},{2,10},{10... | collective-permute-start | bytes 1179656 | tf_op jit(solution)/shard_map/ppermute | solution.py:1034
  22.0 20.0 %collective-permute-start.1 = (bf16[256,768]{1,0:T(8,128)(2,1)}, bf16[256,768]{1,0:T(8,128)(2,1)}, u32[]{:S(2)}, u32[]{:S(2)}) collective-permute-start(bf16[256,768]{1,0:T(8,128)(2,1)} %get-tuple-element.147), channel_id=1, source_target_pairs={{0,16},{8,24},{16,0},{24,8},{1,17},{9,25},{17,1},{25,9},{2,18},{10... | collective-permute-start | bytes 1179656 | tf_op jit(solution)/shard_map/ppermute | solution.py:1034
  23.5 18.5 %collective-permute-start.2 = (bf16[256,768]{1,0:T(8,128)(2,1)}, bf16[256,768]{1,0:T(8,128)(2,1)}, u32[]{:S(2)}, u32[]{:S(2)}) collective-permute-start(bf16[256,768]{1,0:T(8,128)(2,1)} %get-tuple-element.147), channel_id=1, source_target_pairs={{0,24},{8,16},{16,8},{24,0},{1,25},{9,17},{17,9},{25,1},{2,26},{10... | collective-permute-start | bytes 1179656 | tf_op jit(solution)/shard_map/ppermute | solution.py:1034
  72.2 25.9 %all-to-all-start.3 = ((bf16[8,64,768]{2,1,0:T(8,128)(2,1)}), bf16[8,64,768]{2,1,0:T(8,128)(2,1)S(1)}, u32[]{:S(2)}, u32[]{:S(2)}) async-start(bf16[8,64,768]{2,1,0:T(8,128)(2,1)} %bitcast.116), calls=%async_computation.3 | async-start | bytes 1572864 | tf_op jit(solution)/shard_map/all_to_all | solution.py:1019
  98.1 28.7 %all-to-all-start.1 = ((bf16[8,80,768]{2,1,0:T(8,128)(2,1)}), bf16[8,80,768]{2,1,0:T(8,128)(2,1)S(1)}, u32[]{:S(2)}, u32[]{:S(2)}) async-start(bf16[8,80,768]{2,1,0:T(8,128)(2,1)} %bitcast.9), calls=%async_computation.1 | async-start | bytes 1966080 | tf_op jit(solution)/shard_map/all_to_all | solution.py:1019
  126.8 24.7 %all-to-all-start.4 = ((bf16[8,64,768]{2,1,0:T(8,128)(2,1)}), bf16[8,64,768]{2,1,0:T(8,128)(2,1)S(1)}, u32[]{:S(2)}, u32[]{:S(2)}) async-start(bf16[8,64,768]{2,1,0:T(8,128)(2,1)} %bitcast.117), calls=%async_computation.4 | async-start | bytes 1572864 | tf_op jit(solution)/shard_map/all_to_all | solution.py:1022
  151.5 30.4 %all-to-all-start.2 = ((bf16[8,80,768]{2,1,0:T(8,128)(2,1)}), bf16[8,80,768]{2,1,0:T(8,128)(2,1)S(1)}, u32[]{:S(2)}, u32[]{:S(2)}) async-start(bf16[8,80,768]{2,1,0:T(8,128)(2,1)} %bitcast.110), calls=%async_computation.2 | async-start | bytes 1966080 | tf_op jit(solution)/shard_map/all_to_all | solution.py:1022
  156.7 182.9 %reduce-scatter.5.cloned.1.call-start = ((), (), s32[]{:S(2)}) async-start(), calls=%async_computation.9 | async-start | bytes 3932160 | tf_op jit(solution)/shard_map/reduce_scatter | solution.py:1068
  181.9 160.1 %reduce-scatter.3.cloned.1.call-start = ((), (), s32[]{:S(2)}) async-start(), calls=%async_computation.8 | async-start | bytes 7864320 | tf_op jit(solution)/shard_map/reduce_scatter | solution.py:1067
  182.9 92.8 %all-to-all-start.5 = ((bf16[8,144,896]{2,1,0:T(8,128)(2,1)}), bf16[8,144,896]{2,1,0:T(8,128)(2,1)S(1)}, u32[]{:S(2)}, u32[]{:S(2)}) async-start(bf16[8,144,896]{2,1,0:T(8,128)(2,1)} %pad_maximum_fusion), calls=%async_computation.5 | async-start | bytes 4128768 | tf_op jit(solution)/shard_map/all_to_all | solution.py:1022
  216.8 11.8 %collective-permute-start.3 = (bf16[384,1664]{1,0:T(8,128)(2,1)}, bf16[384,1664]{1,0:T(8,128)(2,1)S(1)}, u32[]{:S(2)}, u32[]{:S(2)}) collective-permute-start(bf16[384,1664]{1,0:T(8,128)(2,1)} %get-tuple-element.196), channel_id=1, source_target_pairs={{0,1},{1,0},{2,3},{3,2},{4,5},{5,4},{6,7},{7,6},{8,9},{9,8},{10,11... | collective-permute-start | bytes 3833864 | tf_op jit(solution)/shard_map/ppermute | solution.py:1078
  232.5 30.1 %collective-permute-start.4 = (bf16[1,96,1664]{2,1,0:T(8,128)(2,1)}, bf16[1,96,1664]{2,1,0:T(8,128)(2,1)S(1)}, u32[]{:S(2)}, u32[]{:S(2)}) collective-permute-start(bf16[1,96,1664]{2,1,0:T(8,128)(2,1)} %get-tuple-element.210), channel_id=1, source_target_pairs={{0,2},{1,3},{2,0},{3,1},{4,6},{5,7},{6,4},{7,5},{8,10},{9,11},{10,... | collective-permute-start | bytes 958472 | tf_op jit(solution)/shard_map/ppermute | solution.py:889
  234.2 28.4 %collective-permute-start.5 = (bf16[1,96,1664]{2,1,0:T(8,128)(2,1)}, bf16[1,96,1664]{2,1,0:T(8,128)(2,1)S(1)}, u32[]{:S(2)}, u32[]{:S(2)}) collective-permute-start(bf16[1,96,1664]{2,1,0:T(8,128)(2,1)} %get-tuple-element.211), channel_id=1, source_target_pairs={{0,4},{1,5},{2,6},{3,7},{4,0},{5,1},{6,2},{7,3},{8,12},{9,13},{10,... | collective-permute-start | bytes 958472 | tf_op jit(solution)/shard_map/ppermute | solution.py:889
  236.6 26.1 %collective-permute-start.6 = (bf16[1,96,1664]{2,1,0:T(8,128)(2,1)}, bf16[1,96,1664]{2,1,0:T(8,128)(2,1)S(1)}, u32[]{:S(2)}, u32[]{:S(2)}) collective-permute-start(bf16[1,96,1664]{2,1,0:T(8,128)(2,1)} %get-tuple-element.212), channel_id=1, source_target_pairs={{0,6},{1,7},{2,4},{3,5},{4,2},{5,3},{6,0},{7,1},{8,14},{9,15},{10,... | collective-permute-start | bytes 958472 | tf_op jit(solution)/shard_map/ppermute | solution.py:889
  263.5 20.1 %collective-permute-start.8 = (bf16[256,768]{1,0:T(8,128)(2,1)}, bf16[256,768]{1,0:T(8,128)(2,1)}, u32[]{:S(2)}, u32[]{:S(2)}) collective-permute-start(bf16[256,768]{1,0:T(8,128)(2,1)} %get-tuple-element.221), channel_id=1, source_target_pairs={{0,8},{8,0},{16,24},{24,16},{1,9},{9,1},{17,25},{25,17},{2,10},{10... | collective-permute-start | bytes 1179656 | tf_op jit(solution)/shard_map/ppermute | solution.py:1091
  264.7 18.9 %collective-permute-start.9 = (bf16[256,768]{1,0:T(8,128)(2,1)}, bf16[256,768]{1,0:T(8,128)(2,1)}, u32[]{:S(2)}, u32[]{:S(2)}) collective-permute-start(bf16[256,768]{1,0:T(8,128)(2,1)} %get-tuple-element.222), channel_id=1, source_target_pairs={{0,16},{8,24},{16,0},{24,8},{1,17},{9,25},{17,1},{25,9},{2,18},{10... | collective-permute-start | bytes 1179656 | tf_op jit(solution)/shard_map/ppermute | solution.py:1091
  270.3 16.2 %collective-permute-start.10 = (bf16[1,96,1536]{2,1,0:T(8,128)(2,1)}, bf16[1,96,1536]{2,1,0:T(8,128)(2,1)S(1)}, u32[]{:S(2)}, u32[]{:S(2)}) collective-permute-start(bf16[1,96,1536]{2,1,0:T(8,128)(2,1)} %get-tuple-element.225), channel_id=1, source_target_pairs={{0,2},{1,3},{2,0},{3,1},{4,6},{5,7},{6,4},{7,5},{8,10},{9,11},{10,... | collective-permute-start | bytes 884744 | tf_op jit(solution)/shard_map/ppermute | solution.py:889
  273.3 23.6 %collective-permute-start.11 = (bf16[1,96,1536]{2,1,0:T(8,128)(2,1)}, bf16[1,96,1536]{2,1,0:T(8,128)(2,1)S(1)}, u32[]{:S(2)}, u32[]{:S(2)}) collective-permute-start(bf16[1,96,1536]{2,1,0:T(8,128)(2,1)} %get-tuple-element.226), channel_id=1, source_target_pairs={{0,4},{1,5},{2,6},{3,7},{4,0},{5,1},{6,2},{7,3},{8,12},{9,13},{10,... | collective-permute-start | bytes 884744 | tf_op jit(solution)/shard_map/ppermute | solution.py:889
  274.4 22.6 %collective-permute-start.12 = (bf16[1,96,1536]{2,1,0:T(8,128)(2,1)}, bf16[1,96,1536]{2,1,0:T(8,128)(2,1)S(1)}, u32[]{:S(2)}, u32[]{:S(2)}) collective-permute-start(bf16[1,96,1536]{2,1,0:T(8,128)(2,1)} %get-tuple-element.227), channel_id=1, source_target_pairs={{0,6},{1,7},{2,4},{3,5},{4,2},{5,3},{6,0},{7,1},{8,14},{9,15},{10,... | collective-permute-start | bytes 884744 | tf_op jit(solution)/shard_map/ppermute | solution.py:889
  283.6 37.9 %collective-permute-start.13 = (bf16[256,768]{1,0:T(8,128)(2,1)S(1)}, bf16[256,768]{1,0:T(8,128)(2,1)S(1)}, u32[]{:S(2)}, u32[]{:S(2)}) collective-permute-start(bf16[256,768]{1,0:T(8,128)(2,1)S(1)} %copy-done.34), channel_id=1, source_target_pairs={{0,24},{8,16},{16,8},{24,0},{1,25},{9,17},{17,9},{25,1},{2,26},{10... | collective-permute-start | bytes 1179656 | tf_op jit(solution)/shard_map/ppermute | solution.py:1091
  300.4 10.2 %collective-permute-start.14 = (bf16[1,24,3200]{2,1,0:T(8,128)(2,1)}, bf16[1,24,3200]{2,1,0:T(8,128)(2,1)S(1)}, u32[]{:S(2)}, u32[]{:S(2)}) collective-permute-start(bf16[1,24,3200]{2,1,0:T(8,128)(2,1)} %get-tuple-element.245), channel_id=1, source_target_pairs={{0,8},{8,0},{16,24},{24,16},{1,9},{9,1},{17,25},{25,17},{2,10},{10... | collective-permute-start | bytes 460808 | tf_op jit(solution)/shard_map/ppermute | solution.py:889
  301.7 9.0 %collective-permute-start.15 = (bf16[1,24,3200]{2,1,0:T(8,128)(2,1)}, bf16[1,24,3200]{2,1,0:T(8,128)(2,1)S(1)}, u32[]{:S(2)}, u32[]{:S(2)}) collective-permute-start(bf16[1,24,3200]{2,1,0:T(8,128)(2,1)} %get-tuple-element.246), channel_id=1, source_target_pairs={{0,16},{8,24},{16,0},{24,8},{1,17},{9,25},{17,1},{25,9},{2,18},{10... | collective-permute-start | bytes 460808 | tf_op jit(solution)/shard_map/ppermute | solution.py:889
  303.0 11.6 %collective-permute-start.16 = (bf16[1,24,3200]{2,1,0:T(8,128)(2,1)}, bf16[1,24,3200]{2,1,0:T(8,128)(2,1)S(1)}, u32[]{:S(2)}, u32[]{:S(2)}) collective-permute-start(bf16[1,24,3200]{2,1,0:T(8,128)(2,1)} %get-tuple-element.247), channel_id=1, source_target_pairs={{0,24},{8,16},{16,8},{24,0},{1,25},{9,17},{17,9},{25,1},{2,26},{10... | collective-permute-start | bytes 460808 | tf_op jit(solution)/shard_map/ppermute | solution.py:889
  317.1 14.6 %collective-permute-start.17 = (bf16[1,24,3200]{2,1,0:T(8,128)(2,1)}, bf16[1,24,3200]{2,1,0:T(8,128)(2,1)S(1)}, u32[]{:S(2)}, u32[]{:S(2)}) collective-permute-start(bf16[1,24,3200]{2,1,0:T(8,128)(2,1)} %sum_pieces.7.refs_0_), channel_id=1, source_target_pairs={{0,2},{1,3},{2,0},{3,1},{4,6},{5,7},{6,4},{7,5},{8,10},{9,11},{10,... | collective-permute-start | bytes 460808 | tf_op jit(solution)/shard_map/ppermute | solution.py:889
  318.6 14.2 %collective-permute-start.18 = (bf16[1,24,3200]{2,1,0:T(8,128)(2,1)}, bf16[1,24,3200]{2,1,0:T(8,128)(2,1)S(1)}, u32[]{:S(2)}, u32[]{:S(2)}) collective-permute-start(bf16[1,24,3200]{2,1,0:T(8,128)(2,1)} %sum_pieces.7.refs_0_), channel_id=1, source_target_pairs={{0,4},{1,5},{2,6},{3,7},{4,0},{5,1},{6,2},{7,3},{8,12},{9,13},{10,... | collective-permute-start | bytes 460808 | tf_op jit(solution)/shard_map/ppermute | solution.py:889
  321.0 11.8 %collective-permute-start.19 = (bf16[1,24,3200]{2,1,0:T(8,128)(2,1)}, bf16[1,24,3200]{2,1,0:T(8,128)(2,1)S(1)}, u32[]{:S(2)}, u32[]{:S(2)}) collective-permute-start(bf16[1,24,3200]{2,1,0:T(8,128)(2,1)} %sum_pieces.7.refs_0_), channel_id=1, source_target_pairs={{0,6},{1,7},{2,4},{3,5},{4,2},{5,3},{6,0},{7,1},{8,14},{9,15},{10,... | collective-permute-start | bytes 460808 | tf_op jit(solution)/shard_map/ppermute | solution.py:889
  336.1 17.1 %collective-permute-start.20 = (bf16[4,24,3200]{2,1,0:T(8,128)(2,1)}, bf16[4,24,3200]{2,1,0:T(8,128)(2,1)}, u32[]{:S(2)}, u32[]{:S(2)}) collective-permute-start(bf16[4,24,3200]{2,1,0:T(8,128)(2,1)} %stack_pieces.1.refs_0_), channel_id=1, source_target_pairs={{0,8},{8,0},{16,24},{24,16},{1,9},{9,1},{17,25},{25,17},{2,10},{10... | collective-permute-start | bytes 1843208 | tf_op jit(solution)/shard_map/ppermute | solution.py:889
  336.6 26.8 %collective-permute-start.21 = (bf16[4,24,3200]{2,1,0:T(8,128)(2,1)}, bf16[4,24,3200]{2,1,0:T(8,128)(2,1)}, u32[]{:S(2)}, u32[]{:S(2)}) collective-permute-start(bf16[4,24,3200]{2,1,0:T(8,128)(2,1)} %stack_pieces.1.refs_0_), channel_id=1, source_target_pairs={{0,16},{8,24},{16,0},{24,8},{1,17},{9,25},{17,1},{25,9},{2,18},{10... | collective-permute-start | bytes 1843208 | tf_op jit(solution)/shard_map/ppermute | solution.py:889
  337.3 26.1 %collective-permute-start.22 = (bf16[4,24,3200]{2,1,0:T(8,128)(2,1)}, bf16[4,24,3200]{2,1,0:T(8,128)(2,1)S(1)}, u32[]{:S(2)}, u32[]{:S(2)}) collective-permute-start(bf16[4,24,3200]{2,1,0:T(8,128)(2,1)} %stack_pieces.1.refs_0_), channel_id=1, source_target_pairs={{0,24},{8,16},{16,8},{24,0},{1,25},{9,17},{17,9},{25,1},{2,26},{10... | collective-permute-start | bytes 1843208 | tf_op jit(solution)/shard_map/ppermute | solution.py:889
  364.3 8.2 %collective-permute-start.23 = (bf16[4,24,3200]{2,1,0:T(8,128)(2,1)S(1)}, bf16[4,24,3200]{2,1,0:T(8,128)(2,1)S(1)}, u32[]{:S(2)}, u32[]{:S(2)}) collective-permute-start(bf16[4,24,3200]{2,1,0:T(8,128)(2,1)S(1)} %copy-done.13), channel_id=1, source_target_pairs={{0,1},{1,0},{2,3},{3,2},{4,5},{5,4},{6,7},{7,6},{8,9},{9,8},{10,11... | collective-permute-start | bytes 1843208 | tf_op jit(solution)/shard_map/ppermute | solution.py:1078
  364.3 8.2 %collective-permute-start.24 = (bf16[4,24,3200]{2,1,0:T(8,128)(2,1)}, bf16[4,24,3200]{2,1,0:T(8,128)(2,1)S(1)}, u32[]{:S(2)}, u32[]{:S(2)}) collective-permute-start(bf16[4,24,3200]{2,1,0:T(8,128)(2,1)} %collective-permute-done.20.refs_1_), channel_id=1, source_target_pairs={{0,1},{1,0},{2,3},{3,2},{4,5},{5,4},{6,7},{7,6},{8,9},{9,8},{10,11... | collective-permute-start | bytes 1843208 | tf_op jit(solution)/shard_map/ppermute | solution.py:1078
  (38 other events, 213.7 us)
Sparse Core Ops, SparseCore 0:
  182.0 41.9 reduce-scatter.4
  227.6 84.1 reduce-scatter.2

commit v9 on v8

--- a/solution.py
+++ b/solution.py
@@ -750,7 +750,7 @@
     d_probs = dprobs_ref[...] + jnp.where(lane < ALL_EXPERTS, extra, 0.0)
     probs = probs_ref[...]
     d_logits = probs * (d_probs - jnp.sum(probs * d_probs, axis=1, keepdims=True))
-    dlogits_ref[...] = d_logits.T
+    dlogits_ref[:, 0, :] = d_logits.T[0:ALL_EXPERTS]
 
 
 def finish(chosen, got, groups, local, probs, d_probs):
@@ -760,8 +760,8 @@
         functools.partial(finish_kernel, groups, len(got)),
         grid=(tok // block,),
         in_specs=[tiles(c.shape[1]) for c in chosen] + [fixed(g) for g in got] + [tiles(width), tiles(EXTRA), tiles(EXTRA)],
-        out_specs=[tiles(width), pl.BlockSpec((EXTRA, block), lambda i: (0, i))],
-        out_shape=[jax.ShapeDtypeStruct((tok, width), bf16), jax.ShapeDtypeStruct((EXTRA, tok), f32)],
+        out_specs=[tiles(width), pl.BlockSpec((ALL_EXPERTS, 1, block), lambda i: (0, 0, i))],
+        out_shape=[jax.ShapeDtypeStruct((tok, width), bf16), jax.ShapeDtypeStruct((ALL_EXPERTS, 1, tok), f32)],
         compiler_params=pltpu.CompilerParams(vmem_limit_bytes=60 * 2**20),
         cost_estimate=pl.CostEstimate(flops=2 * tok * 1152 * (width + EXTRA), bytes_accessed=16 * tok * width, transcendentals=0),
         name="finish_outputs",
@@ -1106,17 +1106,17 @@
         far_back = far_back + [send_far(n_ctx - 1)]
     d_inputs = input_gradient([grads_1, grads_2, grads_3], x_low, attn_gain[None], d_hidden, w_qkv, far_back)
 
-    d_prev = d_logits[:ALL_EXPERTS].T[None]
+    d_prev = d_logits.transpose(1, 2, 0)
     total_gate, total_up, total_down = sum_gate_up[0][None], sum_gate_up[1][None], sum_down[None]
     if dense:
         d_inputs, spread_z = lax.optimization_barrier((d_inputs, spread_z))
         column = stack_pieces(spread_z)
-        own = after(spread(column, along_ctx), total_gate, total_up, total_down, d_prev)
+        places = [jnp.stack([half, me_c, z]) for half in (core[0], 1 - core[0])]
+        own, places = after((spread(column, along_ctx), places), total_gate, total_up, total_down)
         other = [across(piece) for piece in own]
-        place_of = lambda half: jnp.stack([half, me_c, z])
-        first = unpack_half(place_of(core[0]), own, w_qkv, left, None, None)
+        first = unpack_half(places[0], own, w_qkv, left, None, None)
         first, other = lax.optimization_barrier((first, other))
-        out_sum, qkv_sum, d_router, d_mixing, d_const_vec, d_moe_gain, d_attn_gain = unpack_half(place_of(1 - core[0]), other, w_qkv, left, attn_gain[None], first)
+        out_sum, qkv_sum, d_router, d_mixing, d_const_vec, d_moe_gain, d_attn_gain = unpack_half(places[1], other, w_qkv, left, attn_gain[None], first)
     else:
         whole = lambda mine, theirs: jnp.where(core == 0, jnp.concatenate([mine, theirs], axis=0), jnp.concatenate([theirs, mine], axis=0))
         total_1, total_2 = [v.astype(f32) for v in lax.psum((whole(mine_1, theirs_1), whole(mine_2, theirs_2)), ("ctx", "exp"))]

time: 392 us -> 390 us (level)
    unnamed x74 -> x73, local copies, waits for them, and re-layouts: 11.4 us -> 10.7 us
  transfers between devices with their start and end apart: 35 -> 35, of which waited for: 12 -> 12; matrix products, arithmetic and copies ran while one was open for 6% -> 6% of each run, Pallas kernels for 53% -> 54%
where the time goes in v9:
time: 390 us; the launch traced here: 386 us
  Pallas kernels  219 us (56%)
  starting transfers between devices  60 us (15%)
  waiting for transfers between devices  59.4 us (15%)
  local copies, waits for them, and re-layouts  17.3 us (4%)
  between operations  14.7 us (4%)
  other arithmetic  9.21 us (2%)
  matrix products  5.98 us (2%)
    pallas_call x3, Pallas kernels, attention_backward(): pl.pallas_call(functools.partial(attention_backward_kernel, plen, bool(st...  55.4 us
    ppermute x15, waiting for transfers between devices, swap(): lax.ppermute(pieces[k], axis, xor_pairs(size, unit * k))  39.9 us
    pallas_call x2, Pallas kernels, expert_pass(): pl.pallas_call(functools.partial(expert_kernel, group), grid=(ff // tile,...  38.6 us
    pallas_call x1, Pallas kernels, attention_forward(): pl.pallas_call(functools.partial(attention_forward_kernel, plen, len(turn...  24.5 us
    ppermute x15, starting transfers between devices, swap(): lax.ppermute(pieces[k], axis, xor_pairs(size, unit * k))  21.2 us
    pallas_call x1, Pallas kernels, weight_gradients(): pl.pallas_call(functools.partial(weight_kernel, count), grid=(ff // tile,...  17.9 us
    all_to_all x3, starting transfers between devices, deal(): return lax.all_to_all(value, 'exp', 0, 0, tiled=True)  15.6 us
    all_to_all x3, starting transfers between devices, give_back(): value = lax.all_to_all(value, 'exp', 0, 0, tiled=True)  12.8 us
  transfers between devices with their start and end apart: 35, of which 12 were waited for; matrix products, arithmetic and copies ran while one was open for 6% of the time, Pallas kernels for 54%

profile of v9, /device:TPU:0, one launch (start us, length us, event | category | flops | bytes accessed | tf_op | source)
XLA Modules:
  0.0 386.0 jit_solution(6865252909139596023)
XLA Ops:
  7.2 6.2 %route_plan.1 = (bf16[640,768]{1,0:T(8,128)(2,1)}, bf16[512,768]{1,0:T(8,128)(2,1)}, bf16[768,640]{1,0:T(8,128)(2,1)}, bf16[768,512]{1,0:T(8,128)(2,1)}, bf16[8,...) custom-call(s32[1]{0:T(128)} %bitcast.home_ref, s32[2,768]{1,0:T(2,128)} %bitcast.117, bf16[768,768]{1,0:T(8,128)(2,1)} %bitcast.98, ...), custom_call_target="tpu_custom_call" | custom-call | flops 1585446912 | bytes 3538944 | tf_op jit(solution)/shard_map/route_plan/pallas_call | solution.py:401
  13.4 7.0 %all-to-all-start = ((bf16[8,152,768]{2,1,0:T(8,128)(2,1)}), bf16[8,152,768]{2,1,0:T(8,128)(2,1)}, u32[]{:S(2)}, u32[]{:S(2)}) async-start(bf16[8,152,768]{2,1,0:T(8,128)(2,1)} %get-tuple-element.159), calls=%async_computation | async-start | bytes 3735552 | tf_op jit(solution)/shard_map/all_to_all | solution.py:1019
  27.7 3.5 turn.2.act_ref
  32.3 6.0 %convolution_convert_fusion.q_ref.k_ref.v_ref = bf16[768,2304]{1,0:T(8,128)(2,1)} fusion(bf16[768,768]{1,0:T(8,128)(2,1)} %fusion.2.in_ref, bf16[768,2304]{1,0:T(8,128)(2,1)S(1)} %copy-done), kind=kOutput, calls=%fused_computation | convolution fusion | flops 2719678464 | bytes 8257536 | tf_op jit(solution)/shard_map/dot_general | solution.py:23
  38.3 3.7 collective-permute-done.1.refs_1_
  42.0 5.7 %far_projection.1 = (bf16[768,768]{1,0:T(8,128)(2,1)}, bf16[768,1536]{1,0:T(8,128)(2,1)}) custom-call(f32[1,768]{1,0:T(1,128)} %broadcast_in_dim.40.gain_ref.refs_5_, bf16[768,2304]{1,0:T(8,128)(2,1)} %refs_4_.3, bf16[768,2304]{1,0:T(8,128)(2,1)} %refs_4_.3, bf16[256,768]{1,0:T(8,128)(2,1)} %copy-done.22, bf16[256,768]{1,0:T(8,128)(2,1)} %collective-permute-done.1.refs_1_, ...), custom_call_target="tpu_custom_call" | custom-call | flops 1811939328 | bytes 7077888 | tf_op jit(solution)/shard_map/far_projection/pallas_call | solution.py:831
  47.7 24.5 %attention_forward.1 = (bf16[768,768]{1,0:T(8,128)(2,1)}, f32[6,16,768]{2,1,0:T(8,128)}, f32[768,768]{1,0:T(8,128)}, bf16[768,768]{1,0:T(8,128)(2,1)}, bf16[640,...) custom-call(f32[3]{0:T(128)} %compare_select_fusion.flags_ref, bf16[768,2304]{1,0:T(8,128)(2,1)} %convolution_convert_fusion.q_ref.k_ref.v_ref, ...), custom_call_target="tpu_custom_call" | custom-call | flops 5435817984 | bytes 14155776 | tf_op jit(solution)/shard_map/attention_forward/pallas_call | solution.py:134
  72.2 5.0 %all-to-all-start.3 = ((bf16[8,64,768]{2,1,0:T(8,128)(2,1)}), bf16[8,64,768]{2,1,0:T(8,128)(2,1)S(1)}, u32[]{:S(2)}, u32[]{:S(2)}) async-start(bf16[8,64,768]{2,1,0:T(8,128)(2,1)} %bitcast.113), calls=%async_computation.3 | async-start | bytes 1572864 | tf_op jit(solution)/shard_map/all_to_all | solution.py:1019
  82.4 12.6 %local_part.1 = (f32[768,768]{1,0:T(8,128)}, f32[768,768]{1,0:T(8,128)}, f32[768,128]{1,0:T(8,128)}, f32[768,128]{1,0:T(8,128)}, f32[24,768]{1,0:T(8,128)}) custom-call(f32[768,768]{1,0:T(8,128)} %get-tuple-element.161.hidden_ref.refs_8_, bf16[768,768]{1,0:T(8,128)(2,1)} %get-tuple-element.162.low_ref, bf16[768,768]{1,0:T(8,128)(2,1)} %bitcast.99, ...), custom_call_target="tpu_custom_call" | custom-call | flops 1056964608 | bytes 9437184 | tf_op jit(solution)/shard_map/local_part/pallas_call | solution.py:646
  98.1 3.6 all-to-all-start.1
  102.4 17.7 %expert_pass.3 = (bf16[512,896]{1,0:T(8,128)(2,1)}, bf16[512,768]{1,0:T(8,128)(2,1)}, bf16[512,768]{1,0:T(8,128)(2,1)}, bf16[512,2048]{1,0:T(8,128)(2,1)}, bf16[...) custom-call(s32[1]{0:T(128)} %bitcast.home_ref, bf16[512,768]{1,0:T(8,128)(2,1)} %bitcast.111, ...), custom_call_target="tpu_custom_call" | custom-call | flops 9663676416 | bytes 19660800 | tf_op jit(solution)/shard_map/expert_pass/pallas_call | solution.py:489
  120.1 6.7 %all-to-all-done.1 = bf16[8,80,768]{2,1,0:T(8,128)(2,1)S(1)} async-done(((bf16[8,80,768]{2,1,0:T(8,128)(2,1)}), bf16[8,80,768]{2,1,0:T(8,128)(2,1)S(1)}, u32[]{:S(2)}, u32[]{:S(2)}) %all-to-all-start.1) | async-done | bytes 983072 | tf_op jit(solution)/shard_map/all_to_all | solution.py:1019
  126.8 3.8 all-to-all-start.4
  130.6 20.9 %expert_pass.2 = (bf16[640,896]{1,0:T(8,128)(2,1)}, bf16[640,768]{1,0:T(8,128)(2,1)}, bf16[640,768]{1,0:T(8,128)(2,1)}, bf16[640,2048]{1,0:T(8,128)(2,1)}, bf16[...) custom-call(s32[1]{0:T(128)} %bitcast.home_ref, bf16[640,768]{1,0:T(8,128)(2,1)} %bitcast.105, ...), custom_call_target="tpu_custom_call" | custom-call | flops 12079595520 | bytes 22216704 | tf_op jit(solution)/shard_map/expert_pass/pallas_call | solution.py:489
  151.5 5.2 %all-to-all-start.2 = ((bf16[8,80,768]{2,1,0:T(8,128)(2,1)}), bf16[8,80,768]{2,1,0:T(8,128)(2,1)S(1)}, u32[]{:S(2)}, u32[]{:S(2)}) async-start(bf16[8,80,768]{2,1,0:T(8,128)(2,1)} %bitcast.107), calls=%async_computation.2 | async-start | bytes 1966080 | tf_op jit(solution)/shard_map/all_to_all | solution.py:1022
  159.4 17.9 %weight_gradients.1 = (bf16[2,768,2048]{2,1,0:T(8,128)(2,1)}, bf16[2048,768]{1,0:T(8,128)(2,1)}) custom-call(bf16[640,768]{1,0:T(8,128)(2,1)} %bitcast.106, bf16[512,768]{1,0:T(8,128)(2,1)} %bitcast.112, bf16[640,768]{1,0:T(8,128)(2,1)} %get-tuple-element.171.refs_2_, bf16[512,768]{1,0:T(8,128)(2,1)} %get-tuple-element.172.refs_3_, ...), custom_call_target="tpu_custom_call" | custom-call | flops 10871635968 | bytes 27131904 | tf_op jit(solution)/shard_map/weight_gradients/pallas_call | solution.py:538
  177.3 4.6 %all-to-all-done.2 = bf16[8,80,768]{2,1,0:T(8,128)(2,1)S(1)} async-done(((bf16[8,80,768]{2,1,0:T(8,128)(2,1)}), bf16[8,80,768]{2,1,0:T(8,128)(2,1)S(1)}, u32[]{:S(2)}, u32[]{:S(2)}) %all-to-all-start.2) | async-done | bytes 983072 | tf_op jit(solution)/shard_map/all_to_all | solution.py:1022
  182.9 3.9 all-to-all-start.5
  186.7 11.5 %combine_gradients.1 = (f32[768,768]{1,0:T(8,128)}, bf16[768,768]{1,0:T(8,128)(2,1)}, bf16[384,1664]{1,0:T(8,128)(2,1)}, bf16[384,1664]{1,0:T(8,128)(2,1)}) custom-call(s32[1]{0:T(128)} %bitcast.18.core_ref, bf16[768,640]{1,0:T(8,128)(2,1)} %get-tuple-element.147.refs_0_, bf16[768,512]{1,0:T(8,128)(2,1)} %get-tuple-element.148.refs_1_, ...), custom_call_target="tpu_custom_call" | custom-call | flops 3170893824 | bytes 15335424 | tf_op jit(solution)/shard_map/combine_gradients/pallas_call | solution.py:717
  198.3 18.5 %attention_backward.3 = (bf16[384,1664]{1,0:T(8,128)(2,1)}, bf16[384,1664]{1,0:T(8,128)(2,1)}, bf16[768,768]{1,0:T(8,128)(2,1)}, f32[768,768]{1,0:T(8,128)}) custom-call(f32[3]{0:T(128)} %compare_select_fusion.flags_ref, s32[1]{0:T(128)} %bitcast.18.core_ref, ...), custom_call_target="tpu_custom_call", output_to_operand_aliasing={{0}: (14, {}), {1}: (15, {})} | custom-call | flops 6039797760 | bytes 14155776 | tf_op jit(solution)/shard_map/attention_backward/pallas_call | solution.py:324
  217.5 11.2 %attention_backward.4 = (bf16[384,1536]{1,0:T(8,128)(2,1)}, bf16[384,1536]{1,0:T(8,128)(2,1)}, bf16[768,384]{1,0:T(8,128)(2,1)}, f32[768,768]{1,0:T(8,128)}) custom-call(f32[3]{0:T(128)} %compare_select_fusion.flags_ref, s32[1]{0:T(128)} %bitcast.18.core_ref, bf16[768,2304]{1,0:T(8,128)(2,1)} %convolution_convert_fusion.q_ref.k_ref.v_ref, ...), custom_call_target="tpu_custom_call" | custom-call | flops 3019898880 | bytes 11796480 | tf_op jit(solution)/shard_map/attention_backward/pallas_call | solution.py:324
  236.9 25.7 %attention_backward.5 = (bf16[384,1536]{1,0:T(8,128)(2,1)}, bf16[384,1536]{1,0:T(8,128)(2,1)}, bf16[768,1152]{1,0:T(8,128)(2,1)}, bf16[256,768]{1,0:T(8,128)(2,1...) custom-call(f32[3]{0:T(128)} %compare_select_fusion.flags_ref, ...), custom_call_target="tpu_custom_call", output_to_operand_aliasing={{0}: (14, {}), {1}: (15, {})} | custom-call | flops 9059696640 | bytes 16515072 | tf_op jit(solution)/shard_map/attention_backward/pallas_call | solution.py:324
  277.0 6.5 %finish_outputs.1 = (bf16[768,768]{1,0:T(8,128)(2,1)}, f32[12,1,768]{2,1,0:T(1,128)}) custom-call(bf16[768,640]{1,0:T(8,128)(2,1)} %get-tuple-element.147.refs_0_, bf16[768,512]{1,0:T(8,128)(2,1)} %get-tuple-element.148.refs_1_, bf16[8,144,896]{2,1,0:T(8,128)(2,1)} %copy-done.4, f32[768,768]{1,0:T(8,128)} %get-tuple-element.218.refs_3_, ...), custom_call_target="tpu_custom_call" | custom-call | flops 1585446912 | bytes 9437184 | tf_op jit(solution)/shard_map/finish_outputs/pallas_call | solution.py:759
  286.5 10.5 %collective-permute-done.11 = bf16[1,96,1536]{2,1,0:T(8,128)(2,1)S(1)} collective-permute-done((bf16[1,96,1536]{2,1,0:T(8,128)(2,1)}, bf16[1,96,1536]{2,1,0:T(8,128)(2,1)S(1)}, u32[]{:S(2)}, u32[]{:S(2)}) %collective-permute-start.11) | collective-permute-done | bytes 294944 | tf_op jit(solution)/shard_map/ppermute | solution.py:889
  304.6 6.1 %collective-permute-done.14.refs_1_ = bf16[1,24,3200]{2,1,0:T(8,128)(2,1)S(1)} collective-permute-done((bf16[1,24,3200]{2,1,0:T(8,128)(2,1)}, bf16[1,24,3200]{2,1,0:T(8,128)(2,1)S(1)}, u32[]{:S(2)}, u32[]{:S(2)}) %collective-permute-start.14) | collective-permute-done | bytes 153632 | tf_op jit(solution)/shard_map/ppermute | solution.py:889
  310.7 3.9 %collective-permute-done.16.refs_3_ = bf16[1,24,3200]{2,1,0:T(8,128)(2,1)S(1)} collective-permute-done((bf16[1,24,3200]{2,1,0:T(8,128)(2,1)}, bf16[1,24,3200]{2,1,0:T(8,128)(2,1)S(1)}, u32[]{:S(2)}, u32[]{:S(2)}) %collective-permute-start.16) | collective-permute-done | bytes 153632 | tf_op jit(solution)/shard_map/ppermute | solution.py:889
  322.3 9.4 %input_gradient.1 = f32[768,768]{1,0:T(8,128)} custom-call(bf16[768,768]{1,0:T(8,128)(2,1)} %bitcast.65, f32[1,768]{1,0:T(1,128)} %broadcast_in_dim.40.gain_ref.refs_5_, f32[768,768]{1,0:T(8,128)} %get-tuple-element.231.dhidden_ref, bf16[768,2304]{1,0:T(8,128)(2,1)} %refs_4_.3, bf16[768,768]{1,0:T(8,128)(2,1)} %get-tuple-element.232.refs_0_, ...), custom_call_target="tpu_custom_call" | custom-call | flops 2717908992 | bytes 12976128 | tf_op jit(solution)/shard_map/input_gradient/pallas_call | solution.py:801
  342.0 3.5 fusion.3
  345.5 7.8 %collective-permute-done.20.refs_1_ = bf16[4,24,3200]{2,1,0:T(8,128)(2,1)} collective-permute-done((bf16[4,24,3200]{2,1,0:T(8,128)(2,1)}, bf16[4,24,3200]{2,1,0:T(8,128)(2,1)}, u32[]{:S(2)}, u32[]{:S(2)}) %collective-permute-start.20) | collective-permute-done | bytes 614432 | tf_op jit(solution)/shard_map/ppermute | solution.py:889
  353.2 10.2 %collective-permute-done.21.refs_2_ = bf16[4,24,3200]{2,1,0:T(8,128)(2,1)} collective-permute-done((bf16[4,24,3200]{2,1,0:T(8,128)(2,1)}, bf16[4,24,3200]{2,1,0:T(8,128)(2,1)}, u32[]{:S(2)}, u32[]{:S(2)}) %collective-permute-start.21) | collective-permute-done | bytes 614432 | tf_op jit(solution)/shard_map/ppermute | solution.py:889
  365.3 5.9 %unpack_half.2 = (f32[768,768]{1,0:T(8,128)}, f32[768,2304]{1,0:T(8,128)}, f32[384,128]{1,0:T(8,128)}) custom-call(s32[3]{0:T(128)} %get-tuple-element.259.index_ref, bf16[4,24,3200]{2,1,0:T(8,128)(2,1)} %stack_pieces.1.refs_0_, bf16[4,24,3200]{2,1,0:T(8,128)(2,1)} %collective-permute-done.20.refs_1_, bf16[4,24,3200]{2,1,0:T(8,128)(2,1)} %collective-permute-done.21.refs_2_, ...), custom_call_target="tpu_custom_call" | custom-call | bytes 8257536 | tf_op jit(solution)/shard_map/unpack_half/pallas_call | solution.py:979
  372.6 6.4 %unpack_half.3 = (f32[768,768]{1,0:T(8,128)}, f32[768,2304]{1,0:T(8,128)}, f32[12,768]{1,0:T(8,128)}, f32[2,2,768]{2,1,0:T(2,128)}, f32[2,768]{1,0:T(2,128)}, /*index=5*/f32[768]{0:T(1024)}, f32[768]{0:T(1024)}) custom-call(s32[3]{0:T(128)} %get-tuple-element.258.index_ref, ...), custom_call_target="tpu_custom_call", output_to_operand_aliasing={{0}: (8, {}), {1}: (9, {})} | custom-call | bytes 8257536 | tf_op jit(solution)/shard_map/unpack_half/pallas_call | solution.py:979
  (151 shorter events, 76.1 us)
Async XLA Ops:
  13.4 58.8 %all-to-all-start = ((bf16[8,152,768]{2,1,0:T(8,128)(2,1)}), bf16[8,152,768]{2,1,0:T(8,128)(2,1)}, u32[]{:S(2)}, u32[]{:S(2)}) async-start(bf16[8,152,768]{2,1,0:T(8,128)(2,1)} %get-tuple-element.159), calls=%async_computation | async-start | bytes 3735552 | tf_op jit(solution)/shard_map/all_to_all | solution.py:1019
  20.4 17.9 %collective-permute-start = (bf16[256,768]{1,0:T(8,128)(2,1)}, bf16[256,768]{1,0:T(8,128)(2,1)S(1)}, u32[]{:S(2)}, u32[]{:S(2)}) collective-permute-start(bf16[256,768]{1,0:T(8,128)(2,1)} %get-tuple-element.149), channel_id=1, source_target_pairs={{0,8},{8,0},{16,24},{24,16},{1,9},{9,1},{17,25},{25,17},{2,10},{10... | collective-permute-start | bytes 1179656 | tf_op jit(solution)/shard_map/ppermute | solution.py:1034
  22.0 20.0 %collective-permute-start.1 = (bf16[256,768]{1,0:T(8,128)(2,1)}, bf16[256,768]{1,0:T(8,128)(2,1)}, u32[]{:S(2)}, u32[]{:S(2)}) collective-permute-start(bf16[256,768]{1,0:T(8,128)(2,1)} %get-tuple-element.149), channel_id=1, source_target_pairs={{0,16},{8,24},{16,0},{24,8},{1,17},{9,25},{17,1},{25,9},{2,18},{10... | collective-permute-start | bytes 1179656 | tf_op jit(solution)/shard_map/ppermute | solution.py:1034
  23.5 18.5 %collective-permute-start.2 = (bf16[256,768]{1,0:T(8,128)(2,1)}, bf16[256,768]{1,0:T(8,128)(2,1)}, u32[]{:S(2)}, u32[]{:S(2)}) collective-permute-start(bf16[256,768]{1,0:T(8,128)(2,1)} %get-tuple-element.149), channel_id=1, source_target_pairs={{0,24},{8,16},{16,8},{24,0},{1,25},{9,17},{17,9},{25,1},{2,26},{10... | collective-permute-start | bytes 1179656 | tf_op jit(solution)/shard_map/ppermute | solution.py:1034
  72.2 25.9 %all-to-all-start.3 = ((bf16[8,64,768]{2,1,0:T(8,128)(2,1)}), bf16[8,64,768]{2,1,0:T(8,128)(2,1)S(1)}, u32[]{:S(2)}, u32[]{:S(2)}) async-start(bf16[8,64,768]{2,1,0:T(8,128)(2,1)} %bitcast.113), calls=%async_computation.3 | async-start | bytes 1572864 | tf_op jit(solution)/shard_map/all_to_all | solution.py:1019
  98.1 28.7 %all-to-all-start.1 = ((bf16[8,80,768]{2,1,0:T(8,128)(2,1)}), bf16[8,80,768]{2,1,0:T(8,128)(2,1)S(1)}, u32[]{:S(2)}, u32[]{:S(2)}) async-start(bf16[8,80,768]{2,1,0:T(8,128)(2,1)} %bitcast.9), calls=%async_computation.1 | async-start | bytes 1966080 | tf_op jit(solution)/shard_map/all_to_all | solution.py:1019
  126.8 24.7 %all-to-all-start.4 = ((bf16[8,64,768]{2,1,0:T(8,128)(2,1)}), bf16[8,64,768]{2,1,0:T(8,128)(2,1)S(1)}, u32[]{:S(2)}, u32[]{:S(2)}) async-start(bf16[8,64,768]{2,1,0:T(8,128)(2,1)} %bitcast.114), calls=%async_computation.4 | async-start | bytes 1572864 | tf_op jit(solution)/shard_map/all_to_all | solution.py:1022
  151.5 30.4 %all-to-all-start.2 = ((bf16[8,80,768]{2,1,0:T(8,128)(2,1)}), bf16[8,80,768]{2,1,0:T(8,128)(2,1)S(1)}, u32[]{:S(2)}, u32[]{:S(2)}) async-start(bf16[8,80,768]{2,1,0:T(8,128)(2,1)} %bitcast.107), calls=%async_computation.2 | async-start | bytes 1966080 | tf_op jit(solution)/shard_map/all_to_all | solution.py:1022
  156.7 182.9 %reduce-scatter.5.cloned.1.call-start = ((), (), s32[]{:S(2)}) async-start(), calls=%async_computation.9 | async-start | bytes 3932160 | tf_op jit(solution)/shard_map/reduce_scatter | solution.py:1068
  181.9 160.1 %reduce-scatter.3.cloned.1.call-start = ((), (), s32[]{:S(2)}) async-start(), calls=%async_computation.8 | async-start | bytes 7864320 | tf_op jit(solution)/shard_map/reduce_scatter | solution.py:1067
  182.9 92.8 %all-to-all-start.5 = ((bf16[8,144,896]{2,1,0:T(8,128)(2,1)}), bf16[8,144,896]{2,1,0:T(8,128)(2,1)S(1)}, u32[]{:S(2)}, u32[]{:S(2)}) async-start(bf16[8,144,896]{2,1,0:T(8,128)(2,1)} %pad_maximum_fusion), calls=%async_computation.5 | async-start | bytes 4128768 | tf_op jit(solution)/shard_map/all_to_all | solution.py:1022
  216.8 11.8 %collective-permute-start.3 = (bf16[384,1664]{1,0:T(8,128)(2,1)}, bf16[384,1664]{1,0:T(8,128)(2,1)S(1)}, u32[]{:S(2)}, u32[]{:S(2)}) collective-permute-start(bf16[384,1664]{1,0:T(8,128)(2,1)} %get-tuple-element.198), channel_id=1, source_target_pairs={{0,1},{1,0},{2,3},{3,2},{4,5},{5,4},{6,7},{7,6},{8,9},{9,8},{10,11... | collective-permute-start | bytes 3833864 | tf_op jit(solution)/shard_map/ppermute | solution.py:1078
  232.5 30.1 %collective-permute-start.4 = (bf16[1,96,1664]{2,1,0:T(8,128)(2,1)}, bf16[1,96,1664]{2,1,0:T(8,128)(2,1)S(1)}, u32[]{:S(2)}, u32[]{:S(2)}) collective-permute-start(bf16[1,96,1664]{2,1,0:T(8,128)(2,1)} %get-tuple-element.212), channel_id=1, source_target_pairs={{0,2},{1,3},{2,0},{3,1},{4,6},{5,7},{6,4},{7,5},{8,10},{9,11},{10,... | collective-permute-start | bytes 958472 | tf_op jit(solution)/shard_map/ppermute | solution.py:889
  234.2 28.4 %collective-permute-start.5 = (bf16[1,96,1664]{2,1,0:T(8,128)(2,1)}, bf16[1,96,1664]{2,1,0:T(8,128)(2,1)S(1)}, u32[]{:S(2)}, u32[]{:S(2)}) collective-permute-start(bf16[1,96,1664]{2,1,0:T(8,128)(2,1)} %get-tuple-element.213), channel_id=1, source_target_pairs={{0,4},{1,5},{2,6},{3,7},{4,0},{5,1},{6,2},{7,3},{8,12},{9,13},{10,... | collective-permute-start | bytes 958472 | tf_op jit(solution)/shard_map/ppermute | solution.py:889
  236.6 26.0 %collective-permute-start.6 = (bf16[1,96,1664]{2,1,0:T(8,128)(2,1)}, bf16[1,96,1664]{2,1,0:T(8,128)(2,1)S(1)}, u32[]{:S(2)}, u32[]{:S(2)}) collective-permute-start(bf16[1,96,1664]{2,1,0:T(8,128)(2,1)} %get-tuple-element.214), channel_id=1, source_target_pairs={{0,6},{1,7},{2,4},{3,5},{4,2},{5,3},{6,0},{7,1},{8,14},{9,15},{10,... | collective-permute-start | bytes 958472 | tf_op jit(solution)/shard_map/ppermute | solution.py:889
  263.5 20.0 %collective-permute-start.8 = (bf16[256,768]{1,0:T(8,128)(2,1)}, bf16[256,768]{1,0:T(8,128)(2,1)}, u32[]{:S(2)}, u32[]{:S(2)}) collective-permute-start(bf16[256,768]{1,0:T(8,128)(2,1)} %get-tuple-element.223), channel_id=1, source_target_pairs={{0,8},{8,0},{16,24},{24,16},{1,9},{9,1},{17,25},{25,17},{2,10},{10... | collective-permute-start | bytes 1179656 | tf_op jit(solution)/shard_map/ppermute | solution.py:1091
  264.7 18.8 %collective-permute-start.9 = (bf16[256,768]{1,0:T(8,128)(2,1)}, bf16[256,768]{1,0:T(8,128)(2,1)}, u32[]{:S(2)}, u32[]{:S(2)}) collective-permute-start(bf16[256,768]{1,0:T(8,128)(2,1)} %get-tuple-element.224), channel_id=1, source_target_pairs={{0,16},{8,24},{16,0},{24,8},{1,17},{9,25},{17,1},{25,9},{2,18},{10... | collective-permute-start | bytes 1179656 | tf_op jit(solution)/shard_map/ppermute | solution.py:1091
  270.2 16.2 %collective-permute-start.10 = (bf16[1,96,1536]{2,1,0:T(8,128)(2,1)}, bf16[1,96,1536]{2,1,0:T(8,128)(2,1)S(1)}, u32[]{:S(2)}, u32[]{:S(2)}) collective-permute-start(bf16[1,96,1536]{2,1,0:T(8,128)(2,1)} %get-tuple-element.227), channel_id=1, source_target_pairs={{0,2},{1,3},{2,0},{3,1},{4,6},{5,7},{6,4},{7,5},{8,10},{9,11},{10,... | collective-permute-start | bytes 884744 | tf_op jit(solution)/shard_map/ppermute | solution.py:889
  273.3 23.6 %collective-permute-start.11 = (bf16[1,96,1536]{2,1,0:T(8,128)(2,1)}, bf16[1,96,1536]{2,1,0:T(8,128)(2,1)S(1)}, u32[]{:S(2)}, u32[]{:S(2)}) collective-permute-start(bf16[1,96,1536]{2,1,0:T(8,128)(2,1)} %get-tuple-element.228), channel_id=1, source_target_pairs={{0,4},{1,5},{2,6},{3,7},{4,0},{5,1},{6,2},{7,3},{8,12},{9,13},{10,... | collective-permute-start | bytes 884744 | tf_op jit(solution)/shard_map/ppermute | solution.py:889
  274.3 22.6 %collective-permute-start.12 = (bf16[1,96,1536]{2,1,0:T(8,128)(2,1)}, bf16[1,96,1536]{2,1,0:T(8,128)(2,1)S(1)}, u32[]{:S(2)}, u32[]{:S(2)}) collective-permute-start(bf16[1,96,1536]{2,1,0:T(8,128)(2,1)} %get-tuple-element.229), channel_id=1, source_target_pairs={{0,6},{1,7},{2,4},{3,5},{4,2},{5,3},{6,0},{7,1},{8,14},{9,15},{10,... | collective-permute-start | bytes 884744 | tf_op jit(solution)/shard_map/ppermute | solution.py:889
  283.5 38.0 %collective-permute-start.13 = (bf16[256,768]{1,0:T(8,128)(2,1)S(1)}, bf16[256,768]{1,0:T(8,128)(2,1)S(1)}, u32[]{:S(2)}, u32[]{:S(2)}) collective-permute-start(bf16[256,768]{1,0:T(8,128)(2,1)S(1)} %copy-done.34), channel_id=1, source_target_pairs={{0,24},{8,16},{16,8},{24,0},{1,25},{9,17},{17,9},{25,1},{2,26},{10... | collective-permute-start | bytes 1179656 | tf_op jit(solution)/shard_map/ppermute | solution.py:1091
  300.4 10.3 %collective-permute-start.14 = (bf16[1,24,3200]{2,1,0:T(8,128)(2,1)}, bf16[1,24,3200]{2,1,0:T(8,128)(2,1)S(1)}, u32[]{:S(2)}, u32[]{:S(2)}) collective-permute-start(bf16[1,24,3200]{2,1,0:T(8,128)(2,1)} %get-tuple-element.247), channel_id=1, source_target_pairs={{0,8},{8,0},{16,24},{24,16},{1,9},{9,1},{17,25},{25,17},{2,10},{10... | collective-permute-start | bytes 460808 | tf_op jit(solution)/shard_map/ppermute | solution.py:889
  301.7 9.0 %collective-permute-start.15 = (bf16[1,24,3200]{2,1,0:T(8,128)(2,1)}, bf16[1,24,3200]{2,1,0:T(8,128)(2,1)S(1)}, u32[]{:S(2)}, u32[]{:S(2)}) collective-permute-start(bf16[1,24,3200]{2,1,0:T(8,128)(2,1)} %get-tuple-element.248), channel_id=1, source_target_pairs={{0,16},{8,24},{16,0},{24,8},{1,17},{9,25},{17,1},{25,9},{2,18},{10... | collective-permute-start | bytes 460808 | tf_op jit(solution)/shard_map/ppermute | solution.py:889
  303.0 11.6 %collective-permute-start.16 = (bf16[1,24,3200]{2,1,0:T(8,128)(2,1)}, bf16[1,24,3200]{2,1,0:T(8,128)(2,1)S(1)}, u32[]{:S(2)}, u32[]{:S(2)}) collective-permute-start(bf16[1,24,3200]{2,1,0:T(8,128)(2,1)} %get-tuple-element.249), channel_id=1, source_target_pairs={{0,24},{8,16},{16,8},{24,0},{1,25},{9,17},{17,9},{25,1},{2,26},{10... | collective-permute-start | bytes 460808 | tf_op jit(solution)/shard_map/ppermute | solution.py:889
  317.1 14.6 %collective-permute-start.17 = (bf16[1,24,3200]{2,1,0:T(8,128)(2,1)}, bf16[1,24,3200]{2,1,0:T(8,128)(2,1)S(1)}, u32[]{:S(2)}, u32[]{:S(2)}) collective-permute-start(bf16[1,24,3200]{2,1,0:T(8,128)(2,1)} %sum_pieces.7.refs_0_), channel_id=1, source_target_pairs={{0,2},{1,3},{2,0},{3,1},{4,6},{5,7},{6,4},{7,5},{8,10},{9,11},{10,... | collective-permute-start | bytes 460808 | tf_op jit(solution)/shard_map/ppermute | solution.py:889
  318.6 14.2 %collective-permute-start.18 = (bf16[1,24,3200]{2,1,0:T(8,128)(2,1)}, bf16[1,24,3200]{2,1,0:T(8,128)(2,1)S(1)}, u32[]{:S(2)}, u32[]{:S(2)}) collective-permute-start(bf16[1,24,3200]{2,1,0:T(8,128)(2,1)} %sum_pieces.7.refs_0_), channel_id=1, source_target_pairs={{0,4},{1,5},{2,6},{3,7},{4,0},{5,1},{6,2},{7,3},{8,12},{9,13},{10,... | collective-permute-start | bytes 460808 | tf_op jit(solution)/shard_map/ppermute | solution.py:889
  321.0 11.8 %collective-permute-start.19 = (bf16[1,24,3200]{2,1,0:T(8,128)(2,1)}, bf16[1,24,3200]{2,1,0:T(8,128)(2,1)S(1)}, u32[]{:S(2)}, u32[]{:S(2)}) collective-permute-start(bf16[1,24,3200]{2,1,0:T(8,128)(2,1)} %sum_pieces.7.refs_0_), channel_id=1, source_target_pairs={{0,6},{1,7},{2,4},{3,5},{4,2},{5,3},{6,0},{7,1},{8,14},{9,15},{10,... | collective-permute-start | bytes 460808 | tf_op jit(solution)/shard_map/ppermute | solution.py:889
  336.1 17.1 %collective-permute-start.20 = (bf16[4,24,3200]{2,1,0:T(8,128)(2,1)}, bf16[4,24,3200]{2,1,0:T(8,128)(2,1)}, u32[]{:S(2)}, u32[]{:S(2)}) collective-permute-start(bf16[4,24,3200]{2,1,0:T(8,128)(2,1)} %stack_pieces.1.refs_0_), channel_id=1, source_target_pairs={{0,8},{8,0},{16,24},{24,16},{1,9},{9,1},{17,25},{25,17},{2,10},{10... | collective-permute-start | bytes 1843208 | tf_op jit(solution)/shard_map/ppermute | solution.py:889
  336.7 26.8 %collective-permute-start.21 = (bf16[4,24,3200]{2,1,0:T(8,128)(2,1)}, bf16[4,24,3200]{2,1,0:T(8,128)(2,1)}, u32[]{:S(2)}, u32[]{:S(2)}) collective-permute-start(bf16[4,24,3200]{2,1,0:T(8,128)(2,1)} %stack_pieces.1.refs_0_), channel_id=1, source_target_pairs={{0,16},{8,24},{16,0},{24,8},{1,17},{9,25},{17,1},{25,9},{2,18},{10... | collective-permute-start | bytes 1843208 | tf_op jit(solution)/shard_map/ppermute | solution.py:889
  337.4 26.1 %collective-permute-start.22 = (bf16[4,24,3200]{2,1,0:T(8,128)(2,1)}, bf16[4,24,3200]{2,1,0:T(8,128)(2,1)S(1)}, u32[]{:S(2)}, u32[]{:S(2)}) collective-permute-start(bf16[4,24,3200]{2,1,0:T(8,128)(2,1)} %stack_pieces.1.refs_0_), channel_id=1, source_target_pairs={{0,24},{8,16},{16,8},{24,0},{1,25},{9,17},{17,9},{25,1},{2,26},{10... | collective-permute-start | bytes 1843208 | tf_op jit(solution)/shard_map/ppermute | solution.py:889
  364.3 6.9 %collective-permute-start.23 = (bf16[4,24,3200]{2,1,0:T(8,128)(2,1)S(1)}, bf16[4,24,3200]{2,1,0:T(8,128)(2,1)S(1)}, u32[]{:S(2)}, u32[]{:S(2)}) collective-permute-start(bf16[4,24,3200]{2,1,0:T(8,128)(2,1)S(1)} %copy-done.13), channel_id=1, source_target_pairs={{0,1},{1,0},{2,3},{3,2},{4,5},{5,4},{6,7},{7,6},{8,9},{9,8},{10,11... | collective-permute-start | bytes 1843208 | tf_op jit(solution)/shard_map/ppermute | solution.py:1078
  364.3 6.9 %collective-permute-start.24 = (bf16[4,24,3200]{2,1,0:T(8,128)(2,1)}, bf16[4,24,3200]{2,1,0:T(8,128)(2,1)S(1)}, u32[]{:S(2)}, u32[]{:S(2)}) collective-permute-start(bf16[4,24,3200]{2,1,0:T(8,128)(2,1)} %collective-permute-done.20.refs_1_), channel_id=1, source_target_pairs={{0,1},{1,0},{2,3},{3,2},{4,5},{5,4},{6,7},{7,6},{8,9},{9,8},{10,11... | collective-permute-start | bytes 1843208 | tf_op jit(solution)/shard_map/ppermute | solution.py:1078
  (38 other events, 211.0 us)
Sparse Core Ops, SparseCore 0:
  182.0 41.9 reduce-scatter.4
  227.6 84.2 reduce-scatter.2
